TPU v7x, 32 devices: a whole 2x2x4 slice. The times are simulated.
32 devices in a mesh: rows: 4 (over x, core), filt: 8 (over z, y).
Axes of the slice: x: 2, y: 2, z: 4, core: 2. Of those that a mesh axis runs over, the one named last changes fastest.
Arguments:
- inputs: bfloat16 [1024, 16, 512], P('filt', 'rows'), may hold values from -6 to 6
- filters: float32 [24, 1024], replicated, may hold values from -0.1875 to 0.1875
- gain_in: float32 [512], replicated, may hold values from 0.5 to 1.5
- mixing: bfloat16 [48, 512, 512], P('filt'), may hold values from -0.0390625 to 0.0390625
- regression: bfloat16 [3, 512, 512], replicated, may hold values from -0.15625 to 0.15625
- gain_mid: float32 [512], replicated, may hold values from 0.5 to 1.5
- w_gate: bfloat16 [512, 2048], P(None, 'filt'), may hold values from -0.25 to 0.25
- w_up: bfloat16 [512, 2048], P(None, 'filt'), may hold values from -0.25 to 0.25
- w_down: bfloat16 [2048, 512], P('filt'), may hold values from -0.1875 to 0.1875
- out_grad: bfloat16 [1024, 16, 512], P('filt', 'rows'), may hold values from -6 to 6
Outputs:
- block_out: bfloat16 [1024, 16, 512], P('filt', 'rows')
- input_grad: float32 [1024, 16, 512], P('filt', 'rows')
- mixing_grad: float32 [48, 512, 512], P('filt')
- regression_grad: float32 [3, 512, 512], replicated
- gain_in_grad: float32 [512], replicated
- gain_mid_grad: float32 [512], replicated
- w_gate_grad: float32 [512, 2048], P(None, 'filt')
- w_up_grad: float32 [512, 2048], P(None, 'filt')
- w_down_grad: float32 [2048, 512], P('filt')
All inputs are finite; a program needn't handle non-finite values.
Results may differ from a plain program's by a relative error of at most 0.013.
Values may be sent and summed in bfloat16 or wider, within the bound.
No kernel may reach another device: no remote copies, remote signals or barrier semaphores. Data moves between devices by JAX's collectives and lax.ppermute only.
A program may use at most 256 MiB of HBM per device.

v0:
```python
import jax
import jax.numpy as jnp
from jax import lax
from jax.sharding import PartitionSpec as P

epsilon = 1e-05


def normalize(values, gain):
    factor = lax.rsqrt(jnp.mean(values * values, axis=-1, keepdims=True) + epsilon)
    normed = values * factor
    return (normed, factor, normed * gain)


def norm_backward(grad_out, normed, factor, gain):
    inner_grad = grad_out * gain
    return factor * (inner_grad - normed * jnp.mean(inner_grad * normed, axis=-1, keepdims=True))


def contract_rows(left, right):
    return lax.dot_general(
        left, right, (((0,), (0,)), ((), ())), preferred_element_type=jnp.float32
    )


def times_transpose(left, right):
    return lax.dot_general(
        left, right, (((1,), (1,)), ((), ())), preferred_element_type=jnp.float32
    )


def activation_grads(gate_pre, up_values, grad_hidden):
    sigmoid_value = jax.nn.sigmoid(gate_pre)
    slope = sigmoid_value * (1.0 + gate_pre * (1.0 - sigmoid_value))
    gate_back = (grad_hidden * up_values * slope).astype(jnp.bfloat16)
    up_back = (grad_hidden * gate_pre * sigmoid_value).astype(jnp.bfloat16)
    return (gate_back, up_back)


def upper_toeplitz(kernel_row):
    seq_length = kernel_row.shape[0]
    padded = jnp.concatenate([kernel_row, jnp.zeros((seq_length,), kernel_row.dtype)])
    tiled = jnp.tile(padded, seq_length)[: seq_length * (2 * seq_length - 1)]
    return tiled.reshape(seq_length, 2 * seq_length - 1)[:, :seq_length]


def kernel_matrix(filters, global_branch):
    seq_length = filters.shape[1]
    alternate = jnp.where(jnp.arange(seq_length) % 2 == 0, 1.0, -1.0).astype(jnp.float32)
    kernel_row = lax.dynamic_slice_in_dim(filters, global_branch // 2, 1, 0)[0]
    kernel_row = jnp.where(global_branch % 2 == 1, kernel_row * alternate, kernel_row)
    return upper_toeplitz(kernel_row.astype(jnp.bfloat16))


def shards(inputs, filters, gain_in, mixing, regression, gain_mid, w_gate, w_up, w_down, out_grad):
    shard_rows, local_seqs, model_width = inputs.shape
    group_count = lax.axis_size("filt")
    seq_length = shard_rows * group_count
    branches = mixing.shape[0]
    lag_count = regression.shape[0]
    row_width = local_seqs * model_width
    own_start = lax.axis_index("filt") * shard_rows
    residual = inputs.astype(jnp.float32)
    normed_in, factor_in, scaled_in = normalize(residual, gain_in)
    states = lax.all_gather(scaled_in.astype(jnp.bfloat16), "filt", axis=0, tiled=True)
    states_rows = states.reshape(seq_length * local_seqs, model_width)
    toeplitz = [
        kernel_matrix(filters, lax.axis_index("filt") * branches + branch)
        for branch in range(branches)
    ]
    projected = [
        jnp.dot(states_rows, mixing[branch], preferred_element_type=jnp.float32)
        .astype(jnp.bfloat16)
        .reshape(seq_length, row_width)
        for branch in range(branches)
    ]
    row_count = lax.axis_size("filt") * shard_rows
    summed = jnp.zeros((row_count, row_width), jnp.float32)
    for project_branch in range(branches):
        slab = toeplitz[project_branch]
        summed = summed + jnp.einsum(
            "ut,un->tn", slab, projected[project_branch], preferred_element_type=jnp.float32
        )
    spectral = lax.psum_scatter(
        summed.reshape(row_count, local_seqs, model_width), "filt", scatter_dimension=0, tiled=True
    )
    padded_states = jnp.concatenate(
        [jnp.zeros((lag_count - 1, local_seqs, model_width), jnp.bfloat16), states], axis=0
    )
    lagged = jnp.stack(
        [
            lax.dynamic_slice_in_dim(
                padded_states, own_start + lag_count - 1 - lag_index, shard_rows, 0
            )
            for lag_index in range(lag_count)
        ]
    )
    regress = jnp.einsum("itsd,ide->tse", lagged, regression, preferred_element_type=jnp.float32)
    middle = residual + spectral + regress
    normed_mid, factor_mid, scaled_mid = normalize(middle, gain_mid)
    middle_low = scaled_mid.astype(jnp.bfloat16)
    middle_all = lax.all_gather(middle_low, "filt", axis=0, tiled=True).reshape(
        seq_length * local_seqs, model_width
    )
    gate_pre = jnp.dot(middle_all, w_gate, preferred_element_type=jnp.float32)
    up_values = jnp.dot(middle_all, w_up, preferred_element_type=jnp.float32)
    hidden = (jax.nn.silu(gate_pre) * up_values).astype(jnp.bfloat16)
    hidden_rows = hidden.reshape(seq_length, local_seqs, hidden.shape[1])
    row_count = shard_rows * lax.axis_size("filt")
    slab = hidden_rows.reshape(row_count * local_seqs, -1)
    block_value = middle + lax.psum_scatter(
        jnp.dot(slab, w_down, preferred_element_type=jnp.float32)
        .reshape(row_count, local_seqs, model_width)
        .astype(jnp.bfloat16),
        "filt",
        scatter_dimension=0,
        tiled=True,
    ).astype(jnp.float32)
    grad_all = lax.all_gather(out_grad, "filt", axis=0, tiled=True).reshape(
        seq_length * local_seqs, model_width
    )
    down_partial = contract_rows(hidden, grad_all)
    grad_hidden = times_transpose(grad_all, w_down)
    gate_back, up_back = activation_grads(gate_pre, up_values, grad_hidden)
    gate_partial = contract_rows(middle_all, gate_back)
    up_partial = contract_rows(middle_all, up_back)
    gate_rows = gate_back.reshape(seq_length, local_seqs, -1)
    up_rows = up_back.reshape(seq_length, local_seqs, -1)
    row_count = lax.axis_size("filt") * shard_rows
    gate_slab = gate_rows.reshape(row_count * local_seqs, -1)
    up_slab = up_rows.reshape(row_count * local_seqs, -1)
    summed = times_transpose(gate_slab, w_gate) + times_transpose(up_slab, w_up)
    mid_back = lax.psum_scatter(
        summed.reshape(row_count, local_seqs, model_width), "filt", scatter_dimension=0, tiled=True
    )
    gain_mid_part = jnp.sum(mid_back * normed_mid, axis=(0, 1))
    middle_grad = out_grad.astype(jnp.float32) + norm_backward(
        mid_back, normed_mid, factor_mid, gain_mid
    )
    mix_back = middle_grad.astype(jnp.bfloat16)
    mix_all = lax.all_gather(mix_back, "filt", axis=0, tiled=True).reshape(seq_length, row_width)
    proj_back = [
        jnp.dot(toeplitz[branch], mix_all, preferred_element_type=jnp.float32).astype(jnp.bfloat16)
        for branch in range(branches)
    ]
    mixing_part = jnp.stack(
        [
            contract_rows(
                states_rows, proj_back[branch].reshape(seq_length * local_seqs, model_width)
            )
            for branch in range(branches)
        ]
    )
    lag_terms = jnp.einsum(
        "tse,ide->itsd", mix_back, regression, preferred_element_type=jnp.float32
    )
    regression_part = jnp.einsum(
        "itsd,tse->ide", lagged, mix_back, preferred_element_type=jnp.float32
    )
    spread = jnp.zeros((seq_length + lag_count - 1, local_seqs, model_width), jnp.float32)
    for lag_index in range(lag_count):
        begin = own_start + lag_count - 1 - lag_index
        current = lax.dynamic_slice_in_dim(spread, begin, shard_rows, 0)
        spread = lax.dynamic_update_slice_in_dim(spread, current + lag_terms[lag_index], begin, 0)
    spread = spread[lag_count - 1 :]
    row_count = lax.axis_size("filt") * shard_rows
    summed = spread.reshape(row_count * local_seqs, model_width)
    for branch in range(branches):
        slab = proj_back[branch]
        summed = summed + times_transpose(
            slab.reshape(row_count * local_seqs, model_width), mixing[branch]
        )
    state_back = lax.psum_scatter(
        summed.reshape(row_count, local_seqs, model_width), "filt", scatter_dimension=0, tiled=True
    )
    gain_in_part = jnp.sum(state_back * normed_in, axis=(0, 1))
    input_grad = middle_grad + norm_backward(state_back, normed_in, factor_in, gain_in)
    mixing_grad, w_gate_grad, w_up_grad, w_down_grad = (
        lax.psum(mixing_part.astype(jnp.bfloat16), "rows").astype(jnp.float32),
        lax.psum(gate_partial.astype(jnp.bfloat16), "rows").astype(jnp.float32),
        lax.psum(up_partial.astype(jnp.bfloat16), "rows").astype(jnp.float32),
        lax.psum(down_partial.astype(jnp.bfloat16), "rows").astype(jnp.float32),
    )
    regression_grad, gain_in_grad, gain_mid_grad = lax.psum(
        (regression_part, gain_in_part, gain_mid_part), ("rows", "filt")
    )
    return (
        block_value.astype(jnp.bfloat16),
        input_grad,
        mixing_grad,
        regression_grad,
        gain_in_grad,
        gain_mid_grad,
        w_gate_grad,
        w_up_grad,
        w_down_grad,
    )


def solution(mesh):
    placed = (
        P("filt", "rows", None),
        P(),
        P(),
        P("filt", None, None),
        P(),
        P(),
        P(None, "filt"),
        P(None, "filt"),
        P("filt", None),
        P("filt", "rows", None),
    )
    return jax.shard_map(
        shards,
        mesh=mesh,
        in_specs=placed,
        out_specs=(
            P("filt", "rows", None),
            P("filt", "rows", None),
            P("filt", None, None),
            P(),
            P(),
            P(),
            P(None, "filt"),
            P(None, "filt"),
            P("filt", None),
        ),
        check_vma=False,
    )
```

profile of v0, /device:TPU:0, one launch (start us, length us, event | category | flops | bytes accessed | tf_op | source)
XLA Modules:
  0.0 1469.2 jit_solution(7512996835774549502)
XLA Ops:
  17.1 10.8 reshape.145
  32.7 10.8 reshape.141
  48.4 10.7 reshape.136
  64.2 10.7 reshape.139
  79.6 10.7 reshape.147
  95.2 10.7 reshape.143
  149.2 7.6 reshape.148
  156.8 7.6 reshape.146
  164.4 7.7 reshape.144
  194.7 10.8 fusion.3
  233.1 24.2 %add_add_fusion.1 = f32[1024,2048]{1,0:T(8,128)} fusion(f32[1024,2048]{1,0:T(8,128)} %fusion.3, f32[1024,2048]{1,0:T(8,128)} %fusion.6, f32[1024,2048]{1,0:T(8,128)} %fusion.9, f32[1024,2048]{1,0:T(8,128)} %fusion.15, f32[1024,2048]{1,0:T(8,128)} %fusion.12, bf16[1024,2048]{1,0:T(8,128)(2,1)} %reshape.148, bf16[1024,2047]{1,0:T(8,128)(2,1)} %reshape.147), kind=kOutput, calls=%fused_computation.2 | convolution fusion | flops 4305453056 | bytes 56623104 | tf_op jit(solution)/shard_map/ut,un->tn/dot_general | solution.py:81
  257.3 8.0 copy.81
  269.0 148.6 %reduce-scatter.5.cloned.1.call-done = f32[128,4,512]{2,0,1:T(8,128)} async-done(((f32[1024,4,512]{2,0,1:T(8,128)}), f32[128,4,512]{2,0,1:T(8,128)}) %reduce-scatter.5.cloned.1.call-update) | async-done | bytes 1048592 | tf_op jit(solution)/shard_map/reduce_scatter | solution.py:84
  421.7 70.7 %all-gather.9.cloned.1.call-done = bf16[1024,4,512]{2,1,0:T(4,128)(2,1)} async-done(((bf16[128,4,512]{2,1,0:T(4,128)(2,1)}), bf16[1024,4,512]{2,1,0:T(4,128)(2,1)}) %all-gather.9.cloned.1.call-update) | async-done | bytes 4194320 | tf_op jit(solution)/shard_map/all_gather | solution.py:119
  499.7 67.2 %all-gather.7.cloned.1.call-done = bf16[1024,4,512]{2,0,1:T(8,128)(2,1)} async-done(((bf16[128,4,512]{2,0,1:T(8,128)(2,1)}), bf16[1024,4,512]{2,0,1:T(8,128)(2,1)}) %all-gather.7.cloned.1.call-update) | async-done | bytes 4194320 | tf_op jit(solution)/shard_map/all_gather | solution.py:102
  597.6 10.0 reshape.152
  607.6 9.4 copy.48
  617.0 147.7 %reduce-scatter.9.cloned.1.call-done = f32[128,4,512]{2,0,1:T(8,128)} async-done(((f32[1024,4,512]{2,0,1:T(8,128)}), f32[128,4,512]{2,0,1:T(8,128)}) %reduce-scatter.9.cloned.1.call-update) | async-done | bytes 1048592 | tf_op jit(solution)/shard_map/reduce_scatter | solution.py:133
  807.6 8.0 slice.109
  815.6 12.1 copy.51
  827.8 10.1 reshape.153
  848.8 9.5 convolution_convert_fusion.7
  940.9 7.7 reshape.156
  948.6 8.1 fusion.64
  990.3 22.8 %add_add_fusion = f32[4096,512]{1,0:T(8,128)} fusion(f32[4096,512]{1,0:T(8,128)} %fusion.55, f32[4096,512]{1,0:T(8,128)} %fusion.58, f32[4096,512]{1,0:T(8,128)} %fusion.61, f32[4096,512]{1,0:T(8,128)} %fusion.64, f32[4096,512]{1,0:T(8,128)} %reshape.153, f32[4096,512]{1,0:T(8,128)} %fusion.67, bf16[4096,512]{1,0:T(8,128)(2,1)} %reshape.160, ...), kind=kOutput, calls=%fused_computation.1 | convolution fusion | flops 2160066560 | bytes 63438848 | tf_op jit(solution)/shard_map/dot_general | solution.py:27
  1013.1 9.8 reshape.161
  1023.0 9.5 copy.53
  1054.7 15.8 %all-reduce.14.cloned.1.call-done = (bf16[6,512,512]{2,1,0:T(8,128)(2,1)}, bf16[512,256]{1,0:T(8,128)(2,1)}, bf16[512,256]{1,0:T(8,128)(2,1)}, bf16[256,512]{1,0:T(8,128)(2,1)}) async-done(((bf16[6,512,512]{2,1,0:T(8,128)(2,1)}, bf16[512,256]{1,0:T(8,128)(2,1)}, bf16[512,256]{1,0:T(8,128)(2,1)}, bf16[256,512]{1,0:T(8,128)(2,1)}), (bf16[6,512,512]{2,1,0:T(8,128)(2,1)}, bf16[512,256]{1,0:T(8,128)(2,1)}, ...) | async-done | bytes 3932176 | tf_op jit(solution)/shard_map/psum | solution.py:179
  1081.5 142.1 %reduce-scatter.11.cloned.1.call-done = f32[128,4,512]{2,0,1:T(8,128)} async-done(((f32[1024,4,512]{2,0,1:T(8,128)}), f32[128,4,512]{2,0,1:T(8,128)}) %reduce-scatter.11.cloned.1.call-update) | async-done | bytes 1048592 | tf_op jit(solution)/shard_map/reduce_scatter | solution.py:173
  1225.3 89.7 %reduce-scatter.7.cloned.1.call-done = bf16[128,4,512]{2,0,1:T(8,128)(2,1)} async-done(((bf16[1024,4,512]{2,0,1:T(8,128)(2,1)}), bf16[128,4,512]{2,0,1:T(8,128)(2,1)}) %reduce-scatter.7.cloned.1.call-update) | async-done | bytes 524304 | tf_op jit(solution)/shard_map/reduce_scatter | solution.py:111
  1319.9 40.7 %all-reduce.7 = (f32[512]{0:T(512)}, f32[512]{0:T(512)}) all-reduce(f32[512]{0:T(512)S(1)} %get-tuple-element.38, f32[512]{0:T(512)S(1)} %copy-done.59), channel_id=1, replica_groups=mesh['rows'=4,'filt'=8] {'rows','filt'}, use_global_device_ids=true, to_apply=%region_11.12 | all-reduce | flops 1024 | bytes 8192 | tf_op jit(solution)/shard_map/psum | solution.py:184
  1360.6 97.4 %all-reduce.12.cloned.1.call-done = f32[3,512,512]{2,1,0:T(8,128)} async-done(((f32[3,512,512]{2,1,0:T(8,128)}), f32[3,512,512]{2,1,0:T(8,128)}) %all-reduce.12.cloned.1.call-update) | async-done | bytes 3145744 | tf_op jit(solution)/shard_map/psum | solution.py:184
  (249 shorter events, 386.3 us)
Async XLA Ops:
  7.2 410.4 %copy-start = (bf16[3,512,512]{2,1,0:T(8,128)(2,1)S(1)}, bf16[3,512,512]{2,1,0:T(8,128)(2,1)}, u32[]{:S(2)}) copy-start(bf16[3,512,512]{2,1,0:T(8,128)(2,1)} %param.14) | copy-start | bytes 4718596
  7.2 98.7 %all-gather.5.cloned.1.call-start = ((), (), s32[]{:S(2)}) async-start(), calls=%async_computation.4 | async-start | bytes 4718592 | tf_op jit(solution)/shard_map/all_gather | solution.py:65
  11.2 406.3 %reduce-scatter.5.cloned.1.call-start = ((), (), s32[]{:S(2)}) async-start(), calls=%async_computation.5 | async-start | bytes 9437184 | tf_op jit(solution)/shard_map/reduce_scatter | solution.py:84
  194.7 10.9 copy-start.29
  194.7 10.9 copy-start.35
  265.3 152.3 %copy-start.14 = (bf16[128,4,512]{2,1,0:T(4,128)(2,1)S(1)}, bf16[128,4,512]{2,1,0:T(4,128)(2,1)}, u32[]{:S(2)}) copy-start(bf16[128,4,512]{2,1,0:T(4,128)(2,1)} %param.10) | copy-start | bytes 1572868
  265.3 227.0 %all-gather.9.cloned.1.call-start = ((), (), s32[]{:S(2)}) async-start(), calls=%async_computation.8 | async-start | bytes 4718592 | tf_op jit(solution)/shard_map/all_gather | solution.py:119
  266.1 300.8 %all-gather.7.cloned.1.call-start = ((), (), s32[]{:S(2)}) async-start(), calls=%async_computation.6 | async-start | bytes 4718592 | tf_op jit(solution)/shard_map/all_gather | solution.py:102
  420.5 346.5 %copy-start.9 = (f32[128,4,512]{2,0,1:T(8,128)}, f32[128,4,512]{2,0,1:T(8,128)S(1)}, u32[]{:S(2)}) copy-start(f32[128,4,512]{2,0,1:T(8,128)S(1)} %get-tuple-element.61) | copy-start | bytes 3145732
  420.5 346.4 %copy-start.50 = (f32[128,4]{0,1:T(4,128)}, f32[128,4]{0,1:T(4,128)S(1)}, u32[]{:S(2)}) copy-start(f32[128,4]{0,1:T(4,128)S(1)} %add_rsqrt_fusion) | copy-start | bytes 6148
  421.6 343.1 %reduce-scatter.9.cloned.1.call-start = ((), (), s32[]{:S(2)}) async-start(), calls=%async_computation.9 | async-start | bytes 9437184 | tf_op jit(solution)/shard_map/reduce_scatter | solution.py:133
  617.0 150.5 %copy-start.20 = (bf16[128,4,512]{2,1,0:T(4,128)(2,1)S(1)}, bf16[128,4,512]{2,1,0:T(4,128)(2,1)}, u32[]{:S(2)}) copy-start(bf16[128,4,512]{2,1,0:T(4,128)(2,1)} %param.19) | copy-start | bytes 1572868
  617.0 225.4 %all-gather.11.cloned.1.call-start = ((), (), s32[]{:S(2)}) async-start(), calls=%async_computation.10 | async-start | bytes 4718592 | tf_op jit(solution)/shard_map/all_gather | solution.py:141
  769.9 300.6 %all-reduce.14.cloned.1.call-start = ((), (), s32[]{:S(2)}) async-start(), calls=%async_computation.13 | async-start | bytes 7864320 | tf_op jit(solution)/shard_map/psum | solution.py:179
  848.8 9.5 copy-start.22
  848.8 9.5 copy-start.34
  948.6 8.2 copy-start.7
  948.6 8.2 copy-start.32
  990.3 233.4 %reduce-scatter.11.cloned.1.call-start = ((), (), s32[]{:S(2)}) async-start(), calls=%async_computation.11 | async-start | bytes 9437184 | tf_op jit(solution)/shard_map/reduce_scatter | solution.py:173
  1032.5 282.5 %reduce-scatter.7.cloned.1.call-start = ((), (), s32[]{:S(2)}) async-start(), calls=%async_computation.7 | async-start | bytes 4718592 | tf_op jit(solution)/shard_map/reduce_scatter | solution.py:111
  1050.5 407.6 %all-reduce.12.cloned.1.call-start = ((), (), s32[]{:S(2)}) async-start(), calls=%async_computation.12 | async-start | bytes 6291456 | tf_op jit(solution)/shard_map/psum | solution.py:184
  1075.8 147.8 %copy-start.15 = (bf16[128,4,512]{2,1,0:T(4,128)(2,1)S(1)}, bf16[128,4,512]{2,1,0:T(4,128)(2,1)}, u32[]{:S(2)}) copy-start(bf16[128,4,512]{2,1,0:T(4,128)(2,1)} %param.10) | copy-start | bytes 1572868
  1075.8 147.8 %copy-start.53 = (f32[128,4]{0,1:T(4,128)S(1)}, f32[128,4]{0,1:T(4,128)}, u32[]{:S(2)}) copy-start(f32[128,4]{0,1:T(4,128)} %copy-done.52) | copy-start | bytes 6148
  1075.8 147.8 %copy-start.56 = (f32[512]{0:T(512)S(1)}, f32[512]{0:T(512)}, u32[]{:S(2)}) copy-start(f32[512]{0:T(512)} %param.12) | copy-start | bytes 6148
  1075.8 239.2 %copy-start.10 = (f32[128,4,512]{2,0,1:T(8,128)S(1)}, f32[128,4,512]{2,0,1:T(8,128)}, u32[]{:S(2)}) copy-start(f32[128,4,512]{2,0,1:T(8,128)} %copy-done.9) | copy-start | bytes 3145732
  1075.8 239.2 %copy-start.13 = (f32[128,4,512]{2,0,1:T(8,128)S(1)}, f32[128,4,512]{2,0,1:T(8,128)}, u32[]{:S(2)}) copy-start(f32[128,4,512]{2,0,1:T(8,128)} %reduce-scatter.9.cloned.1.call-done) | copy-start | bytes 3145732
  1075.8 239.2 %copy-start.21 = (bf16[128,4,512]{2,1,0:T(4,128)(2,1)S(1)}, bf16[128,4,512]{2,1,0:T(4,128)(2,1)}, u32[]{:S(2)}) copy-start(bf16[128,4,512]{2,1,0:T(4,128)(2,1)} %param.19) | copy-start | bytes 1572868
  1075.9 239.2 %copy-start.51 = (f32[128,4]{0,1:T(4,128)S(1)}, f32[128,4]{0,1:T(4,128)}, u32[]{:S(2)}) copy-start(f32[128,4]{0,1:T(4,128)} %copy-done.50) | copy-start | bytes 6148
  1075.9 239.2 %copy-start.55 = (f32[512]{0:T(512)S(1)}, f32[512]{0:T(512)}, u32[]{:S(2)}) copy-start(f32[512]{0:T(512)} %param.15) | copy-start | bytes 6148
  1075.9 239.2 %copy-start.58 = (f32[128,4]{0,1:T(4,128)S(1)}, f32[128,4]{0,1:T(4,128)}, u32[]{:S(2)}) copy-start(f32[128,4]{0,1:T(4,128)} %copy-done.57) | copy-start | bytes 6148
  1225.3 94.6 %copy-start.59 = (f32[512]{0:T(512)S(1)}, f32[512]{0:T(512)}, u32[]{:S(2)}) copy-start(f32[512]{0:T(512)} %get-tuple-element.36) | copy-start | bytes 6148
  1317.0 144.9 %copy-start.1 = (bf16[3,512,512]{2,1,0:T(8,128)(2,1)S(1)}, bf16[3,512,512]{2,1,0:T(8,128)(2,1)}, u32[]{:S(2)}) copy-start(bf16[3,512,512]{2,1,0:T(8,128)(2,1)} %param.14) | copy-start | bytes 4718596
  (38 other events, 149.8 us)
Sparse Core Ops, SparseCore 0:
  11.4 76.0 all-gather.4
  265.4 152.1 reduce-scatter.4
  419.9 72.3 all-gather.8
  495.2 71.6 all-gather.6
  617.1 147.6 reduce-scatter.8
  770.0 72.3 all-gather.10
  990.4 80.0 all-reduce.13
  1074.1 149.5 reduce-scatter.10
  1227.7 87.2 reduce-scatter.6
  1320.3 137.7 all-reduce.11
where the time goes:
time: 1480 us; the launch traced here: 1470 us
  waiting for transfers between devices  785 us (53%)
  local copies, waits for them, and re-layouts  356 us (24%)
  matrix products  245 us (17%)
  blocking collectives  40.7 us (3%)
  other arithmetic  27.2 us (2%)
  between operations  15.4 us (1%)
    reduce_scatter x3, waiting for transfers between devices, shards(): lax.psum_scatter(summed.reshape(row_count, local_seqs, model_width), 'fil...  438 us
    psum x1, waiting for transfers between devices, shards(): lax.psum((regression_part, gain_in_part, gain_mid_part), ('rows', 'filt'))  97.4 us
    reduce_scatter x1, waiting for transfers between devices, shards(): lax.psum_scatter(jnp.dot(slab, w_down, preferred_element_type=jnp.float32...  89.7 us
    all_gather x1, waiting for transfers between devices, shards(): lax.all_gather(out_grad, 'filt', axis=0, tiled=True)  70.7 us
    all_gather x1, waiting for transfers between devices, shards(): lax.all_gather(middle_low, 'filt', axis=0, tiled=True)  67.2 us
    dot_general x9, matrix products, times_transpose(): lax.dot_general(left, right, (((1,), (1,)), ((), ())), preferred_element_...  65.2 us
    reshape x6, local copies, waits for them, and re-layouts, upper_toeplitz(): return tiled.reshape(seq_length, 2 * seq_length - 1)[:, :seq_length]  64.4 us
    dot_general x6, matrix products, shards(): jnp.einsum('ut,un->tn', slab, projected[project_branch], preferred_elemen...  62.5 us
  transfers between devices with their start and end apart: 10, of which 9 were waited for; matrix products, arithmetic and copies ran while one was open for 17% of the time, Pallas kernels for 0%

commit v1 on v0

v1 whole, which is shorter than its diff:
```python
import functools

import jax
import jax.numpy as jnp
from jax import lax
from jax.experimental import pallas as pl
from jax.experimental.pallas import tpu as pltpu
from jax.sharding import PartitionSpec as P

EPSILON = 1e-05
CHUNKS = 2
F32 = jnp.float32
BF16 = jnp.bfloat16


def dot(left, right):
    return jnp.dot(left, right, preferred_element_type=F32)


def contract_rows(left, right):
    return lax.dot_general(left, right, (((0,), (0,)), ((), ())), preferred_element_type=F32)


def times_transpose(left, right):
    return lax.dot_general(left, right, (((1,), (1,)), ((), ())), preferred_element_type=F32)


def rms_factor(values):
    return lax.rsqrt(jnp.mean(values * values, axis=-1, keepdims=True) + EPSILON)


def norm_backward(grad_out, normed, factor, gain):
    inner = grad_out * gain
    return factor * (inner - normed * jnp.mean(inner * normed, axis=-1, keepdims=True))


class Grid:
    def __init__(self, size):
        self.far = 4 if size % 4 == 0 else 1
        self.near = size // self.far
        self.size = size

    def shift(self, far_step, near_step):
        far, near = self.far, self.near
        return [
            (f, ((f // near + far_step) % far) * near + (f % near + near_step) % near)
            for f in range(self.size)
        ]

    def order(self, index, sign):
        far, near = self.far, self.near
        steps = jnp.arange(self.size, dtype=jnp.int32)
        return (
            lax.rem(index // near + sign * (steps // near) + far, far) * near
            + lax.rem(index % near + sign * (steps % near) + near, near)
        ).astype(jnp.int32)


def spread_pieces(grid, own):
    columns = [own] + [
        lax.ppermute(own, "filt", grid.shift(i, 0)) for i in range(1, grid.far)
    ]
    pieces = []
    for column in columns:
        pieces.append(column)
        for j in range(1, grid.near):
            pieces.append(lax.ppermute(column, "filt", grid.shift(0, j)))
    return pieces


def sum_pieces(grid, pieces):
    columns = []
    for i in range(grid.far):
        total = pieces[i * grid.near].astype(F32)
        for j in range(1, grid.near):
            total = total + lax.ppermute(
                pieces[i * grid.near + j], "filt", grid.shift(0, j)
            ).astype(F32)
        columns.append(total)
    total = columns[0]
    for i in range(1, grid.far):
        total = total + lax.ppermute(
            columns[i].astype(BF16), "filt", grid.shift(i, 0)
        ).astype(F32)
    return total


def swap_rows(values, bit):
    count = lax.axis_size("rows")
    return lax.ppermute(values, "rows", [(r, r ^ bit) for r in range(count)])


def row_bits():
    count = lax.axis_size("rows")
    return [1 << n for n in range(count.bit_length() - 1)]


def all_reduce_rows(partial):
    index = lax.axis_index("rows")
    kept = partial
    for bit in row_bits():
        parts, height, width = kept.shape
        halves = kept.reshape(parts, 2, height // 2, width)
        high = (index & bit) != 0
        away = jnp.where(high, halves[:, 0], halves[:, 1]).astype(BF16)
        stay = jnp.where(high, halves[:, 1], halves[:, 0])
        kept = stay + swap_rows(away, bit).astype(F32)
    full = kept.astype(BF16)
    for bit in reversed(row_bits()):
        high = (index & bit) != 0
        other = swap_rows(full, bit)
        full = jnp.concatenate(
            [jnp.where(high, other, full), jnp.where(high, full, other)], axis=1
        )
    return full.astype(F32)


def toeplitz_kernel(half, down_ref, up_ref, t00_ref, t10_ref, u00_ref, u10_ref):
    width = down_ref.shape[-1]
    down = jnp.broadcast_to(down_ref[0], (half, width))
    block = pltpu.roll(down, 0, axis=1, stride=1, stride_axis=0)
    t10_ref[0] = block[:, :half].astype(BF16)
    t00_ref[0] = block[:, half : 2 * half].astype(BF16)
    up = jnp.broadcast_to(up_ref[0], (half, width))
    block = pltpu.roll(up, 0, axis=1, stride=1, stride_axis=0)
    u00_ref[0] = block[:, :half].astype(BF16)
    u10_ref[0] = block[:, half : 2 * half].astype(BF16)


def toeplitz_blocks(filters, first, count):
    seq_length = filters.shape[1]
    half = seq_length // 4
    taps = lax.dynamic_slice_in_dim(
        jnp.pad(filters, ((0, 1), (0, 0))), first, count, 0
    ).astype(BF16).astype(F32)
    taps = taps.reshape(count, seq_length // 2, 2)
    even, odd = taps[:, :, 0], taps[:, :, 1]
    late = jnp.concatenate([jnp.zeros_like(odd[:, :1]), odd[:, :-1]], axis=1)
    rows = jnp.stack([jnp.stack([even, late], 1), jnp.stack([even, odd], 1)], 0)
    rows = rows.reshape(4 * count, seq_length // 2)
    zeros = jnp.zeros_like(rows)
    reverse = rows[:, ::-1]
    down = jnp.concatenate(
        [
            reverse[:, half - 1 :],
            zeros[:, : half - 1],
            zeros[:, : half + 1],
            reverse[:, : half - 1],
        ],
        axis=1,
    )
    up = jnp.concatenate([rows, zeros], axis=1)
    total = 4 * count
    by_column = pl.BlockSpec((1, half, half), lambda n: (n // (2 * count), 0, n % (2 * count)))
    by_row = pl.BlockSpec((1, half, half), lambda n: (n // (2 * count), n % (2 * count), 0))
    line = pl.BlockSpec((1, 1, 4 * half), lambda n: (n, 0, 0))
    wide = jax.ShapeDtypeStruct((2, half, 2 * count * half), BF16)
    tall = jax.ShapeDtypeStruct((2, 2 * count * half, half), BF16)
    return pl.pallas_call(
        functools.partial(toeplitz_kernel, half),
        grid=(total,),
        in_specs=[line, line],
        out_specs=[by_column, by_column, by_row, by_row],
        out_shape=[wide, wide, tall, tall],
        name="toeplitz",
    )(down[:, None], up[:, None])


def assemble(order_ref, pieces, whole_ref):
    length = whole_ref.shape[0] // 2
    height = pieces[0].shape[2]
    for n, piece in enumerate(pieces):
        start = order_ref[n] * height
        for parity in range(2):
            place = pl.multiple_of(parity * length + start, height)
            whole_ref[pl.ds(place, height), :] = piece[0, parity]


def scatter(order_ref, whole_ref, pieces):
    length = whole_ref.shape[0] // 2
    height = pieces[0].shape[2]
    for n, piece in enumerate(pieces):
        start = order_ref[n] * height
        for parity in range(2):
            place = pl.multiple_of(parity * length + start, height)
            piece[0, parity] = whole_ref[pl.ds(place, height), :].astype(piece.dtype)


def mix_kernel(parts, from_ref, to_ref, *refs):
    pieces = refs[:parts]
    mix_ref, t00_ref, t10_ref = refs[parts : parts + 3]
    outs = refs[parts + 3 : 2 * parts + 3]
    states_ref, low_ref, high_ref, sum_ref = refs[2 * parts + 3 :]
    half = t00_ref.shape[1]
    branches = mix_ref.shape[0]
    assemble(from_ref, pieces, states_ref)

    for branch in range(branches):
        slot = pl.ds(branch * half, half)
        for quarter in range(4):
            value = dot(
                states_ref[pl.ds(quarter * half, half), :], mix_ref[branch]
            ).astype(BF16)
            target = (quarter // 2) ^ (branch % 2)
            (low_ref, high_ref)[quarter % 2][target, slot, :] = value

    for parity in range(2):
        base = 2 * parity * half
        sum_ref[pl.ds(base, half), :] = dot(t00_ref[parity], low_ref[parity]).astype(
            sum_ref.dtype
        )
        sum_ref[pl.ds(base + half, half), :] = (
            dot(t10_ref[parity], low_ref[parity]) + dot(t00_ref[parity], high_ref[parity])
        ).astype(sum_ref.dtype)
    scatter(to_ref, sum_ref, outs)


def mix_back_kernel(parts, from_ref, to_ref, own_ref, *refs):
    state_pieces = refs[:parts]
    grad_pieces = refs[parts : 2 * parts]
    turned_ref, u00_ref, u10_ref, before_ref, before_lag_ref = refs[2 * parts : 2 * parts + 5]
    outs = refs[2 * parts + 5 : 3 * parts + 5]
    mixing_ref, lag_ref = refs[3 * parts + 5 : 3 * parts + 7]
    states_ref, grad_ref, flip_ref, back_ref, sum_ref = refs[3 * parts + 7 :]
    half = u00_ref.shape[2]
    branches = mixing_ref.shape[0]
    width = grad_ref.shape[1]
    length = states_ref.shape[0] // 2

    @pl.when(pl.program_id(0) == 0)
    def _():
        mixing_ref[...] = before_ref[...]
        lag_ref[...] = before_lag_ref[...]

    assemble(from_ref, state_pieces, states_ref)
    assemble(from_ref, grad_pieces, grad_ref)
    flip_ref[...] = states_ref[...].T

    for parity in range(2):
        base = 2 * parity * half
        low = grad_ref[pl.ds(base, half), :]
        high = grad_ref[pl.ds(base + half, half), :]
        for branch in range(branches):
            rows = pl.ds(branch * half, half)
            columns = pl.ds(branch * width, width)
            target = 2 * half * (parity ^ (branch % 2))
            back_ref[pl.ds(target, half), columns] = (
                dot(u00_ref[parity, rows, :], low) + dot(u10_ref[parity, rows, :], high)
            ).astype(BF16)
            back_ref[pl.ds(target + half, half), columns] = dot(
                u00_ref[parity, rows, :], high
            ).astype(BF16)

    for quarter in range(4):
        rows = pl.ds(quarter * half, half)
        sum_ref[rows, :] = dot(back_ref[rows, :], turned_ref[...]).astype(sum_ref.dtype)
    scatter(to_ref, sum_ref, outs)

    for branch in range(branches):
        columns = pl.ds(branch * width, width)
        mixing_ref[branch] += dot(flip_ref[...], back_ref[:, columns])

    slab = lag_ref.shape[1]
    start = pl.multiple_of(own_ref[0] * slab, slab)
    own = flip_ref[pl.ds(start, slab), :].astype(F32)
    even, odd = own[:, :length], own[:, length:]
    first = lax.broadcasted_iota(jnp.int32, even.shape, 1) == 0
    even_late = jnp.where(first, 0.0, pltpu.roll(even, 1, axis=1))
    odd_late = jnp.where(first, 0.0, pltpu.roll(odd, 1, axis=1))
    for lag, (on_even, on_odd) in enumerate(
        ((even, odd), (odd_late, even), (even_late, odd_late))
    ):
        lag_ref[lag] += dot(on_even.astype(BF16), grad_ref[:length, :]) + dot(
            on_odd.astype(BF16), grad_ref[length:, :]
        )


def resident(shape):
    zeros = (0,) * len(shape)
    return pl.BlockSpec(shape, lambda *_: zeros, pipeline_mode=pl.Buffered(1))


def mix_sequences(pieces, order_from, order_to, pairs, t00, t10):
    parts = len(pieces)
    count, _, height, width = pieces[0].shape
    half = t00.shape[1]
    block = pl.BlockSpec((1, 2, height, width), lambda n, *_: (n, 0, 0, 0))
    rows = t00.shape[2]
    return pl.pallas_call(
        functools.partial(mix_kernel, parts),
        grid_spec=pltpu.PrefetchScalarGridSpec(
            num_scalar_prefetch=2,
            grid=(count,),
            in_specs=[block] * parts
            + [resident(pairs.shape), resident(t00.shape), resident(t10.shape)],
            out_specs=[block] * parts,
            scratch_shapes=[
                pltpu.VMEM((4 * half, width), BF16),
                pltpu.VMEM((2, rows, width), BF16),
                pltpu.VMEM((2, rows, width), BF16),
                pltpu.VMEM((4 * half, width), F32),
            ],
        ),
        out_shape=[jax.ShapeDtypeStruct(pieces[0].shape, BF16)] * parts,
        compiler_params=pltpu.CompilerParams(vmem_limit_bytes=48 << 20),
        cost_estimate=pl.CostEstimate(
            flops=count * (8 * half * width * pairs.shape[0] * width + 12 * half * rows * width),
            bytes_accessed=2 * parts * pieces[0].size * 2 + 2 * pairs.size + 4 * t00.size,
            transcendentals=0,
        ),
        name="mix",
    )(order_from, order_to, *pieces, pairs, t00, t10)


def mix_sequences_back(
    states, grads, order_from, order_to, own, turned, u00, u10, before, before_lag
):
    parts = len(states)
    count, _, height, width = states[0].shape
    half = u00.shape[2]
    block = pl.BlockSpec((1, 2, height, width), lambda n, *_: (n, 0, 0, 0))
    rows = u00.shape[1]
    return pl.pallas_call(
        functools.partial(mix_back_kernel, parts),
        grid_spec=pltpu.PrefetchScalarGridSpec(
            num_scalar_prefetch=3,
            grid=(count,),
            in_specs=[block] * (2 * parts)
            + [resident(a.shape) for a in (turned, u00, u10, before, before_lag)],
            out_specs=[block] * parts + [resident(before.shape), resident(before_lag.shape)],
            scratch_shapes=[
                pltpu.VMEM((4 * half, width), BF16),
                pltpu.VMEM((4 * half, width), BF16),
                pltpu.VMEM((width, 4 * half), BF16),
                pltpu.VMEM((4 * half, turned.shape[0]), BF16),
                pltpu.VMEM((4 * half, width), F32),
            ],
        ),
        out_shape=[jax.ShapeDtypeStruct(states[0].shape, BF16)] * parts
        + [
            jax.ShapeDtypeStruct(before.shape, F32),
            jax.ShapeDtypeStruct(before_lag.shape, F32),
        ],
        compiler_params=pltpu.CompilerParams(vmem_limit_bytes=56 << 20),
        cost_estimate=pl.CostEstimate(
            flops=count * (16 * half * width * turned.shape[0] + 12 * half * rows * width),
            bytes_accessed=3 * parts * states[0].size * 2 + 2 * turned.size + 8 * before.size,
            transcendentals=0,
        ),
        name="mix_back",
    )(order_from, order_to, own, *states, *grads, turned, u00, u10, before, before_lag)


def lagged(values, edge):
    late = jnp.concatenate([edge, values[:, :, :-1]], axis=2)
    return values, jnp.stack([late[:, 1], values[:, 0]], axis=1), late


def leading(values, edge):
    early = jnp.concatenate([values[:, :, 1:], edge], axis=2)
    return values, jnp.stack([values[:, 1], early[:, 0]], axis=1), early


def row_masks():
    masks = [0]
    for bit in reversed(row_bits()):
        masks = masks + [mask ^ bit for mask in masks]
    return masks


def spread_rows(own):
    full = own[None]
    for bit in reversed(row_bits()):
        full = jnp.concatenate([full, swap_rows(full, bit)], axis=0)
    return full


def shards(inputs, filters, gain_in, mixing, regression, gain_mid, w_gate, w_up, w_down, out_grad):
    shard_rows, local_seqs, width = inputs.shape
    grid = Grid(lax.axis_size("filt"))
    row_count = lax.axis_size("rows")
    index = lax.axis_index("filt")
    branches = mixing.shape[0]
    lag_count = regression.shape[0]
    height = shard_rows // 2
    chunks = CHUNKS
    step = local_seqs // chunks

    def inward(values):
        return values.reshape(height, 2, local_seqs, width).transpose(2, 1, 0, 3)

    def outward(values):
        return values.transpose(2, 1, 0, 3).reshape(shard_rows, local_seqs, width)

    def cut(values):
        return [values[c * step : (c + 1) * step] for c in range(chunks)]

    residual = inward(inputs).astype(F32)
    cotangent_low = inward(out_grad)
    factor_in = rms_factor(residual)
    normed_in = residual * factor_in
    states = (normed_in * gain_in).astype(BF16)
    state_pieces = [spread_pieces(grid, part) for part in cut(states)]

    hidden_own = w_down.shape[0]
    share = hidden_own // row_count
    packed = jnp.stack([w_gate.T, w_up.T, w_down]).reshape(3, row_count, share, width)
    own_share = lax.dynamic_index_in_dim(packed, lax.axis_index("rows"), 1, keepdims=False)
    shares = jnp.stack(spread_pieces(grid, own_share), axis=1)
    weights = spread_rows(shares)
    gate_t, up_t, down = (
        weights[:, n].reshape(row_count * grid.size * share, width) for n in range(3)
    )

    slots = (branches + 1) // 2
    first_branch = index * branches
    t00, t10, u00, u10 = toeplitz_blocks(filters, first_branch // 2, slots)
    if branches % 2:
        odd_start = first_branch % 2
        paired = lax.dynamic_update_slice_in_dim(
            jnp.zeros((2 * slots,) + mixing.shape[1:], mixing.dtype), mixing, odd_start, 0
        )
    else:
        paired = mixing
    paired = paired.astype(F32).reshape(slots, 2, width, width)
    pairs = (
        jnp.stack([paired[:, 0] + paired[:, 1], paired[:, 0] - paired[:, 1]], axis=1)
        .astype(BF16)
        .reshape(2 * slots, width, width)
    )
    turned = pairs.transpose(0, 2, 1).reshape(2 * slots * width, width)

    order_from, order_to = grid.order(index, -1), grid.order(index, 1)

    edge = lax.ppermute(
        states[:, :, -1:], "filt", [(f, f + 1) for f in range(grid.size - 1)]
    )
    regress = sum(
        jnp.einsum("spad,de->spae", lag, regression[n], preferred_element_type=F32)
        for n, lag in enumerate(lagged(states, edge))
    )
    cotangent = cotangent_low.astype(F32)

    spectral = []
    for c in range(chunks):
        partial = mix_sequences(state_pieces[c], order_from, order_to, pairs, t00, t10)
        spectral.append(sum_pieces(grid, partial))

    block_out, middle_grad, grad_pieces, kept = [], [], [], []
    gain_mid_part = jnp.zeros((width,), F32)
    for c in range(chunks):
        part = slice(c * step, (c + 1) * step)
        middle = residual[part] + (spectral[c] + regress[part])
        factor_mid = rms_factor(middle)
        normed_mid = middle * factor_mid
        scaled = (normed_mid * gain_mid).astype(BF16).reshape(-1, width)
        cot_low = cotangent_low[part].reshape(-1, width)
        gate_pre = times_transpose(scaled, gate_t)
        up_values = times_transpose(scaled, up_t)
        sigmoid = jax.nn.sigmoid(gate_pre)
        silu = gate_pre * sigmoid
        hidden = (silu * up_values).astype(BF16)
        block_out.append(
            (middle + dot(hidden, down).reshape(middle.shape)).astype(BF16)
        )
        grad_hidden = times_transpose(cot_low, down)
        gate_back = (
            grad_hidden * up_values * (sigmoid * (1.0 + gate_pre * (1.0 - sigmoid)))
        ).astype(BF16)
        up_back = (grad_hidden * silu).astype(BF16)
        mid_back = (dot(gate_back, gate_t) + dot(up_back, up_t)).reshape(middle.shape)
        gain_mid_part = gain_mid_part + jnp.sum(mid_back * normed_mid, axis=(0, 1, 2))
        grad = cotangent[part] + norm_backward(mid_back, normed_mid, factor_mid, gain_mid)
        middle_grad.append(grad)
        grad_pieces.append(spread_pieces(grid, grad.astype(BF16)))
        kept.append((scaled, cot_low, hidden, gate_back, up_back))

    scaled, cot_low, hidden, gate_back, up_back = (
        jnp.concatenate(values, axis=0) for values in zip(*kept, strict=True)
    )
    grads = jnp.stack(
        [
            contract_rows(gate_back, scaled),
            contract_rows(up_back, scaled),
            contract_rows(hidden, cot_low),
        ]
    ).reshape(3, row_count, grid.size, share, width)
    for bit in row_bits():
        half_count = grads.shape[1] // 2
        grads = grads[:, :half_count] + swap_rows(
            grads[:, half_count:].astype(BF16), bit
        ).astype(F32)
    grads = grads[:, 0].astype(BF16)
    returning = []
    for i in range(grid.far):
        for j in range(grid.near):
            n = ((grid.far - i) % grid.far) * grid.near + (grid.near - j) % grid.near
            returning.append(grads[:, n])
    own_grads = sum_pieces(grid, returning).astype(BF16)

    before = jnp.zeros((2 * slots, width, width), F32)
    before_lag = jnp.zeros((lag_count, width // grid.size, width), F32)
    own = jnp.reshape(index, (1,)).astype(jnp.int32)
    state_back = []
    for c in range(chunks):
        *partial, before, before_lag = mix_sequences_back(
            state_pieces[c], grad_pieces[c], order_from, order_to, own, turned, u00, u10,
            before, before_lag,
        )
        state_back.append(sum_pieces(grid, partial))

    doubled = before.reshape(slots, 2, width, width)
    mixing_part = jnp.stack(
        [doubled[:, 0] + doubled[:, 1], doubled[:, 0] - doubled[:, 1]], axis=1
    ).reshape(2 * slots, width, width)
    if branches % 2:
        mixing_part = lax.dynamic_slice_in_dim(mixing_part, odd_start, branches, 0)
    mixing_grad = all_reduce_rows(mixing_part)

    slab = width // grid.size
    own_regression = lax.dynamic_slice_in_dim(regression, index * slab, slab, 1)
    gain_lag = jnp.sum(own_regression.astype(F32) * before_lag, axis=(0, 2))
    gain_in_part = jnp.sum(mixing.astype(F32) * mixing_part, axis=(0, 2))
    gain_in_part = lax.dynamic_update_slice_in_dim(
        gain_in_part,
        lax.dynamic_slice_in_dim(gain_in_part, index * slab, slab, 0) + gain_lag,
        index * slab,
        0,
    ) / gain_in
    gains = jnp.stack([gain_in_part, gain_mid_part])
    small = jnp.concatenate(
        [before_lag.reshape(lag_count * slab, width), jnp.pad(gains, ((0, 6), (0, 0)))], axis=0
    )
    for bit in row_bits():
        rounded = small[:-8].astype(BF16)
        gain_high = small[-8:].astype(BF16)
        gain_low = (small[-8:] - gain_high.astype(F32)).astype(BF16)
        other = swap_rows(jnp.concatenate([rounded, gain_high, gain_low], axis=0), bit).astype(F32)
        small = small + jnp.concatenate([other[:-16], other[-16:-8] + other[-8:]], axis=0)
    gain_high = small[-8:].astype(BF16)
    gain_low = (small[-8:] - gain_high.astype(F32)).astype(BF16)
    small_low = jnp.concatenate([small[:-8].astype(BF16), gain_high, gain_low], axis=0)
    spread = jnp.stack(spread_pieces(grid, small_low))
    gains = jnp.sum(spread[:, -16:-8].astype(F32) + spread[:, -8:].astype(F32), axis=0)
    regression_grad = jnp.zeros((lag_count, grid.size, slab, width), F32)
    for n in range(grid.size):
        piece = spread[n, :-16].astype(F32).reshape(lag_count, 1, slab, width)
        regression_grad = lax.dynamic_update_slice_in_dim(regression_grad, piece, order_from[n], 1)
    regression_grad = regression_grad.reshape(lag_count, width, width)

    mix_back = jnp.concatenate(middle_grad, axis=0).astype(BF16)
    edge = lax.ppermute(
        mix_back[:, :, :1], "filt", [(f + 1, f) for f in range(grid.size - 1)]
    )
    lag_back = sum(
        jnp.einsum("spae,de->spad", lead, regression[n], preferred_element_type=F32)
        for n, lead in enumerate(leading(mix_back, edge))
    )
    input_grad = []
    for c in range(chunks):
        part = slice(c * step, (c + 1) * step)
        back = state_back[c] + lag_back[part]
        input_grad.append(
            middle_grad[c] + norm_backward(back, normed_in[part], factor_in[part], gain_in)
        )

    full = spread_rows(own_grads)
    row_index = lax.axis_index("rows")
    ordered = jnp.zeros((row_count, 3, share, width), BF16)
    for n, mask in enumerate(row_masks()):
        ordered = lax.dynamic_update_slice_in_dim(ordered, full[n][None], row_index ^ mask, 0)
    ordered = ordered.transpose(1, 0, 2, 3).reshape(3, hidden_own, width).astype(F32)
    return (
        outward(jnp.concatenate(block_out, axis=0)),
        outward(jnp.concatenate(input_grad, axis=0)),
        mixing_grad,
        regression_grad,
        gains[0],
        gains[1],
        ordered[0].T,
        ordered[1].T,
        ordered[2],
    )


def solution(mesh):
    placed = (
        P("filt", "rows", None),
        P(),
        P(),
        P("filt", None, None),
        P(),
        P(),
        P(None, "filt"),
        P(None, "filt"),
        P("filt", None),
        P("filt", "rows", None),
    )
    return jax.shard_map(
        shards,
        mesh=mesh,
        in_specs=placed,
        out_specs=(
            P("filt", "rows", None),
            P("filt", "rows", None),
            P("filt", None, None),
            P(),
            P(),
            P(),
            P(None, "filt"),
            P(None, "filt"),
            P("filt", None),
        ),
        check_vma=False,
    )
```

time: 1480 us -> 616 us (0.42)
  waiting for transfers between devices: 785 us -> 222 us
  local copies, waits for them, and re-layouts: 356 us -> 45.6 us
  matrix products: 245 us -> 26.3 us
  starting transfers between devices: 0.66 us -> 142 us
  Pallas kernels: 0 us -> 94.4 us
  blocking collectives: 40.7 us -> 0 us
  other arithmetic: 27.2 us -> 60.6 us
    reduce_scatter x4 -> x0, waiting for transfers between devices: 528 us -> none  [the longest x3 438 us: shards(): lax.psum_scatter(summed.reshape(row_count, local_seqs, model_width), 'fil...]
    reshape x27 -> x2, local copies, waits for them, and re-layouts: 234 us -> 1.65 us  [the longest x1 1.64 us: toeplitz_blocks(): taps = taps.reshape(count, seq_length // 2, 2)]
    ppermute x0 -> x91, waiting for transfers between devices: none -> 222 us  [the longest x15 74.6 us: sum_pieces(): lax.ppermute(columns[i].astype(BF16), 'filt', grid.shift(i, 0)).astype(F32)]
    all_gather x4 -> x0, waiting for transfers between devices: 142 us -> none  [the longest x1 70.7 us: shards(): lax.all_gather(out_grad, 'filt', axis=0, tiled=True)]
    ppermute x0 -> x91, starting transfers between devices: none -> 142 us  [the longest x15 48.2 us: sum_pieces(): lax.ppermute(columns[i].astype(BF16), 'filt', grid.shift(i, 0)).astype(F32)]
    dot_general x24 -> x12, matrix products: 148 us -> 10.6 us  [the longest x3 5.01 us: shards(): jnp.einsum('spad,de->spae', lag, regression[n], preferred_element_type=F32)]
    psum x2 -> x0, waiting for transfers between devices: 113 us -> none  [the longest x1 97.4 us: shards(): lax.psum((regression_part, gain_in_part, gain_mid_part), ('rows', 'filt'))]
    pallas_call x0 -> x5, Pallas kernels: none -> 94.4 us  [the longest x2 57 us: mix_sequences_back(): pl.pallas_call(functools.partial(mix_back_kernel, parts), grid_spec=pltpu...]
  transfers between devices with their start and end apart: 10 -> 91, of which waited for: 9 -> 34; matrix products, arithmetic and copies ran while one was open for 17% -> 17% of each run, Pallas kernels for 0% -> 11%
where the time goes in v1:
time: 616 us; the launch traced here: 608 us
  waiting for transfers between devices  222 us (36%)
  starting transfers between devices  142 us (23%)
  Pallas kernels  94.4 us (15%)
  other arithmetic  60.6 us (10%)
  local copies, waits for them, and re-layouts  45.6 us (7%)
  matrix products  26.3 us (4%)
  between operations  17.5 us (3%)
    ppermute x15, waiting for transfers between devices, sum_pieces(): lax.ppermute(columns[i].astype(BF16), 'filt', grid.shift(i, 0)).astype(F32)  74.6 us
    pallas_call x2, Pallas kernels, mix_sequences_back(): pl.pallas_call(functools.partial(mix_back_kernel, parts), grid_spec=pltpu...  57 us
    ppermute x12, waiting for transfers between devices, swap_rows(): return lax.ppermute(values, 'rows', [(r, r ^ bit) for r in range(count)])  56.8 us
    ppermute x15, starting transfers between devices, sum_pieces(): lax.ppermute(columns[i].astype(BF16), 'filt', grid.shift(i, 0)).astype(F32)  48.2 us
    ppermute x20, waiting for transfers between devices, sum_pieces(): lax.ppermute(pieces[i * grid.near + j], 'filt', grid.shift(0, j))  47.3 us
    ppermute x18, starting transfers between devices, spread_pieces(): lax.ppermute(own, 'filt', grid.shift(i, 0))  35.4 us
    ppermute x18, waiting for transfers between devices, spread_pieces(): lax.ppermute(own, 'filt', grid.shift(i, 0))  30.8 us
    pallas_call x2, Pallas kernels, mix_sequences(): pl.pallas_call(functools.partial(mix_kernel, parts), grid_spec=pltpu.Pref...  30.1 us
  transfers between devices with their start and end apart: 91, of which 34 were waited for; matrix products, arithmetic and copies ran while one was open for 17% of the time, Pallas kernels for 11%

profile of v1, /device:TPU:0, one launch (start us, length us, event | category | flops | bytes accessed | tf_op | source)
XLA Modules:
  0.0 608.3 jit_solution(10618998078342099924)
XLA Ops:
  45.5 4.7 copy.140
  50.3 7.4 %toeplitz.1 = (bf16[2,256,1536]{2,1,0:T(8,128)(2,1)}, bf16[2,256,1536]{2,1,0:T(8,128)(2,1)}, bf16[2,1536,256]{2,1,0:T(8,128)(2,1)}, bf16[2,1536,256]{2,1,0:T(8,128)(2,1)}) custom-call(f32[12,1,1024]{2,1,0:T(1,128)} %copy.129.down_ref, f32[12,1,1024]{2,1,0:T(1,128)} %broadcast_in_dim.17.up_ref), custom_call_target="tpu_custom_call" | custom-call | tf_op jit(solution)/shard_map/toeplitz/pallas_call | solution.py:159
  65.8 4.2 collective-permute-done.18
  81.7 5.9 collective-permute-start.5
  100.7 9.7 %collective-permute-done.27.refs_4_ = bf16[2,2,64,512]{3,2,1,0:T(8,128)(2,1)S(1)} collective-permute-done((bf16[2,2,64,512]{3,2,1,0:T(8,128)(2,1)S(1)}, bf16[2,2,64,512]{3,2,1,0:T(8,128)(2,1)S(1)}, u32[]{:S(2)}, u32[]{:S(2)}) %collective-permute-start.27) | collective-permute-done | bytes 262176 | tf_op jit(solution)/shard_map/ppermute | solution.py:61
  119.9 15.1 %mix.2 = (bf16[2,2,64,512]{3,2,1,0:T(8,128)(2,1)S(1)}, bf16[2,2,64,512]{3,2,1,0:T(8,128)(2,1)S(1)}, bf16[2,2,64,512]{3,2,1,0:T(8,128)(2,1)S(1)}, bf16[2,2,64,512...) custom-call(s32[8]{0:T(128)S(1)} %get-tuple-element.204.from_ref, ...), custom_call_target="tpu_custom_call" | custom-call | flops 11274289152 | bytes 10485760 | tf_op jit(solution)/shard_map/mix/pallas_call | solution.py:289
  142.4 15.0 %mix.3 = (bf16[2,2,64,512]{3,2,1,0:T(8,128)(2,1)S(1)}, bf16[2,2,64,512]{3,2,1,0:T(8,128)(2,1)S(1)}, bf16[2,2,64,512]{3,2,1,0:T(8,128)(2,1)S(1)}, bf16[2,2,64,512...) custom-call(s32[8]{0:T(128)S(1)} %get-tuple-element.204.from_ref, ...), custom_call_target="tpu_custom_call" | custom-call | flops 11274289152 | bytes 10485760 | tf_op jit(solution)/shard_map/mix/pallas_call | solution.py:289
  161.1 5.6 collective-permute-done.36
  167.8 4.4 collective-permute-done.34
  172.3 8.9 %collective-permute-start.13 = (bf16[2,2,64,512]{3,2,1,0:T(8,128)(2,1)S(1)}, bf16[2,2,64,512]{3,2,1,0:T(8,128)(2,1)S(1)}, u32[]{:S(2)}, u32[]{:S(2)}) collective-permute-start(bf16[2,2,64,512]{3,2,1,0:T(8,128)(2,1)S(1)} %add_convert_fusion.10), channel_id=1, source_target_pairs={{0,6},{1,7},{2,0},{3,1},{4,2},{5,3},{6,4},{7,5},{8,14},{9,15},{10,... | collective-permute-start | bytes 786440 | tf_op jit(solution)/shard_map/ppermute | solution.py:82
  190.8 13.4 %collective-permute-done.11 = bf16[2,2,64,512]{3,2,1,0:T(8,128)(2,1)S(1)} collective-permute-done((bf16[2,2,64,512]{3,2,1,0:T(8,128)(2,1)S(1)}, bf16[2,2,64,512]{3,2,1,0:T(8,128)(2,1)S(1)}, u32[]{:S(2)}, u32[]{:S(2)}) %collective-permute-start.11) | collective-permute-done | bytes 262176 | tf_op jit(solution)/shard_map/ppermute | solution.py:82
  204.7 18.9 %collective-permute-done.35 = bf16[2,2,64,512]{3,2,1,0:T(8,128)(2,1)S(1)} collective-permute-done((bf16[2,2,64,512]{3,2,1,0:T(8,128)(2,1)S(1)}, bf16[2,2,64,512]{3,2,1,0:T(8,128)(2,1)S(1)}, u32[]{:S(2)}, u32[]{:S(2)}) %collective-permute-start.35) | collective-permute-done | bytes 262176 | tf_op jit(solution)/shard_map/ppermute | solution.py:82
  259.9 12.1 %pad_maximum_fusion = f32[3,4,8,64,512]{4,3,0,2,1:T(8,128)} fusion(f32[1,4,8,64,512]{4,3,0,2,1:T(8,128)} %bitcast.356, f32[1,4,8,64,512]{4,3,0,2,1:T(8,128)} %bitcast.354, f32[1,4,8,64,512]{4,3,0,2,1:T(8,128)} %bitcast.355), kind=kLoop, calls=%fused_computation | loop fusion | flops 6291456 | bytes 25165824 | tf_op jit(solution)/shard_map/stack | solution.py:481
  273.2 5.0 slice.606
  292.5 6.3 %collective-permute-done.56.refs_12_ = bf16[2,2,64,512]{3,2,1,0:T(8,128)(2,1)S(1)} collective-permute-done((bf16[2,2,64,512]{3,2,1,0:T(8,128)(2,1)S(1)}, bf16[2,2,64,512]{3,2,1,0:T(8,128)(2,1)S(1)}, u32[]{:S(2)}, u32[]{:S(2)}) %collective-permute-start.56) | collective-permute-done | bytes 262176 | tf_op jit(solution)/shard_map/ppermute | solution.py:61
  308.7 28.4 %mix_back.2 = (bf16[2,2,64,512]{3,2,1,0:T(8,128)(2,1)}, bf16[2,2,64,512]{3,2,1,0:T(8,128)(2,1)}, bf16[2,2,64,512]{3,2,1,0:T(8,128)(2,1)}, bf16[2,2,64,512]{3,2,1...) custom-call(s32[8]{0:T(128)} %copy-done.2, ...), custom_call_target="tpu_custom_call" | custom-call | flops 17716740096 | bytes 22020096 | tf_op jit(solution)/shard_map/mix_back/pallas_call | solution.py:323
  338.1 28.6 %mix_back.3 = (bf16[2,2,64,512]{3,2,1,0:T(8,128)(2,1)}, bf16[2,2,64,512]{3,2,1,0:T(8,128)(2,1)}, bf16[2,2,64,512]{3,2,1,0:T(8,128)(2,1)}, bf16[2,2,64,512]{3,2,1...) custom-call(s32[8]{0:T(128)} %copy-done.2, ...), custom_call_target="tpu_custom_call" | custom-call | flops 17716740096 | bytes 22020096 | tf_op jit(solution)/shard_map/mix_back/pallas_call | solution.py:323
  383.9 4.6 collective-permute-done.48
  389.5 4.6 collective-permute-done.46
  395.2 10.2 %collective-permute-done.65 = bf16[2,2,64,512]{3,2,1,0:T(8,128)(2,1)S(1)} collective-permute-done((bf16[2,2,64,512]{3,2,1,0:T(8,128)(2,1)S(1)}, bf16[2,2,64,512]{3,2,1,0:T(8,128)(2,1)S(1)}, u32[]{:S(2)}, u32[]{:S(2)}) %collective-permute-start.65) | collective-permute-done | bytes 262176 | tf_op jit(solution)/shard_map/ppermute | solution.py:76
  407.0 4.0 collective-permute-done.63
  411.0 6.5 %collective-permute-start.51 = (bf16[2,2,64,512]{3,2,1,0:T(8,128)(2,1)S(1)}, bf16[2,2,64,512]{3,2,1,0:T(8,128)(2,1)S(1)}, u32[]{:S(2)}, u32[]{:S(2)}) collective-permute-start(bf16[2,2,64,512]{3,2,1,0:T(8,128)(2,1)S(1)} %add_convert_fusion.4), channel_id=1, source_target_pairs={{0,6},{1,7},{2,0},{3,1},{4,2},{5,3},{6,4},{7,5},{8,14},{9,15},{10,... | collective-permute-start | bytes 786440 | tf_op jit(solution)/shard_map/ppermute | solution.py:82
  425.1 8.6 %collective-permute-start.62 = (bf16[2,2,64,512]{3,2,1,0:T(8,128)(2,1)S(1)}, bf16[2,2,64,512]{3,2,1,0:T(8,128)(2,1)S(1)}, u32[]{:S(2)}, u32[]{:S(2)}) collective-permute-start(bf16[2,2,64,512]{3,2,1,0:T(8,128)(2,1)S(1)} %add_convert_fusion.3), channel_id=1, source_target_pairs={{0,2},{1,3},{2,4},{3,5},{4,6},{5,7},{6,0},{7,1},{8,10},{9,11},{10,... | collective-permute-start | bytes 786440 | tf_op jit(solution)/shard_map/ppermute | solution.py:82
  436.6 15.5 %collective-permute-done.49 = bf16[2,2,64,512]{3,2,1,0:T(8,128)(2,1)S(1)} collective-permute-done((bf16[2,2,64,512]{3,2,1,0:T(8,128)(2,1)S(1)}, bf16[2,2,64,512]{3,2,1,0:T(8,128)(2,1)S(1)}, u32[]{:S(2)}, u32[]{:S(2)}) %collective-permute-start.49) | collective-permute-done | bytes 262176 | tf_op jit(solution)/shard_map/ppermute | solution.py:82
  456.2 12.9 %collective-permute-done.64 = bf16[2,2,64,512]{3,2,1,0:T(8,128)(2,1)S(1)} collective-permute-done((bf16[2,2,64,512]{3,2,1,0:T(8,128)(2,1)S(1)}, bf16[2,2,64,512]{3,2,1,0:T(8,128)(2,1)S(1)}, u32[]{:S(2)}, u32[]{:S(2)}) %collective-permute-start.64) | collective-permute-done | bytes 262176 | tf_op jit(solution)/shard_map/ppermute | solution.py:82
  471.9 4.1 collective-permute-done.76
  497.2 13.4 %collective-permute-done.68 = bf16[6,128,512]{2,1,0:T(8,128)(2,1)S(1)} collective-permute-done((bf16[6,128,512]{2,1,0:T(8,128)(2,1)S(1)}, bf16[6,128,512]{2,1,0:T(8,128)(2,1)S(1)}, u32[]{:S(2)}, u32[]{:S(2)}) %collective-permute-start.68) | collective-permute-done | bytes 786464 | tf_op jit(solution)/shard_map/ppermute | solution.py:90
  516.0 38.4 %collective-permute-done.69 = bf16[6,128,512]{2,1,0:T(8,128)(2,1)S(1)} collective-permute-done((bf16[6,128,512]{2,1,0:T(8,128)(2,1)S(1)}, bf16[6,128,512]{2,1,0:T(8,128)(2,1)S(1)}, u32[]{:S(2)}, u32[]{:S(2)}) %collective-permute-start.69) | collective-permute-done | bytes 786464 | tf_op jit(solution)/shard_map/ppermute | solution.py:90
  563.3 4.2 collective-permute-done.87
  567.6 4.2 collective-permute-done.85
  571.9 7.0 %collective-permute-start.88 = (bf16[3,64,512]{2,1,0:T(8,128)(2,1)S(1)}, bf16[3,64,512]{2,1,0:T(8,128)(2,1)S(1)}, u32[]{:S(2)}, u32[]{:S(2)}) collective-permute-start(bf16[3,64,512]{2,1,0:T(8,128)(2,1)S(1)} %get-tuple-element.169), channel_id=1, source_target_pairs={{0,6},{1,7},{2,0},{3,1},{4,2},{5,3},{6,4},{7,5},{8,14},{9,15},{10,... | collective-permute-start | bytes 589832 | tf_op jit(solution)/shard_map/ppermute | solution.py:82
  584.3 9.9 %collective-permute-done.86 = bf16[3,64,512]{2,1,0:T(8,128)(2,1)S(1)} collective-permute-done((bf16[3,64,512]{2,1,0:T(8,128)(2,1)S(1)}, bf16[3,64,512]{2,1,0:T(8,128)(2,1)S(1)}, u32[]{:S(2)}, u32[]{:S(2)}) %collective-permute-start.86) | collective-permute-done | bytes 196640 | tf_op jit(solution)/shard_map/ppermute | solution.py:82
  (482 shorter events, 249.1 us)
Async XLA Ops:
  4.3 83.2 %collective-permute-start = (bf16[2,2,64,512]{3,2,1,0:T(8,128)(2,1)S(1)}, bf16[2,2,64,512]{3,2,1,0:T(8,128)(2,1)S(1)}, u32[]{:S(2)}, u32[]{:S(2)}) collective-permute-start(bf16[2,2,64,512]{3,2,1,0:T(8,128)(2,1)S(1)} %get-tuple-element.181.refs_0_), channel_id=1, source_target_pairs={{0,1},{1,0},{2,3},{3,2},{4,5},{5,4},{6,7},{7,6},{8,9},{9,8},{10,11... | collective-permute-start | bytes 786440 | tf_op jit(solution)/shard_map/ppermute | solution.py:67
  7.4 82.0 %collective-permute-start.1 = (bf16[2,2,64,512]{3,2,1,0:T(8,128)(2,1)S(1)}, bf16[2,2,64,512]{3,2,1,0:T(8,128)(2,1)S(1)}, u32[]{:S(2)}, u32[]{:S(2)}) collective-permute-start(bf16[2,2,64,512]{3,2,1,0:T(8,128)(2,1)S(1)} %get-tuple-element.181.refs_0_), channel_id=1, source_target_pairs={{0,2},{1,3},{2,4},{3,5},{4,6},{5,7},{6,0},{7,1},{8,10},{9,11},{10,... | collective-permute-start | bytes 786440 | tf_op jit(solution)/shard_map/ppermute | solution.py:61
  8.9 86.2 %collective-permute-start.3 = (bf16[2,2,64,512]{3,2,1,0:T(8,128)(2,1)S(1)}, bf16[2,2,64,512]{3,2,1,0:T(8,128)(2,1)S(1)}, u32[]{:S(2)}, u32[]{:S(2)}) collective-permute-start(bf16[2,2,64,512]{3,2,1,0:T(8,128)(2,1)S(1)} %get-tuple-element.181.refs_0_), channel_id=1, source_target_pairs={{0,4},{1,5},{2,6},{3,7},{4,0},{5,1},{6,2},{7,3},{8,12},{9,13},{10,... | collective-permute-start | bytes 786440 | tf_op jit(solution)/shard_map/ppermute | solution.py:61
  14.4 44.7 %collective-permute-start.15 = (bf16[3,64,512]{2,1,0:T(8,128)(2,1)}, bf16[3,64,512]{2,1,0:T(8,128)(2,1)}, u32[]{:S(2)}, u32[]{:S(2)}) collective-permute-start(bf16[3,64,512]{2,1,0:T(8,128)(2,1)} %bitcast.22), channel_id=1, source_target_pairs={{0,1},{1,0},{2,3},{3,2},{4,5},{5,4},{6,7},{7,6},{8,9},{9,8},{10,11... | collective-permute-start | bytes 589832 | tf_op jit(solution)/shard_map/ppermute | solution.py:67
  14.9 46.1 %collective-permute-start.16 = (bf16[3,64,512]{2,1,0:T(8,128)(2,1)}, bf16[3,64,512]{2,1,0:T(8,128)(2,1)}, u32[]{:S(2)}, u32[]{:S(2)}) collective-permute-start(bf16[3,64,512]{2,1,0:T(8,128)(2,1)} %bitcast.22), channel_id=1, source_target_pairs={{0,2},{1,3},{2,4},{3,5},{4,6},{5,7},{6,0},{7,1},{8,10},{9,11},{10,... | collective-permute-start | bytes 589832 | tf_op jit(solution)/shard_map/ppermute | solution.py:61
  89.3 45.8 %collective-permute-start.22 = (bf16[1,3,8,64,512]{4,3,2,1,0:T(8,128)(2,1)}, bf16[1,3,8,64,512]{4,3,2,1,0:T(8,128)(2,1)}, u32[]{:S(2)}, u32[]{:S(2)}) collective-permute-start(bf16[1,3,8,64,512]{4,3,2,1,0:T(8,128)(2,1)} %bitcast.36), channel_id=1, source_target_pairs={{0,16},{8,24},{16,0},{24,8},{1,17},{9,25},{17,1},{25,9},{2,18},{10... | collective-permute-start | bytes 4718600 | tf_op jit(solution)/shard_map/ppermute | solution.py:90
  112.6 26.8 %collective-permute-start.24 = (bf16[2,2,64,512]{3,2,1,0:T(8,128)(2,1)S(1)}, bf16[2,2,64,512]{3,2,1,0:T(8,128)(2,1)S(1)}, u32[]{:S(2)}, u32[]{:S(2)}) collective-permute-start(bf16[2,2,64,512]{3,2,1,0:T(8,128)(2,1)S(1)} %get-tuple-element.182.refs_0_), channel_id=1, source_target_pairs={{0,1},{1,0},{2,3},{3,2},{4,5},{5,4},{6,7},{7,6},{8,9},{9,8},{10,11... | collective-permute-start | bytes 786440 | tf_op jit(solution)/shard_map/ppermute | solution.py:67
  114.7 26.8 %collective-permute-start.28 = (bf16[2,2,64,512]{3,2,1,0:T(8,128)(2,1)S(1)}, bf16[2,2,64,512]{3,2,1,0:T(8,128)(2,1)S(1)}, u32[]{:S(2)}, u32[]{:S(2)}) collective-permute-start(bf16[2,2,64,512]{3,2,1,0:T(8,128)(2,1)S(1)} %collective-permute-done.27.refs_4_), channel_id=1, source_target_pairs={{0,1},{1,0},{2,3},{3,2},{4,5},{5,4},{6,7},{7,6},{8,9},{9,8},{10,11... | collective-permute-start | bytes 786440 | tf_op jit(solution)/shard_map/ppermute | solution.py:67
  141.5 42.8 %collective-permute-start.7 = (bf16[2,2,64,512]{3,2,1,0:T(8,128)(2,1)S(1)}, bf16[2,2,64,512]{3,2,1,0:T(8,128)(2,1)S(1)}, u32[]{:S(2)}, u32[]{:S(2)}) collective-permute-start(bf16[2,2,64,512]{3,2,1,0:T(8,128)(2,1)S(1)} %get-tuple-element.52), channel_id=1, source_target_pairs={{0,1},{1,0},{2,3},{3,2},{4,5},{5,4},{6,7},{7,6},{8,9},{9,8},{10,11... | collective-permute-start | bytes 786440 | tf_op jit(solution)/shard_map/ppermute | solution.py:76
  142.4 82.0 %collective-permute-start.23 = (bf16[2,3,8,64,512]{4,3,2,1,0:T(8,128)(2,1)S(1)}, bf16[2,3,8,64,512]{4,3,2,1,0:T(8,128)(2,1)}, u32[]{:S(2)}, u32[]{:S(2)}) collective-permute-start(bf16[2,3,8,64,512]{4,3,2,1,0:T(8,128)(2,1)S(1)} %pad_maximum_fusion.4), channel_id=1, source_target_pairs={{0,8},{8,0},{16,24},{24,16},{1,9},{9,1},{17,25},{25,17},{2,10},{10... | collective-permute-start | bytes 9437192 | tf_op jit(solution)/shard_map/ppermute | solution.py:90
  190.8 32.7 %collective-permute-start.35 = (bf16[2,2,64,512]{3,2,1,0:T(8,128)(2,1)S(1)}, bf16[2,2,64,512]{3,2,1,0:T(8,128)(2,1)S(1)}, u32[]{:S(2)}, u32[]{:S(2)}) collective-permute-start(bf16[2,2,64,512]{3,2,1,0:T(8,128)(2,1)S(1)} %add_convert_fusion.8), channel_id=1, source_target_pairs={{0,4},{1,5},{2,6},{3,7},{4,0},{5,1},{6,2},{7,3},{8,12},{9,13},{10,... | collective-permute-start | bytes 786440 | tf_op jit(solution)/shard_map/ppermute | solution.py:82
  239.7 43.0 %collective-permute-start.38 = (bf16[2,2,64,512]{3,2,1,0:T(8,128)(2,1)S(1)}, bf16[2,2,64,512]{3,2,1,0:T(8,128)(2,1)S(1)}, u32[]{:S(2)}, u32[]{:S(2)}) collective-permute-start(bf16[2,2,64,512]{3,2,1,0:T(8,128)(2,1)S(1)} %get-tuple-element.132.refs_8_), channel_id=1, source_target_pairs={{0,1},{1,0},{2,3},{3,2},{4,5},{5,4},{6,7},{7,6},{8,9},{9,8},{10,11... | collective-permute-start | bytes 786440 | tf_op jit(solution)/shard_map/ppermute | solution.py:67
  240.8 42.0 %collective-permute-start.39 = (bf16[2,2,64,512]{3,2,1,0:T(8,128)(2,1)S(1)}, bf16[2,2,64,512]{3,2,1,0:T(8,128)(2,1)S(1)}, u32[]{:S(2)}, u32[]{:S(2)}) collective-permute-start(bf16[2,2,64,512]{3,2,1,0:T(8,128)(2,1)S(1)} %get-tuple-element.132.refs_8_), channel_id=1, source_target_pairs={{0,2},{1,3},{2,4},{3,5},{4,6},{5,7},{6,0},{7,1},{8,10},{9,11},{10,... | collective-permute-start | bytes 786440 | tf_op jit(solution)/shard_map/ppermute | solution.py:61
  242.1 43.2 %collective-permute-start.41 = (bf16[2,2,64,512]{3,2,1,0:T(8,128)(2,1)S(1)}, bf16[2,2,64,512]{3,2,1,0:T(8,128)(2,1)S(1)}, u32[]{:S(2)}, u32[]{:S(2)}) collective-permute-start(bf16[2,2,64,512]{3,2,1,0:T(8,128)(2,1)S(1)} %get-tuple-element.132.refs_8_), channel_id=1, source_target_pairs={{0,4},{1,5},{2,6},{3,7},{4,0},{5,1},{6,2},{7,3},{8,12},{9,13},{10,... | collective-permute-start | bytes 786440 | tf_op jit(solution)/shard_map/ppermute | solution.py:61
  244.1 41.4 %collective-permute-start.43 = (bf16[2,2,64,512]{3,2,1,0:T(8,128)(2,1)S(1)}, bf16[2,2,64,512]{3,2,1,0:T(8,128)(2,1)S(1)}, u32[]{:S(2)}, u32[]{:S(2)}) collective-permute-start(bf16[2,2,64,512]{3,2,1,0:T(8,128)(2,1)S(1)} %get-tuple-element.132.refs_8_), channel_id=1, source_target_pairs={{0,6},{1,7},{2,0},{3,1},{4,2},{5,3},{6,4},{7,5},{8,14},{9,15},{10,... | collective-permute-start | bytes 786440 | tf_op jit(solution)/shard_map/ppermute | solution.py:61
  298.7 38.4 %collective-permute-start.53 = (bf16[2,2,64,512]{3,2,1,0:T(8,128)(2,1)S(1)}, bf16[2,2,64,512]{3,2,1,0:T(8,128)(2,1)S(1)}, u32[]{:S(2)}, u32[]{:S(2)}) collective-permute-start(bf16[2,2,64,512]{3,2,1,0:T(8,128)(2,1)S(1)} %get-tuple-element.173.refs_8_), channel_id=1, source_target_pairs={{0,1},{1,0},{2,3},{3,2},{4,5},{5,4},{6,7},{7,6},{8,9},{9,8},{10,11... | collective-permute-start | bytes 786440 | tf_op jit(solution)/shard_map/ppermute | solution.py:67
  301.2 35.9 %collective-permute-start.55 = (bf16[2,2,64,512]{3,2,1,0:T(8,128)(2,1)S(1)}, bf16[2,2,64,512]{3,2,1,0:T(8,128)(2,1)S(1)}, u32[]{:S(2)}, u32[]{:S(2)}) collective-permute-start(bf16[2,2,64,512]{3,2,1,0:T(8,128)(2,1)S(1)} %collective-permute-done.54.refs_10_), channel_id=1, source_target_pairs={{0,1},{1,0},{2,3},{3,2},{4,5},{5,4},{6,7},{7,6},{8,9},{9,8},{10,11... | collective-permute-start | bytes 786440 | tf_op jit(solution)/shard_map/ppermute | solution.py:67
  301.3 35.9 %collective-permute-start.57 = (bf16[2,2,64,512]{3,2,1,0:T(8,128)(2,1)S(1)}, bf16[2,2,64,512]{3,2,1,0:T(8,128)(2,1)S(1)}, u32[]{:S(2)}, u32[]{:S(2)}) collective-permute-start(bf16[2,2,64,512]{3,2,1,0:T(8,128)(2,1)S(1)} %collective-permute-done.56.refs_12_), channel_id=1, source_target_pairs={{0,1},{1,0},{2,3},{3,2},{4,5},{5,4},{6,7},{7,6},{8,9},{9,8},{10,11... | collective-permute-start | bytes 786440 | tf_op jit(solution)/shard_map/ppermute | solution.py:67
  303.2 33.9 %collective-permute-start.59 = (bf16[2,2,64,512]{3,2,1,0:T(8,128)(2,1)S(1)}, bf16[2,2,64,512]{3,2,1,0:T(8,128)(2,1)S(1)}, u32[]{:S(2)}, u32[]{:S(2)}) collective-permute-start(bf16[2,2,64,512]{3,2,1,0:T(8,128)(2,1)S(1)} %collective-permute-done.58.refs_14_), channel_id=1, source_target_pairs={{0,1},{1,0},{2,3},{3,2},{4,5},{5,4},{6,7},{7,6},{8,9},{9,8},{10,11... | collective-permute-start | bytes 786440 | tf_op jit(solution)/shard_map/ppermute | solution.py:67
  376.6 45.8 %collective-permute-start.45 = (bf16[2,2,64,512]{3,2,1,0:T(8,128)(2,1)S(1)}, bf16[2,2,64,512]{3,2,1,0:T(8,128)(2,1)S(1)}, u32[]{:S(2)}, u32[]{:S(2)}) collective-permute-start(bf16[2,2,64,512]{3,2,1,0:T(8,128)(2,1)S(1)} %copy-done.45), channel_id=1, source_target_pairs={{0,1},{1,0},{2,3},{3,2},{4,5},{5,4},{6,7},{7,6},{8,9},{9,8},{10,11... | collective-permute-start | bytes 786440 | tf_op jit(solution)/shard_map/ppermute | solution.py:76
  382.9 28.1 %collective-permute-start.63 = (bf16[2,2,64,512]{3,2,1,0:T(8,128)(2,1)S(1)}, bf16[2,2,64,512]{3,2,1,0:T(8,128)(2,1)S(1)}, u32[]{:S(2)}, u32[]{:S(2)}) collective-permute-start(bf16[2,2,64,512]{3,2,1,0:T(8,128)(2,1)S(1)} %copy-done.52), channel_id=1, source_target_pairs={{0,1},{1,0},{2,3},{3,2},{4,5},{5,4},{6,7},{7,6},{8,9},{9,8},{10,11... | collective-permute-start | bytes 786440 | tf_op jit(solution)/shard_map/ppermute | solution.py:76
  388.6 29.0 %collective-permute-start.61 = (bf16[2,2,64,512]{3,2,1,0:T(8,128)(2,1)S(1)}, bf16[2,2,64,512]{3,2,1,0:T(8,128)(2,1)S(1)}, u32[]{:S(2)}, u32[]{:S(2)}) collective-permute-start(bf16[2,2,64,512]{3,2,1,0:T(8,128)(2,1)S(1)} %copy-done.48), channel_id=1, source_target_pairs={{0,1},{1,0},{2,3},{3,2},{4,5},{5,4},{6,7},{7,6},{8,9},{9,8},{10,11... | collective-permute-start | bytes 786440 | tf_op jit(solution)/shard_map/ppermute | solution.py:76
  394.2 30.9 %collective-permute-start.60 = (bf16[2,2,64,512]{3,2,1,0:T(8,128)(2,1)S(1)}, bf16[2,2,64,512]{3,2,1,0:T(8,128)(2,1)S(1)}, u32[]{:S(2)}, u32[]{:S(2)}) collective-permute-start(bf16[2,2,64,512]{3,2,1,0:T(8,128)(2,1)S(1)} %copy-done.46), channel_id=1, source_target_pairs={{0,1},{1,0},{2,3},{3,2},{4,5},{5,4},{6,7},{7,6},{8,9},{9,8},{10,11... | collective-permute-start | bytes 786440 | tf_op jit(solution)/shard_map/ppermute | solution.py:76
  417.6 34.5 %collective-permute-start.49 = (bf16[2,2,64,512]{3,2,1,0:T(8,128)(2,1)S(1)}, bf16[2,2,64,512]{3,2,1,0:T(8,128)(2,1)S(1)}, u32[]{:S(2)}, u32[]{:S(2)}) collective-permute-start(bf16[2,2,64,512]{3,2,1,0:T(8,128)(2,1)S(1)} %add_convert_fusion.5), channel_id=1, source_target_pairs={{0,4},{1,5},{2,6},{3,7},{4,0},{5,1},{6,2},{7,3},{8,12},{9,13},{10,... | collective-permute-start | bytes 786440 | tf_op jit(solution)/shard_map/ppermute | solution.py:82
  420.8 31.3 %collective-permute-start.47 = (bf16[2,2,64,512]{3,2,1,0:T(8,128)(2,1)S(1)}, bf16[2,2,64,512]{3,2,1,0:T(8,128)(2,1)S(1)}, u32[]{:S(2)}, u32[]{:S(2)}) collective-permute-start(bf16[2,2,64,512]{3,2,1,0:T(8,128)(2,1)S(1)} %add_convert_fusion.6), channel_id=1, source_target_pairs={{0,2},{1,3},{2,4},{3,5},{4,6},{5,7},{6,0},{7,1},{8,10},{9,11},{10,... | collective-permute-start | bytes 786440 | tf_op jit(solution)/shard_map/ppermute | solution.py:82
  422.5 30.0 %collective-permute-start.66 = (bf16[2,2,64,512]{3,2,1,0:T(8,128)(2,1)S(1)}, bf16[2,2,64,512]{3,2,1,0:T(8,128)(2,1)S(1)}, u32[]{:S(2)}, u32[]{:S(2)}) collective-permute-start(bf16[2,2,64,512]{3,2,1,0:T(8,128)(2,1)S(1)} %add_convert_fusion.1), channel_id=1, source_target_pairs={{0,6},{1,7},{2,0},{3,1},{4,2},{5,3},{6,4},{7,5},{8,14},{9,15},{10,... | collective-permute-start | bytes 786440 | tf_op jit(solution)/shard_map/ppermute | solution.py:82
  425.0 44.1 %collective-permute-start.64 = (bf16[2,2,64,512]{3,2,1,0:T(8,128)(2,1)S(1)}, bf16[2,2,64,512]{3,2,1,0:T(8,128)(2,1)S(1)}, u32[]{:S(2)}, u32[]{:S(2)}) collective-permute-start(bf16[2,2,64,512]{3,2,1,0:T(8,128)(2,1)S(1)} %add_convert_fusion.2), channel_id=1, source_target_pairs={{0,4},{1,5},{2,6},{3,7},{4,0},{5,1},{6,2},{7,3},{8,12},{9,13},{10,... | collective-permute-start | bytes 786440 | tf_op jit(solution)/shard_map/ppermute | solution.py:82
  425.1 44.1 %collective-permute-start.62 = (bf16[2,2,64,512]{3,2,1,0:T(8,128)(2,1)S(1)}, bf16[2,2,64,512]{3,2,1,0:T(8,128)(2,1)S(1)}, u32[]{:S(2)}, u32[]{:S(2)}) collective-permute-start(bf16[2,2,64,512]{3,2,1,0:T(8,128)(2,1)S(1)} %add_convert_fusion.3), channel_id=1, source_target_pairs={{0,2},{1,3},{2,4},{3,5},{4,6},{5,7},{6,0},{7,1},{8,10},{9,11},{10,... | collective-permute-start | bytes 786440 | tf_op jit(solution)/shard_map/ppermute | solution.py:82
  452.1 40.8 %collective-permute-start.80 = (bf16[3,2,8,64,512]{4,3,0,2,1:T(8,128)(2,1)}, bf16[3,2,8,64,512]{4,3,0,2,1:T(8,128)(2,1)}, u32[]{:S(2)}, u32[]{:S(2)}) collective-permute-start(bf16[3,2,8,64,512]{4,3,0,2,1:T(8,128)(2,1)} %slice.606), channel_id=1, source_target_pairs={{0,8},{8,0},{16,24},{24,16},{1,9},{9,1},{17,25},{25,17},{2,10},{10... | collective-permute-start | bytes 9437192 | tf_op jit(solution)/shard_map/ppermute | solution.py:90
  496.6 58.2 %collective-permute-start.81 = (bf16[3,1,8,64,512]{4,3,0,2,1:T(8,128)(2,1)S(1)}, bf16[3,1,8,64,512]{4,3,0,2,1:T(8,128)(2,1)S(1)}, u32[]{:S(2)}, u32[]{:S(2)}) collective-permute-start(bf16[3,1,8,64,512]{4,3,0,2,1:T(8,128)(2,1)S(1)} %slice.607), channel_id=1, source_target_pairs={{0,16},{8,24},{16,0},{24,8},{1,17},{9,25},{17,1},{25,9},{2,18},{10... | collective-permute-start | bytes 4718600 | tf_op jit(solution)/shard_map/ppermute | solution.py:90
  511.2 43.3 %collective-permute-start.69 = (bf16[6,128,512]{2,1,0:T(8,128)(2,1)S(1)}, bf16[6,128,512]{2,1,0:T(8,128)(2,1)S(1)}, u32[]{:S(2)}, u32[]{:S(2)}) collective-permute-start(bf16[6,128,512]{2,1,0:T(8,128)(2,1)S(1)} %fusion.22), channel_id=1, source_target_pairs={{0,16},{8,24},{16,0},{24,8},{1,17},{9,25},{17,1},{25,9},{2,18},{10... | collective-permute-start | bytes 2359304 | tf_op jit(solution)/shard_map/ppermute | solution.py:90
  554.7 45.7 %collective-permute-start.70 = (bf16[6,256,512]{2,1,0:T(8,128)(2,1)S(1)}, bf16[6,256,512]{2,1,0:T(8,128)(2,1)S(1)}, u32[]{:S(2)}, u32[]{:S(2)}) collective-permute-start(bf16[6,256,512]{2,1,0:T(8,128)(2,1)S(1)} %pad_maximum_fusion.5), channel_id=1, source_target_pairs={{0,8},{8,0},{16,24},{24,16},{1,9},{9,1},{17,25},{25,17},{2,10},{10... | collective-permute-start | bytes 4718600 | tf_op jit(solution)/shard_map/ppermute | solution.py:90
  (130 other events, 2503.1 us)

commit v2 on v1

--- a/solution.py
+++ b/solution.py
@@ -40,48 +40,39 @@
         self.near = size // self.far
         self.size = size
 
-    def shift(self, far_step, near_step):
-        far, near = self.far, self.near
-        return [
-            (f, ((f // near + far_step) % far) * near + (f % near + near_step) % near)
-            for f in range(self.size)
+    def near_shift(self, step):
+        near = self.near
+        return [(f, f // near * near + (f % near + step) % near) for f in range(self.size)]
+
+    def swap_far(self, values):
+        groups = [
+            [i * self.near + j for i in range(self.far)] for j in range(self.near)
         ]
-
-    def order(self, index, sign):
-        far, near = self.far, self.near
-        steps = jnp.arange(self.size, dtype=jnp.int32)
-        return (
-            lax.rem(index // near + sign * (steps // near) + far, far) * near
-            + lax.rem(index % near + sign * (steps % near) + near, near)
-        ).astype(jnp.int32)
-
-
-def spread_pieces(grid, own):
-    columns = [own] + [
-        lax.ppermute(own, "filt", grid.shift(i, 0)) for i in range(1, grid.far)
+        return lax.all_to_all(values, "filt", 0, 0, axis_index_groups=groups, tiled=True)
+
+
+def tie(value, *others):
+    return lax.optimization_barrier((value, *others))[0] if others else value
+
+
+def tie_all(values, *others):
+    count = len(values)
+    return list(lax.optimization_barrier((*values, *others))[:count]) if others else list(values)
+
+
+def near_swaps(grid, values):
+    return [
+        lax.ppermute(
+            values[j] if isinstance(values, list) else values, "filt", grid.near_shift(j)
+        )
+        for j in range(1, grid.near)
     ]
-    pieces = []
-    for column in columns:
-        pieces.append(column)
-        for j in range(1, grid.near):
-            pieces.append(lax.ppermute(column, "filt", grid.shift(0, j)))
-    return pieces
-
-
-def sum_pieces(grid, pieces):
-    columns = []
-    for i in range(grid.far):
-        total = pieces[i * grid.near].astype(F32)
-        for j in range(1, grid.near):
-            total = total + lax.ppermute(
-                pieces[i * grid.near + j], "filt", grid.shift(0, j)
-            ).astype(F32)
-        columns.append(total)
-    total = columns[0]
-    for i in range(1, grid.far):
-        total = total + lax.ppermute(
-            columns[i].astype(BF16), "filt", grid.shift(i, 0)
-        ).astype(F32)
+
+
+def total_of(values):
+    total = values[0].astype(F32)
+    for value in values[1:]:
+        total = total + value.astype(F32)
     return total
 
 
@@ -166,40 +157,43 @@
     )(down[:, None], up[:, None])
 
 
-def assemble(order_ref, pieces, whole_ref):
+def places(near, pieces, whole_ref, sign):
     length = whole_ref.shape[0] // 2
-    height = pieces[0].shape[2]
-    for n, piece in enumerate(pieces):
-        start = order_ref[n] * height
-        for parity in range(2):
-            place = pl.multiple_of(parity * length + start, height)
-            whole_ref[pl.ds(place, height), :] = piece[0, parity]
-
-
-def scatter(order_ref, whole_ref, pieces):
-    length = whole_ref.shape[0] // 2
-    height = pieces[0].shape[2]
-    for n, piece in enumerate(pieces):
-        start = order_ref[n] * height
-        for parity in range(2):
-            place = pl.multiple_of(parity * length + start, height)
-            piece[0, parity] = whole_ref[pl.ds(place, height), :].astype(piece.dtype)
-
-
-def mix_kernel(parts, from_ref, to_ref, *refs):
+    nears = len(pieces)
+    fars, _, _, height, _ = pieces[0].shape
+    for j, piece in enumerate(pieces):
+        at = lax.rem(near + sign * j + nears, nears)
+        for i in range(fars):
+            for parity in range(2):
+                start = parity * length + (i * nears + at) * height
+                yield piece.at[i, 0, parity], pl.ds(pl.multiple_of(start, height), height)
+
+
+def assemble(near, pieces, whole_ref):
+    for piece, rows in places(near, pieces, whole_ref, -1):
+        whole_ref[rows, :] = piece[...]
+
+
+def scatter(near, whole_ref, pieces):
+    for piece, rows in places(near, pieces, whole_ref, 1):
+        piece[...] = whole_ref[rows, :].astype(piece.dtype)
+
+
+def mix_kernel(parts, near_ref, *refs):
     pieces = refs[:parts]
-    mix_ref, t00_ref, t10_ref = refs[parts : parts + 3]
-    outs = refs[parts + 3 : 2 * parts + 3]
-    states_ref, low_ref, high_ref, sum_ref = refs[2 * parts + 3 :]
+    mixes = refs[parts : parts + 2]
+    t00_ref, t10_ref = refs[parts + 2 : parts + 4]
+    outs = refs[parts + 4 : 2 * parts + 4]
+    states_ref, low_ref, high_ref, sum_ref = refs[2 * parts + 4 :]
     half = t00_ref.shape[1]
-    branches = mix_ref.shape[0]
-    assemble(from_ref, pieces, states_ref)
+    branches = 2 * mixes[0].shape[0]
+    assemble(near_ref[0], pieces, states_ref)
 
     for branch in range(branches):
         slot = pl.ds(branch * half, half)
         for quarter in range(4):
             value = dot(
-                states_ref[pl.ds(quarter * half, half), :], mix_ref[branch]
+                states_ref[pl.ds(quarter * half, half), :], mixes[branch % 2][branch // 2]
             ).astype(BF16)
             target = (quarter // 2) ^ (branch % 2)
             (low_ref, high_ref)[quarter % 2][target, slot, :] = value
@@ -212,28 +206,35 @@
         sum_ref[pl.ds(base + half, half), :] = (
             dot(t10_ref[parity], low_ref[parity]) + dot(t00_ref[parity], high_ref[parity])
         ).astype(sum_ref.dtype)
-    scatter(to_ref, sum_ref, outs)
-
-
-def mix_back_kernel(parts, from_ref, to_ref, own_ref, *refs):
+    scatter(near_ref[0], sum_ref, outs)
+
+
+def mix_back_kernel(parts, near_ref, own_ref, *refs):
     state_pieces = refs[:parts]
     grad_pieces = refs[parts : 2 * parts]
-    turned_ref, u00_ref, u10_ref, before_ref, before_lag_ref = refs[2 * parts : 2 * parts + 5]
-    outs = refs[2 * parts + 5 : 3 * parts + 5]
-    mixing_ref, lag_ref = refs[3 * parts + 5 : 3 * parts + 7]
-    states_ref, grad_ref, flip_ref, back_ref, sum_ref = refs[3 * parts + 7 :]
+    turned = refs[2 * parts : 2 * parts + 2]
+    u00_ref, u10_ref = refs[2 * parts + 2 : 2 * parts + 4]
+    before = refs[2 * parts + 4 : -parts - 7]
+    outs = refs[-parts - 7 : -7]
+    mixing_ref, lag_ref = refs[-7:-5]
+    states_ref, grad_ref, flip_ref, back_ref, sum_ref = refs[-5:]
     half = u00_ref.shape[2]
     branches = mixing_ref.shape[0]
+    slots = branches // 2
     width = grad_ref.shape[1]
     length = states_ref.shape[0] // 2
 
     @pl.when(pl.program_id(0) == 0)
     def _():
-        mixing_ref[...] = before_ref[...]
-        lag_ref[...] = before_lag_ref[...]
-
-    assemble(from_ref, state_pieces, states_ref)
-    assemble(from_ref, grad_pieces, grad_ref)
+        if before:
+            mixing_ref[...] = before[0][...]
+            lag_ref[...] = before[1][...]
+        else:
+            mixing_ref[...] = jnp.zeros_like(mixing_ref)
+            lag_ref[...] = jnp.zeros_like(lag_ref)
+
+    assemble(near_ref[0], state_pieces, states_ref)
+    assemble(near_ref[0], grad_pieces, grad_ref)
     flip_ref[...] = states_ref[...].T
 
     for parity in range(2):
@@ -242,7 +243,7 @@
         high = grad_ref[pl.ds(base + half, half), :]
         for branch in range(branches):
             rows = pl.ds(branch * half, half)
-            columns = pl.ds(branch * width, width)
+            columns = pl.ds((branch % 2 * slots + branch // 2) * width, width)
             target = 2 * half * (parity ^ (branch % 2))
             back_ref[pl.ds(target, half), columns] = (
                 dot(u00_ref[parity, rows, :], low) + dot(u10_ref[parity, rows, :], high)
@@ -253,11 +254,13 @@
 
     for quarter in range(4):
         rows = pl.ds(quarter * half, half)
-        sum_ref[rows, :] = dot(back_ref[rows, :], turned_ref[...]).astype(sum_ref.dtype)
-    scatter(to_ref, sum_ref, outs)
+        sum_ref[rows, :] = dot(back_ref[rows, : slots * width], turned[0][...]) + dot(
+            back_ref[rows, slots * width :], turned[1][...]
+        )
+    scatter(near_ref[0], sum_ref, outs)
 
     for branch in range(branches):
-        columns = pl.ds(branch * width, width)
+        columns = pl.ds((branch % 2 * slots + branch // 2) * width, width)
         mixing_ref[branch] += dot(flip_ref[...], back_ref[:, columns])
 
     slab = lag_ref.shape[1]
@@ -280,19 +283,19 @@
     return pl.BlockSpec(shape, lambda *_: zeros, pipeline_mode=pl.Buffered(1))
 
 
-def mix_sequences(pieces, order_from, order_to, pairs, t00, t10):
+def mix_sequences(pieces, near, pairs, t00, t10):
     parts = len(pieces)
-    count, _, height, width = pieces[0].shape
+    fars, count, _, height, width = pieces[0].shape
     half = t00.shape[1]
-    block = pl.BlockSpec((1, 2, height, width), lambda n, *_: (n, 0, 0, 0))
+    block = pl.BlockSpec((fars, 1, 2, height, width), lambda n, *_: (0, n, 0, 0, 0))
     rows = t00.shape[2]
     return pl.pallas_call(
         functools.partial(mix_kernel, parts),
         grid_spec=pltpu.PrefetchScalarGridSpec(
-            num_scalar_prefetch=2,
+            num_scalar_prefetch=1,
             grid=(count,),
             in_specs=[block] * parts
-            + [resident(pairs.shape), resident(t00.shape), resident(t10.shape)],
+            + [resident(a.shape) for a in (*pairs, t00, t10)],
             out_specs=[block] * parts,
             scratch_shapes=[
                 pltpu.VMEM((4 * half, width), BF16),
@@ -304,51 +307,53 @@
         out_shape=[jax.ShapeDtypeStruct(pieces[0].shape, BF16)] * parts,
         compiler_params=pltpu.CompilerParams(vmem_limit_bytes=48 << 20),
         cost_estimate=pl.CostEstimate(
-            flops=count * (8 * half * width * pairs.shape[0] * width + 12 * half * rows * width),
-            bytes_accessed=2 * parts * pieces[0].size * 2 + 2 * pairs.size + 4 * t00.size,
+            flops=count * (16 * half * pairs[0].size + 12 * half * rows * width),
+            bytes_accessed=4 * parts * pieces[0].size + 4 * pairs[0].size + 4 * t00.size,
             transcendentals=0,
         ),
         name="mix",
-    )(order_from, order_to, *pieces, pairs, t00, t10)
+    )(near, *pieces, *pairs, t00, t10)
 
 
 def mix_sequences_back(
-    states, grads, order_from, order_to, own, turned, u00, u10, before, before_lag
+    states, grads, near, own, turned, u00, u10, lag_count, before
 ):
     parts = len(states)
-    count, _, height, width = states[0].shape
+    fars, count, _, height, width = states[0].shape
     half = u00.shape[2]
-    block = pl.BlockSpec((1, 2, height, width), lambda n, *_: (n, 0, 0, 0))
+    block = pl.BlockSpec((fars, 1, 2, height, width), lambda n, *_: (0, n, 0, 0, 0))
     rows = u00.shape[1]
+    mixing_shape = (2 * turned[0].shape[0] // width, width, width)
+    lag_shape = (lag_count, width // (parts * fars), width)
     return pl.pallas_call(
         functools.partial(mix_back_kernel, parts),
         grid_spec=pltpu.PrefetchScalarGridSpec(
-            num_scalar_prefetch=3,
+            num_scalar_prefetch=2,
             grid=(count,),
             in_specs=[block] * (2 * parts)
-            + [resident(a.shape) for a in (turned, u00, u10, before, before_lag)],
-            out_specs=[block] * parts + [resident(before.shape), resident(before_lag.shape)],
+            + [resident(a.shape) for a in (*turned, u00, u10, *before)],
+            out_specs=[block] * parts + [resident(mixing_shape), resident(lag_shape)],
             scratch_shapes=[
                 pltpu.VMEM((4 * half, width), BF16),
                 pltpu.VMEM((4 * half, width), BF16),
                 pltpu.VMEM((width, 4 * half), BF16),
-                pltpu.VMEM((4 * half, turned.shape[0]), BF16),
+                pltpu.VMEM((4 * half, 2 * turned[0].shape[0]), BF16),
                 pltpu.VMEM((4 * half, width), F32),
             ],
         ),
         out_shape=[jax.ShapeDtypeStruct(states[0].shape, BF16)] * parts
         + [
-            jax.ShapeDtypeStruct(before.shape, F32),
-            jax.ShapeDtypeStruct(before_lag.shape, F32),
+            jax.ShapeDtypeStruct(mixing_shape, F32),
+            jax.ShapeDtypeStruct(lag_shape, F32),
         ],
         compiler_params=pltpu.CompilerParams(vmem_limit_bytes=56 << 20),
         cost_estimate=pl.CostEstimate(
-            flops=count * (16 * half * width * turned.shape[0] + 12 * half * rows * width),
-            bytes_accessed=3 * parts * states[0].size * 2 + 2 * turned.size + 8 * before.size,
+            flops=count * (32 * half * turned[0].size + 12 * half * rows * width),
+            bytes_accessed=3 * parts * states[0].size * 2 + 20 * turned[0].size,
             transcendentals=0,
         ),
         name="mix_back",
-    )(order_from, order_to, own, *states, *grads, turned, u00, u10, before, before_lag)
+    )(near, own, *states, *grads, *turned, u00, u10, *before)
 
 
 def lagged(values, edge):
@@ -400,18 +405,17 @@
     factor_in = rms_factor(residual)
     normed_in = residual * factor_in
     states = (normed_in * gain_in).astype(BF16)
-    state_pieces = [spread_pieces(grid, part) for part in cut(states)]
+    state_far = []
+    for c, part in enumerate(cut(states)):
+        if c:
+            part = tie(part, state_far[-1])
+        state_far.append(grid.swap_far(jnp.stack([part] * grid.far)))
 
     hidden_own = w_down.shape[0]
     share = hidden_own // row_count
     packed = jnp.stack([w_gate.T, w_up.T, w_down]).reshape(3, row_count, share, width)
     own_share = lax.dynamic_index_in_dim(packed, lax.axis_index("rows"), 1, keepdims=False)
-    shares = jnp.stack(spread_pieces(grid, own_share), axis=1)
-    weights = spread_rows(shares)
-    gate_t, up_t, down = (
-        weights[:, n].reshape(row_count * grid.size * share, width) for n in range(3)
-    )
-
+    shares = lax.all_gather(tie(own_share, state_far[0]), "filt", axis=1)
     slots = (branches + 1) // 2
     first_branch = index * branches
     t00, t10, u00, u10 = toeplitz_blocks(filters, first_branch // 2, slots)
@@ -422,15 +426,10 @@
         )
     else:
         paired = mixing
-    paired = paired.astype(F32).reshape(slots, 2, width, width)
-    pairs = (
-        jnp.stack([paired[:, 0] + paired[:, 1], paired[:, 0] - paired[:, 1]], axis=1)
-        .astype(BF16)
-        .reshape(2 * slots, width, width)
-    )
-    turned = pairs.transpose(0, 2, 1).reshape(2 * slots * width, width)
-
-    order_from, order_to = grid.order(index, -1), grid.order(index, 1)
+    first, second = (paired[n::2].astype(F32) for n in range(2))
+    pairs = ((first + second).astype(BF16), (first - second).astype(BF16))
+
+    near = jnp.reshape(index % grid.near, (1,)).astype(jnp.int32)
 
     edge = lax.ppermute(
         states[:, :, -1:], "filt", [(f, f + 1) for f in range(grid.size - 1)]
@@ -441,16 +440,51 @@
     )
     cotangent = cotangent_low.astype(F32)
 
+    state_pieces, partials = [], []
+    for c in range(chunks):
+        received = near_swaps(grid, state_far[c])
+        if c:
+            received = tie_all(received, partials[-1][0])
+        pieces = [state_far[c], *received]
+        state_pieces.append(pieces)
+        ahead = [] if c else [regress]
+        if c + 1 < chunks:
+            ahead.append(state_far[c + 1])
+        pieces = [tie(pieces[0], *ahead), *pieces[1:]]
+        partials.append(list(mix_sequences(pieces, near, pairs, t00, t10)))
+    near_received = [near_swaps(grid, partial) for partial in partials]
+    for c in range(chunks - 1):
+        near_received[c] = tie_all(near_received[c], partials[c + 1][0])
+    arrivals = near_received[0] or partials[-1][:1]
+    shares = tie(shares, partials[0][0])
+    full_shares = shares[None]
+    for n, bit in enumerate(reversed(row_bits())):
+        received = swap_rows(full_shares, bit)
+        if n == 0:
+            received = tie(received, *arrivals)
+        full_shares = jnp.concatenate([full_shares, received], axis=0)
+    gate_t, up_t, down = (
+        full_shares[:, n].reshape(row_count * grid.size * share, width) for n in range(3)
+    )
+    late_pairs = tie_all(pairs, *arrivals)
+    turned = [value.transpose(0, 2, 1).reshape(slots * width, width) for value in late_pairs]
+
     spectral = []
     for c in range(chunks):
-        partial = mix_sequences(state_pieces[c], order_from, order_to, pairs, t00, t10)
-        spectral.append(sum_pieces(grid, partial))
-
-    block_out, middle_grad, grad_pieces, kept = [], [], [], []
+        spectral.append(
+            grid.swap_far(total_of([partials[c][0], *near_received[c]]).astype(BF16))
+        )
+
+    block_out, middle_grad, grad_far, kept = [], [], [], []
     gain_mid_part = jnp.zeros((width,), F32)
     for c in range(chunks):
         part = slice(c * step, (c + 1) * step)
-        middle = residual[part] + (spectral[c] + regress[part])
+        arrived = spectral[c]
+        if c:
+            arrived = tie(arrived, middle_grad[-1])
+        if c + 1 < chunks:
+            arrived = tie(arrived, *near_received[c + 1], *turned)
+        middle = residual[part] + (total_of(arrived) + regress[part])
         factor_mid = rms_factor(middle)
         normed_mid = middle * factor_mid
         scaled = (normed_mid * gain_mid).astype(BF16).reshape(-1, width)
@@ -472,44 +506,75 @@
         gain_mid_part = gain_mid_part + jnp.sum(mid_back * normed_mid, axis=(0, 1, 2))
         grad = cotangent[part] + norm_backward(mid_back, normed_mid, factor_mid, gain_mid)
         middle_grad.append(grad)
-        grad_pieces.append(spread_pieces(grid, grad.astype(BF16)))
+        own_grad = grad.astype(BF16)
+        grad_far.append(grid.swap_far(jnp.stack([own_grad] * grid.far)))
         kept.append((scaled, cot_low, hidden, gate_back, up_back))
 
     scaled, cot_low, hidden, gate_back, up_back = (
         jnp.concatenate(values, axis=0) for values in zip(*kept, strict=True)
     )
-    grads = jnp.stack(
-        [
-            contract_rows(gate_back, scaled),
-            contract_rows(up_back, scaled),
-            contract_rows(hidden, cot_low),
-        ]
-    ).reshape(3, row_count, grid.size, share, width)
-    for bit in row_bits():
-        half_count = grads.shape[1] // 2
-        grads = grads[:, :half_count] + swap_rows(
-            grads[:, half_count:].astype(BF16), bit
-        ).astype(F32)
-    grads = grads[:, 0].astype(BF16)
-    returning = []
-    for i in range(grid.far):
-        for j in range(grid.near):
-            n = ((grid.far - i) % grid.far) * grid.near + (grid.near - j) % grid.near
-            returning.append(grads[:, n])
-    own_grads = sum_pieces(grid, returning).astype(BF16)
-
-    before = jnp.zeros((2 * slots, width, width), F32)
-    before_lag = jnp.zeros((lag_count, width // grid.size, width), F32)
+    sources = ((gate_back, scaled), (up_back, scaled), (hidden, cot_low))
+    middle_unit = hidden.shape[1] // 2
+    grads = [
+        [contract_rows(left[:, n * middle_unit : (n + 1) * middle_unit], right) for left, right in sources]
+        for n in range(2)
+    ]
+    bits = row_bits()
+    kept_grads = [
+        stay + swap_rows(away.astype(BF16), bits[0]).astype(F32)
+        for stay, away in zip(*grads, strict=True)
+    ]
+
     own = jnp.reshape(index, (1,)).astype(jnp.int32)
+    before = ()
+    back_partials = []
+    ahead = list(kept_grads)
+    for c in range(chunks):
+        received = near_swaps(grid, grad_far[c])
+        if c:
+            received = tie_all(received, back_partials[-1][0])
+        if c + 1 < chunks:
+            ahead.append(grad_far[c + 1])
+        pieces = [tie(grad_far[c], *ahead), *received]
+        *partial, mixing_sum, lag_sum = mix_sequences_back(
+            state_pieces[c], pieces, near, own, turned, u00, u10, lag_count, before
+        )
+        before = (mixing_sum, lag_sum)
+        back_partials.append(partial)
+        ahead = []
+        if c == 0:
+            for n, bit in enumerate(bits[1:]):
+                half_count = kept_grads[0].shape[0] // 2
+                received = [swap_rows(g[half_count:].astype(BF16), bit) for g in kept_grads]
+                if n == 0:
+                    received = tie_all(received, partial[0])
+                kept_grads = [
+                    g[:half_count] + value.astype(F32)
+                    for g, value in zip(kept_grads, received, strict=True)
+                ]
+            filt_grads = jnp.stack(
+                [g.astype(BF16).reshape(grid.size, share, width) for g in kept_grads], axis=1
+            )
+            ahead = [filt_grads]
+    near_received = [near_swaps(grid, partial) for partial in back_partials]
+    for c in range(chunks - 1):
+        near_received[c] = tie_all(near_received[c], back_partials[c + 1][0])
+    arrivals = near_received[0] or back_partials[-1][:1]
+    filt_grads = tie(
+        lax.all_to_all(filt_grads, "filt", 0, 0, tiled=True), back_partials[-1][0]
+    )
+    mixing_sum, lag_sum = tie_all([mixing_sum, lag_sum], *arrivals)
+    near_received[0] = tie_all(near_received[0], filt_grads)
     state_back = []
     for c in range(chunks):
-        *partial, before, before_lag = mix_sequences_back(
-            state_pieces[c], grad_pieces[c], order_from, order_to, own, turned, u00, u10,
-            before, before_lag,
-        )
-        state_back.append(sum_pieces(grid, partial))
-
-    doubled = before.reshape(slots, 2, width, width)
+        state_back.append(
+            total_of(
+                grid.swap_far(total_of([back_partials[c][0], *near_received[c]]).astype(BF16))
+            )
+        )
+    own_grads = jnp.sum(filt_grads.astype(F32), axis=0).astype(BF16)
+
+    doubled = mixing_sum.reshape(slots, 2, width, width)
     mixing_part = jnp.stack(
         [doubled[:, 0] + doubled[:, 1], doubled[:, 0] - doubled[:, 1]], axis=1
     ).reshape(2 * slots, width, width)
@@ -519,7 +584,7 @@
 
     slab = width // grid.size
     own_regression = lax.dynamic_slice_in_dim(regression, index * slab, slab, 1)
-    gain_lag = jnp.sum(own_regression.astype(F32) * before_lag, axis=(0, 2))
+    gain_lag = jnp.sum(own_regression.astype(F32) * lag_sum, axis=(0, 2))
     gain_in_part = jnp.sum(mixing.astype(F32) * mixing_part, axis=(0, 2))
     gain_in_part = lax.dynamic_update_slice_in_dim(
         gain_in_part,
@@ -529,7 +594,7 @@
     ) / gain_in
     gains = jnp.stack([gain_in_part, gain_mid_part])
     small = jnp.concatenate(
-        [before_lag.reshape(lag_count * slab, width), jnp.pad(gains, ((0, 6), (0, 0)))], axis=0
+        [lag_sum.reshape(lag_count * slab, width), jnp.pad(gains, ((0, 6), (0, 0)))], axis=0
     )
     for bit in row_bits():
         rounded = small[:-8].astype(BF16)
@@ -540,13 +605,15 @@
     gain_high = small[-8:].astype(BF16)
     gain_low = (small[-8:] - gain_high.astype(F32)).astype(BF16)
     small_low = jnp.concatenate([small[:-8].astype(BF16), gain_high, gain_low], axis=0)
-    spread = jnp.stack(spread_pieces(grid, small_low))
+    spread = lax.all_gather(small_low, "filt", axis=0)
     gains = jnp.sum(spread[:, -16:-8].astype(F32) + spread[:, -8:].astype(F32), axis=0)
-    regression_grad = jnp.zeros((lag_count, grid.size, slab, width), F32)
-    for n in range(grid.size):
-        piece = spread[n, :-16].astype(F32).reshape(lag_count, 1, slab, width)
-        regression_grad = lax.dynamic_update_slice_in_dim(regression_grad, piece, order_from[n], 1)
-    regression_grad = regression_grad.reshape(lag_count, width, width)
+    regression_grad = (
+        spread[:, :-16]
+        .reshape(grid.size, lag_count, slab, width)
+        .transpose(1, 0, 2, 3)
+        .reshape(lag_count, width, width)
+        .astype(F32)
+    )
 
     mix_back = jnp.concatenate(middle_grad, axis=0).astype(BF16)
     edge = lax.ppermute(

time: 616 us -> 492 us (0.80)
  starting transfers between devices: 142 us -> 73.2 us
  waiting for transfers between devices: 222 us -> 157 us
  matrix products: 26.3 us -> 35.9 us
  other arithmetic: 60.6 us -> 67.1 us
    ppermute x77 -> x8, waiting for transfers between devices: 165 us -> 36.9 us  [near_swaps(): lax.ppermute(values[j] if isinstance(values, list) else values, 'filt', g...]
    ppermute x77 -> x8, starting transfers between devices: 128 us -> 14.1 us  [near_swaps(): lax.ppermute(values[j] if isinstance(values, list) else values, 'filt', g...]
    all_to_all x0 -> x9, waiting for transfers between devices: none -> 74 us  [the longest x8 74 us: swap_far(): lax.all_to_all(values, 'filt', 0, 0, axis_index_groups=groups, tiled=True)]
    all_to_all x0 -> x9, starting transfers between devices: none -> 43 us  [the longest x8 37.9 us: swap_far(): lax.all_to_all(values, 'filt', 0, 0, axis_index_groups=groups, tiled=True)]
    ppermute x12 -> x16, waiting for transfers between devices: 56.8 us -> 38.3 us  [swap_rows(): return lax.ppermute(values, 'rows', [(r, r ^ bit) for r in range(count)])]
    another operation x3 -> x1, other arithmetic: 16.2 us -> 1.31 us  [shards(): jnp.stack([g.astype(BF16).reshape(grid.size, share, width) for g in kept_...]
    convert_element_type x15 -> x10, other arithmetic: 1.99 us -> 16.7 us  [the longest x2 3.93 us: shards(): total_of([partials[c][0], *near_received[c]]).astype(BF16)]
    all_gather x0 -> x2, waiting for transfers between devices: none -> 7.65 us  [the longest x1 7.64 us: shards(): shares = lax.all_gather(tie(own_share, state_far[0]), 'filt', axis=1)]
  transfers between devices with their start and end apart: 91 -> 37, of which waited for: 34 -> 16; matrix products, arithmetic and copies ran while one was open for 17% -> 24% of each run, Pallas kernels for 11% -> 20%
where the time goes in v2:
time: 492 us; the launch traced here: 487 us
  waiting for transfers between devices  157 us (32%)
  Pallas kernels  95.4 us (19%)
  starting transfers between devices  73.2 us (15%)
  other arithmetic  67.1 us (14%)
  local copies, waits for them, and re-layouts  42.6 us (9%)
  matrix products  35.9 us (7%)
  between operations  15.8 us (3%)
    all_to_all x8, waiting for transfers between devices, swap_far(): lax.all_to_all(values, 'filt', 0, 0, axis_index_groups=groups, tiled=True)  74 us
    pallas_call x2, Pallas kernels, mix_sequences_back(): pl.pallas_call(functools.partial(mix_back_kernel, parts), grid_spec=pltpu...  57.1 us
    ppermute x16, waiting for transfers between devices, swap_rows(): return lax.ppermute(values, 'rows', [(r, r ^ bit) for r in range(count)])  38.3 us
    all_to_all x8, starting transfers between devices, swap_far(): lax.all_to_all(values, 'filt', 0, 0, axis_index_groups=groups, tiled=True)  37.9 us
    ppermute x8, waiting for transfers between devices, near_swaps(): lax.ppermute(values[j] if isinstance(values, list) else values, 'filt', g...  36.9 us
    pallas_call x2, Pallas kernels, mix_sequences(): pl.pallas_call(functools.partial(mix_kernel, parts), grid_spec=pltpu.Pref...  30.8 us
    ppermute x8, starting transfers between devices, near_swaps(): lax.ppermute(values[j] if isinstance(values, list) else values, 'filt', g...  14.1 us
    dot_general x6, matrix products, contract_rows(): lax.dot_general(left, right, (((0,), (0,)), ((), ())), preferred_element_...  11.6 us
  transfers between devices with their start and end apart: 37, of which 16 were waited for; matrix products, arithmetic and copies ran while one was open for 24% of the time, Pallas kernels for 20%

profile of v2, /device:TPU:0, one launch (start us, length us, event | category | flops | bytes accessed | tf_op | source)
XLA Modules:
  0.0 486.9 jit_solution(5381146694498568170)
XLA Ops:
  11.9 6.4 %all-to-all-start = ((bf16[4,2,2,64,512]{4,3,2,1,0:T(8,128)(2,1)}), bf16[4,2,2,64,512]{4,3,2,1,0:T(8,128)(2,1)S(1)}, u32[]{:S(2)}, u32[]{:S(2)}) async-start(bf16[4,2,2,64,512]{4,3,2,1,0:T(8,128)(2,1)} %stack.79), calls=%async_computation | async-start | bytes 2097152 | tf_op jit(solution)/shard_map/all_to_all | solution.py:51
  25.2 18.9 %all-to-all-done.refs_0_ = bf16[4,2,2,64,512]{4,3,2,1,0:T(8,128)(2,1)S(1)} async-done(((bf16[4,2,2,64,512]{4,3,2,1,0:T(8,128)(2,1)}), bf16[4,2,2,64,512]{4,3,2,1,0:T(8,128)(2,1)S(1)}, u32[]{:S(2)}, u32[]{:S(2)}) %all-to-all-start) | async-done | bytes 1048608 | tf_op jit(solution)/shard_map/all_to_all | solution.py:51
  46.1 4.5 all-to-all-start.1
  51.3 3.8 fusion.2
  62.0 7.4 %toeplitz.1 = (bf16[2,256,1536]{2,1,0:T(8,128)(2,1)}, bf16[2,256,1536]{2,1,0:T(8,128)(2,1)}, bf16[2,1536,256]{2,1,0:T(8,128)(2,1)}, bf16[2,1536,256]{2,1,0:T(8,128)(2,1)}) custom-call(f32[12,1,1024]{2,1,0:T(1,128)} %copy.94.down_ref, f32[12,1,1024]{2,1,0:T(1,128)} %broadcast_in_dim.11.up_ref), custom_call_target="tpu_custom_call" | custom-call | tf_op jit(solution)/shard_map/toeplitz/pallas_call | solution.py:150
  73.8 8.4 %all-to-all-done.1.refs_0_ = bf16[4,2,2,64,512]{4,3,2,1,0:T(8,128)(2,1)} async-done(((bf16[4,2,2,64,512]{4,3,2,1,0:T(8,128)(2,1)}), bf16[4,2,2,64,512]{4,3,2,1,0:T(8,128)(2,1)}, u32[]{:S(2)}, u32[]{:S(2)}) %all-to-all-start.1) | async-done | bytes 1048608 | tf_op jit(solution)/shard_map/all_to_all | solution.py:51
  83.7 15.1 %mix.2 = (bf16[4,2,2,64,512]{4,3,2,1,0:T(8,128)(2,1)S(1)}, bf16[4,2,2,64,512]{4,3,2,1,0:T(8,128)(2,1)S(1)}) custom-call(s32[1]{0:T(128)} %bitcast.2.near_ref, bf16[4,2,2,64,512]{4,3,2,1,0:T(8,128)(2,1)S(1)} %all-to-all-done.refs_0_, bf16[4,2,2,64,512]{4,3,2,1,0:T(8,128)(2,1)} %collective-permute-done.1.refs_1_, ...), custom_call_target="tpu_custom_call" | custom-call | flops 11274289152 | bytes 10485760 | tf_op jit(solution)/shard_map/mix/pallas_call | solution.py:292
  100.8 7.6 %all-gather.5.cloned.1.call-done = bf16[3,512,512]{2,1,0:T(8,128)(2,1)} async-done(((bf16[3,64,512]{2,1,0:T(8,128)(2,1)}), bf16[3,512,512]{2,1,0:T(8,128)(2,1)}) %all-gather.5.cloned.1.call-update) | async-done | bytes 1572880 | tf_op jit(solution)/shard_map/all_gather | solution.py:418
  111.0 4.5 collective-permute-done.3.refs_1_
  115.6 15.7 %mix.3 = (bf16[4,2,2,64,512]{4,3,2,1,0:T(8,128)(2,1)S(1)}, bf16[4,2,2,64,512]{4,3,2,1,0:T(8,128)(2,1)S(1)}) custom-call(s32[1]{0:T(128)} %bitcast.2.near_ref, bf16[4,2,2,64,512]{4,3,2,1,0:T(8,128)(2,1)} %all-to-all-done.1.refs_0_, bf16[4,2,2,64,512]{4,3,2,1,0:T(8,128)(2,1)} %collective-permute-done.3.refs_1_, ...), custom_call_target="tpu_custom_call" | custom-call | flops 11274289152 | bytes 10485760 | tf_op jit(solution)/shard_map/mix/pallas_call | solution.py:292
  131.3 6.0 %collective-permute-done.2 = bf16[4,2,2,64,512]{4,3,2,1,0:T(8,128)(2,1)S(1)} collective-permute-done((bf16[4,2,2,64,512]{4,3,2,1,0:T(8,128)(2,1)}, bf16[4,2,2,64,512]{4,3,2,1,0:T(8,128)(2,1)S(1)}, u32[]{:S(2)}, u32[]{:S(2)}) %collective-permute-start.2) | collective-permute-done | bytes 1048608 | tf_op jit(solution)/shard_map/ppermute | solution.py:65
  137.3 6.9 %collective-permute-done.5 = bf16[1,3,8,64,512]{4,3,2,0,1:T(8,128)(2,1)S(1)} collective-permute-done((bf16[1,3,8,64,512]{4,3,2,0,1:T(8,128)(2,1)}, bf16[1,3,8,64,512]{4,3,2,0,1:T(8,128)(2,1)S(1)}, u32[]{:S(2)}, u32[]{:S(2)}) %collective-permute-start.5) | collective-permute-done | bytes 1572896 | tf_op jit(solution)/shard_map/ppermute | solution.py:81
  147.8 4.2 all-to-all-start.2
  163.1 14.8 %collective-permute-done.4 = bf16[4,2,2,64,512]{4,3,2,1,0:T(8,128)(2,1)} collective-permute-done((bf16[4,2,2,64,512]{4,3,2,1,0:T(8,128)(2,1)}, bf16[4,2,2,64,512]{4,3,2,1,0:T(8,128)(2,1)}, u32[]{:S(2)}, u32[]{:S(2)}) %collective-permute-start.4) | collective-permute-done | bytes 1048608 | tf_op jit(solution)/shard_map/ppermute | solution.py:65
  180.5 4.8 all-to-all-start.3
  197.9 12.9 %all-to-all-done.3 = bf16[4,2,2,64,512]{4,3,2,1,0:T(8,128)(2,1)} async-done(((bf16[4,2,2,64,512]{4,3,2,1,0:T(8,128)(2,1)}), bf16[4,2,2,64,512]{4,3,2,1,0:T(8,128)(2,1)}, u32[]{:S(2)}, u32[]{:S(2)}) %all-to-all-start.3) | async-done | bytes 1048608 | tf_op jit(solution)/shard_map/all_to_all | solution.py:51
  224.8 4.6 all-to-all-start.4
  241.8 12.7 %all-to-all-done.4.refs_2_ = bf16[4,2,2,64,512]{4,3,2,1,0:T(8,128)(2,1)} async-done(((bf16[4,2,2,64,512]{4,3,2,1,0:T(8,128)(2,1)}), bf16[4,2,2,64,512]{4,3,2,1,0:T(8,128)(2,1)}, u32[]{:S(2)}, u32[]{:S(2)}) %all-to-all-start.4) | async-done | bytes 1048608 | tf_op jit(solution)/shard_map/all_to_all | solution.py:51
  255.6 4.4 all-to-all-start.5
  277.5 7.8 %all-to-all-done.5.refs_2_ = bf16[4,2,2,64,512]{4,3,2,1,0:T(8,128)(2,1)} async-done(((bf16[4,2,2,64,512]{4,3,2,1,0:T(8,128)(2,1)}), bf16[4,2,2,64,512]{4,3,2,1,0:T(8,128)(2,1)}, u32[]{:S(2)}, u32[]{:S(2)}) %all-to-all-start.5) | async-done | bytes 1048608 | tf_op jit(solution)/shard_map/all_to_all | solution.py:51
  288.6 27.8 %mix_back.2 = (bf16[4,2,2,64,512]{4,3,2,1,0:T(8,128)(2,1)}, bf16[4,2,2,64,512]{4,3,2,1,0:T(8,128)(2,1)}, f32[6,512,512]{2,1,0:T(8,128)}, f32[3,64,512]{2,1,0:T(8,128)}) custom-call(s32[1]{0:T(128)} %bitcast.2.near_ref, s32[1]{0:T(128)} %bitcast.47.own_ref, bf16[4,2,2,64,512]{4,3,2,1,0:T(8,128)(2,1)} %copy-done.2, ...), custom_call_target="tpu_custom_call" | custom-call | flops 17716740096 | bytes 22020096 | tf_op jit(solution)/shard_map/mix_back/pallas_call | solution.py:328
  322.5 5.0 %all-to-all-start.6 = ((bf16[8,3,64,512]{3,2,1,0:T(8,128)(2,1)}), bf16[8,3,64,512]{3,2,1,0:T(8,128)(2,1)S(1)}, u32[]{:S(2)}, u32[]{:S(2)}) async-start(bf16[8,3,64,512]{3,2,1,0:T(8,128)(2,1)} %pad_maximum_fusion.3), calls=%async_computation.6 | async-start | bytes 3145728 | tf_op jit(solution)/shard_map/all_to_all | solution.py:564
  327.6 29.4 %mix_back.3 = (bf16[4,2,2,64,512]{4,3,2,1,0:T(8,128)(2,1)}, bf16[4,2,2,64,512]{4,3,2,1,0:T(8,128)(2,1)}, f32[6,512,512]{2,1,0:T(8,128)}, f32[3,64,512]{2,1,0:T(8,128)}) custom-call(s32[1]{0:T(128)} %bitcast.2.near_ref, s32[1]{0:T(128)} %bitcast.47.own_ref, bf16[4,2,2,64,512]{4,3,2,1,0:T(8,128)(2,1)} %all-to-all-done.1.refs_0_, ...), custom_call_target="tpu_custom_call" | custom-call | flops 17716740096 | bytes 22020096 | tf_op jit(solution)/shard_map/mix_back/pallas_call | solution.py:328
  359.0 4.0 slice_add_fusion
  371.3 10.6 %collective-permute-done.17 = bf16[4,2,2,64,512]{4,3,2,1,0:T(8,128)(2,1)S(1)} collective-permute-done((bf16[4,2,2,64,512]{4,3,2,1,0:T(8,128)(2,1)}, bf16[4,2,2,64,512]{4,3,2,1,0:T(8,128)(2,1)S(1)}, u32[]{:S(2)}, u32[]{:S(2)}) %collective-permute-start.17) | collective-permute-done | bytes 1048608 | tf_op jit(solution)/shard_map/ppermute | solution.py:65
  383.5 4.3 all-to-all-start.8
  388.6 4.2 fusion.4
  399.3 17.3 %collective-permute-done.24 = bf16[1,3,64,512]{3,2,0,1:T(8,128)(2,1)S(1)} collective-permute-done((bf16[1,3,64,512]{3,2,0,1:T(8,128)(2,1)S(1)}, bf16[1,3,64,512]{3,2,0,1:T(8,128)(2,1)S(1)}, u32[]{:S(2)}, u32[]{:S(2)}) %collective-permute-start.24) | collective-permute-done | bytes 196640 | tf_op jit(solution)/shard_map/ppermute | solution.py:81
  420.6 4.7 all-to-all-start.7
  434.9 13.4 %collective-permute-done.20 = bf16[6,128,512]{2,1,0:T(8,128)(2,1)S(1)} collective-permute-done((bf16[6,128,512]{2,1,0:T(8,128)(2,1)}, bf16[6,128,512]{2,1,0:T(8,128)(2,1)S(1)}, u32[]{:S(2)}, u32[]{:S(2)}) %collective-permute-start.20) | collective-permute-done | bytes 786464 | tf_op jit(solution)/shard_map/ppermute | solution.py:81
  450.9 13.3 %all-to-all-done.7 = bf16[4,2,2,64,512]{4,3,2,1,0:T(8,128)(2,1)} async-done(((bf16[4,2,2,64,512]{4,3,2,1,0:T(8,128)(2,1)}), bf16[4,2,2,64,512]{4,3,2,1,0:T(8,128)(2,1)}, u32[]{:S(2)}, u32[]{:S(2)}) %all-to-all-start.7) | async-done | bytes 1048608 | tf_op jit(solution)/shard_map/all_to_all | solution.py:51
  476.0 3.6 maximum_convert_fusion
  (338 shorter events, 161.8 us)
Async XLA Ops:
  11.9 32.2 %all-to-all-start = ((bf16[4,2,2,64,512]{4,3,2,1,0:T(8,128)(2,1)}), bf16[4,2,2,64,512]{4,3,2,1,0:T(8,128)(2,1)S(1)}, u32[]{:S(2)}, u32[]{:S(2)}) async-start(bf16[4,2,2,64,512]{4,3,2,1,0:T(8,128)(2,1)} %stack.79), calls=%async_computation | async-start | bytes 2097152 | tf_op jit(solution)/shard_map/all_to_all | solution.py:51
  18.4 90.1 %all-gather.5.cloned.1.call-start = ((), (), s32[]{:S(2)}) async-start(), calls=%async_computation.9 | async-start | bytes 1769472 | tf_op jit(solution)/shard_map/all_gather | solution.py:418
  19.0 50.4 %collective-permute-start = (bf16[4,2,1,512]{3,2,1,0:T(2,128)(2,1)}, bf16[4,2,1,512]{3,2,1,0:T(2,128)(2,1)S(1)}, u32[]{:S(2)}, u32[]{:S(2)}) collective-permute-start(bf16[4,2,1,512]{3,2,1,0:T(2,128)(2,1)} %slice.371), channel_id=1, source_target_pairs={{0,1},{1,2},{2,3},{3,4},{4,5},{5,6},{6,7},{8,9},{9,10},{10,11},{11... | collective-permute-start | bytes 24584 | tf_op jit(solution)/shard_map/ppermute | solution.py:434
  46.1 36.1 %all-to-all-start.1 = ((bf16[4,2,2,64,512]{4,3,2,1,0:T(8,128)(2,1)}), bf16[4,2,2,64,512]{4,3,2,1,0:T(8,128)(2,1)}, u32[]{:S(2)}, u32[]{:S(2)}) async-start(bf16[4,2,2,64,512]{4,3,2,1,0:T(8,128)(2,1)} %stack.81), calls=%async_computation.1 | async-start | bytes 2097152 | tf_op jit(solution)/shard_map/all_to_all | solution.py:51
  55.1 28.6 %collective-permute-start.1 = (bf16[4,2,2,64,512]{4,3,2,1,0:T(8,128)(2,1)S(1)}, bf16[4,2,2,64,512]{4,3,2,1,0:T(8,128)(2,1)}, u32[]{:S(2)}, u32[]{:S(2)}) collective-permute-start(bf16[4,2,2,64,512]{4,3,2,1,0:T(8,128)(2,1)S(1)} %all-to-all-done.refs_0_), channel_id=1, source_target_pairs={{0,1},{1,0},{2,3},{3,2},{4,5},{5,4},{6,7},{7,6},{8,9},{9,8},{10,11... | collective-permute-start | bytes 3145736 | tf_op jit(solution)/shard_map/ppermute | solution.py:65
  82.1 33.4 %collective-permute-start.3 = (bf16[4,2,2,64,512]{4,3,2,1,0:T(8,128)(2,1)}, bf16[4,2,2,64,512]{4,3,2,1,0:T(8,128)(2,1)}, u32[]{:S(2)}, u32[]{:S(2)}) collective-permute-start(bf16[4,2,2,64,512]{4,3,2,1,0:T(8,128)(2,1)} %all-to-all-done.1.refs_0_), channel_id=1, source_target_pairs={{0,1},{1,0},{2,3},{3,2},{4,5},{5,4},{6,7},{7,6},{8,9},{9,8},{10,11... | collective-permute-start | bytes 3145736 | tf_op jit(solution)/shard_map/ppermute | solution.py:65
  108.4 35.8 %collective-permute-start.5 = (bf16[1,3,8,64,512]{4,3,2,0,1:T(8,128)(2,1)}, bf16[1,3,8,64,512]{4,3,2,0,1:T(8,128)(2,1)S(1)}, u32[]{:S(2)}, u32[]{:S(2)}) collective-permute-start(bf16[1,3,8,64,512]{4,3,2,0,1:T(8,128)(2,1)} %bitcast.243), channel_id=1, source_target_pairs={{0,16},{8,24},{16,0},{24,8},{1,17},{9,25},{17,1},{25,9},{2,18},{10... | collective-permute-start | bytes 4718600 | tf_op jit(solution)/shard_map/ppermute | solution.py:81
  109.9 27.4 %collective-permute-start.2 = (bf16[4,2,2,64,512]{4,3,2,1,0:T(8,128)(2,1)}, bf16[4,2,2,64,512]{4,3,2,1,0:T(8,128)(2,1)S(1)}, u32[]{:S(2)}, u32[]{:S(2)}) collective-permute-start(bf16[4,2,2,64,512]{4,3,2,1,0:T(8,128)(2,1)} %copy-done.4), channel_id=1, source_target_pairs={{0,1},{1,0},{2,3},{3,2},{4,5},{5,4},{6,7},{7,6},{8,9},{9,8},{10,11... | collective-permute-start | bytes 3145736 | tf_op jit(solution)/shard_map/ppermute | solution.py:65
  146.4 40.8 %collective-permute-start.6 = (bf16[2,3,8,64,512]{4,3,2,0,1:T(8,128)(2,1)}, bf16[2,3,8,64,512]{4,3,2,0,1:T(8,128)(2,1)}, u32[]{:S(2)}, u32[]{:S(2)}) collective-permute-start(bf16[2,3,8,64,512]{4,3,2,0,1:T(8,128)(2,1)} %pad_maximum_fusion.2), channel_id=1, source_target_pairs={{0,8},{8,0},{16,24},{24,16},{1,9},{9,1},{17,25},{25,17},{2,10},{10... | collective-permute-start | bytes 9437192 | tf_op jit(solution)/shard_map/ppermute | solution.py:81
  147.8 32.7 %all-to-all-start.2 = ((bf16[4,2,2,64,512]{4,3,2,1,0:T(8,128)(2,1)}), bf16[4,2,2,64,512]{4,3,2,1,0:T(8,128)(2,1)}, u32[]{:S(2)}, u32[]{:S(2)}) async-start(bf16[4,2,2,64,512]{4,3,2,1,0:T(8,128)(2,1)} %add_convert_fusion.3), calls=%async_computation.2 | async-start | bytes 2097152 | tf_op jit(solution)/shard_map/all_to_all | solution.py:51
  152.0 26.0 %collective-permute-start.4 = (bf16[4,2,2,64,512]{4,3,2,1,0:T(8,128)(2,1)}, bf16[4,2,2,64,512]{4,3,2,1,0:T(8,128)(2,1)}, u32[]{:S(2)}, u32[]{:S(2)}) collective-permute-start(bf16[4,2,2,64,512]{4,3,2,1,0:T(8,128)(2,1)} %copy-done.3), channel_id=1, source_target_pairs={{0,1},{1,0},{2,3},{3,2},{4,5},{5,4},{6,7},{7,6},{8,9},{9,8},{10,11... | collective-permute-start | bytes 3145736 | tf_op jit(solution)/shard_map/ppermute | solution.py:65
  180.5 30.3 %all-to-all-start.3 = ((bf16[4,2,2,64,512]{4,3,2,1,0:T(8,128)(2,1)}), bf16[4,2,2,64,512]{4,3,2,1,0:T(8,128)(2,1)}, u32[]{:S(2)}, u32[]{:S(2)}) async-start(bf16[4,2,2,64,512]{4,3,2,1,0:T(8,128)(2,1)} %add_convert_fusion.2), calls=%async_computation.3 | async-start | bytes 2097152 | tf_op jit(solution)/shard_map/all_to_all | solution.py:51
  222.4 38.8 %collective-permute-start.16 = (bf16[4,2,1,512]{3,2,1,0:T(2,128)(2,1)S(1)}, bf16[4,2,1,512]{3,2,1,0:T(2,128)(2,1)S(1)}, u32[]{:S(2)}, u32[]{:S(2)}) collective-permute-start(bf16[4,2,1,512]{3,2,1,0:T(2,128)(2,1)S(1)} %fusion.72), channel_id=1, source_target_pairs={{1,0},{2,1},{3,2},{4,3},{5,4},{6,5},{7,6},{9,8},{10,9},{11,10},{12... | collective-permute-start | bytes 24584 | tf_op jit(solution)/shard_map/ppermute | solution.py:619
  224.8 29.7 %all-to-all-start.4 = ((bf16[4,2,2,64,512]{4,3,2,1,0:T(8,128)(2,1)}), bf16[4,2,2,64,512]{4,3,2,1,0:T(8,128)(2,1)}, u32[]{:S(2)}, u32[]{:S(2)}) async-start(bf16[4,2,2,64,512]{4,3,2,1,0:T(8,128)(2,1)} %stack.92), calls=%async_computation.4 | async-start | bytes 2097152 | tf_op jit(solution)/shard_map/all_to_all | solution.py:51
  232.7 33.0 %collective-permute-start.7 = (bf16[1024,512]{1,0:T(8,128)(2,1)}, bf16[1024,512]{1,0:T(8,128)(2,1)}, u32[]{:S(2)}, u32[]{:S(2)}) collective-permute-start(bf16[1024,512]{1,0:T(8,128)(2,1)} %convolution_convert_fusion.2), channel_id=1, source_target_pairs={{0,8},{8,0},{16,24},{24,16},{1,9},{9,1},{17,25},{25,17},{2,10},{10... | collective-permute-start | bytes 3145736 | tf_op jit(solution)/shard_map/ppermute | solution.py:81
  234.6 35.6 %collective-permute-start.8 = (bf16[1024,512]{1,0:T(8,128)(2,1)}, bf16[1024,512]{1,0:T(8,128)(2,1)}, u32[]{:S(2)}, u32[]{:S(2)}) collective-permute-start(bf16[1024,512]{1,0:T(8,128)(2,1)} %convolution_convert_fusion.1), channel_id=1, source_target_pairs={{0,8},{8,0},{16,24},{24,16},{1,9},{9,1},{17,25},{25,17},{2,10},{10... | collective-permute-start | bytes 3145736 | tf_op jit(solution)/shard_map/ppermute | solution.py:81
  255.6 29.7 %all-to-all-start.5 = ((bf16[4,2,2,64,512]{4,3,2,1,0:T(8,128)(2,1)}), bf16[4,2,2,64,512]{4,3,2,1,0:T(8,128)(2,1)}, u32[]{:S(2)}, u32[]{:S(2)}) async-start(bf16[4,2,2,64,512]{4,3,2,1,0:T(8,128)(2,1)} %stack.93), calls=%async_computation.5 | async-start | bytes 2097152 | tf_op jit(solution)/shard_map/all_to_all | solution.py:51
  261.8 26.8 %collective-permute-start.10 = (bf16[4,2,2,64,512]{4,3,2,1,0:T(8,128)(2,1)}, bf16[4,2,2,64,512]{4,3,2,1,0:T(8,128)(2,1)}, u32[]{:S(2)}, u32[]{:S(2)}) collective-permute-start(bf16[4,2,2,64,512]{4,3,2,1,0:T(8,128)(2,1)} %all-to-all-done.4.refs_2_), channel_id=1, source_target_pairs={{0,1},{1,0},{2,3},{3,2},{4,5},{5,4},{6,7},{7,6},{8,9},{9,8},{10,11... | collective-permute-start | bytes 3145736 | tf_op jit(solution)/shard_map/ppermute | solution.py:65
  268.7 49.7 %collective-permute-start.12 = (bf16[512,512]{1,0:T(8,128)(2,1)}, bf16[512,512]{1,0:T(8,128)(2,1)}, u32[]{:S(2)}, u32[]{:S(2)}) collective-permute-start(bf16[512,512]{1,0:T(8,128)(2,1)} %slice.594), channel_id=1, source_target_pairs={{0,16},{8,24},{16,0},{24,8},{1,17},{9,25},{17,1},{25,9},{2,18},{10... | collective-permute-start | bytes 1572872 | tf_op jit(solution)/shard_map/ppermute | solution.py:81
  273.2 45.2 %collective-permute-start.13 = (bf16[512,512]{1,0:T(8,128)(2,1)}, bf16[512,512]{1,0:T(8,128)(2,1)}, u32[]{:S(2)}, u32[]{:S(2)}) collective-permute-start(bf16[512,512]{1,0:T(8,128)(2,1)} %slice.593), channel_id=1, source_target_pairs={{0,16},{8,24},{16,0},{24,8},{1,17},{9,25},{17,1},{25,9},{2,18},{10... | collective-permute-start | bytes 1572872 | tf_op jit(solution)/shard_map/ppermute | solution.py:81
  276.2 42.2 %collective-permute-start.14 = (bf16[512,512]{1,0:T(8,128)(2,1)}, bf16[512,512]{1,0:T(8,128)(2,1)}, u32[]{:S(2)}, u32[]{:S(2)}) collective-permute-start(bf16[512,512]{1,0:T(8,128)(2,1)} %slice.592), channel_id=1, source_target_pairs={{0,16},{8,24},{16,0},{24,8},{1,17},{9,25},{17,1},{25,9},{2,18},{10... | collective-permute-start | bytes 1572872 | tf_op jit(solution)/shard_map/ppermute | solution.py:81
  285.3 42.3 %collective-permute-start.15 = (bf16[4,2,2,64,512]{4,3,2,1,0:T(8,128)(2,1)}, bf16[4,2,2,64,512]{4,3,2,1,0:T(8,128)(2,1)}, u32[]{:S(2)}, u32[]{:S(2)}) collective-permute-start(bf16[4,2,2,64,512]{4,3,2,1,0:T(8,128)(2,1)} %all-to-all-done.5.refs_2_), channel_id=1, source_target_pairs={{0,1},{1,0},{2,3},{3,2},{4,5},{5,4},{6,7},{7,6},{8,9},{9,8},{10,11... | collective-permute-start | bytes 3145736 | tf_op jit(solution)/shard_map/ppermute | solution.py:65
  316.4 42.6 %collective-permute-start.11 = (bf16[4,2,2,64,512]{4,3,2,1,0:T(8,128)(2,1)}, bf16[4,2,2,64,512]{4,3,2,1,0:T(8,128)(2,1)S(1)}, u32[]{:S(2)}, u32[]{:S(2)}) collective-permute-start(bf16[4,2,2,64,512]{4,3,2,1,0:T(8,128)(2,1)} %get-tuple-element.68), channel_id=1, source_target_pairs={{0,1},{1,0},{2,3},{3,2},{4,5},{5,4},{6,7},{7,6},{8,9},{9,8},{10,11... | collective-permute-start | bytes 3145736 | tf_op jit(solution)/shard_map/ppermute | solution.py:65
  322.5 61.0 %all-to-all-start.6 = ((bf16[8,3,64,512]{3,2,1,0:T(8,128)(2,1)}), bf16[8,3,64,512]{3,2,1,0:T(8,128)(2,1)S(1)}, u32[]{:S(2)}, u32[]{:S(2)}) async-start(bf16[8,3,64,512]{3,2,1,0:T(8,128)(2,1)} %pad_maximum_fusion.3), calls=%async_computation.6 | async-start | bytes 3145728 | tf_op jit(solution)/shard_map/all_to_all | solution.py:564
  356.9 25.0 %collective-permute-start.17 = (bf16[4,2,2,64,512]{4,3,2,1,0:T(8,128)(2,1)}, bf16[4,2,2,64,512]{4,3,2,1,0:T(8,128)(2,1)S(1)}, u32[]{:S(2)}, u32[]{:S(2)}) collective-permute-start(bf16[4,2,2,64,512]{4,3,2,1,0:T(8,128)(2,1)} %get-tuple-element.80), channel_id=1, source_target_pairs={{0,1},{1,0},{2,3},{3,2},{4,5},{5,4},{6,7},{7,6},{8,9},{9,8},{10,11... | collective-permute-start | bytes 3145736 | tf_op jit(solution)/shard_map/ppermute | solution.py:65
  368.3 20.3 %collective-permute-start.18 = (bf16[6,256,512]{2,1,0:T(8,128)(2,1)S(1)}, bf16[6,256,512]{2,1,0:T(8,128)(2,1)}, u32[]{:S(2)}, u32[]{:S(2)}) collective-permute-start(bf16[6,256,512]{2,1,0:T(8,128)(2,1)S(1)} %fusion.7), channel_id=1, source_target_pairs={{0,8},{8,0},{16,24},{24,16},{1,9},{9,1},{17,25},{25,17},{2,10},{10... | collective-permute-start | bytes 4718600 | tf_op jit(solution)/shard_map/ppermute | solution.py:81
  383.5 37.1 %all-to-all-start.8 = ((bf16[4,2,2,64,512]{4,3,2,1,0:T(8,128)(2,1)}), bf16[4,2,2,64,512]{4,3,2,1,0:T(8,128)(2,1)}, u32[]{:S(2)}, u32[]{:S(2)}) async-start(bf16[4,2,2,64,512]{4,3,2,1,0:T(8,128)(2,1)} %add_convert_fusion), calls=%async_computation.8 | async-start | bytes 2097152 | tf_op jit(solution)/shard_map/all_to_all | solution.py:51
  387.8 80.8 %all-gather.7.cloned.1.call-start = ((), (), s32[]{:S(2)}) async-start(), calls=%async_computation.10 | async-start | bytes 1916928 | tf_op jit(solution)/shard_map/all_gather | solution.py:608
  393.9 32.2 %collective-permute-start.19 = (bf16[6,128,512]{2,1,0:T(8,128)(2,1)}, bf16[6,128,512]{2,1,0:T(8,128)(2,1)}, u32[]{:S(2)}, u32[]{:S(2)}) collective-permute-start(bf16[6,128,512]{2,1,0:T(8,128)(2,1)} %fusion.34), channel_id=1, source_target_pairs={{0,16},{8,24},{16,0},{24,8},{1,17},{9,25},{17,1},{25,9},{2,18},{10... | collective-permute-start | bytes 2359304 | tf_op jit(solution)/shard_map/ppermute | solution.py:81
  420.6 43.6 %all-to-all-start.7 = ((bf16[4,2,2,64,512]{4,3,2,1,0:T(8,128)(2,1)}), bf16[4,2,2,64,512]{4,3,2,1,0:T(8,128)(2,1)}, u32[]{:S(2)}, u32[]{:S(2)}) async-start(bf16[4,2,2,64,512]{4,3,2,1,0:T(8,128)(2,1)} %add_convert_fusion.1), calls=%async_computation.7 | async-start | bytes 2097152 | tf_op jit(solution)/shard_map/all_to_all | solution.py:51
  428.5 19.9 %collective-permute-start.20 = (bf16[6,128,512]{2,1,0:T(8,128)(2,1)}, bf16[6,128,512]{2,1,0:T(8,128)(2,1)S(1)}, u32[]{:S(2)}, u32[]{:S(2)}) collective-permute-start(bf16[6,128,512]{2,1,0:T(8,128)(2,1)} %fusion.10), channel_id=1, source_target_pairs={{0,16},{8,24},{16,0},{24,8},{1,17},{9,25},{17,1},{25,9},{2,18},{10... | collective-permute-start | bytes 2359304 | tf_op jit(solution)/shard_map/ppermute | solution.py:81
  450.9 23.2 %collective-permute-start.21 = (bf16[6,256,512]{2,1,0:T(8,128)(2,1)}, bf16[6,256,512]{2,1,0:T(8,128)(2,1)}, u32[]{:S(2)}, u32[]{:S(2)}) collective-permute-start(bf16[6,256,512]{2,1,0:T(8,128)(2,1)} %pad_maximum_fusion.4), channel_id=1, source_target_pairs={{0,8},{8,0},{16,24},{24,16},{1,9},{9,1},{17,25},{25,17},{2,10},{10... | collective-permute-start | bytes 4718600 | tf_op jit(solution)/shard_map/ppermute | solution.py:81
  (73 other events, 523.5 us)
Sparse Core Ops, SparseCore 0:
  44.3 64.1 all-gather.4
  390.8 63.3 all-gather.6

commit v3 on v2

v3 whole, which is shorter than its diff:
```python
import functools

import jax
import jax.numpy as jnp
from jax import lax
from jax.experimental import pallas as pl
from jax.experimental.pallas import tpu as pltpu
from jax.sharding import PartitionSpec as P

EPSILON = 1e-05
CHUNKS = 2
F32 = jnp.float32
BF16 = jnp.bfloat16


def dot(left, right):
    return jnp.dot(left, right, preferred_element_type=F32)


def contract_rows(left, right):
    return lax.dot_general(left, right, (((0,), (0,)), ((), ())), preferred_element_type=F32)


def times_transpose(left, right):
    return lax.dot_general(left, right, (((1,), (1,)), ((), ())), preferred_element_type=F32)


def rms_factor(values):
    return lax.rsqrt(jnp.mean(values * values, axis=-1, keepdims=True) + EPSILON)


def norm_backward(grad_out, normed, factor, gain):
    inner = grad_out * gain
    return factor * (inner - normed * jnp.mean(inner * normed, axis=-1, keepdims=True))


class Grid:
    def __init__(self, size):
        self.far = 4 if size % 4 == 0 else 1
        self.near = size // self.far
        self.size = size

    def near_shift(self, step):
        near = self.near
        return [(f, f // near * near + (f % near + step) % near) for f in range(self.size)]

    def swap_far(self, values):
        groups = [
            [i * self.near + j for i in range(self.far)] for j in range(self.near)
        ]
        return lax.all_to_all(values, "filt", 0, 0, axis_index_groups=groups, tiled=True)


def tie(value, *others):
    return lax.optimization_barrier((value, *others))[0] if others else value


def tied(*values):
    return list(lax.optimization_barrier(values))


def copies(grid, own):
    return jnp.broadcast_to(own[None], (grid.far, *own.shape))


def tie_all(values, *others):
    count = len(values)
    return list(lax.optimization_barrier((*values, *others))[:count]) if others else list(values)


def near_swaps(grid, values):
    return [
        lax.ppermute(
            values[j] if isinstance(values, list) else values, "filt", grid.near_shift(j)
        )
        for j in range(1, grid.near)
    ]


def total_of(values):
    total = values[0].astype(F32)
    for value in values[1:]:
        total = total + value.astype(F32)
    return total


def swap_rows(values, bit):
    count = lax.axis_size("rows")
    return lax.ppermute(values, "rows", [(r, r ^ bit) for r in range(count)])


def row_bits():
    count = lax.axis_size("rows")
    return [1 << n for n in range(count.bit_length() - 1)]


def row_step(values, bit):
    parts, height, width = values.shape
    halves = values.reshape(parts, 2, height // 2, width)
    high = (lax.axis_index("rows") & bit) != 0
    away = jnp.where(high, halves[:, 0], halves[:, 1]).astype(BF16)
    return jnp.where(high, halves[:, 1], halves[:, 0]), swap_rows(away, bit)


def gather_rows(full):
    index = lax.axis_index("rows")
    for bit in reversed(row_bits()):
        high = (index & bit) != 0
        other = swap_rows(full, bit)
        full = jnp.concatenate(
            [jnp.where(high, other, full), jnp.where(high, full, other)], axis=1
        )
    return full


def gather_near(grid, own):
    at = lax.axis_index("filt") % grid.near
    whole = jnp.zeros((grid.near, *own.shape), own.dtype)
    for j, value in enumerate([own, *near_swaps(grid, own)]):
        place = lax.rem(at - j + grid.near, grid.near)
        whole = lax.dynamic_update_slice_in_dim(whole, value[None], place, 0)
    return whole


def all_sum(values):
    for axis in ("filt", "rows"):
        count = lax.axis_size(axis)
        for bit in (1 << n for n in range(count.bit_length() - 1)):
            values = values + lax.ppermute(values, axis, [(r, r ^ bit) for r in range(count)])
    return values


def toeplitz_kernel(half, count, up_ref, t00_ref, t10_ref, u00_ref, u10_ref):
    width = up_ref.shape[-1]
    step = pl.program_id(0)
    up = up_ref[0]
    first = lax.broadcasted_iota(jnp.int32, up.shape, 1) == 0
    late = jnp.where(first, 0.0, pltpu.roll(up, 1, axis=1))
    up = jnp.where((step < 2 * count) & (step % 2 == 1), late, up)
    block = pltpu.roll(
        jnp.broadcast_to(up, (half, width)), 0, axis=1, stride=1, stride_axis=0
    )
    u00, u10 = block[:, :half], block[:, half : 2 * half]
    u00_ref[0] = u00.astype(BF16)
    u10_ref[0] = u10.astype(BF16)
    t00_ref[0] = u00.T.astype(BF16)
    t10_ref[0] = u10.T.astype(BF16)


def toeplitz_blocks(filters, first, count):
    length = filters.shape[1] // 2
    half = length // 2
    taps = lax.dynamic_slice_in_dim(filters, first, count, 0).astype(BF16).astype(F32)
    taps = taps.reshape(count, length, 2).transpose(0, 2, 1).reshape(2 * count, 1, length)
    up = jnp.pad(taps, ((0, 0), (0, 0), (0, length)))
    by_column = pl.BlockSpec((1, half, half), lambda n: (n // (2 * count), 0, n % (2 * count)))
    by_row = pl.BlockSpec((1, half, half), lambda n: (n // (2 * count), n % (2 * count), 0))
    line = pl.BlockSpec((1, 1, 2 * length), lambda n: (n % (2 * count), 0, 0))
    wide = jax.ShapeDtypeStruct((2, half, 2 * count * half), BF16)
    tall = jax.ShapeDtypeStruct((2, 2 * count * half, half), BF16)
    return pl.pallas_call(
        functools.partial(toeplitz_kernel, half, count),
        grid=(4 * count,),
        in_specs=[line],
        out_specs=[by_column, by_column, by_row, by_row],
        out_shape=[wide, wide, tall, tall],
        name="toeplitz",
    )(up)


def places(near, pieces, whole_ref, sign):
    length = whole_ref.shape[0] // 2
    nears = len(pieces)
    fars, _, _, height, _ = pieces[0].shape
    for j, piece in enumerate(pieces):
        at = lax.rem(near + sign * j + nears, nears)
        for i in range(fars):
            for parity in range(2):
                start = parity * length + (i * nears + at) * height
                yield piece.at[i, 0, parity], pl.ds(pl.multiple_of(start, height), height)


def assemble(near, pieces, whole_ref):
    for piece, rows in places(near, pieces, whole_ref, -1):
        whole_ref[rows, :] = piece[...]


def scatter(near, whole_ref, pieces):
    for piece, rows in places(near, pieces, whole_ref, 1):
        piece[...] = whole_ref[rows, :].astype(piece.dtype)


def mix_kernel(parts, near_ref, *refs):
    pieces = refs[:parts]
    mixes = refs[parts : parts + 2]
    t00_ref, t10_ref = refs[parts + 2 : parts + 4]
    outs = refs[-parts - 5 : -5]
    flip_ref, states_ref, low_ref, high_ref, sum_ref = refs[-5:]
    half = t00_ref.shape[1]
    branches = 2 * mixes[0].shape[0]
    assemble(near_ref[0], pieces, states_ref)

    for branch in range(branches):
        slot = pl.ds(branch * half, half)
        for quarter in range(4):
            value = dot(
                states_ref[pl.ds(quarter * half, half), :], mixes[branch % 2][branch // 2]
            ).astype(BF16)
            target = (quarter // 2) ^ (branch % 2)
            (low_ref, high_ref)[quarter % 2][target, slot, :] = value

    for parity in range(2):
        base = 2 * parity * half
        sum_ref[pl.ds(base, half), :] = dot(t00_ref[parity], low_ref[parity]).astype(
            sum_ref.dtype
        )
        sum_ref[pl.ds(base + half, half), :] = (
            dot(t10_ref[parity], low_ref[parity]) + dot(t00_ref[parity], high_ref[parity])
        ).astype(sum_ref.dtype)
    scatter(near_ref[0], sum_ref, outs)
    flip_ref[0] = states_ref[...].T


def mix_back_kernel(parts, near_ref, own_ref, *refs):
    pieces = refs[:parts]
    turned = refs[parts : parts + 2]
    u00_ref, u10_ref, slab_ref = refs[parts + 2 : parts + 5]
    before = refs[parts + 5 : -parts - 4]
    outs = refs[-parts - 4 : -4]
    back_ref, lag_ref, grad_ref, sum_ref = refs[-4:]
    half = u00_ref.shape[2]
    width = grad_ref.shape[1]
    length = grad_ref.shape[0] // 2
    branches = back_ref.shape[2] // width
    slots = branches // 2

    @pl.when(pl.program_id(0) == 0)
    def _():
        lag_ref[...] = before[1][...] if before else jnp.zeros_like(lag_ref)

    assemble(near_ref[0], pieces, grad_ref)

    for parity in range(2):
        base = 2 * parity * half
        low = grad_ref[pl.ds(base, half), :]
        high = grad_ref[pl.ds(base + half, half), :]
        for branch in range(branches):
            rows = pl.ds(branch * half, half)
            columns = pl.ds((branch % 2 * slots + branch // 2) * width, width)
            target = 2 * half * (parity ^ (branch % 2))
            back_ref[0, pl.ds(target, half), columns] = (
                dot(u00_ref[parity, rows, :], low) + dot(u10_ref[parity, rows, :], high)
            ).astype(BF16)
            back_ref[0, pl.ds(target + half, half), columns] = dot(
                u00_ref[parity, rows, :], high
            ).astype(BF16)

    for quarter in range(4):
        rows = pl.ds(quarter * half, half)
        sum_ref[rows, :] = dot(back_ref[0, rows, : slots * width], turned[0][...]) + dot(
            back_ref[0, rows, slots * width :], turned[1][...]
        )
    scatter(near_ref[0], sum_ref, outs)

    own = slab_ref[0].astype(F32)
    even, odd = own[:, :length], own[:, length:]
    first = lax.broadcasted_iota(jnp.int32, even.shape, 1) == 0
    even_late = jnp.where(first, 0.0, pltpu.roll(even, 1, axis=1))
    odd_late = jnp.where(first, 0.0, pltpu.roll(odd, 1, axis=1))
    for lag, (on_even, on_odd) in enumerate(
        ((even, odd), (odd_late, even), (even_late, odd_late))
    ):
        lag_ref[lag] += dot(on_even.astype(BF16), grad_ref[:length, :]) + dot(
            on_odd.astype(BF16), grad_ref[length:, :]
        )


def feed_forward_kernel(
    shares, earlier, last, arrived, inputs, states, late, lag_ref, gain_ref, cot_ref, *refs
):
    weights = refs[:shares]
    saved = refs[shares : shares + 5 * earlier]
    block, grad, low, gain_out, *rest = refs[shares + 5 * earlier :]
    if last:
        stay_ref, away_ref = rest
    else:
        scaled_ref, hidden_ref, gate_ref, up_ref = rest
    width = gain_ref.shape[1]
    shape = inputs.shape
    flat = (shape[0] * shape[1] * shape[2], width)

    spectral = arrived[0].astype(F32)
    for i in range(1, arrived.shape[0]):
        spectral = spectral + arrived[i].astype(F32)
    lags = (
        states[...],
        jnp.stack([late[:, 1], states[:, 0]], axis=1),
        late[...],
    )
    regress = sum(dot(lag.reshape(flat), lag_ref[n]) for n, lag in enumerate(lags))
    middle = (inputs[...].astype(F32) + spectral).reshape(flat) + regress
    factor = rms_factor(middle)
    normed = middle * factor
    gain = gain_ref[...]
    scaled = (normed * gain).astype(BF16)
    if not last:
        scaled_ref[...] = scaled
    cot = cot_ref[...].reshape(flat)
    value = middle
    mid_back = jnp.zeros(flat, F32)
    for n, weight in enumerate(weights):
        units = weight.shape[0] * weight.shape[2]
        columns = pl.ds(n * units, units)
        gate_t, up_t, down = (weight[:, m].reshape(units, width) for m in range(3))
        gate_pre = times_transpose(scaled, gate_t)
        up_values = times_transpose(scaled, up_t)
        grad_hidden = times_transpose(cot, down)
        sigmoid = 1.0 / (1.0 + jnp.exp(-gate_pre))
        silu = gate_pre * sigmoid
        hidden = (silu * up_values).astype(BF16)
        gate_back = (
            grad_hidden * up_values * (sigmoid * (1.0 + gate_pre * (1.0 - sigmoid)))
        ).astype(BF16)
        up_back = (grad_hidden * silu).astype(BF16)
        if last:
            sums = [
                contract_rows(gate_back, scaled),
                contract_rows(up_back, scaled),
                contract_rows(hidden, cot),
            ]
            for e in range(earlier):
                *parts, right, right_cot = saved[5 * e : 5 * e + 5]
                right_cot = right_cot[...].reshape(-1, width)
                for m, part in enumerate(parts):
                    sums[m] += contract_rows(
                        part[:, columns], right_cot if m == 2 else right[...]
                    )
            for m in range(3):
                split = (weight.shape[0], weight.shape[2], width)
                if n < shares // 2 or shares == 1:
                    stay_ref[n, :, m] = sums[m].reshape(split)
                else:
                    away_ref[n - shares // 2, :, m] = sums[m].astype(BF16).reshape(split)
        else:
            hidden_ref[:, columns] = hidden
            gate_ref[:, columns] = gate_back
            up_ref[:, columns] = up_back
        value = value + dot(hidden, down)
        mid_back = mid_back + (dot(gate_back, gate_t) + dot(up_back, up_t))
    block[...] = value.astype(BF16).reshape(shape)
    gain_out[...] = jnp.sum(mid_back * normed, axis=0, keepdims=True)
    total = cot.astype(F32) + norm_backward(mid_back, normed, factor, gain)
    grad[...] = total.reshape(shape)
    rounded = total.astype(BF16).reshape(shape)
    for i in range(low.shape[0]):
        low[i] = rounded


def mixing_kernel(
    bit_ref, flip_ref, plus_ref, minus_ref, sum_ref, rest_ref, stay_ref, away_ref, gain_ref
):
    rows = stay_ref.shape[1]

    @pl.when(pl.program_id(0) == 0)
    def _():
        gain_ref[...] = jnp.zeros_like(gain_ref)

    for n, out_ref in enumerate((stay_ref, away_ref)):
        here = pl.ds(pl.multiple_of((bit_ref[0] ^ n) * rows, rows), rows)
        plus, minus = (
            sum(dot(flip_ref[s, here, :], ref[s]) for s in range(flip_ref.shape[0]))
            for ref in (plus_ref, minus_ref)
        )
        out_ref[0] = (plus + minus).astype(out_ref.dtype)
        out_ref[1] = (plus - minus).astype(out_ref.dtype)
        gain_ref[here, :] += jnp.sum(
            plus * sum_ref[0, here, :].astype(F32) + minus * rest_ref[0, here, :].astype(F32),
            axis=1,
            keepdims=True,
        )


def resident(shape):
    zeros = (0,) * len(shape)
    return pl.BlockSpec(shape, lambda *_: zeros, pipeline_mode=pl.Buffered(1))


def mix_sequences(pieces, near, pairs, t00, t10, start, total, flips):
    parts = len(pieces)
    fars, count, _, height, width = pieces[0].shape
    half = t00.shape[1]
    block = pl.BlockSpec((fars, 1, 2, height, width), lambda n, *_: (0, n, 0, 0, 0))
    rows = t00.shape[2]
    flip = pl.BlockSpec((1, width, 4 * half), lambda n, *_: (start + n, 0, 0))
    return pl.pallas_call(
        functools.partial(mix_kernel, parts),
        grid_spec=pltpu.PrefetchScalarGridSpec(
            num_scalar_prefetch=1,
            grid=(count,),
            in_specs=[block] * parts
            + [resident(a.shape) for a in (*pairs, t00, t10)]
            + [pl.BlockSpec(memory_space=pl.ANY)] * len(flips),
            out_specs=[block] * parts + [flip],
            scratch_shapes=[
                pltpu.VMEM((4 * half, width), BF16),
                pltpu.VMEM((2, rows, width), BF16),
                pltpu.VMEM((2, rows, width), BF16),
                pltpu.VMEM((4 * half, width), F32),
            ],
        ),
        out_shape=[jax.ShapeDtypeStruct(pieces[0].shape, BF16)] * parts
        + [jax.ShapeDtypeStruct((total, width, 4 * half), BF16)],
        input_output_aliases={parts + 5: parts} if flips else {},
        compiler_params=pltpu.CompilerParams(vmem_limit_bytes=48 << 20),
        cost_estimate=pl.CostEstimate(
            flops=count * (16 * half * pairs[0].size + 12 * half * rows * width),
            bytes_accessed=4 * parts * pieces[0].size + 4 * pairs[0].size + 4 * t00.size,
            transcendentals=0,
        ),
        name="mix",
    )(near, *pieces, *pairs, t00, t10, *flips)


def mix_sequences_back(pieces, near, own, turned, u00, u10, lag_count, start, flips, before):
    parts = len(pieces)
    fars, count, _, height, width = pieces[0].shape
    half = u00.shape[2]
    block = pl.BlockSpec((fars, 1, 2, height, width), lambda n, *_: (0, n, 0, 0, 0))
    rows = u00.shape[1]
    slab = width // (parts * fars)
    lag_shape = (lag_count, slab, width)
    back_shape = (flips.shape[0], 4 * half, 2 * turned[0].shape[0])
    back = pl.BlockSpec((1, *back_shape[1:]), lambda n, *_: (start + n, 0, 0))
    slab_spec = pl.BlockSpec((1, slab, 4 * half), lambda n, _, own: (start + n, own[0], 0))
    return pl.pallas_call(
        functools.partial(mix_back_kernel, parts),
        grid_spec=pltpu.PrefetchScalarGridSpec(
            num_scalar_prefetch=2,
            grid=(count,),
            in_specs=[block] * parts
            + [resident(a.shape) for a in (*turned, u00, u10)]
            + [slab_spec]
            + ([pl.BlockSpec(memory_space=pl.ANY), resident(lag_shape)] if before else []),
            out_specs=[block] * parts + [back, resident(lag_shape)],
            scratch_shapes=[
                pltpu.VMEM((4 * half, width), BF16),
                pltpu.VMEM((4 * half, width), F32),
            ],
        ),
        out_shape=[jax.ShapeDtypeStruct(pieces[0].shape, BF16)] * parts
        + [
            jax.ShapeDtypeStruct(back_shape, BF16),
            jax.ShapeDtypeStruct(lag_shape, F32),
        ],
        input_output_aliases={parts + 7: parts} if before else {},
        compiler_params=pltpu.CompilerParams(vmem_limit_bytes=56 << 20),
        cost_estimate=pl.CostEstimate(
            flops=count * (16 * half * turned[0].size + 12 * half * rows * width),
            bytes_accessed=4 * parts * pieces[0].size + 8 * turned[0].size,
            transcendentals=0,
        ),
        name="mix_back",
    )(near, own, *pieces, *turned, u00, u10, flips, *before)


def mixing_products(flips, backs, pairs, bit):
    count, width, length = flips.shape
    slots = pairs[0].shape[0]
    plus = pl.BlockSpec((count, length, width), lambda k, _: (0, 0, k))
    minus = pl.BlockSpec((count, length, width), lambda k, _: (0, 0, slots + k))
    pair = pl.BlockSpec((1, width, width), lambda k, _: (k, 0, 0))
    half = pl.BlockSpec((2, width // 2, width), lambda k, _: (k, 0, 0))
    return pl.pallas_call(
        mixing_kernel,
        grid_spec=pltpu.PrefetchScalarGridSpec(
            num_scalar_prefetch=1,
            grid=(slots,),
            in_specs=[resident(flips.shape), plus, minus, pair, pair],
            out_specs=[half, half, resident((width, 1))],
        ),
        out_shape=[
            jax.ShapeDtypeStruct((2 * slots, width // 2, width), F32),
            jax.ShapeDtypeStruct((2 * slots, width // 2, width), BF16),
            jax.ShapeDtypeStruct((width, 1), F32),
        ],
        compiler_params=pltpu.CompilerParams(vmem_limit_bytes=56 << 20),
        cost_estimate=pl.CostEstimate(
            flops=2 * backs.size * width,
            bytes_accessed=2 * (flips.size + backs.size) + 8 * slots * width * width,
            transcendentals=0,
        ),
        name="mixing_products",
    )(bit, flips, backs, backs, *pairs)


def feed_forward(arrived, inputs, states, late, lag, gain, cot, weights, saved, last):
    rows, width = inputs.size // inputs.shape[-1], inputs.shape[-1]
    shares = len(weights)
    units = weights[0].shape[0] * weights[0].shape[2]
    flat_saved = [value for values in saved for value in values] if last else []
    operands = (arrived, inputs, states, late, lag, gain, cot, *weights, *flat_saved)
    whole = pl.BlockSpec(memory_space=pltpu.VMEM)
    kept = max(shares // 2, 1)
    if last:
        extra = [
            jax.ShapeDtypeStruct((kept, *weights[0].shape), F32),
            jax.ShapeDtypeStruct((kept, *weights[0].shape), BF16),
        ]
    else:
        extra = [jax.ShapeDtypeStruct((rows, width), BF16)] + [
            jax.ShapeDtypeStruct((rows, shares * units), BF16)
        ] * 3
    return pl.pallas_call(
        functools.partial(feed_forward_kernel, shares, len(flat_saved) // 5, last),
        in_specs=[whole] * len(operands),
        out_specs=[whole] * (4 + len(extra)),
        out_shape=[
            jax.ShapeDtypeStruct(inputs.shape, BF16),
            jax.ShapeDtypeStruct(inputs.shape, F32),
            jax.ShapeDtypeStruct(arrived.shape, BF16),
            jax.ShapeDtypeStruct((1, width), F32),
            *extra,
        ],
        compiler_params=pltpu.CompilerParams(vmem_limit_bytes=56 << 20),
        cost_estimate=pl.CostEstimate(
            flops=(24 if last else 12) * rows * width * shares * units,
            bytes_accessed=6 * shares * units * width + 40 * rows * width,
            transcendentals=rows * shares * units,
        ),
        name="feed_forward",
    )(*operands)


def leading(values, edge):
    early = jnp.concatenate([values[:, :, 1:], edge], axis=2)
    return values, jnp.stack([values[:, 1], early[:, 0]], axis=1), early


def row_masks():
    masks = [0]
    for bit in reversed(row_bits()):
        masks = masks + [mask ^ bit for mask in masks]
    return masks


def spread_rows(own):
    full = own[None]
    for bit in reversed(row_bits()):
        full = jnp.concatenate([full, swap_rows(full, bit)], axis=0)
    return full


def shards(inputs, filters, gain_in, mixing, regression, gain_mid, w_gate, w_up, w_down, out_grad):
    shard_rows, local_seqs, width = inputs.shape
    grid = Grid(lax.axis_size("filt"))
    row_count = lax.axis_size("rows")
    index = lax.axis_index("filt")
    branches = mixing.shape[0]
    lag_count = regression.shape[0]
    height = shard_rows // 2
    chunks = CHUNKS
    step = local_seqs // chunks

    def inward(values):
        return values.reshape(height, 2, local_seqs, width).transpose(2, 1, 0, 3)

    def outward(values):
        return values.transpose(2, 1, 0, 3).reshape(shard_rows, local_seqs, width)

    def cut(values):
        return [values[c * step : (c + 1) * step] for c in range(chunks)]

    inputs_low = inward(inputs)
    residual = inputs_low.astype(F32)
    cotangent_low = inward(out_grad)
    factor_in = rms_factor(residual)
    normed_in = residual * factor_in
    states = (normed_in * gain_in).astype(BF16)
    hidden_own = w_down.shape[0]
    share = hidden_own // row_count
    packed = jnp.stack([w_gate.T, w_up.T, w_down]).reshape(3, row_count, share, width)
    own_share = lax.dynamic_index_in_dim(packed, lax.axis_index("rows"), 1, keepdims=False)
    near_shares = gather_near(grid, own_share)

    slots = (branches + 1) // 2
    first_branch = index * branches
    t00, t10, u00, u10 = toeplitz_blocks(filters, first_branch // 2, slots)
    if branches % 2:
        odd_start = first_branch % 2
        paired = lax.dynamic_update_slice_in_dim(
            jnp.zeros((2 * slots,) + mixing.shape[1:], mixing.dtype), mixing, odd_start, 0
        )
    else:
        paired = mixing
    first, second = (paired[n::2].astype(F32) for n in range(2))
    pairs = ((first + second).astype(BF16), (first - second).astype(BF16))

    near = jnp.reshape(index % grid.near, (1,)).astype(jnp.int32)

    edge = lax.ppermute(
        states[:, :, -1:], "filt", [(f, f + 1) for f in range(grid.size - 1)]
    )
    late = jnp.concatenate([edge, states[:, :, :-1]], axis=2)
    partials, flips = [], []
    ready = [late, inputs_low, cotangent_low, t00, t10, u00, u10, *pairs, copies(grid, near_shares)]
    state_far = []
    for c, part in enumerate(cut(states)):
        if c:
            part = tie(part, state_far[-1])
        state_far.append(grid.swap_far(copies(grid, part)))
        if c == 0:
            state_far[0], *ready = tied(state_far[0], *ready)
    late, inputs_low, cotangent_low, t00, t10, u00, u10, *pairs, shares = ready
    state_far[-1], shares = tied(state_far[-1], shares)
    shares = grid.swap_far(shares)
    state_near = [near_swaps(grid, values) for values in state_far]
    for c in range(chunks):
        pieces = [state_far[c], *state_near[c]]
        ahead = [] if c else state_far[1:]
        pieces = [tie(pieces[0], *ahead), *pieces[1:]]
        *partial, flip = mix_sequences(
            pieces, near, pairs, t00, t10, c * step, local_seqs, flips
        )
        if c + 1 < chunks:
            state_near[c + 1] = tie_all(state_near[c + 1], partial[0])
            partial = tie_all(partial, *state_near[c + 1])
        partials.append(partial)
        flips = [flip]
    near_received = [near_swaps(grid, partial) for partial in partials]
    for c in range(chunks - 1):
        near_received[c] = tie_all(near_received[c], partials[c + 1][0])
    weights = [tie(shares, partials[0][0]).reshape(grid.size, 3, share, width)]
    for n, bit in enumerate(reversed(row_bits())):
        received = [swap_rows(weight, bit) for weight in weights]
        if n == 0:
            received = tie_all(received, *(near_received[-1] or partials[-1][:1]))
        weights = weights + received

    spectral = []
    for c in range(chunks):
        spectral.append(
            grid.swap_far(total_of([partials[c][0], *near_received[c]]).astype(BF16))
        )

    block_out, middle_grad, lows, grad_far, kept = [], [], [], [], []
    gain_mid_part = jnp.zeros((1, width), F32)
    for c in range(chunks):
        part = slice(c * step, (c + 1) * step)
        arrived = spectral[c]
        if c:
            arrived = tie(arrived, middle_grad[-1])
        if c + 1 < chunks:
            arrived = tie(arrived, *near_received[c + 1])
        if c == chunks - 1:
            turned = [
                value.transpose(0, 2, 1).reshape(slots * width, width)
                for value in (tie_all(pairs, middle_grad[-1]) if c else pairs)
            ]
            arrived = tie(arrived, *turned)
        cot = cotangent_low[part]
        value, grad, low, gain_part, *rest = feed_forward(
            arrived, inputs_low[part], states[part], late[part], regression, gain_mid[None], cot,
            weights, kept, c + 1 == chunks,
        )
        block_out.append(value)
        middle_grad.append(grad)
        lows.append(low[0])
        gain_mid_part = gain_mid_part + gain_part
        grad_far.append(grid.swap_far(low))
        if c + 1 < chunks:
            scaled, hidden, gate_back, up_back = rest
            kept.append((gate_back, up_back, hidden, scaled, cot))
    gain_mid_part = gain_mid_part[0]

    bits = row_bits()
    stay, away = tie_all(rest, grad_far[0]) if chunks > 1 else rest
    grad_near = [near_swaps(grid, values) for values in grad_far]
    if bits:
        value = swap_rows(away, bits[0])
        value, *grad_near[0] = tied(value, *grad_near[0])
        stay = stay + value.astype(F32)

    own = jnp.reshape(index, (1,)).astype(jnp.int32)
    before = ()
    back_partials = []
    mix_back = jnp.concatenate(lows, axis=0)
    next_edge = lax.ppermute(
        mix_back[:, :, :1], "filt", [(f + 1, f) for f in range(grid.size - 1)]
    )
    grad_far[0], stay, next_edge = tied(grad_far[0], stay, next_edge)
    ahead = []
    for c in range(chunks):
        received = grad_near[c]
        if c + 1 < chunks:
            ahead.append(grad_far[c + 1])
        pieces = [tie(grad_far[c], *ahead), *received]
        *partial, backs, lag_sum = mix_sequences_back(
            pieces, near, own, turned, u00, u10, lag_count, c * step, flip, before
        )
        before = (backs, lag_sum)
        if c + 1 < chunks:
            grad_near[c + 1] = tie_all(grad_near[c + 1], partial[0])
            partial = tie_all(partial, *grad_near[c + 1])
        back_partials.append(partial)
        ahead = []
    near_received = [near_swaps(grid, partial) for partial in back_partials]
    near_received[0] = tie_all(near_received[0], back_partials[-1][0])
    columns = [total_of([back_partials[0][0], *near_received[0]]).astype(BF16)]
    later = bits[1:2]
    half_count = stay.shape[0] // 2
    from_rows = [swap_rows(stay[half_count:].astype(BF16), bit) for bit in later]
    kept, value = row_step(tie(lag_sum, columns[0]), bits[0])
    lag_share = kept + value.astype(F32)
    core_bit = jnp.reshape(lax.axis_index("rows") & 1, (1,)).astype(jnp.int32)
    mixing_stay, mixing_away, gain_column = mixing_products(
        flip, tie(backs, columns[0], *from_rows, lag_share), pairs, core_bit
    )
    for bit in later:
        kept, value = row_step(lag_share, bit)
        lag_share = kept + tie(value, gain_column).astype(F32)
    for c in range(1, chunks):
        received = tie_all(near_received[c], gain_column)
        columns.append(total_of([back_partials[c][0], *received]).astype(BF16))
    arrived = [grid.swap_far(column) for column in columns]
    arrived[0], mixing_stay, mixing_away = tie_all(
        [arrived[0], mixing_stay, mixing_away], *columns[1:]
    )
    state_back = [total_of(values) for values in arrived]

    mixing_share = mixing_stay + swap_rows(mixing_away, bits[0]).astype(F32)
    mixing_share, stay = tied(mixing_share, stay)
    value = mixing_away
    for bit in bits[1:]:
        kept, value = row_step(mixing_share, bit)
        mixing_share = kept + value.astype(F32)
    row_done = value
    mixing_low, gain_column, gain_mid_part, lag_sum, lag_share, mix_back, next_edge, *block_out = (
        tied(
            mixing_share.astype(BF16), gain_column, gain_mid_part, lag_sum, lag_share, mix_back,
            next_edge, *block_out,
        )
    )
    mixing_grad = gather_rows(mixing_low).astype(F32)
    if branches % 2:
        mixing_grad = lax.dynamic_slice_in_dim(mixing_grad, odd_start, branches, 0)

    slab = width // grid.size
    own_regression = lax.dynamic_slice_in_dim(regression, index * slab, slab, 1)
    gain_lag = jnp.sum(own_regression.astype(F32) * lag_sum, axis=(0, 2))
    gain_in_part = gain_column[:, 0]
    gain_in_part = lax.dynamic_update_slice_in_dim(
        gain_in_part,
        lax.dynamic_slice_in_dim(gain_in_part, index * slab, slab, 0) + gain_lag,
        index * slab,
        0,
    ) / gain_in
    gains = all_sum(jnp.pad(jnp.stack([gain_in_part, gain_mid_part]), ((0, 6), (0, 0))))

    for value in from_rows:
        stay = stay[:half_count] + value.astype(F32)
    for bit in bits[2:]:
        half_count = stay.shape[0] // 2
        value = swap_rows(stay[half_count:].astype(BF16), bit)
        stay = stay[:half_count] + value.astype(F32)
        kept, value = row_step(lag_share, bit)
        lag_share = kept + value.astype(F32)
    by_filt = stay[0].reshape(grid.far, grid.near, 3, share, width)
    at = index % grid.near
    away = [
        lax.dynamic_index_in_dim(by_filt, lax.rem(at + j, grid.near), 1, keepdims=False)
        for j in range(grid.near)
    ]
    returned = near_swaps(grid, [part.astype(BF16) for part in away])
    far_grads = total_of([away[0], *tie_all(returned, row_done)]).astype(BF16)
    far_grads = grid.swap_far(tie(far_grads, arrived[-1]))
    own_grads = total_of(far_grads).astype(BF16)

    lag_share = copies(grid, gather_near(grid, lag_share.astype(BF16)))
    spread = grid.swap_far(tie(lag_share, far_grads))
    spread = gather_rows(spread.reshape(grid.size * lag_count, -1, width))
    regression_grad = (
        spread.reshape(grid.size, lag_count, slab, width)
        .transpose(1, 0, 2, 3)
        .reshape(lag_count, width, width)
        .astype(F32)
    )

    lag_back = sum(
        jnp.einsum("spae,de->spad", lead, regression[n], preferred_element_type=F32)
        for n, lead in enumerate(leading(mix_back, next_edge))
    )
    input_grad = []
    for c in range(chunks):
        part = slice(c * step, (c + 1) * step)
        back = state_back[c] + lag_back[part]
        input_grad.append(
            middle_grad[c] + norm_backward(back, normed_in[part], factor_in[part], gain_in)
        )

    full = spread_rows(own_grads)
    row_index = lax.axis_index("rows")
    ordered = jnp.zeros((row_count, 3, share, width), BF16)
    for n, mask in enumerate(row_masks()):
        ordered = lax.dynamic_update_slice_in_dim(ordered, full[n][None], row_index ^ mask, 0)
    ordered = ordered.transpose(1, 0, 2, 3).reshape(3, hidden_own, width).astype(F32)
    return (
        outward(jnp.concatenate(block_out, axis=0)),
        outward(jnp.concatenate(input_grad, axis=0)),
        mixing_grad,
        regression_grad,
        gains[0],
        gains[1],
        ordered[0].T,
        ordered[1].T,
        ordered[2],
    )


def solution(mesh):
    placed = (
        P("filt", "rows", None),
        P(),
        P(),
        P("filt", None, None),
        P(),
        P(),
        P(None, "filt"),
        P(None, "filt"),
        P("filt", None),
        P("filt", "rows", None),
    )
    return jax.shard_map(
        shards,
        mesh=mesh,
        in_specs=placed,
        out_specs=(
            P("filt", "rows", None),
            P("filt", "rows", None),
            P("filt", None, None),
            P(),
            P(),
            P(),
            P(None, "filt"),
            P(None, "filt"),
            P("filt", None),
        ),
        check_vma=False,
    )
```

time: 492 us -> 452 us (0.919)
  Pallas kernels: 95.4 us -> 131 us
  matrix products: 35.9 us -> 2.44 us
  other arithmetic: 67.1 us -> 51.4 us
  waiting for transfers between devices: 157 us -> 143 us
  between operations: 15.8 us -> 1.8 us
  starting transfers between devices: 73.2 us -> 82.2 us
  local copies, waits for them, and re-layouts: 42.6 us -> 34.5 us
    pallas_call x1 -> x4, Pallas kernels: 7.42 us -> 56.7 us  [the longest x2 27 us: feed_forward(): pl.pallas_call(functools.partial(feed_forward_kernel, shares, len(flat_sa...]
    dot_general x21 -> x0, matrix products: 31.5 us -> none  [the longest x6 11.6 us: contract_rows(): lax.dot_general(left, right, (((0,), (0,)), ((), ())), preferred_element_...]
    pallas_call x2, Pallas kernels: 57.1 us -> 42.4 us  [mix_sequences_back(): pl.pallas_call(functools.partial(mix_back_kernel, parts), grid_spec=pltpu...]
    all_to_all x8 -> x11, starting transfers between devices: 37.9 us -> 50.8 us  [swap_far(): lax.all_to_all(values, 'filt', 0, 0, axis_index_groups=groups, tiled=True)]
    convert_element_type x23 -> x9, other arithmetic: 23.2 us -> 11.8 us  [the longest x1 3.6 us: shards(): mixing_grad = gather_rows(mixing_low).astype(F32)]
    ppermute x16 -> x15, waiting for transfers between devices: 38.3 us -> 27.7 us  [swap_rows(): return lax.ppermute(values, 'rows', [(r, r ^ bit) for r in range(count)])]
    ppermute x0 -> x5, starting transfers between devices: none -> 8.97 us  [all_sum(): lax.ppermute(values, axis, [(r, r ^ bit) for r in range(count)])]
    all_gather x2 -> x0, waiting for transfers between devices: 7.65 us -> none  [the longest x1 7.64 us: shards(): shares = lax.all_gather(tie(own_share, state_far[0]), 'filt', axis=1)]
  transfers between devices with their start and end apart: 37 -> 44, of which waited for: 16 -> 16; matrix products, arithmetic and copies ran while one was open for 24% -> 16% of each run, Pallas kernels for 20% -> 29%
where the time goes in v3:
time: 452 us; the launch traced here: 447 us
  waiting for transfers between devices  143 us (32%)
  Pallas kernels  131 us (29%)
  starting transfers between devices  82.2 us (18%)
  other arithmetic  51.4 us (11%)
  local copies, waits for them, and re-layouts  34.5 us (8%)
    all_to_all x11, waiting for transfers between devices, swap_far(): lax.all_to_all(values, 'filt', 0, 0, axis_index_groups=groups, tiled=True)  72.2 us
    all_to_all x11, starting transfers between devices, swap_far(): lax.all_to_all(values, 'filt', 0, 0, axis_index_groups=groups, tiled=True)  50.8 us
    pallas_call x2, Pallas kernels, mix_sequences_back(): pl.pallas_call(functools.partial(mix_back_kernel, parts), grid_spec=pltpu...  42.4 us
    ppermute x11, waiting for transfers between devices, near_swaps(): lax.ppermute(values[j] if isinstance(values, list) else values, 'filt', g...  35.8 us
    pallas_call x2, Pallas kernels, mix_sequences(): pl.pallas_call(functools.partial(mix_kernel, parts), grid_spec=pltpu.Pref...  32.3 us
    ppermute x15, waiting for transfers between devices, swap_rows(): return lax.ppermute(values, 'rows', [(r, r ^ bit) for r in range(count)])  27.7 us
    pallas_call x2, Pallas kernels, feed_forward(): pl.pallas_call(functools.partial(feed_forward_kernel, shares, len(flat_sa...  27 us
    pallas_call x1, Pallas kernels, mixing_products(): pl.pallas_call(mixing_kernel, grid_spec=pltpu.PrefetchScalarGridSpec(num_...  21.8 us
  transfers between devices with their start and end apart: 44, of which 16 were waited for; matrix products, arithmetic and copies ran while one was open for 16% of the time, Pallas kernels for 29%

profile of v3, /device:TPU:0, one launch (start us, length us, event | category | flops | bytes accessed | tf_op | source)
XLA Modules:
  0.0 446.7 jit_solution(5005305212155335142)
XLA Ops:
  6.1 6.4 %all-to-all-start = ((bf16[4,2,2,64,512]{4,3,2,1,0:T(8,128)(2,1)}), bf16[4,2,2,64,512]{4,3,2,1,0:T(8,128)(2,1)S(1)}, u32[]{:S(2)}, u32[]{:S(2)}) async-start(bf16[4,2,2,64,512]{4,3,2,1,0:T(8,128)(2,1)} %broadcast_in_dim.24), calls=%async_computation | async-start | bytes 2097152 | tf_op jit(solution)/shard_map/all_to_all | solution.py:51
  21.9 3.7 fusion.1
  26.3 7.9 %toeplitz.1 = (bf16[2,256,1536]{2,1,0:T(8,128)(2,1)}, bf16[2,256,1536]{2,1,0:T(8,128)(2,1)}, bf16[2,1536,256]{2,1,0:T(8,128)(2,1)}, bf16[2,1536,256]{2,1,0:T(8,128)(2,1)}) custom-call(f32[6,1,1024]{2,1,0:T(1,128)} %pad_convert_fusion.up_ref), custom_call_target="tpu_custom_call" | custom-call | tf_op jit(solution)/shard_map/toeplitz/pallas_call | solution.py:161
  41.7 5.7 %all-to-all-start.1 = ((bf16[4,2,2,64,512]{4,3,2,1,0:T(8,128)(2,1)}), bf16[4,2,2,64,512]{4,3,2,1,0:T(8,128)(2,1)}, u32[]{:S(2)}, u32[]{:S(2)}) async-start(bf16[4,2,2,64,512]{4,3,2,1,0:T(8,128)(2,1)} %broadcast_in_dim.29), calls=%async_computation.1 | async-start | bytes 2097152 | tf_op jit(solution)/shard_map/all_to_all | solution.py:51
  47.6 24.8 %all-to-all-done.1.refs_0_ = bf16[4,2,2,64,512]{4,3,2,1,0:T(8,128)(2,1)} async-done(((bf16[4,2,2,64,512]{4,3,2,1,0:T(8,128)(2,1)}), bf16[4,2,2,64,512]{4,3,2,1,0:T(8,128)(2,1)}, u32[]{:S(2)}, u32[]{:S(2)}) %all-to-all-start.1) | async-done | bytes 1048608 | tf_op jit(solution)/shard_map/all_to_all | solution.py:51
  72.4 4.9 %all-to-all-start.3 = ((bf16[4,2,3,64,512]{4,3,2,1,0:T(8,128)(2,1)}), bf16[4,2,3,64,512]{4,3,2,1,0:T(8,128)(2,1)}, u32[]{:S(2)}, u32[]{:S(2)}) async-start(bf16[4,2,3,64,512]{4,3,2,1,0:T(8,128)(2,1)} %broadcast_in_dim.28), calls=%async_computation.3 | async-start | bytes 3145728 | tf_op jit(solution)/shard_map/all_to_all | solution.py:51
  77.8 16.2 %mix.2 = (bf16[4,2,2,64,512]{4,3,2,1,0:T(8,128)(2,1)S(1)}, bf16[4,2,2,64,512]{4,3,2,1,0:T(8,128)(2,1)}, bf16[4,512,1024]{2,1,0:T(8,128)(2,1)}) custom-call(s32[1]{0:T(128)} %bitcast.near_ref, bf16[4,2,2,64,512]{4,3,2,1,0:T(8,128)(2,1)S(1)} %all-to-all-done.refs_0_, bf16[4,2,2,64,512]{4,3,2,1,0:T(8,128)(2,1)} %collective-permute-done.2.refs_1_, ...), custom_call_target="tpu_custom_call" | custom-call | flops 11274289152 | bytes 10485760 | tf_op jit(solution)/shard_map/mix/pallas_call | solution.py:395
  95.0 7.3 %collective-permute-done.3.refs_1_ = bf16[4,2,2,64,512]{4,3,2,1,0:T(8,128)(2,1)S(1)} collective-permute-done((bf16[4,2,2,64,512]{4,3,2,1,0:T(8,128)(2,1)}, bf16[4,2,2,64,512]{4,3,2,1,0:T(8,128)(2,1)S(1)}, u32[]{:S(2)}, u32[]{:S(2)}) %collective-permute-start.3) | collective-permute-done | bytes 1048608 | tf_op jit(solution)/shard_map/ppermute | solution.py:73
  102.6 16.1 %mix.3 = (bf16[4,2,2,64,512]{4,3,2,1,0:T(8,128)(2,1)S(1)}, bf16[4,2,2,64,512]{4,3,2,1,0:T(8,128)(2,1)S(1)}, bf16[4,512,1024]{2,1,0:T(8,128)(2,1)}) custom-call(s32[1]{0:T(128)} %bitcast.near_ref, bf16[4,2,2,64,512]{4,3,2,1,0:T(8,128)(2,1)} %all-to-all-done.1.refs_0_, ...), custom_call_target="tpu_custom_call", output_to_operand_aliasing={{2}: (7, {})} | custom-call | flops 11274289152 | bytes 10485760 | tf_op jit(solution)/shard_map/mix/pallas_call | solution.py:395
  121.1 5.4 %collective-permute-done.4 = bf16[4,2,2,64,512]{4,3,2,1,0:T(8,128)(2,1)} collective-permute-done((bf16[4,2,2,64,512]{4,3,2,1,0:T(8,128)(2,1)}, bf16[4,2,2,64,512]{4,3,2,1,0:T(8,128)(2,1)}, u32[]{:S(2)}, u32[]{:S(2)}) %collective-permute-start.4) | collective-permute-done | bytes 1048608 | tf_op jit(solution)/shard_map/ppermute | solution.py:73
  129.4 4.4 all-to-all-start.2
  134.0 22.9 %collective-permute-done.5 = bf16[4,2,2,64,512]{4,3,2,1,0:T(8,128)(2,1)S(1)} collective-permute-done((bf16[4,2,2,64,512]{4,3,2,1,0:T(8,128)(2,1)}, bf16[4,2,2,64,512]{4,3,2,1,0:T(8,128)(2,1)S(1)}, u32[]{:S(2)}, u32[]{:S(2)}) %collective-permute-start.5) | collective-permute-done | bytes 1048608 | tf_op jit(solution)/shard_map/ppermute | solution.py:73
  158.3 5.0 %all-to-all-start.5 = ((bf16[4,2,2,64,512]{4,3,2,1,0:T(8,128)(2,1)}), bf16[4,2,2,64,512]{4,3,2,1,0:T(8,128)(2,1)}, u32[]{:S(2)}, u32[]{:S(2)}) async-start(bf16[4,2,2,64,512]{4,3,2,1,0:T(8,128)(2,1)} %add_convert_fusion.2), calls=%async_computation.5 | async-start | bytes 2097152 | tf_op jit(solution)/shard_map/all_to_all | solution.py:51
  165.8 10.2 %feed_forward.2 = (bf16[2,2,64,512]{3,2,1,0:T(8,128)(2,1)}, f32[2,2,64,512]{3,2,1,0:T(8,128)}, bf16[4,2,2,64,512]{4,3,2,1,0:T(8,128)(2,1)}, f32[1,512]{1,0:T(1,1...) custom-call(bf16[4,2,2,64,512]{4,3,2,1,0:T(8,128)(2,1)} %all-to-all-, ...), custom_call_target="tpu_custom_call" | custom-call | flops 3221225472 | bytes 11534336 | tf_op jit(solution)/shard_map/feed_forward/pallas_call | solution.py:513
  176.0 13.8 %all-to-all-done.5.arrived = bf16[4,2,2,64,512]{4,3,2,1,0:T(8,128)(2,1)} async-done(((bf16[4,2,2,64,512]{4,3,2,1,0:T(8,128)(2,1)}), bf16[4,2,2,64,512]{4,3,2,1,0:T(8,128)(2,1)}, u32[]{:S(2)}, u32[]{:S(2)}) %all-to-all-start.5) | async-done | bytes 1048608 | tf_op jit(solution)/shard_map/all_to_all | solution.py:51
  197.5 16.8 %feed_forward.3 = (bf16[2,2,64,512]{3,2,1,0:T(8,128)(2,1)}, f32[2,2,64,512]{3,2,1,0:T(8,128)}, bf16[4,2,2,64,512]{4,3,2,1,0:T(8,128)(2,1)}, f32[1,512]{1,0:T(1,1...) custom-call(bf16[4,2,2,64,512]{4,3,2,1,0:T(8,128)(2,1)} %all-to-all-done.5.arrived, ...), custom_call_target="tpu_custom_call" | custom-call | flops 6442450944 | bytes 11534336 | tf_op jit(solution)/shard_map/feed_forward/pallas_call | solution.py:513
  214.3 4.6 %all-to-all-done.4.refs_0_ = bf16[4,2,2,64,512]{4,3,2,1,0:T(8,128)(2,1)S(1)} async-done(((bf16[4,2,2,64,512]{4,3,2,1,0:T(8,128)(2,1)}), bf16[4,2,2,64,512]{4,3,2,1,0:T(8,128)(2,1)S(1)}, u32[]{:S(2)}, u32[]{:S(2)}) %all-to-all-start.4) | async-done | bytes 1048608 | tf_op jit(solution)/shard_map/all_to_all | solution.py:51
  226.9 22.3 %all-to-all-done.6.refs_0_ = bf16[4,2,2,64,512]{4,3,2,1,0:T(8,128)(2,1)S(1)} async-done(((bf16[4,2,2,64,512]{4,3,2,1,0:T(8,128)(2,1)}), bf16[4,2,2,64,512]{4,3,2,1,0:T(8,128)(2,1)S(1)}, u32[]{:S(2)}, u32[]{:S(2)}) %all-to-all-start.6) | async-done | bytes 1048608 | tf_op jit(solution)/shard_map/all_to_all | solution.py:51
  249.3 5.5 %convert_add_fusion = f32[2,8,3,64,512]{4,3,2,1,0:T(8,128)S(1)} fusion(f32[2,8,3,64,512]{4,3,2,1,0:T(8,128)} %get-tuple-element.144, bf16[2,8,3,64,512]{4,3,2,1,0:T(8,128)(2,1)} %collective-permute-done.9), kind=kLoop, calls=%fused_computation | loop fusion | flops 3145728 | bytes 15728640 | tf_op jit(solution)/shard_map/add | solution.py:681
  254.8 22.2 %mix_back.2 = (bf16[4,2,2,64,512]{4,3,2,1,0:T(8,128)(2,1)}, bf16[4,2,2,64,512]{4,3,2,1,0:T(8,128)(2,1)}, bf16[4,1024,3072]{2,1,0:T(8,128)(2,1)}, f32[3,64,512]{2,1,0:T(8,128)}) custom-call(s32[1]{0:T(128)} %bitcast.near_ref, s32[1]{0:T(128)} %bitcast.1.own_ref, bf16[4,2,2,64,512]{4,3,2,1,0:T(8,128)(2,1)} %copy-done.25, ...), custom_call_target="tpu_custom_call" | custom-call | flops 11274289152 | bytes 10485760 | tf_op jit(solution)/shard_map/mix_back/pallas_call | solution.py:435
  281.7 20.2 %mix_back.3 = (bf16[4,2,2,64,512]{4,3,2,1,0:T(8,128)(2,1)}, bf16[4,2,2,64,512]{4,3,2,1,0:T(8,128)(2,1)}, bf16[4,1024,3072]{2,1,0:T(8,128)(2,1)}, f32[3,64,512]{2,1,0:T(8,128)}) custom-call(s32[1]{0:T(128)} %bitcast.near_ref, s32[1]{0:T(128)} %bitcast.1.own_ref, bf16[4,2,2,64,512]{4,3,2,1,0:T(8,128)(2,1)} %copy-done.26, ...), custom_call_target="tpu_custom_call", output_to_operand_aliasing={{2}: (9, {})} | custom-call | flops 11274289152 | bytes 10485760 | tf_op jit(solution)/shard_map/mix_back/pallas_call | solution.py:435
  306.2 3.9 all-to-all-start.7
  310.9 4.8 %collective-permute-done.14 = bf16[1,8,3,64,512]{4,3,2,1,0:T(8,128)(2,1)S(1)} collective-permute-done((bf16[1,8,3,64,512]{4,3,2,1,0:T(8,128)(2,1)}, bf16[1,8,3,64,512]{4,3,2,1,0:T(8,128)(2,1)S(1)}, u32[]{:S(2)}, u32[]{:S(2)}) %collective-permute-start.14) | collective-permute-done | bytes 1572896 | tf_op jit(solution)/shard_map/ppermute | solution.py:89
  315.7 21.8 %mixing_products.1 = (f32[6,256,512]{2,1,0:T(8,128)}, bf16[6,256,512]{2,1,0:T(8,128)(2,1)}, f32[512,1]{1,0:T(8,128)}) custom-call(s32[1]{0:T(128)} %bitcast.23.bit_ref, bf16[4,512,1024]{2,1,0:T(8,128)(2,1)} %get-tuple-element.153.refs_6_.flip_ref, bf16[4,1024,3072]{2,1,0:T(8,128)(2,1)} %get-tuple-element.167.plus_ref.minus_ref, ...), custom_call_target="tpu_custom_call" | custom-call | flops 12884901888 | bytes 35651584 | tf_op jit(solution)/shard_map/mixing_products/pallas_call | solution.py:473
  340.7 4.4 all-to-all-start.8
  353.5 15.9 %collective-permute-done.19 = bf16[3,16,512]{2,1,0:T(8,128)(2,1)S(1)} collective-permute-done((bf16[3,16,512]{2,1,0:T(8,128)(2,1)S(1)}, bf16[3,16,512]{2,1,0:T(8,128)(2,1)S(1)}, u32[]{:S(2)}, u32[]{:S(2)}) %collective-permute-start.19) | collective-permute-done | bytes 49184 | tf_op jit(solution)/shard_map/ppermute | solution.py:89
  372.1 4.9 %all-to-all-start.9 = ((bf16[4,3,64,512]{3,2,1,0:T(8,128)(2,1)}), bf16[4,3,64,512]{3,2,1,0:T(8,128)(2,1)S(1)}, u32[]{:S(2)}, u32[]{:S(2)}) async-start(bf16[4,3,64,512]{3,2,1,0:T(8,128)(2,1)} %fusion.2), calls=%async_computation.9 | async-start | bytes 1572864 | tf_op jit(solution)/shard_map/all_to_all | solution.py:51
  389.9 4.6 %collective-permute-start.28 = (f32[8,512]{1,0:T(8,128)S(1)}, f32[8,512]{1,0:T(8,128)S(1)}, u32[]{:S(2)}, u32[]{:S(2)}) collective-permute-start(f32[8,512]{1,0:T(8,128)S(1)} %fusion.46), channel_id=1, source_target_pairs={{0,4},{1,5},{2,6},{3,7},{4,0},{5,1},{6,2},{7,3},{8,12},{9,13},{10,... | collective-permute-start | bytes 49160 | tf_op jit(solution)/shard_map/ppermute | solution.py:129
  402.0 4.1 collective-permute-done.30
  410.6 4.2 all-to-all-start.10
  418.8 5.3 %all-to-all-done.10 = bf16[4,2,3,16,512]{4,3,2,1,0:T(8,128)(2,1)S(1)} async-done(((bf16[4,2,3,16,512]{4,3,2,1,0:T(8,128)(2,1)}), bf16[4,2,3,16,512]{4,3,2,1,0:T(8,128)(2,1)S(1)}, u32[]{:S(2)}, u32[]{:S(2)}) %all-to-all-start.10) | async-done | bytes 393248 | tf_op jit(solution)/shard_map/all_to_all | solution.py:51
  424.9 7.0 %collective-permute-done.24 = bf16[24,16,512]{2,1,0:T(8,128)(2,1)S(1)} collective-permute-done((bf16[24,16,512]{2,1,0:T(8,128)(2,1)S(1)}, bf16[24,16,512]{2,1,0:T(8,128)(2,1)S(1)}, u32[]{:S(2)}, u32[]{:S(2)}) %collective-permute-start.24) | collective-permute-done | bytes 393248 | tf_op jit(solution)/shard_map/ppermute | solution.py:89
  (259 shorter events, 117.8 us)
Async XLA Ops:
  6.1 32.2 %all-to-all-start = ((bf16[4,2,2,64,512]{4,3,2,1,0:T(8,128)(2,1)}), bf16[4,2,2,64,512]{4,3,2,1,0:T(8,128)(2,1)S(1)}, u32[]{:S(2)}, u32[]{:S(2)}) async-start(bf16[4,2,2,64,512]{4,3,2,1,0:T(8,128)(2,1)} %broadcast_in_dim.24), calls=%async_computation | async-start | bytes 2097152 | tf_op jit(solution)/shard_map/all_to_all | solution.py:51
  14.5 20.7 %collective-permute-start.1 = (bf16[3,64,512]{2,1,0:T(8,128)(2,1)}, bf16[3,64,512]{2,1,0:T(8,128)(2,1)}, u32[]{:S(2)}, u32[]{:S(2)}) collective-permute-start(bf16[3,64,512]{2,1,0:T(8,128)(2,1)} %bitcast.13), channel_id=1, source_target_pairs={{0,1},{1,0},{2,3},{3,2},{4,5},{5,4},{6,7},{7,6},{8,9},{9,8},{10,11... | collective-permute-start | bytes 589832 | tf_op jit(solution)/shard_map/ppermute | solution.py:73
  16.0 18.2 %collective-permute-start = (bf16[4,2,1,512]{3,2,1,0:T(2,128)(2,1)S(1)}, bf16[4,2,1,512]{3,2,1,0:T(2,128)(2,1)S(1)}, u32[]{:S(2)}, u32[]{:S(2)}) collective-permute-start(bf16[4,2,1,512]{3,2,1,0:T(2,128)(2,1)S(1)} %slice.207), channel_id=1, source_target_pairs={{0,1},{1,2},{2,3},{3,4},{4,5},{5,6},{6,7},{8,9},{9,10},{10,11},{11... | collective-permute-start | bytes 24584 | tf_op jit(solution)/shard_map/ppermute | solution.py:600
  41.7 30.7 %all-to-all-start.1 = ((bf16[4,2,2,64,512]{4,3,2,1,0:T(8,128)(2,1)}), bf16[4,2,2,64,512]{4,3,2,1,0:T(8,128)(2,1)}, u32[]{:S(2)}, u32[]{:S(2)}) async-start(bf16[4,2,2,64,512]{4,3,2,1,0:T(8,128)(2,1)} %broadcast_in_dim.29), calls=%async_computation.1 | async-start | bytes 2097152 | tf_op jit(solution)/shard_map/all_to_all | solution.py:51
  47.4 30.3 %collective-permute-start.2 = (bf16[4,2,2,64,512]{4,3,2,1,0:T(8,128)(2,1)S(1)}, bf16[4,2,2,64,512]{4,3,2,1,0:T(8,128)(2,1)}, u32[]{:S(2)}, u32[]{:S(2)}) collective-permute-start(bf16[4,2,2,64,512]{4,3,2,1,0:T(8,128)(2,1)S(1)} %all-to-all-done.refs_0_), channel_id=1, source_target_pairs={{0,1},{1,0},{2,3},{3,2},{4,5},{5,4},{6,7},{7,6},{8,9},{9,8},{10,11... | collective-permute-start | bytes 3145736 | tf_op jit(solution)/shard_map/ppermute | solution.py:73
  72.4 47.3 %all-to-all-start.3 = ((bf16[4,2,3,64,512]{4,3,2,1,0:T(8,128)(2,1)}), bf16[4,2,3,64,512]{4,3,2,1,0:T(8,128)(2,1)}, u32[]{:S(2)}, u32[]{:S(2)}) async-start(bf16[4,2,3,64,512]{4,3,2,1,0:T(8,128)(2,1)} %broadcast_in_dim.28), calls=%async_computation.3 | async-start | bytes 3145728 | tf_op jit(solution)/shard_map/all_to_all | solution.py:51
  77.3 25.0 %collective-permute-start.3 = (bf16[4,2,2,64,512]{4,3,2,1,0:T(8,128)(2,1)}, bf16[4,2,2,64,512]{4,3,2,1,0:T(8,128)(2,1)S(1)}, u32[]{:S(2)}, u32[]{:S(2)}) collective-permute-start(bf16[4,2,2,64,512]{4,3,2,1,0:T(8,128)(2,1)} %all-to-all-done.1.refs_0_), channel_id=1, source_target_pairs={{0,1},{1,0},{2,3},{3,2},{4,5},{5,4},{6,7},{7,6},{8,9},{9,8},{10,11... | collective-permute-start | bytes 3145736 | tf_op jit(solution)/shard_map/ppermute | solution.py:73
  102.3 24.3 %collective-permute-start.4 = (bf16[4,2,2,64,512]{4,3,2,1,0:T(8,128)(2,1)}, bf16[4,2,2,64,512]{4,3,2,1,0:T(8,128)(2,1)}, u32[]{:S(2)}, u32[]{:S(2)}) collective-permute-start(bf16[4,2,2,64,512]{4,3,2,1,0:T(8,128)(2,1)} %get-tuple-element.120), channel_id=1, source_target_pairs={{0,1},{1,0},{2,3},{3,2},{4,5},{5,4},{6,7},{7,6},{8,9},{9,8},{10,11... | collective-permute-start | bytes 3145736 | tf_op jit(solution)/shard_map/ppermute | solution.py:73
  119.6 37.3 %collective-permute-start.6 = (bf16[8,3,64,512]{3,2,1,0:T(8,128)(2,1)}, bf16[8,3,64,512]{3,2,1,0:T(8,128)(2,1)}, u32[]{:S(2)}, u32[]{:S(2)}) collective-permute-start(bf16[8,3,64,512]{3,2,1,0:T(8,128)(2,1)} %bitcast.16.refs_0_), channel_id=1, source_target_pairs={{0,16},{8,24},{16,0},{24,8},{1,17},{9,25},{17,1},{25,9},{2,18},{10... | collective-permute-start | bytes 4718600 | tf_op jit(solution)/shard_map/ppermute | solution.py:89
  129.4 28.9 %all-to-all-start.2 = ((bf16[4,2,2,64,512]{4,3,2,1,0:T(8,128)(2,1)}), bf16[4,2,2,64,512]{4,3,2,1,0:T(8,128)(2,1)}, u32[]{:S(2)}, u32[]{:S(2)}) async-start(bf16[4,2,2,64,512]{4,3,2,1,0:T(8,128)(2,1)} %add_convert_fusion.3), calls=%async_computation.2 | async-start | bytes 2097152 | tf_op jit(solution)/shard_map/all_to_all | solution.py:51
  133.8 23.2 %collective-permute-start.5 = (bf16[4,2,2,64,512]{4,3,2,1,0:T(8,128)(2,1)}, bf16[4,2,2,64,512]{4,3,2,1,0:T(8,128)(2,1)S(1)}, u32[]{:S(2)}, u32[]{:S(2)}) collective-permute-start(bf16[4,2,2,64,512]{4,3,2,1,0:T(8,128)(2,1)} %copy-done.4), channel_id=1, source_target_pairs={{0,1},{1,0},{2,3},{3,2},{4,5},{5,4},{6,7},{7,6},{8,9},{9,8},{10,11... | collective-permute-start | bytes 3145736 | tf_op jit(solution)/shard_map/ppermute | solution.py:73
  134.0 31.8 %collective-permute-start.7 = (bf16[8,3,64,512]{3,2,1,0:T(8,128)(2,1)}, bf16[8,3,64,512]{3,2,1,0:T(8,128)(2,1)}, u32[]{:S(2)}, u32[]{:S(2)}) collective-permute-start(bf16[8,3,64,512]{3,2,1,0:T(8,128)(2,1)} %bitcast.16.refs_0_), channel_id=1, source_target_pairs={{0,8},{8,0},{16,24},{24,16},{1,9},{9,1},{17,25},{25,17},{2,10},{10... | collective-permute-start | bytes 4718600 | tf_op jit(solution)/shard_map/ppermute | solution.py:89
  158.3 31.5 %all-to-all-start.5 = ((bf16[4,2,2,64,512]{4,3,2,1,0:T(8,128)(2,1)}), bf16[4,2,2,64,512]{4,3,2,1,0:T(8,128)(2,1)}, u32[]{:S(2)}, u32[]{:S(2)}) async-start(bf16[4,2,2,64,512]{4,3,2,1,0:T(8,128)(2,1)} %add_convert_fusion.2), calls=%async_computation.5 | async-start | bytes 2097152 | tf_op jit(solution)/shard_map/all_to_all | solution.py:51
  189.8 29.1 %all-to-all-start.4 = ((bf16[4,2,2,64,512]{4,3,2,1,0:T(8,128)(2,1)}), bf16[4,2,2,64,512]{4,3,2,1,0:T(8,128)(2,1)S(1)}, u32[]{:S(2)}, u32[]{:S(2)}) async-start(bf16[4,2,2,64,512]{4,3,2,1,0:T(8,128)(2,1)} %get-tuple-element.132), calls=%async_computation.4 | async-start | bytes 2097152 | tf_op jit(solution)/shard_map/all_to_all | solution.py:51
  218.8 30.5 %collective-permute-start.9 = (bf16[2,8,3,64,512]{4,3,2,1,0:T(8,128)(2,1)}, bf16[2,8,3,64,512]{4,3,2,1,0:T(8,128)(2,1)}, u32[]{:S(2)}, u32[]{:S(2)}) collective-permute-start(bf16[2,8,3,64,512]{4,3,2,1,0:T(8,128)(2,1)} %get-tuple-element.145), channel_id=1, source_target_pairs={{0,8},{8,0},{16,24},{24,16},{1,9},{9,1},{17,25},{25,17},{2,10},{10... | collective-permute-start | bytes 9437192 | tf_op jit(solution)/shard_map/ppermute | solution.py:89
  218.8 30.3 %all-to-all-start.6 = ((bf16[4,2,2,64,512]{4,3,2,1,0:T(8,128)(2,1)}), bf16[4,2,2,64,512]{4,3,2,1,0:T(8,128)(2,1)S(1)}, u32[]{:S(2)}, u32[]{:S(2)}) async-start(bf16[4,2,2,64,512]{4,3,2,1,0:T(8,128)(2,1)} %get-tuple-element.147), calls=%async_computation.6 | async-start | bytes 2097152 | tf_op jit(solution)/shard_map/all_to_all | solution.py:51
  222.4 26.9 %collective-permute-start.10 = (bf16[4,2,2,64,512]{4,3,2,1,0:T(8,128)(2,1)S(1)}, bf16[4,2,2,64,512]{4,3,2,1,0:T(8,128)(2,1)}, u32[]{:S(2)}, u32[]{:S(2)}) collective-permute-start(bf16[4,2,2,64,512]{4,3,2,1,0:T(8,128)(2,1)S(1)} %all-to-all-done.4.refs_0_), channel_id=1, source_target_pairs={{0,1},{1,0},{2,3},{3,2},{4,5},{5,4},{6,7},{7,6},{8,9},{9,8},{10,11... | collective-permute-start | bytes 3145736 | tf_op jit(solution)/shard_map/ppermute | solution.py:73
  225.4 29.4 %collective-permute-start.11 = (bf16[4,2,1,512]{3,2,1,0:T(2,128)(2,1)S(1)}, bf16[4,2,1,512]{3,2,1,0:T(2,128)(2,1)S(1)}, u32[]{:S(2)}, u32[]{:S(2)}) collective-permute-start(bf16[4,2,1,512]{3,2,1,0:T(2,128)(2,1)S(1)} %fusion.31), channel_id=1, source_target_pairs={{1,0},{2,1},{3,2},{4,3},{5,4},{6,5},{7,6},{9,8},{10,9},{11,10},{12... | collective-permute-start | bytes 24584 | tf_op jit(solution)/shard_map/ppermute | solution.py:687
  249.2 27.9 %collective-permute-start.12 = (bf16[4,2,2,64,512]{4,3,2,1,0:T(8,128)(2,1)S(1)}, bf16[4,2,2,64,512]{4,3,2,1,0:T(8,128)(2,1)}, u32[]{:S(2)}, u32[]{:S(2)}) collective-permute-start(bf16[4,2,2,64,512]{4,3,2,1,0:T(8,128)(2,1)S(1)} %all-to-all-done.6.refs_0_), channel_id=1, source_target_pairs={{0,1},{1,0},{2,3},{3,2},{4,5},{5,4},{6,7},{7,6},{8,9},{9,8},{10,11... | collective-permute-start | bytes 3145736 | tf_op jit(solution)/shard_map/ppermute | solution.py:73
  277.1 25.0 %collective-permute-start.13 = (bf16[4,2,2,64,512]{4,3,2,1,0:T(8,128)(2,1)}, bf16[4,2,2,64,512]{4,3,2,1,0:T(8,128)(2,1)}, u32[]{:S(2)}, u32[]{:S(2)}) collective-permute-start(bf16[4,2,2,64,512]{4,3,2,1,0:T(8,128)(2,1)} %get-tuple-element.158), channel_id=1, source_target_pairs={{0,1},{1,0},{2,3},{3,2},{4,5},{5,4},{6,7},{7,6},{8,9},{9,8},{10,11... | collective-permute-start | bytes 3145736 | tf_op jit(solution)/shard_map/ppermute | solution.py:73
  280.2 35.5 %collective-permute-start.14 = (bf16[1,8,3,64,512]{4,3,2,1,0:T(8,128)(2,1)}, bf16[1,8,3,64,512]{4,3,2,1,0:T(8,128)(2,1)S(1)}, u32[]{:S(2)}, u32[]{:S(2)}) collective-permute-start(bf16[1,8,3,64,512]{4,3,2,1,0:T(8,128)(2,1)} %slice.307), channel_id=1, source_target_pairs={{0,16},{8,24},{16,0},{24,8},{1,17},{9,25},{17,1},{25,9},{2,18},{10... | collective-permute-start | bytes 4718600 | tf_op jit(solution)/shard_map/ppermute | solution.py:89
  304.8 32.7 %collective-permute-start.16 = (bf16[4,2,2,64,512]{4,3,2,1,0:T(8,128)(2,1)}, bf16[4,2,2,64,512]{4,3,2,1,0:T(8,128)(2,1)}, u32[]{:S(2)}, u32[]{:S(2)}) collective-permute-start(bf16[4,2,2,64,512]{4,3,2,1,0:T(8,128)(2,1)} %get-tuple-element.170), channel_id=1, source_target_pairs={{0,1},{1,0},{2,3},{3,2},{4,5},{5,4},{6,7},{7,6},{8,9},{9,8},{10,11... | collective-permute-start | bytes 3145736 | tf_op jit(solution)/shard_map/ppermute | solution.py:73
  306.2 33.9 %all-to-all-start.7 = ((bf16[4,2,2,64,512]{4,3,2,1,0:T(8,128)(2,1)}), bf16[4,2,2,64,512]{4,3,2,1,0:T(8,128)(2,1)S(1)}, u32[]{:S(2)}, u32[]{:S(2)}) async-start(bf16[4,2,2,64,512]{4,3,2,1,0:T(8,128)(2,1)} %add_convert_fusion.1), calls=%async_computation.7 | async-start | bytes 2097152 | tf_op jit(solution)/shard_map/all_to_all | solution.py:51
  340.7 31.4 %all-to-all-start.8 = ((bf16[4,2,2,64,512]{4,3,2,1,0:T(8,128)(2,1)}), bf16[4,2,2,64,512]{4,3,2,1,0:T(8,128)(2,1)}, u32[]{:S(2)}, u32[]{:S(2)}) async-start(bf16[4,2,2,64,512]{4,3,2,1,0:T(8,128)(2,1)} %add_convert_fusion), calls=%async_computation.8 | async-start | bytes 2097152 | tf_op jit(solution)/shard_map/all_to_all | solution.py:51
  348.3 21.1 %collective-permute-start.18 = (bf16[6,128,512]{2,1,0:T(8,128)(2,1)S(1)}, bf16[6,128,512]{2,1,0:T(8,128)(2,1)S(1)}, u32[]{:S(2)}, u32[]{:S(2)}) collective-permute-start(bf16[6,128,512]{2,1,0:T(8,128)(2,1)S(1)} %fusion.5), channel_id=1, source_target_pairs={{0,16},{8,24},{16,0},{24,8},{1,17},{9,25},{17,1},{25,9},{2,18},{10... | collective-permute-start | bytes 2359304 | tf_op jit(solution)/shard_map/ppermute | solution.py:89
  350.7 20.3 %collective-permute-start.23 = (bf16[4,3,64,512]{3,2,1,0:T(8,128)(2,1)S(1)}, bf16[4,3,64,512]{3,2,1,0:T(8,128)(2,1)S(1)}, u32[]{:S(2)}, u32[]{:S(2)}) collective-permute-start(bf16[4,3,64,512]{3,2,1,0:T(8,128)(2,1)S(1)} %fusion.6), channel_id=1, source_target_pairs={{0,1},{1,0},{2,3},{3,2},{4,5},{5,4},{6,7},{7,6},{8,9},{9,8},{10,11... | collective-permute-start | bytes 2359304 | tf_op jit(solution)/shard_map/ppermute | solution.py:73
  351.4 18.0 %collective-permute-start.19 = (bf16[3,16,512]{2,1,0:T(8,128)(2,1)S(1)}, bf16[3,16,512]{2,1,0:T(8,128)(2,1)S(1)}, u32[]{:S(2)}, u32[]{:S(2)}) collective-permute-start(bf16[3,16,512]{2,1,0:T(8,128)(2,1)S(1)} %fusion.30), channel_id=1, source_target_pairs={{0,16},{8,24},{16,0},{24,8},{1,17},{9,25},{17,1},{25,9},{2,18},{10... | collective-permute-start | bytes 147464 | tf_op jit(solution)/shard_map/ppermute | solution.py:89
  372.1 34.0 %all-to-all-start.9 = ((bf16[4,3,64,512]{3,2,1,0:T(8,128)(2,1)}), bf16[4,3,64,512]{3,2,1,0:T(8,128)(2,1)S(1)}, u32[]{:S(2)}, u32[]{:S(2)}) async-start(bf16[4,3,64,512]{3,2,1,0:T(8,128)(2,1)} %fusion.2), calls=%async_computation.9 | async-start | bytes 1572864 | tf_op jit(solution)/shard_map/all_to_all | solution.py:51
  379.3 22.8 %collective-permute-start.22 = (bf16[3,16,512]{2,1,0:T(8,128)(2,1)S(1)}, bf16[3,16,512]{2,1,0:T(8,128)(2,1)S(1)}, u32[]{:S(2)}, u32[]{:S(2)}) collective-permute-start(bf16[3,16,512]{2,1,0:T(8,128)(2,1)S(1)} %fusion.29), channel_id=1, source_target_pairs={{0,1},{1,0},{2,3},{3,2},{4,5},{5,4},{6,7},{7,6},{8,9},{9,8},{10,11... | collective-permute-start | bytes 147464 | tf_op jit(solution)/shard_map/ppermute | solution.py:73
  388.2 20.3 %collective-permute-start.20 = (bf16[6,128,512]{2,1,0:T(8,128)(2,1)S(1)}, bf16[6,128,512]{2,1,0:T(8,128)(2,1)}, u32[]{:S(2)}, u32[]{:S(2)}) collective-permute-start(bf16[6,128,512]{2,1,0:T(8,128)(2,1)S(1)} %copy-done.10), channel_id=1, source_target_pairs={{0,16},{8,24},{16,0},{24,8},{1,17},{9,25},{17,1},{25,9},{2,18},{10... | collective-permute-start | bytes 2359304 | tf_op jit(solution)/shard_map/ppermute | solution.py:89
  410.6 13.5 %all-to-all-start.10 = ((bf16[4,2,3,16,512]{4,3,2,1,0:T(8,128)(2,1)}), bf16[4,2,3,16,512]{4,3,2,1,0:T(8,128)(2,1)S(1)}, u32[]{:S(2)}, u32[]{:S(2)}) async-start(bf16[4,2,3,16,512]{4,3,2,1,0:T(8,128)(2,1)} %broadcast_in_dim.66), calls=%async_computation.10 | async-start | bytes 786432 | tf_op jit(solution)/shard_map/all_to_all | solution.py:51
  417.7 19.1 %collective-permute-start.21 = (bf16[6,256,512]{2,1,0:T(8,128)(2,1)}, bf16[6,256,512]{2,1,0:T(8,128)(2,1)}, u32[]{:S(2)}, u32[]{:S(2)}) collective-permute-start(bf16[6,256,512]{2,1,0:T(8,128)(2,1)} %pad_maximum_fusion), channel_id=1, source_target_pairs={{0,8},{8,0},{16,24},{24,16},{1,9},{9,1},{17,25},{25,17},{2,10},{10... | collective-permute-start | bytes 4718600 | tf_op jit(solution)/shard_map/ppermute | solution.py:89
  (61 other events, 596.6 us)

commit v4 on v3

--- a/solution.py
+++ b/solution.py
@@ -36,19 +36,46 @@
 
 class Grid:
     def __init__(self, size):
-        self.far = 4 if size % 4 == 0 else 1
-        self.near = size // self.far
         self.size = size
+        self.near = size // 4
+        self.mate = self.near
+        self.far = 2 * self.near
+
+    def near_bits(self):
+        return [1 << n for n in range(self.near.bit_length() - 1)]
 
     def near_shift(self, step):
         near = self.near
         return [(f, f // near * near + (f % near + step) % near) for f in range(self.size)]
 
-    def swap_far(self, values):
-        groups = [
-            [i * self.near + j for i in range(self.far)] for j in range(self.near)
-        ]
-        return lax.all_to_all(values, "filt", 0, 0, axis_index_groups=groups, tiled=True)
+    def flag(self, bit):
+        return (lax.axis_index("filt") & bit) != 0
+
+    def swap(self, values, bit):
+        return lax.ppermute(values, "filt", [(f, f ^ bit) for f in range(self.size)])
+
+    def split(self, halves, bit):
+        flag = self.flag(bit)
+        return jnp.where(flag, halves[1], halves[0]), jnp.where(flag, halves[0], halves[1])
+
+    def join(self, own, other, bit):
+        return jnp.where(self.flag(bit), jnp.stack([other, own]), jnp.stack([own, other]))
+
+    def spread_bits(self):
+        return [self.far, self.mate, *self.near_bits()]
+
+
+def gather_filt(grid, values):
+    for bit in grid.spread_bits():
+        values = grid.join(values, grid.swap(values, bit), bit)
+    return values
+
+
+def reduce_filt(grid, values, bits):
+    for bit in bits:
+        own, away = grid.split(values, bit)
+        values = own.astype(F32) + grid.swap(away.astype(BF16), bit).astype(F32)
+    return values
 
 
 def tie(value, *others):
@@ -57,10 +84,6 @@
 
 def tied(*values):
     return list(lax.optimization_barrier(values))
-
-
-def copies(grid, own):
-    return jnp.broadcast_to(own[None], (grid.far, *own.shape))
 
 
 def tie_all(values, *others):
@@ -94,32 +117,30 @@
     return [1 << n for n in range(count.bit_length() - 1)]
 
 
-def row_step(values, bit):
+def row_halves(values, bit):
     parts, height, width = values.shape
     halves = values.reshape(parts, 2, height // 2, width)
     high = (lax.axis_index("rows") & bit) != 0
     away = jnp.where(high, halves[:, 0], halves[:, 1]).astype(BF16)
-    return jnp.where(high, halves[:, 1], halves[:, 0]), swap_rows(away, bit)
-
-
-def gather_rows(full):
+    return jnp.where(high, halves[:, 1], halves[:, 0]), away
+
+
+def row_step(values, bit):
+    kept, away = row_halves(values, bit)
+    return kept, swap_rows(away, bit)
+
+
+def gather_rows(full, after=()):
     index = lax.axis_index("rows")
-    for bit in reversed(row_bits()):
+    for n, bit in enumerate(reversed(row_bits())):
         high = (index & bit) != 0
         other = swap_rows(full, bit)
+        if n == 0:
+            other = tie(other, *after)
         full = jnp.concatenate(
             [jnp.where(high, other, full), jnp.where(high, full, other)], axis=1
         )
     return full
-
-
-def gather_near(grid, own):
-    at = lax.axis_index("filt") % grid.near
-    whole = jnp.zeros((grid.near, *own.shape), own.dtype)
-    for j, value in enumerate([own, *near_swaps(grid, own)]):
-        place = lax.rem(at - j + grid.near, grid.near)
-        whole = lax.dynamic_update_slice_in_dim(whole, value[None], place, 0)
-    return whole
 
 
 def all_sum(values):
@@ -147,10 +168,13 @@
     t10_ref[0] = u10.T.astype(BF16)
 
 
-def toeplitz_blocks(filters, first, count):
+def toeplitz_blocks(filters, firsts, each):
+    count = each * len(firsts)
     length = filters.shape[1] // 2
     half = length // 2
-    taps = lax.dynamic_slice_in_dim(filters, first, count, 0).astype(BF16).astype(F32)
+    taps = jnp.concatenate(
+        [lax.dynamic_slice_in_dim(filters, first, each, 0) for first in firsts], axis=0
+    ).astype(BF16).astype(F32)
     taps = taps.reshape(count, length, 2).transpose(0, 2, 1).reshape(2 * count, 1, length)
     up = jnp.pad(taps, ((0, 0), (0, 0), (0, length)))
     by_column = pl.BlockSpec((1, half, half), lambda n: (n // (2 * count), 0, n % (2 * count)))
@@ -164,6 +188,9 @@
         in_specs=[line],
         out_specs=[by_column, by_column, by_row, by_row],
         out_shape=[wide, wide, tall, tall],
+        cost_estimate=pl.CostEstimate(
+            flops=0, bytes_accessed=64 * count * half * half * 4, transcendentals=0
+        ),
         name="toeplitz",
     )(up)
 
@@ -198,13 +225,15 @@
     flip_ref, states_ref, low_ref, high_ref, sum_ref = refs[-5:]
     half = t00_ref.shape[1]
     branches = 2 * mixes[0].shape[0]
+    slots = branches // 4
     assemble(near_ref[0], pieces, states_ref)
 
     for branch in range(branches):
         slot = pl.ds(branch * half, half)
         for quarter in range(4):
             value = dot(
-                states_ref[pl.ds(quarter * half, half), :], mixes[branch % 2][branch // 2]
+                states_ref[pl.ds(quarter * half, half), :],
+                mixes[branch // 2 // slots][branch % 2 * slots + branch // 2 % slots],
             ).astype(BF16)
             target = (quarter // 2) ^ (branch % 2)
             (low_ref, high_ref)[quarter % 2][target, slot, :] = value
@@ -232,7 +261,7 @@
     width = grad_ref.shape[1]
     length = grad_ref.shape[0] // 2
     branches = back_ref.shape[2] // width
-    slots = branches // 2
+    slots = branches // 4
 
     @pl.when(pl.program_id(0) == 0)
     def _():
@@ -246,7 +275,8 @@
         high = grad_ref[pl.ds(base + half, half), :]
         for branch in range(branches):
             rows = pl.ds(branch * half, half)
-            columns = pl.ds((branch % 2 * slots + branch // 2) * width, width)
+            set_of, slot = branch // 2 // slots, branch // 2 % slots
+            columns = pl.ds(((2 * set_of + branch % 2) * slots + slot) * width, width)
             target = 2 * half * (parity ^ (branch % 2))
             back_ref[0, pl.ds(target, half), columns] = (
                 dot(u00_ref[parity, rows, :], low) + dot(u10_ref[parity, rows, :], high)
@@ -257,8 +287,8 @@
 
     for quarter in range(4):
         rows = pl.ds(quarter * half, half)
-        sum_ref[rows, :] = dot(back_ref[0, rows, : slots * width], turned[0][...]) + dot(
-            back_ref[0, rows, slots * width :], turned[1][...]
+        sum_ref[rows, :] = dot(back_ref[0, rows, : 2 * slots * width], turned[0][...]) + dot(
+            back_ref[0, rows, 2 * slots * width :], turned[1][...]
         )
     scatter(near_ref[0], sum_ref, outs)
 
@@ -282,7 +312,7 @@
     saved = refs[shares : shares + 5 * earlier]
     block, grad, low, gain_out, *rest = refs[shares + 5 * earlier :]
     if last:
-        stay_ref, away_ref = rest
+        sum_refs = rest
     else:
         scaled_ref, hidden_ref, gate_ref, up_ref = rest
     width = gain_ref.shape[1]
@@ -337,10 +367,7 @@
                     )
             for m in range(3):
                 split = (weight.shape[0], weight.shape[2], width)
-                if n < shares // 2 or shares == 1:
-                    stay_ref[n, :, m] = sums[m].reshape(split)
-                else:
-                    away_ref[n - shares // 2, :, m] = sums[m].astype(BF16).reshape(split)
+                sum_refs[n][:, m] = sums[m].astype(sum_refs[n].dtype).reshape(split)
         else:
             hidden_ref[:, columns] = hidden
             gate_ref[:, columns] = gate_back
@@ -427,7 +454,7 @@
     half = u00.shape[2]
     block = pl.BlockSpec((fars, 1, 2, height, width), lambda n, *_: (0, n, 0, 0, 0))
     rows = u00.shape[1]
-    slab = width // (parts * fars)
+    slab = 2 * width // (parts * fars)
     lag_shape = (lag_count, slab, width)
     back_shape = (flips.shape[0], 4 * half, 2 * turned[0].shape[0])
     back = pl.BlockSpec((1, *back_shape[1:]), lambda n, *_: (start + n, 0, 0))
@@ -463,19 +490,22 @@
     )(near, own, *pieces, *turned, u00, u10, flips, *before)
 
 
-def mixing_products(flips, backs, pairs, bit):
+def mixing_products(flips, backs, pairs, bit, set_of):
     count, width, length = flips.shape
-    slots = pairs[0].shape[0]
-    plus = pl.BlockSpec((count, length, width), lambda k, _: (0, 0, k))
-    minus = pl.BlockSpec((count, length, width), lambda k, _: (0, 0, slots + k))
+    slots = pairs.shape[0] // 2
+    plus = pl.BlockSpec((count, length, width), lambda k, _: (0, 0, 2 * set_of * slots + k))
+    minus = pl.BlockSpec(
+        (count, length, width), lambda k, _: (0, 0, (2 * set_of + 1) * slots + k)
+    )
     pair = pl.BlockSpec((1, width, width), lambda k, _: (k, 0, 0))
+    rest = pl.BlockSpec((1, width, width), lambda k, _: (slots + k, 0, 0))
     half = pl.BlockSpec((2, width // 2, width), lambda k, _: (k, 0, 0))
     return pl.pallas_call(
         mixing_kernel,
         grid_spec=pltpu.PrefetchScalarGridSpec(
             num_scalar_prefetch=1,
             grid=(slots,),
-            in_specs=[resident(flips.shape), plus, minus, pair, pair],
+            in_specs=[resident(flips.shape), plus, minus, pair, rest],
             out_specs=[half, half, resident((width, 1))],
         ),
         out_shape=[
@@ -485,12 +515,12 @@
         ],
         compiler_params=pltpu.CompilerParams(vmem_limit_bytes=56 << 20),
         cost_estimate=pl.CostEstimate(
-            flops=2 * backs.size * width,
-            bytes_accessed=2 * (flips.size + backs.size) + 8 * slots * width * width,
+            flops=backs.size * width,
+            bytes_accessed=2 * flips.size + backs.size + 8 * slots * width * width,
             transcendentals=0,
         ),
         name="mixing_products",
-    )(bit, flips, backs, backs, *pairs)
+    )(bit, flips, backs, backs, pairs, pairs)
 
 
 def feed_forward(arrived, inputs, states, late, lag, gain, cot, weights, saved, last):
@@ -500,11 +530,10 @@
     flat_saved = [value for values in saved for value in values] if last else []
     operands = (arrived, inputs, states, late, lag, gain, cot, *weights, *flat_saved)
     whole = pl.BlockSpec(memory_space=pltpu.VMEM)
-    kept = max(shares // 2, 1)
     if last:
         extra = [
-            jax.ShapeDtypeStruct((kept, *weights[0].shape), F32),
-            jax.ShapeDtypeStruct((kept, *weights[0].shape), BF16),
+            jax.ShapeDtypeStruct(weights[0].shape, F32 if n < shares // 2 else BF16)
+            for n in range(shares)
         ]
     else:
         extra = [jax.ShapeDtypeStruct((rows, width), BF16)] + [
@@ -554,12 +583,16 @@
     shard_rows, local_seqs, width = inputs.shape
     grid = Grid(lax.axis_size("filt"))
     row_count = lax.axis_size("rows")
+    row_index = lax.axis_index("rows")
+    bits = row_bits()
     index = lax.axis_index("filt")
     branches = mixing.shape[0]
     lag_count = regression.shape[0]
     height = shard_rows // 2
     chunks = CHUNKS
     step = local_seqs // chunks
+    own_seqs = step // 2
+    block = (own_seqs, 2, height, width)
 
     def inward(values):
         return values.reshape(height, 2, local_seqs, width).transpose(2, 1, 0, 3)
@@ -570,21 +603,38 @@
     def cut(values):
         return [values[c * step : (c + 1) * step] for c in range(chunks)]
 
+    def to_mate(part):
+        keep, away = grid.split(part.reshape(2, *block), grid.mate)
+        return keep, grid.swap(away, grid.mate)
+
+    def to_far(keep, received):
+        pair = grid.join(keep, received, grid.mate)
+        return pair, grid.swap(pair, grid.far)
+
+    def to_near(pair, received):
+        quad = grid.join(pair, received, grid.far).reshape(4, *block)
+        return quad, near_swaps(grid, quad)
+
+    def from_near(partial, received):
+        total = total_of([partial[0], *received]).reshape(2, 2, *block)
+        keep, away = grid.split(total, grid.far)
+        return keep, away.astype(BF16)
+
+    def from_far(keep, received):
+        return grid.split((keep + received.astype(F32)).astype(BF16), grid.mate)
+
+    def from_mate(keep, received):
+        return grid.join(keep, received, grid.mate).reshape(step, 2, height, width)
+
     inputs_low = inward(inputs)
     residual = inputs_low.astype(F32)
-    cotangent_low = inward(out_grad)
     factor_in = rms_factor(residual)
     normed_in = residual * factor_in
     states = (normed_in * gain_in).astype(BF16)
-    hidden_own = w_down.shape[0]
-    share = hidden_own // row_count
-    packed = jnp.stack([w_gate.T, w_up.T, w_down]).reshape(3, row_count, share, width)
-    own_share = lax.dynamic_index_in_dim(packed, lax.axis_index("rows"), 1, keepdims=False)
-    near_shares = gather_near(grid, own_share)
+    mates = [to_mate(part) for part in cut(states)]
 
     slots = (branches + 1) // 2
     first_branch = index * branches
-    t00, t10, u00, u10 = toeplitz_blocks(filters, first_branch // 2, slots)
     if branches % 2:
         odd_start = first_branch % 2
         paired = lax.dynamic_update_slice_in_dim(
@@ -592,194 +642,260 @@
         )
     else:
         paired = mixing
+    paired = tie(paired, mates[0][0])
     first, second = (paired[n::2].astype(F32) for n in range(2))
-    pairs = ((first + second).astype(BF16), (first - second).astype(BF16))
+    own_pairs = jnp.concatenate([first + second, first - second], axis=0).astype(BF16)
+    part_rows = width // row_count
+    start = sum(
+        jnp.where((row_index & bit) != 0, width >> (n + 1), 0) for n, bit in enumerate(bits)
+    )
+    own_part = lax.dynamic_slice_in_dim(own_pairs, start, part_rows, 1)
+    hidden_own = w_down.shape[0]
+    share = hidden_own // row_count
+    packed = jnp.stack([w_gate.T, w_up.T, w_down]).reshape(3, row_count, share, width)
+    *early_bits, last_bit = grid.spread_bits()
+    shares = lax.dynamic_index_in_dim(packed, row_index, 1, keepdims=False)
+    shares = grid.join(shares, grid.swap(shares, early_bits[0]), early_bits[0])
+    mates = [(keep, tie(received, own_part)) for keep, received in mates]
+    fars = [to_far(*values) for values in mates]
+    mate_part = grid.swap(tie(own_part, shares, *(pair for pair, _ in fars)), grid.mate)
+    received = [received for _, received in fars]
+    edge = lax.ppermute(
+        tie(states[:, :, -1:], *(pair for pair, _ in fars)),
+        "filt",
+        [(f, f + 1) for f in range(grid.size - 1)],
+    )
+    t00, t10, u00, u10 = toeplitz_blocks(
+        tie(filters, *(pair for pair, _ in fars)),
+        [first_branch // 2, (index ^ grid.mate) * branches // 2],
+        slots,
+    )
+    mate_part, edge = tie_all([mate_part, edge], t00, *received)
+    mate_part = tie(mate_part, edge)
+    for bit in early_bits[1:]:
+        shares = tie(shares, mate_part)
+        shares = grid.join(shares, grid.swap(shares, bit), bit)
+    quads = [to_near(*values) for values in fars]
+    mate_pairs = gather_rows(
+        mate_part, [shares, *(value for _, values in quads for value in values)]
+    )
+    pairs = [own_pairs, mate_pairs]
+    cotangent_low = inward(tie(out_grad, *received))
 
     near = jnp.reshape(index % grid.near, (1,)).astype(jnp.int32)
-
-    edge = lax.ppermute(
-        states[:, :, -1:], "filt", [(f, f + 1) for f in range(grid.size - 1)]
-    )
     late = jnp.concatenate([edge, states[:, :, :-1]], axis=2)
-    partials, flips = [], []
-    ready = [late, inputs_low, cotangent_low, t00, t10, u00, u10, *pairs, copies(grid, near_shares)]
-    state_far = []
-    for c, part in enumerate(cut(states)):
+    quads[0] = (quads[0][0], tie_all(quads[0][1], *quads[-1][1]))
+    late, inputs_low, cotangent_low, shares, *pieces = tied(
+        late, inputs_low, cotangent_low, shares, quads[0][0], *quads[0][1]
+    )
+
+    partials, flips, near_received = [], [], []
+    received = grid.swap(shares, last_bit)
+    for c in range(chunks):
         if c:
-            part = tie(part, state_far[-1])
-        state_far.append(grid.swap_far(copies(grid, part)))
+            pieces = [quads[c][0], *quads[c][1]]
+        *partial, flip = mix_sequences(
+            pieces, near, pairs, t00, t10, c * own_seqs, chunks * own_seqs, flips
+        )
         if c == 0:
-            state_far[0], *ready = tied(state_far[0], *ready)
-    late, inputs_low, cotangent_low, t00, t10, u00, u10, *pairs, shares = ready
-    state_far[-1], shares = tied(state_far[-1], shares)
-    shares = grid.swap_far(shares)
-    state_near = [near_swaps(grid, values) for values in state_far]
+            received = tie(received, partial[0])
+            shares = grid.join(shares, received, last_bit)
+        else:
+            near_received[-1] = tie_all(near_received[-1], partial[0])
+            partial = tie_all(partial, *near_received[-1])
+        partials.append(partial)
+        near_received.append(near_swaps(grid, partial))
+        flips = [flip]
+    kept_sums, from_fars, turned = [], [], []
     for c in range(chunks):
-        pieces = [state_far[c], *state_near[c]]
-        ahead = [] if c else state_far[1:]
-        pieces = [tie(pieces[0], *ahead), *pieces[1:]]
-        *partial, flip = mix_sequences(
-            pieces, near, pairs, t00, t10, c * step, local_seqs, flips
-        )
-        if c + 1 < chunks:
-            state_near[c + 1] = tie_all(state_near[c + 1], partial[0])
-            partial = tie_all(partial, *state_near[c + 1])
-        partials.append(partial)
-        flips = [flip]
-    near_received = [near_swaps(grid, partial) for partial in partials]
-    for c in range(chunks - 1):
-        near_received[c] = tie_all(near_received[c], partials[c + 1][0])
-    weights = [tie(shares, partials[0][0]).reshape(grid.size, 3, share, width)]
-    for n, bit in enumerate(reversed(row_bits())):
+        kept_sums.append(from_near(partials[c], tie_all(near_received[c], *from_fars, *turned)))
+        from_fars.append(grid.swap(kept_sums[c][1], grid.far))
+        if c == 0:
+            turned = [
+                value.transpose(0, 2, 1).reshape(2 * slots * width, width)
+                for value in tie_all(pairs, kept_sums[0][1])
+            ]
+    weights = [shares.reshape(grid.size, 3, share, width)]
+    for n, bit in enumerate(reversed(bits)):
         received = [swap_rows(weight, bit) for weight in weights]
         if n == 0:
-            received = tie_all(received, *(near_received[-1] or partials[-1][:1]))
+            received = tie_all(received, from_fars[0])
         weights = weights + received
 
-    spectral = []
-    for c in range(chunks):
-        spectral.append(
-            grid.swap_far(total_of([partials[c][0], *near_received[c]]).astype(BF16))
-        )
-
-    block_out, middle_grad, lows, grad_far, kept = [], [], [], [], []
+    block_out, middle_grad, lows, fars, kept = [], [], [], [], []
     gain_mid_part = jnp.zeros((1, width), F32)
     for c in range(chunks):
         part = slice(c * step, (c + 1) * step)
-        arrived = spectral[c]
+        keep, away = from_far(kept_sums[c][0], from_fars[c])
+        arrived = from_mate(keep, grid.swap(away, grid.mate))
         if c:
-            arrived = tie(arrived, middle_grad[-1])
+            arrived = tie(arrived, fars[-1][0])
         if c + 1 < chunks:
-            arrived = tie(arrived, *near_received[c + 1])
-        if c == chunks - 1:
-            turned = [
-                value.transpose(0, 2, 1).reshape(slots * width, width)
-                for value in (tie_all(pairs, middle_grad[-1]) if c else pairs)
-            ]
-            arrived = tie(arrived, *turned)
+            arrived = tie(arrived, kept_sums[c + 1][1])
         cot = cotangent_low[part]
         value, grad, low, gain_part, *rest = feed_forward(
-            arrived, inputs_low[part], states[part], late[part], regression, gain_mid[None], cot,
-            weights, kept, c + 1 == chunks,
+            arrived[None], inputs_low[part], states[part], late[part], regression,
+            gain_mid[None], cot, weights, kept, c + 1 == chunks,
         )
         block_out.append(value)
         middle_grad.append(grad)
+        gain_mid_part = gain_mid_part + gain_part
+        if c + 1 < chunks:
+            from_fars[c + 1] = tie(from_fars[c + 1], grad)
+            low = tie(low, from_fars[c + 1])
+        if c:
+            fars[-1] = (fars[-1][0], tie(fars[-1][1], grad))
+            low, *rest = tie_all([low, *rest], fars[-1][1])
         lows.append(low[0])
-        gain_mid_part = gain_mid_part + gain_part
-        grad_far.append(grid.swap_far(low))
+        fars.append(to_far(*to_mate(low[0])))
         if c + 1 < chunks:
             scaled, hidden, gate_back, up_back = rest
             kept.append((gate_back, up_back, hidden, scaled, cot))
     gain_mid_part = gain_mid_part[0]
 
-    bits = row_bits()
-    stay, away = tie_all(rest, grad_far[0]) if chunks > 1 else rest
-    grad_near = [near_swaps(grid, values) for values in grad_far]
-    if bits:
-        value = swap_rows(away, bits[0])
-        value, *grad_near[0] = tied(value, *grad_near[0])
-        stay = stay + value.astype(F32)
-
-    own = jnp.reshape(index, (1,)).astype(jnp.int32)
+    quads = [to_near(*values) for values in fars]
+
+    half_count = len(rest) // 2
+    values = [swap_rows(away, bits[0]) for away in rest[half_count:]]
+    values = tie_all(values, *quads[0][1])
+    sums_of = [[stay, value] for stay, value in zip(rest[:half_count], values, strict=True)]
+
+    group = index // grid.far * grid.near + index % grid.near
+    own = jnp.reshape(group, (1,)).astype(jnp.int32)
     before = ()
-    back_partials = []
+    back_partials, near_received = [], []
     mix_back = jnp.concatenate(lows, axis=0)
     next_edge = lax.ppermute(
         mix_back[:, :, :1], "filt", [(f + 1, f) for f in range(grid.size - 1)]
     )
-    grad_far[0], stay, next_edge = tied(grad_far[0], stay, next_edge)
-    ahead = []
+    for bit in bits[1:-1]:
+        half_count = len(sums_of) // 2
+        values = [swap_rows(total_of(v).astype(BF16), bit) for v in sums_of[half_count:]]
+        sums_of = [[*v, value] for v, value in zip(sums_of[:half_count], values, strict=True)]
+    parts, away = sums_of
+    half_count = away[0].shape[0] // 2
+    away = total_of(away).astype(BF16)
+    away = [away[:half_count], away[half_count:]]
+    from_rows = [swap_rows(value, bits[-1]) for value in away]
+    first_quad, next_edge = tie_all([quads[0][0], next_edge], *away)
+    quads[0] = (first_quad, quads[0][1])
     for c in range(chunks):
-        received = grad_near[c]
+        quad, received = quads[c]
         if c + 1 < chunks:
-            ahead.append(grad_far[c + 1])
-        pieces = [tie(grad_far[c], *ahead), *received]
+            quad = tie(quad, quads[c + 1][0])
         *partial, backs, lag_sum = mix_sequences_back(
-            pieces, near, own, turned, u00, u10, lag_count, c * step, flip, before
+            [quad, *received], near, own, turned, u00, u10, lag_count, c * own_seqs, flip, before
         )
         before = (backs, lag_sum)
         if c + 1 < chunks:
-            grad_near[c + 1] = tie_all(grad_near[c + 1], partial[0])
-            partial = tie_all(partial, *grad_near[c + 1])
+            later_received = tie_all(quads[c + 1][1], partial[0])
+            quads[c + 1] = (quads[c + 1][0], later_received)
+            from_rows[c] = tie(from_rows[c], partial[0])
+            partial = tie_all(partial, *later_received, from_rows[c])
+        if c:
+            near_received[-1] = tie_all(near_received[-1], partial[0])
+            from_rows[-1] = tie(from_rows[-1], partial[0])
+            lag_sum, backs, *partial = tie_all(
+                [lag_sum, backs, *partial], *near_received[-1], from_rows[-1]
+            )
         back_partials.append(partial)
-        ahead = []
-    near_received = [near_swaps(grid, partial) for partial in back_partials]
-    near_received[0] = tie_all(near_received[0], back_partials[-1][0])
-    columns = [total_of([back_partials[0][0], *near_received[0]]).astype(BF16)]
-    later = bits[1:2]
-    half_count = stay.shape[0] // 2
-    from_rows = [swap_rows(stay[half_count:].astype(BF16), bit) for bit in later]
-    kept, value = row_step(tie(lag_sum, columns[0]), bits[0])
+        near_received.append(near_swaps(grid, partial))
+    sums = [from_near(back_partials[0], near_received[0])]
+    kept, value = row_step(tie(lag_sum, sums[0][1]), bits[0])
     lag_share = kept + value.astype(F32)
-    core_bit = jnp.reshape(lax.axis_index("rows") & 1, (1,)).astype(jnp.int32)
-    mixing_stay, mixing_away, gain_column = mixing_products(
-        flip, tie(backs, columns[0], *from_rows, lag_share), pairs, core_bit
-    )
-    for bit in later:
+    kept, value = row_step(lag_share, bits[1])
+    core_bit = jnp.reshape(row_index & 1, (1,)).astype(jnp.int32)
+    mate_stay, mate_away, mate_gain = mixing_products(
+        flip, tie(backs, sums[0][1], kept), mate_pairs, core_bit, 1
+    )
+    from_fars = [tie(grid.swap(sums[0][1], grid.far), mate_gain)]
+    mate_stay, mate_away, mate_gain = tie_all([mate_stay, mate_away, mate_gain], from_fars[0])
+    lag_share = kept + tie(value, mate_gain).astype(F32)
+    for bit in bits[2:]:
         kept, value = row_step(lag_share, bit)
-        lag_share = kept + tie(value, gain_column).astype(F32)
+        lag_share = kept + value.astype(F32)
+    lag_rows = lag_share.shape[1] // 2
+    lag_share, lag_away = grid.split(
+        lag_share.reshape(lag_count, 2, lag_rows, width).transpose(1, 0, 2, 3), grid.mate
+    )
+    lag_away = lag_away.astype(BF16)
+    mate_sends = [from_far(sums[0][0], from_fars[0])]
+    mate_share = mate_stay + swap_rows(mate_away, bits[0]).astype(F32)
     for c in range(1, chunks):
-        received = tie_all(near_received[c], gain_column)
-        columns.append(total_of([back_partials[c][0], *received]).astype(BF16))
-    arrived = [grid.swap_far(column) for column in columns]
-    arrived[0], mixing_stay, mixing_away = tie_all(
-        [arrived[0], mixing_stay, mixing_away], *columns[1:]
-    )
-    state_back = [total_of(values) for values in arrived]
-
-    mixing_share = mixing_stay + swap_rows(mixing_away, bits[0]).astype(F32)
-    mixing_share, stay = tied(mixing_share, stay)
-    value = mixing_away
+        sums.append(from_near(back_partials[c], tie_all(near_received[c], mate_gain)))
+        from_fars.append(grid.swap(sums[c][1], grid.far))
+    twos = (2,) * len(grid.spread_bits())
+    grads = jnp.concatenate(
+        [
+            total_of([*(part[n * half_count : (n + 1) * half_count] for part in parts), value])
+            for n, value in enumerate(tie_all(from_rows, mate_gain))
+        ]
+    ).reshape(*twos, 3, share, width)
+    last_bits = grid.spread_bits()[::-1]
+    grads, away = grid.split(grads, last_bits[0])
+    away = away.astype(BF16)
+    mate_kept, mate_away = row_halves(mate_share, bits[1])
+    own_stay, own_away, own_gain = mixing_products(
+        flip,
+        tie(backs, mate_away, mate_sends[0][1], away, lag_away, *(v for _, v in sums[1:])),
+        own_pairs, core_bit, 0,
+    )
+    from_mates = [tie(grid.swap(mate_sends[0][1], grid.mate), own_gain)]
+    value = tie(swap_rows(mate_away, bits[1]), own_gain)
+    mate_share = mate_kept + value.astype(F32)
+    for bit in bits[2:]:
+        kept, value = row_step(mate_share, bit)
+        mate_share = kept + value.astype(F32)
+    from_fars[1:] = tie_all(from_fars[1:], own_gain)
+    own_gain = tie(own_gain, value, *from_mates, *from_fars[1:])
+    grads = grads + tie(grid.swap(away, last_bits[0]), own_gain).astype(F32)
+    lag_share = lag_share + tie(grid.swap(lag_away, grid.mate), own_gain).astype(F32)
+    own_stay, own_away = tie_all([own_stay, own_away], own_gain)
+    own_share = own_stay + swap_rows(own_away, bits[0]).astype(F32)
     for bit in bits[1:]:
-        kept, value = row_step(mixing_share, bit)
-        mixing_share = kept + value.astype(F32)
-    row_done = value
-    mixing_low, gain_column, gain_mid_part, lag_sum, lag_share, mix_back, next_edge, *block_out = (
-        tied(
-            mixing_share.astype(BF16), gain_column, gain_mid_part, lag_sum, lag_share, mix_back,
-            next_edge, *block_out,
-        )
-    )
+        kept, value = row_step(own_share, bit)
+        own_share = kept + value.astype(F32)
+    received = grid.swap(mate_share.astype(BF16), grid.mate)
+    mixing_low = (own_share + received.astype(F32)).astype(BF16)
+    gain_mid_part, lag_sum, lag_share, mix_back, next_edge, grads, own_gain, *block_out = tie_all(
+        [gain_mid_part, lag_sum, lag_share, mix_back, next_edge, grads, own_gain, *block_out],
+        mixing_low,
+    )
+    gain_column = mate_gain + own_gain
+    for c in range(1, chunks):
+        mate_sends.append(from_far(sums[c][0], from_fars[c]))
+    from_mates += [grid.swap(away, grid.mate) for _, away in mate_sends[1:]]
+    state_back = [
+        from_mate(keep, received).astype(F32)
+        for (keep, _), received in zip(mate_sends, from_mates, strict=True)
+    ]
     mixing_grad = gather_rows(mixing_low).astype(F32)
     if branches % 2:
         mixing_grad = lax.dynamic_slice_in_dim(mixing_grad, odd_start, branches, 0)
 
-    slab = width // grid.size
-    own_regression = lax.dynamic_slice_in_dim(regression, index * slab, slab, 1)
+    slab = width // grid.size * 2
+    own_regression = lax.dynamic_slice_in_dim(regression, group * slab, slab, 1)
     gain_lag = jnp.sum(own_regression.astype(F32) * lag_sum, axis=(0, 2))
     gain_in_part = gain_column[:, 0]
     gain_in_part = lax.dynamic_update_slice_in_dim(
         gain_in_part,
-        lax.dynamic_slice_in_dim(gain_in_part, index * slab, slab, 0) + gain_lag,
-        index * slab,
+        lax.dynamic_slice_in_dim(gain_in_part, group * slab, slab, 0) + gain_lag,
+        group * slab,
         0,
     ) / gain_in
     gains = all_sum(jnp.pad(jnp.stack([gain_in_part, gain_mid_part]), ((0, 6), (0, 0))))
 
-    for value in from_rows:
-        stay = stay[:half_count] + value.astype(F32)
-    for bit in bits[2:]:
-        half_count = stay.shape[0] // 2
-        value = swap_rows(stay[half_count:].astype(BF16), bit)
-        stay = stay[:half_count] + value.astype(F32)
-        kept, value = row_step(lag_share, bit)
-        lag_share = kept + value.astype(F32)
-    by_filt = stay[0].reshape(grid.far, grid.near, 3, share, width)
-    at = index % grid.near
-    away = [
-        lax.dynamic_index_in_dim(by_filt, lax.rem(at + j, grid.near), 1, keepdims=False)
-        for j in range(grid.near)
-    ]
-    returned = near_swaps(grid, [part.astype(BF16) for part in away])
-    far_grads = total_of([away[0], *tie_all(returned, row_done)]).astype(BF16)
-    far_grads = grid.swap_far(tie(far_grads, arrived[-1]))
-    own_grads = total_of(far_grads).astype(BF16)
-
-    lag_share = copies(grid, gather_near(grid, lag_share.astype(BF16)))
-    spread = grid.swap_far(tie(lag_share, far_grads))
-    spread = gather_rows(spread.reshape(grid.size * lag_count, -1, width))
+    own_grads = reduce_filt(grid, grads, last_bits[1:]).astype(BF16)
+
+    spread = gather_filt(grid, lag_share.astype(BF16))
+    spread = (
+        spread.reshape(grid.near, 2, 2, lag_count, lag_rows, width)
+        .transpose(2, 0, 3, 1, 4, 5)
+        .reshape(2 * grid.near * lag_count, 2 * lag_rows, width)
+    )
     regression_grad = (
-        spread.reshape(grid.size, lag_count, slab, width)
+        gather_rows(spread)
+        .reshape(2 * grid.near, lag_count, slab, width)
         .transpose(1, 0, 2, 3)
         .reshape(lag_count, width, width)
         .astype(F32)
@@ -798,7 +914,6 @@
         )
 
     full = spread_rows(own_grads)
-    row_index = lax.axis_index("rows")
     ordered = jnp.zeros((row_count, 3, share, width), BF16)
     for n, mask in enumerate(row_masks()):
         ordered = lax.dynamic_update_slice_in_dim(ordered, full[n][None], row_index ^ mask, 0)

time: 452 us -> 427 us (0.945)
  waiting for transfers between devices: 143 us -> 103 us
  Pallas kernels: 131 us -> 145 us
  other arithmetic: 51.4 us -> 63.5 us
  starting transfers between devices: 82.2 us -> 70.3 us
    all_to_all x11 -> x0, waiting for transfers between devices: 72.2 us -> none  [swap_far(): lax.all_to_all(values, 'filt', 0, 0, axis_index_groups=groups, tiled=True)]
    ppermute x1 -> x29, waiting for transfers between devices: 0.01 us -> 70.1 us  [the longest x28 70.1 us: swap(): lax.ppermute(values, 'filt', [(f, f ^ bit) for f in range(self.size)])]
    all_to_all x11 -> x0, starting transfers between devices: 50.8 us -> none  [swap_far(): lax.all_to_all(values, 'filt', 0, 0, axis_index_groups=groups, tiled=True)]
    ppermute x1 -> x29, starting transfers between devices: 2.41 us -> 39.3 us  [the longest x28 35.9 us: swap(): lax.ppermute(values, 'filt', [(f, f ^ bit) for f in range(self.size)])]
    ppermute x11 -> x8, waiting for transfers between devices: 35.8 us -> 11.6 us  [near_swaps(): lax.ppermute(values[j] if isinstance(values, list) else values, 'filt', g...]
    select_n x0 -> x26, other arithmetic: none -> 19.5 us  [the longest x21 14.2 us: join(): jnp.where(self.flag(bit), jnp.stack([other, own]), jnp.stack([own, other]))]
    ppermute x15 -> x21, waiting for transfers between devices: 27.7 us -> 13.5 us  [swap_rows(): return lax.ppermute(values, 'rows', [(r, r ^ bit) for r in range(count)])]
    convert_element_type x11 -> x19, other arithmetic: 16.1 us -> 8.14 us  [the longest x1 1.98 us: shards(): away = total_of(away).astype(BF16)]
  transfers between devices with their start and end apart: 44 -> 64, of which waited for: 16 -> 27; matrix products, arithmetic and copies ran while one was open for 16% -> 19% of each run, Pallas kernels for 29% -> 34%
where the time goes in v4:
time: 427 us; the launch traced here: 422 us
  Pallas kernels  145 us (34%)
  waiting for transfers between devices  103 us (24%)
  starting transfers between devices  70.3 us (16%)
  other arithmetic  63.5 us (15%)
  local copies, waits for them, and re-layouts  36.5 us (9%)
    ppermute x28, waiting for transfers between devices, swap(): lax.ppermute(values, 'filt', [(f, f ^ bit) for f in range(self.size)])  70.1 us
    pallas_call x2, Pallas kernels, mix_sequences_back(): pl.pallas_call(functools.partial(mix_back_kernel, parts), grid_spec=pltpu...  45 us
    ppermute x28, starting transfers between devices, swap(): lax.ppermute(values, 'filt', [(f, f ^ bit) for f in range(self.size)])  35.9 us
    pallas_call x2, Pallas kernels, mix_sequences(): pl.pallas_call(functools.partial(mix_kernel, parts), grid_spec=pltpu.Pref...  34.1 us
    pallas_call x2, Pallas kernels, mixing_products(): pl.pallas_call(mixing_kernel, grid_spec=pltpu.PrefetchScalarGridSpec(num_...  25.7 us
    pallas_call x2, Pallas kernels, feed_forward(): pl.pallas_call(functools.partial(feed_forward_kernel, shares, len(flat_sa...  24.7 us
    pallas_call x1, Pallas kernels, toeplitz_blocks(): pl.pallas_call(functools.partial(toeplitz_kernel, half, count), grid=(4 *...  15.4 us
    select_n x21, other arithmetic, join(): jnp.where(self.flag(bit), jnp.stack([other, own]), jnp.stack([own, other]))  14.2 us
  transfers between devices with their start and end apart: 64, of which 27 were waited for; matrix products, arithmetic and copies ran while one was open for 19% of the time, Pallas kernels for 34%

profile of v4, /device:TPU:0, one launch (start us, length us, event | category | flops | bytes accessed | tf_op | source)
XLA Modules:
  0.0 422.0 jit_solution(189112208750697125)
XLA Ops:
  3.8 4.1 collective-permute-start
  17.0 3.1 collective-permute-done.1
  29.4 3.4 collective-permute-start.4
  37.6 15.4 %toeplitz.1 = (bf16[2,256,3072]{2,1,0:T(8,128)(2,1)}, bf16[2,256,3072]{2,1,0:T(8,128)(2,1)}, bf16[2,3072,256]{2,1,0:T(8,128)(2,1)}, bf16[2,3072,256]{2,1,0:T(8,128)(2,1)}) custom-call(f32[12,1,1024]{2,1,0:T(1,128)} %pad_convert_fusion.up_ref), custom_call_target="tpu_custom_call" | custom-call | bytes 100663296 | tf_op jit(solution)/shard_map/toeplitz/pallas_call | solution.py:185
  63.2 6.6 %collective-permute-done.7 = bf16[2,3,64,512]{3,2,1,0:T(8,128)(2,1)S(1)} collective-permute-done((bf16[2,3,64,512]{3,2,1,0:T(8,128)(2,1)S(1)}, bf16[2,3,64,512]{3,2,1,0:T(8,128)(2,1)S(1)}, u32[]{:S(2)}, u32[]{:S(2)}) %collective-permute-start.7) | collective-permute-done | bytes 393248 | tf_op jit(solution)/shard_map/ppermute | solution.py:55
  70.9 3.4 collective-permute-done.8.refs_1_
  75.1 7.5 %collective-permute-done.9.refs_1_ = bf16[4,1,2,64,512]{4,3,2,1,0:T(8,128)(2,1)S(1)} collective-permute-done((bf16[4,1,2,64,512]{4,3,2,1,0:T(8,128)(2,1)S(1)}, bf16[4,1,2,64,512]{4,3,2,1,0:T(8,128)(2,1)S(1)}, u32[]{:S(2)}, u32[]{:S(2)}) %collective-permute-start.9) | collective-permute-done | bytes 524320 | tf_op jit(solution)/shard_map/ppermute | solution.py:96
  86.2 3.4 pad_maximum_fusion.refs_2_.sum_ref.rest_ref
  96.6 16.5 %mix.2 = (bf16[4,1,2,64,512]{4,3,2,1,0:T(8,128)(2,1)S(1)}, bf16[4,1,2,64,512]{4,3,2,1,0:T(8,128)(2,1)S(1)}, bf16[2,512,1024]{2,1,0:T(8,128)(2,1)S(1)}) custom-call(s32[1]{0:T(128)} %bitcast.near_ref, bf16[4,1,2,64,512]{4,3,2,1,0:T(8,128)(2,1)S(1)} %bitcast.318, bf16[4,1,2,64,512]{4,3,2,1,0:T(8,128)(2,1)S(1)} %copy-done.4, ...), custom_call_target="tpu_custom_call" | custom-call | flops 11274289152 | bytes 14680064 | tf_op jit(solution)/shard_map/mix/pallas_call | solution.py:422
  115.6 17.6 %mix.3 = (bf16[4,1,2,64,512]{4,3,2,1,0:T(8,128)(2,1)S(1)}, bf16[4,1,2,64,512]{4,3,2,1,0:T(8,128)(2,1)}, bf16[2,512,1024]{2,1,0:T(8,128)(2,1)S(1)}) custom-call(s32[1]{0:T(128)} %bitcast.near_ref, bf16[4,1,2,64,512]{4,3,2,1,0:T(8,128)(2,1)S(1)} %bitcast.316, bf16[4,1,2,64,512]{4,3,2,1,0:T(8,128)(2,1)S(1)} %copy-done.2, ...), custom_call_target="tpu_custom_call", output_to_operand_aliasing={{2}: (7, {})} | custom-call | flops 11274289152 | bytes 14680064 | tf_op jit(solution)/shard_map/mix/pallas_call | solution.py:422
  136.5 11.4 %collective-permute-done.13 = bf16[2,1,2,64,512]{4,3,2,1,0:T(8,128)(2,1)S(1)} collective-permute-done((bf16[2,1,2,64,512]{4,3,2,1,0:T(8,128)(2,1)S(1)}, bf16[2,1,2,64,512]{4,3,2,1,0:T(8,128)(2,1)S(1)}, u32[]{:S(2)}, u32[]{:S(2)}) %collective-permute-start.13) | collective-permute-done | bytes 262176 | tf_op jit(solution)/shard_map/ppermute | solution.py:55
  147.9 3.8 collective-permute-done.17.refs_1_
  156.0 4.7 %copy.201 = bf16[6,512,512]{2,1,0:T(8,128)(2,1)} copy(bf16[6,512,512]{1,2,0:T(8,128)(2,1)} %bitcast.319) | data formatting | bytes 6291456 | tf_op jit(solution)/shard_map/transpose | solution.py:715
  160.7 5.1 %copy.202 = bf16[6,512,512]{2,1,0:T(8,128)(2,1)} copy(bf16[6,512,512]{1,2,0:T(8,128)(2,1)} %bitcast.320) | data formatting | bytes 6291456 | tf_op jit(solution)/shard_map/transpose | solution.py:715
  169.9 9.6 %feed_forward.2 = (bf16[2,2,64,512]{3,2,1,0:T(8,128)(2,1)}, f32[2,2,64,512]{3,2,1,0:T(8,128)}, bf16[1,2,2,64,512]{4,3,2,1,0:T(8,128)(2,1)}, f32[1,512]{1,0:T(1,1...) custom-call(bf16[1,2,2,64,512]{4,3,2,1,0:T(8,128)(2,1)} %bitcast.381, ...), custom_call_target="tpu_custom_call" | custom-call | flops 3221225472 | bytes 11534336 | tf_op jit(solution)/shard_map/feed_forward/pallas_call | solution.py:542
  184.2 3.5 collective-permute-done.22
  190.1 15.1 %feed_forward.3 = (bf16[2,2,64,512]{3,2,1,0:T(8,128)(2,1)}, f32[2,2,64,512]{3,2,1,0:T(8,128)}, bf16[1,2,2,64,512]{4,3,2,1,0:T(8,128)(2,1)}, f32[1,512]{1,0:T(1,1...) custom-call(bf16[1,2,2,64,512]{4,3,2,1,0:T(8,128)(2,1)} %bitcast.382, ...), custom_call_target="tpu_custom_call" | custom-call | flops 6442450944 | bytes 11534336 | tf_op jit(solution)/shard_map/feed_forward/pallas_call | solution.py:542
  219.6 9.1 %collective-permute-done.25 = bf16[2,1,2,64,512]{4,3,2,0,1:T(8,128)(2,1)} collective-permute-done((bf16[2,1,2,64,512]{4,3,2,0,1:T(8,128)(2,1)}, bf16[2,1,2,64,512]{4,3,2,0,1:T(8,128)(2,1)}, u32[]{:S(2)}, u32[]{:S(2)}) %collective-permute-start.25) | collective-permute-done | bytes 262176 | tf_op jit(solution)/shard_map/ppermute | solution.py:55
  235.6 22.4 %mix_back.2 = (bf16[4,1,2,64,512]{4,3,2,1,0:T(8,128)(2,1)}, bf16[4,1,2,64,512]{4,3,2,1,0:T(8,128)(2,1)}, bf16[2,1024,6144]{2,1,0:T(8,128)(2,1)}, f32[3,128,512]{2,1,0:T(8,128)}) custom-call(s32[1]{0:T(128)} %bitcast.near_ref, s32[1]{0:T(128)} %bitcast.55.own_ref, bf16[4,1,2,64,512]{4,3,2,1,0:T(8,128)(2,1)} %bitcast.73.refs_0_, ...), custom_call_target="tpu_custom_call" | custom-call | flops 11274289152 | bytes 14680064 | tf_op jit(solution)/shard_map/mix_back/pallas_call | solution.py:462
  258.9 22.6 %mix_back.3 = (bf16[4,1,2,64,512]{4,3,2,1,0:T(8,128)(2,1)}, bf16[4,1,2,64,512]{4,3,2,1,0:T(8,128)(2,1)}, bf16[2,1024,6144]{2,1,0:T(8,128)(2,1)}, f32[3,128,512]{2,1,0:T(8,128)}) custom-call(s32[1]{0:T(128)} %bitcast.near_ref, s32[1]{0:T(128)} %bitcast.55.own_ref, bf16[4,1,2,64,512]{4,3,2,1,0:T(8,128)(2,1)} %bitcast.371, ...), custom_call_target="tpu_custom_call", output_to_operand_aliasing={{2}: (9, {})} | custom-call | flops 11274289152 | bytes 14680064 | tf_op jit(solution)/shard_map/mix_back/pallas_call | solution.py:462
  285.5 13.1 %mixing_products.2 = (f32[6,256,512]{2,1,0:T(8,128)}, bf16[6,256,512]{2,1,0:T(8,128)(2,1)}, f32[512,1]{1,0:T(8,128)}) custom-call(s32[1]{0:T(128)} %bitcast.83.bit_ref, bf16[2,512,1024]{2,1,0:T(8,128)(2,1)} %copy-done, bf16[2,1024,6144]{2,1,0:T(8,128)(2,1)} %get-tuple-element.225.plus_ref.minus_ref, ...), custom_call_target="tpu_custom_call" | custom-call | flops 6442450944 | bytes 20971520 | tf_op jit(solution)/shard_map/mixing_products/pallas_call | solution.py:503
  302.3 3.6 broadcast_select_fusion.6
  309.6 12.5 %mixing_products.3 = (f32[6,256,512]{2,1,0:T(8,128)}, bf16[6,256,512]{2,1,0:T(8,128)(2,1)}, f32[512,1]{1,0:T(8,128)}) custom-call(s32[1]{0:T(128)} %bitcast.83.bit_ref, bf16[2,512,1024]{2,1,0:T(8,128)(2,1)} %copy-done, bf16[2,1024,6144]{2,1,0:T(8,128)(2,1)} %get-tuple-element.225.plus_ref.minus_ref, ...), custom_call_target="tpu_custom_call" | custom-call | flops 6442450944 | bytes 20971520 | tf_op jit(solution)/shard_map/mixing_products/pallas_call | solution.py:503
  323.8 3.8 collective-permute-done.40
  338.7 10.2 %collective-permute-done.43 = bf16[2,2,3,64,512]{4,3,2,1,0:T(8,128)(2,1)S(1)} collective-permute-done((bf16[2,2,3,64,512]{4,3,2,1,0:T(8,128)(2,1)}, bf16[2,2,3,64,512]{4,3,2,1,0:T(8,128)(2,1)S(1)}, u32[]{:S(2)}, u32[]{:S(2)}) %collective-permute-start.43) | collective-permute-done | bytes 786464 | tf_op jit(solution)/shard_map/ppermute | solution.py:55
  349.3 3.9 collective-permute-done.46
  375.7 3.5 collective-permute-done.57
  384.1 4.5 %collective-permute-done.52 = bf16[2,2,3,16,512]{4,3,2,1,0:T(8,128)(2,1)S(1)} collective-permute-done((bf16[2,2,3,16,512]{4,3,2,1,0:T(8,128)(2,1)S(1)}, bf16[2,2,3,16,512]{4,3,2,1,0:T(8,128)(2,1)S(1)}, u32[]{:S(2)}, u32[]{:S(2)}) %collective-permute-start.52) | collective-permute-done | bytes 196640 | tf_op jit(solution)/shard_map/ppermute | solution.py:55
  389.6 3.4 collective-permute-start.61
  393.6 7.4 %collective-permute-done.61 = bf16[3,64,512]{2,1,0:T(8,128)(2,1)S(1)} collective-permute-done((bf16[3,64,512]{2,1,0:T(8,128)(2,1)S(1)}, bf16[3,64,512]{2,1,0:T(8,128)(2,1)S(1)}, u32[]{:S(2)}, u32[]{:S(2)}) %collective-permute-start.61) | collective-permute-done | bytes 196640 | tf_op jit(solution)/shard_map/ppermute | solution.py:55
  403.8 3.2 collective-permute-done.62
  418.3 3.6 maximum_convert_fusion
  (349 shorter events, 158.6 us)
Async XLA Ops:
  3.8 20.3 %collective-permute-start = (bf16[3,64,512]{2,1,0:T(8,128)(2,1)S(1)}, bf16[3,64,512]{2,1,0:T(8,128)(2,1)}, u32[]{:S(2)}, u32[]{:S(2)}) collective-permute-start(bf16[3,64,512]{2,1,0:T(8,128)(2,1)S(1)} %bitcast.359), channel_id=1, source_target_pairs={{0,4},{1,5},{2,6},{3,7},{4,0},{5,1},{6,2},{7,3},{8,12},{9,13},{10,... | collective-permute-start | bytes 589832 | tf_op jit(solution)/shard_map/ppermute | solution.py:55
  25.3 30.4 %collective-permute-start.3 = (bf16[6,128,512]{2,1,0:T(8,128)(2,1)}, bf16[6,128,512]{2,1,0:T(8,128)(2,1)}, u32[]{:S(2)}, u32[]{:S(2)}) collective-permute-start(bf16[6,128,512]{2,1,0:T(8,128)(2,1)} %fusion.8), channel_id=1, source_target_pairs={{0,2},{1,3},{2,0},{3,1},{4,6},{5,7},{6,4},{7,5},{8,10},{9,11},{10,... | collective-permute-start | bytes 2359304 | tf_op jit(solution)/shard_map/ppermute | solution.py:55
  26.3 26.7 %collective-permute-start.5 = (bf16[2,1,2,64,512]{4,3,2,0,1:T(8,128)(2,1)S(1)}, bf16[2,1,2,64,512]{4,3,2,0,1:T(8,128)(2,1)}, u32[]{:S(2)}, u32[]{:S(2)}) collective-permute-start(bf16[2,1,2,64,512]{4,3,2,0,1:T(8,128)(2,1)S(1)} %maximum_select_fusion.6), channel_id=1, source_target_pairs={{0,4},{1,5},{2,6},{3,7},{4,0},{5,1},{6,2},{7,3},{8,12},{9,13},{10,... | collective-permute-start | bytes 786440 | tf_op jit(solution)/shard_map/ppermute | solution.py:55
  29.3 24.0 %collective-permute-start.6 = (bf16[2,1,2,64,512]{4,3,2,0,1:T(8,128)(2,1)S(1)}, bf16[2,1,2,64,512]{4,3,2,0,1:T(8,128)(2,1)S(1)}, u32[]{:S(2)}, u32[]{:S(2)}) collective-permute-start(bf16[2,1,2,64,512]{4,3,2,0,1:T(8,128)(2,1)S(1)} %maximum_select_fusion.7), channel_id=1, source_target_pairs={{0,4},{1,5},{2,6},{3,7},{4,0},{5,1},{6,2},{7,3},{8,12},{9,13},{10,... | collective-permute-start | bytes 786440 | tf_op jit(solution)/shard_map/ppermute | solution.py:55
  29.4 23.6 %collective-permute-start.4 = (bf16[4,2,1,512]{3,2,1,0:T(2,128)(2,1)S(1)}, bf16[4,2,1,512]{3,2,1,0:T(2,128)(2,1)S(1)}, u32[]{:S(2)}, u32[]{:S(2)}) collective-permute-start(bf16[4,2,1,512]{3,2,1,0:T(2,128)(2,1)S(1)} %slice.379), channel_id=1, source_target_pairs={{0,1},{1,2},{2,3},{3,4},{4,5},{5,6},{6,7},{8,9},{9,10},{10,11},{11... | collective-permute-start | bytes 24584 | tf_op jit(solution)/shard_map/ppermute | solution.py:663
  55.7 27.8 %collective-permute-start.10 = (bf16[6,128,512]{2,1,0:T(8,128)(2,1)}, bf16[6,128,512]{2,1,0:T(8,128)(2,1)S(1)}, u32[]{:S(2)}, u32[]{:S(2)}) collective-permute-start(bf16[6,128,512]{2,1,0:T(8,128)(2,1)} %collective-permute-done.3), channel_id=1, source_target_pairs={{0,16},{8,24},{16,0},{24,8},{1,17},{9,25},{17,1},{25,9},{2,18},{10... | collective-permute-start | bytes 2359304 | tf_op jit(solution)/shard_map/ppermute | solution.py:112
  61.5 21.2 %collective-permute-start.9 = (bf16[4,1,2,64,512]{4,3,2,1,0:T(8,128)(2,1)S(1)}, bf16[4,1,2,64,512]{4,3,2,1,0:T(8,128)(2,1)S(1)}, u32[]{:S(2)}, u32[]{:S(2)}) collective-permute-start(bf16[4,1,2,64,512]{4,3,2,1,0:T(8,128)(2,1)S(1)} %bitcast.315), channel_id=1, source_target_pairs={{0,1},{1,0},{2,3},{3,2},{4,5},{5,4},{6,7},{7,6},{8,9},{9,8},{10,11... | collective-permute-start | bytes 1572872 | tf_op jit(solution)/shard_map/ppermute | solution.py:96
  90.9 22.8 %collective-permute-start.16 = (bf16[2,2,3,64,512]{4,3,2,1,0:T(8,128)(2,1)S(1)}, bf16[2,2,3,64,512]{4,3,2,1,0:T(8,128)(2,1)S(1)}, u32[]{:S(2)}, u32[]{:S(2)}) collective-permute-start(bf16[2,2,3,64,512]{4,3,2,1,0:T(8,128)(2,1)S(1)} %copy-done.22), channel_id=1, source_target_pairs={{0,1},{1,0},{2,3},{3,2},{4,5},{5,4},{6,7},{7,6},{8,9},{9,8},{10,11... | collective-permute-start | bytes 2359304 | tf_op jit(solution)/shard_map/ppermute | solution.py:55
  113.1 20.1 %collective-permute-start.12 = (bf16[4,1,2,64,512]{4,3,2,1,0:T(8,128)(2,1)S(1)}, bf16[4,1,2,64,512]{4,3,2,1,0:T(8,128)(2,1)S(1)}, u32[]{:S(2)}, u32[]{:S(2)}) collective-permute-start(bf16[4,1,2,64,512]{4,3,2,1,0:T(8,128)(2,1)S(1)} %get-tuple-element.147), channel_id=1, source_target_pairs={{0,1},{1,0},{2,3},{3,2},{4,5},{5,4},{6,7},{7,6},{8,9},{9,8},{10,11... | collective-permute-start | bytes 1572872 | tf_op jit(solution)/shard_map/ppermute | solution.py:96
  115.2 36.6 %collective-permute-start.17 = (bf16[8,3,64,512]{3,2,1,0:T(8,128)(2,1)}, bf16[8,3,64,512]{3,2,1,0:T(8,128)(2,1)}, u32[]{:S(2)}, u32[]{:S(2)}) collective-permute-start(bf16[8,3,64,512]{3,2,1,0:T(8,128)(2,1)} %bitcast.46.refs_0_), channel_id=1, source_target_pairs={{0,16},{8,24},{16,0},{24,8},{1,17},{9,25},{17,1},{25,9},{2,18},{10... | collective-permute-start | bytes 4718600 | tf_op jit(solution)/shard_map/ppermute | solution.py:112
  136.5 32.3 %collective-permute-start.18 = (bf16[8,3,64,512]{3,2,1,0:T(8,128)(2,1)}, bf16[8,3,64,512]{3,2,1,0:T(8,128)(2,1)S(1)}, u32[]{:S(2)}, u32[]{:S(2)}) collective-permute-start(bf16[8,3,64,512]{3,2,1,0:T(8,128)(2,1)} %bitcast.46.refs_0_), channel_id=1, source_target_pairs={{0,8},{8,0},{16,24},{24,16},{1,9},{9,1},{17,25},{25,17},{2,10},{10... | collective-permute-start | bytes 4718600 | tf_op jit(solution)/shard_map/ppermute | solution.py:112
  151.7 17.1 %collective-permute-start.19 = (bf16[8,3,64,512]{3,2,1,0:T(8,128)(2,1)}, bf16[8,3,64,512]{3,2,1,0:T(8,128)(2,1)}, u32[]{:S(2)}, u32[]{:S(2)}) collective-permute-start(bf16[8,3,64,512]{3,2,1,0:T(8,128)(2,1)} %collective-permute-done.17.refs_1_), channel_id=1, source_target_pairs={{0,8},{8,0},{16,24},{24,16},{1,9},{9,1},{17,25},{25,17},{2,10},{10... | collective-permute-start | bytes 4718600 | tf_op jit(solution)/shard_map/ppermute | solution.py:112
  187.8 17.4 %collective-permute-start.23 = (bf16[2,1,2,64,512]{4,3,2,0,1:T(8,128)(2,1)S(1)}, bf16[2,1,2,64,512]{4,3,2,0,1:T(8,128)(2,1)S(1)}, u32[]{:S(2)}, u32[]{:S(2)}) collective-permute-start(bf16[2,1,2,64,512]{4,3,2,0,1:T(8,128)(2,1)S(1)} %fusion.29), channel_id=1, source_target_pairs={{0,4},{1,5},{2,6},{3,7},{4,0},{5,1},{6,2},{7,3},{8,12},{9,13},{10,... | collective-permute-start | bytes 786440 | tf_op jit(solution)/shard_map/ppermute | solution.py:55
  205.2 26.2 %collective-permute-start.28 = (bf16[8,3,64,512]{3,2,1,0:T(8,128)(2,1)}, bf16[8,3,64,512]{3,2,1,0:T(8,128)(2,1)}, u32[]{:S(2)}, u32[]{:S(2)}) collective-permute-start(bf16[8,3,64,512]{3,2,1,0:T(8,128)(2,1)} %get-tuple-element.184), channel_id=1, source_target_pairs={{0,8},{8,0},{16,24},{24,16},{1,9},{9,1},{17,25},{25,17},{2,10},{10... | collective-permute-start | bytes 4718600 | tf_op jit(solution)/shard_map/ppermute | solution.py:112
  205.3 26.2 %collective-permute-start.29 = (bf16[8,3,64,512]{3,2,1,0:T(8,128)(2,1)}, bf16[8,3,64,512]{3,2,1,0:T(8,128)(2,1)}, u32[]{:S(2)}, u32[]{:S(2)}) collective-permute-start(bf16[8,3,64,512]{3,2,1,0:T(8,128)(2,1)} %get-tuple-element.185), channel_id=1, source_target_pairs={{0,8},{8,0},{16,24},{24,16},{1,9},{9,1},{17,25},{25,17},{2,10},{10... | collective-permute-start | bytes 4718600 | tf_op jit(solution)/shard_map/ppermute | solution.py:112
  210.4 21.1 %collective-permute-start.30 = (bf16[4,1,2,64,512]{4,3,2,1,0:T(8,128)(2,1)}, bf16[4,1,2,64,512]{4,3,2,1,0:T(8,128)(2,1)}, u32[]{:S(2)}, u32[]{:S(2)}) collective-permute-start(bf16[4,1,2,64,512]{4,3,2,1,0:T(8,128)(2,1)} %bitcast.72), channel_id=1, source_target_pairs={{0,1},{1,0},{2,3},{3,2},{4,5},{5,4},{6,7},{7,6},{8,9},{9,8},{10,11... | collective-permute-start | bytes 1572872 | tf_op jit(solution)/shard_map/ppermute | solution.py:96
  217.1 18.5 %collective-permute-start.27 = (bf16[4,2,1,512]{3,2,1,0:T(2,128)(2,1)S(1)}, bf16[4,2,1,512]{3,2,1,0:T(2,128)(2,1)S(1)}, u32[]{:S(2)}, u32[]{:S(2)}) collective-permute-start(bf16[4,2,1,512]{3,2,1,0:T(2,128)(2,1)S(1)} %fusion.44), channel_id=1, source_target_pairs={{1,0},{2,1},{3,2},{4,3},{5,4},{6,5},{7,6},{9,8},{10,9},{11,10},{12... | collective-permute-start | bytes 24584 | tf_op jit(solution)/shard_map/ppermute | solution.py:768
  229.9 28.2 %collective-permute-start.26 = (bf16[4,1,2,64,512]{4,3,2,1,0:T(8,128)(2,1)S(1)}, bf16[4,1,2,64,512]{4,3,2,1,0:T(8,128)(2,1)S(1)}, u32[]{:S(2)}, u32[]{:S(2)}) collective-permute-start(bf16[4,1,2,64,512]{4,3,2,1,0:T(8,128)(2,1)S(1)} %bitcast.370), channel_id=1, source_target_pairs={{0,1},{1,0},{2,3},{3,2},{4,5},{5,4},{6,7},{7,6},{8,9},{9,8},{10,11... | collective-permute-start | bytes 1572872 | tf_op jit(solution)/shard_map/ppermute | solution.py:96
  233.6 24.6 %collective-permute-start.31 = (bf16[4,3,64,512]{3,2,1,0:T(8,128)(2,1)S(1)}, bf16[4,3,64,512]{3,2,1,0:T(8,128)(2,1)S(1)}, u32[]{:S(2)}, u32[]{:S(2)}) collective-permute-start(bf16[4,3,64,512]{3,2,1,0:T(8,128)(2,1)S(1)} %get-tuple-element.307), channel_id=1, source_target_pairs={{0,16},{8,24},{16,0},{24,8},{1,17},{9,25},{17,1},{25,9},{2,18},{10... | collective-permute-start | bytes 2359304 | tf_op jit(solution)/shard_map/ppermute | solution.py:112
  234.2 47.3 %collective-permute-start.33 = (bf16[4,3,64,512]{3,2,1,0:T(8,128)(2,1)S(1)}, bf16[4,3,64,512]{3,2,1,0:T(8,128)(2,1)S(1)}, u32[]{:S(2)}, u32[]{:S(2)}) collective-permute-start(bf16[4,3,64,512]{3,2,1,0:T(8,128)(2,1)S(1)} %get-tuple-element.306), channel_id=1, source_target_pairs={{0,16},{8,24},{16,0},{24,8},{1,17},{9,25},{17,1},{25,9},{2,18},{10... | collective-permute-start | bytes 2359304 | tf_op jit(solution)/shard_map/ppermute | solution.py:112
  258.1 23.4 %collective-permute-start.32 = (bf16[4,1,2,64,512]{4,3,2,1,0:T(8,128)(2,1)}, bf16[4,1,2,64,512]{4,3,2,1,0:T(8,128)(2,1)S(1)}, u32[]{:S(2)}, u32[]{:S(2)}) collective-permute-start(bf16[4,1,2,64,512]{4,3,2,1,0:T(8,128)(2,1)} %get-tuple-element.202), channel_id=1, source_target_pairs={{0,1},{1,0},{2,3},{3,2},{4,5},{5,4},{6,7},{7,6},{8,9},{9,8},{10,11... | collective-permute-start | bytes 1572872 | tf_op jit(solution)/shard_map/ppermute | solution.py:96
  282.7 15.9 %collective-permute-start.36 = (bf16[2,1,2,64,512]{4,3,2,1,0:T(8,128)(2,1)S(1)}, bf16[2,1,2,64,512]{4,3,2,1,0:T(8,128)(2,1)S(1)}, u32[]{:S(2)}, u32[]{:S(2)}) collective-permute-start(bf16[2,1,2,64,512]{4,3,2,1,0:T(8,128)(2,1)S(1)} %select_convert_fusion.5), channel_id=1, source_target_pairs={{0,4},{1,5},{2,6},{3,7},{4,0},{5,1},{6,2},{7,3},{8,12},{9,13},{10,... | collective-permute-start | bytes 786440 | tf_op jit(solution)/shard_map/ppermute | solution.py:55
  282.8 23.9 %collective-permute-start.39 = (bf16[4,1,2,64,512]{4,3,2,1,0:T(8,128)(2,1)}, bf16[4,1,2,64,512]{4,3,2,1,0:T(8,128)(2,1)S(1)}, u32[]{:S(2)}, u32[]{:S(2)}) collective-permute-start(bf16[4,1,2,64,512]{4,3,2,1,0:T(8,128)(2,1)} %get-tuple-element.223), channel_id=1, source_target_pairs={{0,1},{1,0},{2,3},{3,2},{4,5},{5,4},{6,7},{7,6},{8,9},{9,8},{10,11... | collective-permute-start | bytes 1572872 | tf_op jit(solution)/shard_map/ppermute | solution.py:96
  285.0 21.0 %collective-permute-start.35 = (bf16[3,32,512]{2,1,0:T(8,128)(2,1)}, bf16[3,32,512]{2,1,0:T(8,128)(2,1)S(1)}, u32[]{:S(2)}, u32[]{:S(2)}) collective-permute-start(bf16[3,32,512]{2,1,0:T(8,128)(2,1)} %fusion.36), channel_id=1, source_target_pairs={{0,16},{8,24},{16,0},{24,8},{1,17},{9,25},{17,1},{25,9},{2,18},{10... | collective-permute-start | bytes 294920 | tf_op jit(solution)/shard_map/ppermute | solution.py:112
  299.6 22.5 %collective-permute-start.41 = (bf16[1,2,64,512]{3,2,1,0:T(8,128)(2,1)}, bf16[1,2,64,512]{3,2,1,0:T(8,128)(2,1)S(1)}, u32[]{:S(2)}, u32[]{:S(2)}) collective-permute-start(bf16[1,2,64,512]{3,2,1,0:T(8,128)(2,1)} %get-tuple-element.330), channel_id=1, source_target_pairs={{0,2},{1,3},{2,0},{3,1},{4,6},{5,7},{6,4},{7,5},{8,10},{9,11},{10,... | collective-permute-start | bytes 393224 | tf_op jit(solution)/shard_map/ppermute | solution.py:55
  307.8 19.8 %collective-permute-start.40 = (bf16[6,128,512]{2,1,0:T(8,128)(2,1)S(1)}, bf16[6,128,512]{2,1,0:T(8,128)(2,1)}, u32[]{:S(2)}, u32[]{:S(2)}) collective-permute-start(bf16[6,128,512]{2,1,0:T(8,128)(2,1)S(1)} %fusion.6), channel_id=1, source_target_pairs={{0,16},{8,24},{16,0},{24,8},{1,17},{9,25},{17,1},{25,9},{2,18},{10... | collective-permute-start | bytes 2359304 | tf_op jit(solution)/shard_map/ppermute | solution.py:112
  328.8 20.2 %collective-permute-start.43 = (bf16[2,2,3,64,512]{4,3,2,1,0:T(8,128)(2,1)}, bf16[2,2,3,64,512]{4,3,2,1,0:T(8,128)(2,1)S(1)}, u32[]{:S(2)}, u32[]{:S(2)}) collective-permute-start(bf16[2,2,3,64,512]{4,3,2,1,0:T(8,128)(2,1)} %bitcast.358), channel_id=1, source_target_pairs={{0,1},{1,0},{2,3},{3,2},{4,5},{5,4},{6,7},{7,6},{8,9},{9,8},{10,11... | collective-permute-start | bytes 2359304 | tf_op jit(solution)/shard_map/ppermute | solution.py:55
  332.7 20.5 %collective-permute-start.46 = (bf16[6,128,512]{2,1,0:T(8,128)(2,1)S(1)}, bf16[6,128,512]{2,1,0:T(8,128)(2,1)S(1)}, u32[]{:S(2)}, u32[]{:S(2)}) collective-permute-start(bf16[6,128,512]{2,1,0:T(8,128)(2,1)S(1)} %fusion.2), channel_id=1, source_target_pairs={{0,2},{1,3},{2,0},{3,1},{4,6},{5,7},{6,4},{7,5},{8,10},{9,11},{10,... | collective-permute-start | bytes 2359304 | tf_op jit(solution)/shard_map/ppermute | solution.py:55
  336.8 19.1 %collective-permute-start.45 = (bf16[6,128,512]{2,1,0:T(8,128)(2,1)S(1)}, bf16[6,128,512]{2,1,0:T(8,128)(2,1)S(1)}, u32[]{:S(2)}, u32[]{:S(2)}) collective-permute-start(bf16[6,128,512]{2,1,0:T(8,128)(2,1)S(1)} %fusion.7), channel_id=1, source_target_pairs={{0,16},{8,24},{16,0},{24,8},{1,17},{9,25},{17,1},{25,9},{2,18},{10... | collective-permute-start | bytes 2359304 | tf_op jit(solution)/shard_map/ppermute | solution.py:112
  338.4 21.3 %collective-permute-start.47 = (bf16[1,2,64,512]{3,2,1,0:T(8,128)(2,1)S(1)}, bf16[1,2,64,512]{3,2,1,0:T(8,128)(2,1)S(1)}, u32[]{:S(2)}, u32[]{:S(2)}) collective-permute-start(bf16[1,2,64,512]{3,2,1,0:T(8,128)(2,1)S(1)} %get-tuple-element.328), channel_id=1, source_target_pairs={{0,2},{1,3},{2,0},{3,1},{4,6},{5,7},{6,4},{7,5},{8,10},{9,11},{10,... | collective-permute-start | bytes 393224 | tf_op jit(solution)/shard_map/ppermute | solution.py:55
  356.6 50.5 %collective-permute-start.48 = (bf16[6,128,512]{2,1,0:T(8,128)(2,1)S(1)}, bf16[6,128,512]{2,1,0:T(8,128)(2,1)S(1)}, u32[]{:S(2)}, u32[]{:S(2)}) collective-permute-start(bf16[6,128,512]{2,1,0:T(8,128)(2,1)S(1)} %fusion.4), channel_id=1, source_target_pairs={{0,16},{8,24},{16,0},{24,8},{1,17},{9,25},{17,1},{25,9},{2,18},{10... | collective-permute-start | bytes 2359304 | tf_op jit(solution)/shard_map/ppermute | solution.py:112
  370.0 19.4 %collective-permute-start.60 = (bf16[2,3,64,512]{3,2,1,0:T(8,128)(2,1)S(1)}, bf16[2,3,64,512]{3,2,1,0:T(8,128)(2,1)S(1)}, u32[]{:S(2)}, u32[]{:S(2)}) collective-permute-start(bf16[2,3,64,512]{3,2,1,0:T(8,128)(2,1)S(1)} %fusion.25), channel_id=1, source_target_pairs={{0,2},{1,3},{2,0},{3,1},{4,6},{5,7},{6,4},{7,5},{8,10},{9,11},{10,... | collective-permute-start | bytes 1179656 | tf_op jit(solution)/shard_map/ppermute | solution.py:55
  (83 other events, 555.3 us)

commit v5 on v4

--- a/solution.py
+++ b/solution.py
@@ -143,29 +143,37 @@
     return full
 
 
-def all_sum(values):
-    for axis in ("filt", "rows"):
-        count = lax.axis_size(axis)
-        for bit in (1 << n for n in range(count.bit_length() - 1)):
-            values = values + lax.ppermute(values, axis, [(r, r ^ bit) for r in range(count)])
+def pair_sum(values, axis):
+    count = lax.axis_size(axis)
+    for bit in (1 << n for n in range(count.bit_length() - 1)):
+        values = values + lax.ppermute(values, axis, [(r, r ^ bit) for r in range(count)])
     return values
 
 
-def toeplitz_kernel(half, count, up_ref, t00_ref, t10_ref, u00_ref, u10_ref):
+def toeplitz_kernel(half, up_ref, t00_ref, t10_ref, u00_ref, u10_ref):
     width = up_ref.shape[-1]
-    step = pl.program_id(0)
     up = up_ref[0]
-    first = lax.broadcasted_iota(jnp.int32, up.shape, 1) == 0
-    late = jnp.where(first, 0.0, pltpu.roll(up, 1, axis=1))
-    up = jnp.where((step < 2 * count) & (step % 2 == 1), late, up)
-    block = pltpu.roll(
-        jnp.broadcast_to(up, (half, width)), 0, axis=1, stride=1, stride_axis=0
-    )
-    u00, u10 = block[:, :half], block[:, half : 2 * half]
-    u00_ref[0] = u00.astype(BF16)
-    u10_ref[0] = u10.astype(BF16)
-    t00_ref[0] = u00.T.astype(BF16)
-    t10_ref[0] = u10.T.astype(BF16)
+
+    def build(row, parities):
+        block = pltpu.roll(
+            jnp.broadcast_to(row, (half, width)), 0, axis=1, stride=1, stride_axis=0
+        )
+        u00, u10 = block[:, :half], block[:, half : 2 * half]
+        for parity in parities:
+            u00_ref[parity] = u00.astype(BF16)
+            u10_ref[parity] = u10.astype(BF16)
+            t00_ref[parity] = u00.T.astype(BF16)
+            t10_ref[parity] = u10.T.astype(BF16)
+
+    @pl.when(pl.program_id(0) % 2 == 0)
+    def _():
+        build(up, (0, 1))
+
+    @pl.when(pl.program_id(0) % 2 == 1)
+    def _():
+        first = lax.broadcasted_iota(jnp.int32, up.shape, 1) == 0
+        build(jnp.where(first, 0.0, pltpu.roll(up, 1, axis=1)), (0,))
+        build(up, (1,))
 
 
 def toeplitz_blocks(filters, firsts, each):
@@ -176,20 +184,20 @@
         [lax.dynamic_slice_in_dim(filters, first, each, 0) for first in firsts], axis=0
     ).astype(BF16).astype(F32)
     taps = taps.reshape(count, length, 2).transpose(0, 2, 1).reshape(2 * count, 1, length)
-    up = jnp.pad(taps, ((0, 0), (0, 0), (0, length)))
-    by_column = pl.BlockSpec((1, half, half), lambda n: (n // (2 * count), 0, n % (2 * count)))
-    by_row = pl.BlockSpec((1, half, half), lambda n: (n // (2 * count), n % (2 * count), 0))
-    line = pl.BlockSpec((1, 1, 2 * length), lambda n: (n % (2 * count), 0, 0))
+    up = jnp.pad(taps, ((0, 0), (0, 0), (0, half)))
+    by_column = pl.BlockSpec((2, half, half), lambda n: (0, 0, n))
+    by_row = pl.BlockSpec((2, half, half), lambda n: (0, n, 0))
+    line = pl.BlockSpec((1, 1, length + half), lambda n: (n, 0, 0))
     wide = jax.ShapeDtypeStruct((2, half, 2 * count * half), BF16)
     tall = jax.ShapeDtypeStruct((2, 2 * count * half, half), BF16)
     return pl.pallas_call(
-        functools.partial(toeplitz_kernel, half, count),
-        grid=(4 * count,),
+        functools.partial(toeplitz_kernel, half),
+        grid=(2 * count,),
         in_specs=[line],
         out_specs=[by_column, by_column, by_row, by_row],
         out_shape=[wide, wide, tall, tall],
         cost_estimate=pl.CostEstimate(
-            flops=0, bytes_accessed=64 * count * half * half * 4, transcendentals=0
+            flops=0, bytes_accessed=48 * count * half * half * 4, transcendentals=0
         ),
         name="toeplitz",
     )(up)
@@ -565,20 +573,6 @@
     return values, jnp.stack([values[:, 1], early[:, 0]], axis=1), early
 
 
-def row_masks():
-    masks = [0]
-    for bit in reversed(row_bits()):
-        masks = masks + [mask ^ bit for mask in masks]
-    return masks
-
-
-def spread_rows(own):
-    full = own[None]
-    for bit in reversed(row_bits()):
-        full = jnp.concatenate([full, swap_rows(full, bit)], axis=0)
-    return full
-
-
 def shards(inputs, filters, gain_in, mixing, regression, gain_mid, w_gate, w_up, w_down, out_grad):
     shard_rows, local_seqs, width = inputs.shape
     grid = Grid(lax.axis_size("filt"))
@@ -652,13 +646,17 @@
     own_part = lax.dynamic_slice_in_dim(own_pairs, start, part_rows, 1)
     hidden_own = w_down.shape[0]
     share = hidden_own // row_count
-    packed = jnp.stack([w_gate.T, w_up.T, w_down]).reshape(3, row_count, share, width)
+    w_gate, w_up, w_down = tie_all([w_gate, w_up, w_down], mates[0][0])
+    packed = jnp.stack([w_gate.T, w_up.T, w_down])
     *early_bits, last_bit = grid.spread_bits()
-    shares = lax.dynamic_index_in_dim(packed, row_index, 1, keepdims=False)
+    start = sum(
+        jnp.where((row_index & bit) != 0, hidden_own >> (n + 1), 0) for n, bit in enumerate(bits)
+    )
+    shares = lax.dynamic_slice_in_dim(packed, start, share, 1)
     shares = grid.join(shares, grid.swap(shares, early_bits[0]), early_bits[0])
     mates = [(keep, tie(received, own_part)) for keep, received in mates]
+    mate_part = grid.swap(tie(own_part, *(received for _, received in mates)), grid.mate)
     fars = [to_far(*values) for values in mates]
-    mate_part = grid.swap(tie(own_part, shares, *(pair for pair, _ in fars)), grid.mate)
     received = [received for _, received in fars]
     edge = lax.ppermute(
         tie(states[:, :, -1:], *(pair for pair, _ in fars)),
@@ -670,7 +668,7 @@
         [first_branch // 2, (index ^ grid.mate) * branches // 2],
         slots,
     )
-    mate_part, edge = tie_all([mate_part, edge], t00, *received)
+    mate_part, edge = tie_all([mate_part, edge], t00, received[0])
     mate_part = tie(mate_part, edge)
     for bit in early_bits[1:]:
         shares = tie(shares, mate_part)
@@ -708,13 +706,14 @@
         flips = [flip]
     kept_sums, from_fars, turned = [], [], []
     for c in range(chunks):
-        kept_sums.append(from_near(partials[c], tie_all(near_received[c], *from_fars, *turned)))
+        kept_sums.append(from_near(partials[c], near_received[c]))
         from_fars.append(grid.swap(kept_sums[c][1], grid.far))
         if c == 0:
             turned = [
                 value.transpose(0, 2, 1).reshape(2 * slots * width, width)
                 for value in tie_all(pairs, kept_sums[0][1])
             ]
+            from_fars[0] = tie(from_fars[0], *turned, *near_received[1])
     weights = [shares.reshape(grid.size, 3, share, width)]
     for n, bit in enumerate(reversed(bits)):
         received = [swap_rows(weight, bit) for weight in weights]
@@ -776,7 +775,7 @@
     half_count = away[0].shape[0] // 2
     away = total_of(away).astype(BF16)
     away = [away[:half_count], away[half_count:]]
-    from_rows = [swap_rows(value, bits[-1]) for value in away]
+    from_rows = [swap_rows(away[0], bits[-1])]
     first_quad, next_edge = tie_all([quads[0][0], next_edge], *away)
     quads[0] = (first_quad, quads[0][1])
     for c in range(chunks):
@@ -790,8 +789,10 @@
         if c + 1 < chunks:
             later_received = tie_all(quads[c + 1][1], partial[0])
             quads[c + 1] = (quads[c + 1][0], later_received)
-            from_rows[c] = tie(from_rows[c], partial[0])
-            partial = tie_all(partial, *later_received, from_rows[c])
+            from_rows = [
+                tie(from_rows[0], partial[0]), swap_rows(tie(away[1], partial[0]), bits[-1])
+            ]
+            partial = tie_all(partial, *later_received, from_rows[0])
         if c:
             near_received[-1] = tie_all(near_received[-1], partial[0])
             from_rows[-1] = tie(from_rows[-1], partial[0])
@@ -857,9 +858,8 @@
         own_share = kept + value.astype(F32)
     received = grid.swap(mate_share.astype(BF16), grid.mate)
     mixing_low = (own_share + received.astype(F32)).astype(BF16)
-    gain_mid_part, lag_sum, lag_share, mix_back, next_edge, grads, own_gain, *block_out = tie_all(
-        [gain_mid_part, lag_sum, lag_share, mix_back, next_edge, grads, own_gain, *block_out],
-        mixing_low,
+    lag_share, mix_back, next_edge, grads, *block_out = tie_all(
+        [lag_share, mix_back, next_edge, grads, *block_out], mixing_low
     )
     gain_column = mate_gain + own_gain
     for c in range(1, chunks):
@@ -883,7 +883,10 @@
         group * slab,
         0,
     ) / gain_in
-    gains = all_sum(jnp.pad(jnp.stack([gain_in_part, gain_mid_part]), ((0, 6), (0, 0))))
+    gains = pair_sum(
+        jnp.pad(jnp.stack([gain_in_part, gain_mid_part]), ((0, 6), (0, 0))), "rows"
+    )
+    gains = pair_sum(tie(gains, mixing_low), "filt")
 
     own_grads = reduce_filt(grid, grads, last_bits[1:]).astype(BF16)
 
@@ -913,11 +916,7 @@
             middle_grad[c] + norm_backward(back, normed_in[part], factor_in[part], gain_in)
         )
 
-    full = spread_rows(own_grads)
-    ordered = jnp.zeros((row_count, 3, share, width), BF16)
-    for n, mask in enumerate(row_masks()):
-        ordered = lax.dynamic_update_slice_in_dim(ordered, full[n][None], row_index ^ mask, 0)
-    ordered = ordered.transpose(1, 0, 2, 3).reshape(3, hidden_own, width).astype(F32)
+    ordered = gather_rows(own_grads).astype(F32)
     return (
         outward(jnp.concatenate(block_out, axis=0)),
         outward(jnp.concatenate(input_grad, axis=0)),

time: 427 us -> 406 us (0.951)
  waiting for transfers between devices: 103 us -> 82.9 us
  Pallas kernels: 145 us -> 140 us
  starting transfers between devices: 70.3 us -> 75.3 us
  local copies, waits for them, and re-layouts: 36.5 us -> 32 us
    ppermute x28, waiting for transfers between devices: 70.1 us -> 42.3 us  [swap(): lax.ppermute(values, 'filt', [(f, f ^ bit) for f in range(self.size)])]
    ppermute x5, waiting for transfers between devices: 8.11 us -> 20.4 us  [pair_sum(): lax.ppermute(values, axis, [(r, r ^ bit) for r in range(count)])]
    ppermute x28, starting transfers between devices: 35.9 us -> 45.5 us  [swap(): lax.ppermute(values, 'filt', [(f, f ^ bit) for f in range(self.size)])]
    pallas_call x1, Pallas kernels: 15.4 us -> 9.9 us  [toeplitz_blocks(): pl.pallas_call(functools.partial(toeplitz_kernel, half), grid=(2 * count,...]
    unnamed x106 -> x96, local copies, waits for them, and re-layouts: 12.4 us -> 7.76 us
    ppermute x21, waiting for transfers between devices: 13.5 us -> 9.17 us  [swap_rows(): return lax.ppermute(values, 'rows', [(r, r ^ bit) for r in range(count)])]
  transfers between devices with their start and end apart: 64 -> 64, of which waited for: 27 -> 19; matrix products, arithmetic and copies ran while one was open for 19% -> 21% of each run, Pallas kernels for 34% -> 35%
where the time goes in v5:
time: 406 us; the launch traced here: 401 us
  Pallas kernels  140 us (34%)
  waiting for transfers between devices  82.9 us (20%)
  starting transfers between devices  75.3 us (19%)
  other arithmetic  67.7 us (17%)
  local copies, waits for them, and re-layouts  32 us (8%)
    ppermute x28, starting transfers between devices, swap(): lax.ppermute(values, 'filt', [(f, f ^ bit) for f in range(self.size)])  45.5 us
    pallas_call x2, Pallas kernels, mix_sequences_back(): pl.pallas_call(functools.partial(mix_back_kernel, parts), grid_spec=pltpu...  45.1 us
    ppermute x28, waiting for transfers between devices, swap(): lax.ppermute(values, 'filt', [(f, f ^ bit) for f in range(self.size)])  42.3 us
    pallas_call x2, Pallas kernels, mix_sequences(): pl.pallas_call(functools.partial(mix_kernel, parts), grid_spec=pltpu.Pref...  34.1 us
    pallas_call x2, Pallas kernels, mixing_products(): pl.pallas_call(mixing_kernel, grid_spec=pltpu.PrefetchScalarGridSpec(num_...  25.7 us
    pallas_call x2, Pallas kernels, feed_forward(): pl.pallas_call(functools.partial(feed_forward_kernel, shares, len(flat_sa...  24.8 us
    ppermute x5, waiting for transfers between devices, pair_sum(): lax.ppermute(values, axis, [(r, r ^ bit) for r in range(count)])  20.4 us
    select_n x21, other arithmetic, join(): jnp.where(self.flag(bit), jnp.stack([other, own]), jnp.stack([own, other]))  15.1 us
  transfers between devices with their start and end apart: 64, of which 19 were waited for; matrix products, arithmetic and copies ran while one was open for 21% of the time, Pallas kernels for 35%

profile of v5, /device:TPU:0, one launch (start us, length us, event | category | flops | bytes accessed | tf_op | source)
XLA Modules:
  0.0 400.9 jit_solution(15550124146141847072)
XLA Ops:
  5.1 3.0 collective-permute-start.3
  9.2 3.0 collective-permute-start.8
  24.1 3.6 collective-permute-start.5
  33.5 9.9 %toeplitz.1 = (bf16[2,256,3072]{2,1,0:T(8,128)(2,1)}, bf16[2,256,3072]{2,1,0:T(8,128)(2,1)}, bf16[2,3072,256]{2,1,0:T(8,128)(2,1)}, bf16[2,3072,256]{2,1,0:T(8,128)(2,1)}) custom-call(f32[12,1,768]{2,1,0:T(1,128)} %pad_convert_fusion.up_ref), custom_call_target="tpu_custom_call" | custom-call | bytes 75497472 | tf_op jit(solution)/shard_map/toeplitz/pallas_call | solution.py:193
  43.4 5.9 %collective-permute-done.4 = bf16[6,128,512]{2,1,0:T(8,128)(2,1)} collective-permute-done((bf16[6,128,512]{2,1,0:T(8,128)(2,1)}, bf16[6,128,512]{2,1,0:T(8,128)(2,1)}, u32[]{:S(2)}, u32[]{:S(2)}) %collective-permute-start.4) | collective-permute-done | bytes 786464 | tf_op jit(solution)/shard_map/ppermute | solution.py:55
  57.5 5.5 %collective-permute-done.9 = bf16[2,3,64,512]{3,2,1,0:T(8,128)(2,1)S(1)} collective-permute-done((bf16[2,3,64,512]{3,2,1,0:T(8,128)(2,1)S(1)}, bf16[2,3,64,512]{3,2,1,0:T(8,128)(2,1)S(1)}, u32[]{:S(2)}, u32[]{:S(2)}) %collective-permute-start.9) | collective-permute-done | bytes 393248 | tf_op jit(solution)/shard_map/ppermute | solution.py:55
  64.0 3.7 collective-permute-done.2.refs_1_
  68.4 7.3 %collective-permute-done.10.refs_1_ = bf16[4,1,2,64,512]{4,3,2,1,0:T(8,128)(2,1)S(1)} collective-permute-done((bf16[4,1,2,64,512]{4,3,2,1,0:T(8,128)(2,1)S(1)}, bf16[4,1,2,64,512]{4,3,2,1,0:T(8,128)(2,1)S(1)}, u32[]{:S(2)}, u32[]{:S(2)}) %collective-permute-start.10) | collective-permute-done | bytes 524320 | tf_op jit(solution)/shard_map/ppermute | solution.py:96
  79.3 3.4 pad_maximum_fusion.refs_2_.sum_ref.rest_ref
  90.4 16.5 %mix.2 = (bf16[4,1,2,64,512]{4,3,2,1,0:T(8,128)(2,1)S(1)}, bf16[4,1,2,64,512]{4,3,2,1,0:T(8,128)(2,1)S(1)}, bf16[2,512,1024]{2,1,0:T(8,128)(2,1)S(1)}) custom-call(s32[1]{0:T(128)} %bitcast.near_ref, bf16[4,1,2,64,512]{4,3,2,1,0:T(8,128)(2,1)S(1)} %bitcast.311, bf16[4,1,2,64,512]{4,3,2,1,0:T(8,128)(2,1)S(1)} %copy-done.4, ...), custom_call_target="tpu_custom_call" | custom-call | flops 11274289152 | bytes 14680064 | tf_op jit(solution)/shard_map/mix/pallas_call | solution.py:430
  110.1 17.6 %mix.3 = (bf16[4,1,2,64,512]{4,3,2,1,0:T(8,128)(2,1)S(1)}, bf16[4,1,2,64,512]{4,3,2,1,0:T(8,128)(2,1)}, bf16[2,512,1024]{2,1,0:T(8,128)(2,1)S(1)}) custom-call(s32[1]{0:T(128)} %bitcast.near_ref, bf16[4,1,2,64,512]{4,3,2,1,0:T(8,128)(2,1)S(1)} %bitcast.309, bf16[4,1,2,64,512]{4,3,2,1,0:T(8,128)(2,1)S(1)} %copy-done.2, ...), custom_call_target="tpu_custom_call", output_to_operand_aliasing={{2}: (7, {})} | custom-call | flops 11274289152 | bytes 14680064 | tf_op jit(solution)/shard_map/mix/pallas_call | solution.py:430
  129.6 3.4 collective-permute-start.15
  134.7 4.7 %copy.198 = bf16[6,512,512]{2,1,0:T(8,128)(2,1)} copy(bf16[6,512,512]{1,2,0:T(8,128)(2,1)} %bitcast.313) | data formatting | bytes 6291456 | tf_op jit(solution)/shard_map/transpose | solution.py:713
  139.3 5.1 %copy.197 = bf16[6,512,512]{2,1,0:T(8,128)(2,1)} copy(bf16[6,512,512]{1,2,0:T(8,128)(2,1)} %bitcast.312) | data formatting | bytes 6291456 | tf_op jit(solution)/shard_map/transpose | solution.py:713
  149.4 4.9 %collective-permute-start.14 = (bf16[2,1,2,64,512]{4,3,2,1,0:T(8,128)(2,1)S(1)}, bf16[2,1,2,64,512]{4,3,2,1,0:T(8,128)(2,1)S(1)}, u32[]{:S(2)}, u32[]{:S(2)}) collective-permute-start(bf16[2,1,2,64,512]{4,3,2,1,0:T(8,128)(2,1)S(1)} %select_convert_fusion.7), channel_id=1, source_target_pairs={{0,4},{1,5},{2,6},{3,7},{4,0},{5,1},{6,2},{7,3},{8,12},{9,13},{10,... | collective-permute-start | bytes 786440 | tf_op jit(solution)/shard_map/ppermute | solution.py:55
  156.2 9.6 %feed_forward.2 = (bf16[2,2,64,512]{3,2,1,0:T(8,128)(2,1)}, f32[2,2,64,512]{3,2,1,0:T(8,128)}, bf16[1,2,2,64,512]{4,3,2,1,0:T(8,128)(2,1)}, f32[1,512]{1,0:T(1,1...) custom-call(bf16[1,2,2,64,512]{4,3,2,1,0:T(8,128)(2,1)} %bitcast.372, ...), custom_call_target="tpu_custom_call" | custom-call | flops 3221225472 | bytes 11534336 | tf_op jit(solution)/shard_map/feed_forward/pallas_call | solution.py:550
  169.0 4.3 %collective-permute-done.22 = bf16[1,2,64,512]{3,2,1,0:T(8,128)(2,1)S(1)} collective-permute-done((bf16[1,2,64,512]{3,2,1,0:T(8,128)(2,1)S(1)}, bf16[1,2,64,512]{3,2,1,0:T(8,128)(2,1)S(1)}, u32[]{:S(2)}, u32[]{:S(2)}) %collective-permute-start.22) | collective-permute-done | bytes 131104 | tf_op jit(solution)/shard_map/ppermute | solution.py:55
  173.3 4.9 %collective-permute-start.23 = (bf16[2,1,2,64,512]{4,3,2,0,1:T(8,128)(2,1)S(1)}, bf16[2,1,2,64,512]{4,3,2,0,1:T(8,128)(2,1)S(1)}, u32[]{:S(2)}, u32[]{:S(2)}) collective-permute-start(bf16[2,1,2,64,512]{4,3,2,0,1:T(8,128)(2,1)S(1)} %fusion.29), channel_id=1, source_target_pairs={{0,4},{1,5},{2,6},{3,7},{4,0},{5,1},{6,2},{7,3},{8,12},{9,13},{10,... | collective-permute-start | bytes 786440 | tf_op jit(solution)/shard_map/ppermute | solution.py:55
  178.9 15.1 %feed_forward.3 = (bf16[2,2,64,512]{3,2,1,0:T(8,128)(2,1)}, f32[2,2,64,512]{3,2,1,0:T(8,128)}, bf16[1,2,2,64,512]{4,3,2,1,0:T(8,128)(2,1)}, f32[1,512]{1,0:T(1,1...) custom-call(bf16[1,2,2,64,512]{4,3,2,1,0:T(8,128)(2,1)} %bitcast.371, ...), custom_call_target="tpu_custom_call" | custom-call | flops 6442450944 | bytes 11534336 | tf_op jit(solution)/shard_map/feed_forward/pallas_call | solution.py:550
  208.5 9.3 %collective-permute-done.25 = bf16[2,1,2,64,512]{4,3,2,0,1:T(8,128)(2,1)} collective-permute-done((bf16[2,1,2,64,512]{4,3,2,0,1:T(8,128)(2,1)}, bf16[2,1,2,64,512]{4,3,2,0,1:T(8,128)(2,1)}, u32[]{:S(2)}, u32[]{:S(2)}) %collective-permute-start.25) | collective-permute-done | bytes 262176 | tf_op jit(solution)/shard_map/ppermute | solution.py:55
  222.1 22.4 %mix_back.2 = (bf16[4,1,2,64,512]{4,3,2,1,0:T(8,128)(2,1)}, bf16[4,1,2,64,512]{4,3,2,1,0:T(8,128)(2,1)}, bf16[2,1024,6144]{2,1,0:T(8,128)(2,1)}, f32[3,128,512]{2,1,0:T(8,128)}) custom-call(s32[1]{0:T(128)} %bitcast.near_ref, s32[1]{0:T(128)} %bitcast.1.own_ref, bf16[4,1,2,64,512]{4,3,2,1,0:T(8,128)(2,1)} %bitcast.71.refs_0_, ...), custom_call_target="tpu_custom_call" | custom-call | flops 11274289152 | bytes 14680064 | tf_op jit(solution)/shard_map/mix_back/pallas_call | solution.py:470
  247.7 22.7 %mix_back.3 = (bf16[4,1,2,64,512]{4,3,2,1,0:T(8,128)(2,1)}, bf16[4,1,2,64,512]{4,3,2,1,0:T(8,128)(2,1)}, bf16[2,1024,6144]{2,1,0:T(8,128)(2,1)}, f32[3,128,512]{2,1,0:T(8,128)}) custom-call(s32[1]{0:T(128)} %bitcast.near_ref, s32[1]{0:T(128)} %bitcast.1.own_ref, bf16[4,1,2,64,512]{4,3,2,1,0:T(8,128)(2,1)} %bitcast.363, ...), custom_call_target="tpu_custom_call", output_to_operand_aliasing={{2}: (9, {})} | custom-call | flops 11274289152 | bytes 14680064 | tf_op jit(solution)/shard_map/mix_back/pallas_call | solution.py:470
  274.4 13.1 %mixing_products.2 = (f32[6,256,512]{2,1,0:T(8,128)}, bf16[6,256,512]{2,1,0:T(8,128)(2,1)}, f32[512,1]{1,0:T(8,128)}) custom-call(s32[1]{0:T(128)} %bitcast.81.bit_ref, bf16[2,512,1024]{2,1,0:T(8,128)(2,1)} %copy-done, bf16[2,1024,6144]{2,1,0:T(8,128)(2,1)} %get-tuple-element.229.plus_ref.minus_ref, ...), custom_call_target="tpu_custom_call" | custom-call | flops 6442450944 | bytes 20971520 | tf_op jit(solution)/shard_map/mixing_products/pallas_call | solution.py:511
  289.9 3.2 broadcast_select_fusion.6
  300.0 12.5 %mixing_products.3 = (f32[6,256,512]{2,1,0:T(8,128)}, bf16[6,256,512]{2,1,0:T(8,128)(2,1)}, f32[512,1]{1,0:T(8,128)}) custom-call(s32[1]{0:T(128)} %bitcast.81.bit_ref, bf16[2,512,1024]{2,1,0:T(8,128)(2,1)} %copy-done, bf16[2,1024,6144]{2,1,0:T(8,128)(2,1)} %get-tuple-element.229.plus_ref.minus_ref, ...), custom_call_target="tpu_custom_call" | custom-call | flops 6442450944 | bytes 20971520 | tf_op jit(solution)/shard_map/mixing_products/pallas_call | solution.py:511
  314.0 3.9 collective-permute-done.40
  328.9 16.6 %collective-permute-done.56 = f32[8,512]{1,0:T(8,128)S(1)} collective-permute-done((f32[8,512]{1,0:T(8,128)S(1)}, f32[8,512]{1,0:T(8,128)S(1)}, u32[]{:S(2)}, u32[]{:S(2)}) %collective-permute-start.56) | collective-permute-done | bytes 16416 | tf_op jit(solution)/shard_map/ppermute | solution.py:149
  356.9 5.9 %collective-permute-done.51 = bf16[2,3,16,512]{3,2,1,0:T(8,128)(2,1)S(1)} collective-permute-done((bf16[2,3,16,512]{3,2,1,0:T(8,128)(2,1)S(1)}, bf16[2,3,16,512]{3,2,1,0:T(8,128)(2,1)S(1)}, u32[]{:S(2)}, u32[]{:S(2)}) %collective-permute-start.51) | collective-permute-done | bytes 98336 | tf_op jit(solution)/shard_map/ppermute | solution.py:55
  364.6 4.0 collective-permute-done.52
  375.7 3.8 collective-permute-done.59
  381.9 3.4 collective-permute-done.62
  397.2 3.6 maximum_convert_fusion
  (340 shorter events, 143.0 us)
Async XLA Ops:
  9.2 41.3 %collective-permute-start.8 = (bf16[3,64,512]{2,1,0:T(8,128)(2,1)}, bf16[3,64,512]{2,1,0:T(8,128)(2,1)}, u32[]{:S(2)}, u32[]{:S(2)}) collective-permute-start(bf16[3,64,512]{2,1,0:T(8,128)(2,1)} %fusion.33), channel_id=1, source_target_pairs={{0,4},{1,5},{2,6},{3,7},{4,0},{5,1},{6,2},{7,3},{8,12},{9,13},{10,... | collective-permute-start | bytes 589832 | tf_op jit(solution)/shard_map/ppermute | solution.py:55
  19.0 30.3 %collective-permute-start.4 = (bf16[6,128,512]{2,1,0:T(8,128)(2,1)}, bf16[6,128,512]{2,1,0:T(8,128)(2,1)}, u32[]{:S(2)}, u32[]{:S(2)}) collective-permute-start(bf16[6,128,512]{2,1,0:T(8,128)(2,1)} %fusion.8), channel_id=1, source_target_pairs={{0,2},{1,3},{2,0},{3,1},{4,6},{5,7},{6,4},{7,5},{8,10},{9,11},{10,... | collective-permute-start | bytes 2359304 | tf_op jit(solution)/shard_map/ppermute | solution.py:55
  20.0 23.4 %collective-permute-start.6 = (bf16[2,1,2,64,512]{4,3,2,0,1:T(8,128)(2,1)S(1)}, bf16[2,1,2,64,512]{4,3,2,0,1:T(8,128)(2,1)}, u32[]{:S(2)}, u32[]{:S(2)}) collective-permute-start(bf16[2,1,2,64,512]{4,3,2,0,1:T(8,128)(2,1)S(1)} %maximum_select_fusion.7), channel_id=1, source_target_pairs={{0,4},{1,5},{2,6},{3,7},{4,0},{5,1},{6,2},{7,3},{8,12},{9,13},{10,... | collective-permute-start | bytes 786440 | tf_op jit(solution)/shard_map/ppermute | solution.py:55
  23.3 28.3 %collective-permute-start.1 = (bf16[2,1,2,64,512]{4,3,2,0,1:T(8,128)(2,1)S(1)}, bf16[2,1,2,64,512]{4,3,2,0,1:T(8,128)(2,1)}, u32[]{:S(2)}, u32[]{:S(2)}) collective-permute-start(bf16[2,1,2,64,512]{4,3,2,0,1:T(8,128)(2,1)S(1)} %maximum_select_fusion.6), channel_id=1, source_target_pairs={{0,4},{1,5},{2,6},{3,7},{4,0},{5,1},{6,2},{7,3},{8,12},{9,13},{10,... | collective-permute-start | bytes 786440 | tf_op jit(solution)/shard_map/ppermute | solution.py:55
  24.1 19.3 %collective-permute-start.5 = (bf16[4,2,1,512]{3,2,1,0:T(2,128)(2,1)S(1)}, bf16[4,2,1,512]{3,2,1,0:T(2,128)(2,1)S(1)}, u32[]{:S(2)}, u32[]{:S(2)}) collective-permute-start(bf16[4,2,1,512]{3,2,1,0:T(2,128)(2,1)S(1)} %slice.368), channel_id=1, source_target_pairs={{0,1},{1,2},{2,3},{3,4},{4,5},{5,6},{6,7},{8,9},{9,10},{10,11},{11... | collective-permute-start | bytes 24584 | tf_op jit(solution)/shard_map/ppermute | solution.py:661
  49.3 27.3 %collective-permute-start.7 = (bf16[6,128,512]{2,1,0:T(8,128)(2,1)}, bf16[6,128,512]{2,1,0:T(8,128)(2,1)S(1)}, u32[]{:S(2)}, u32[]{:S(2)}) collective-permute-start(bf16[6,128,512]{2,1,0:T(8,128)(2,1)} %collective-permute-done.4), channel_id=1, source_target_pairs={{0,16},{8,24},{16,0},{24,8},{1,17},{9,25},{17,1},{25,9},{2,18},{10... | collective-permute-start | bytes 2359304 | tf_op jit(solution)/shard_map/ppermute | solution.py:112
  55.5 20.3 %collective-permute-start.10 = (bf16[4,1,2,64,512]{4,3,2,1,0:T(8,128)(2,1)S(1)}, bf16[4,1,2,64,512]{4,3,2,1,0:T(8,128)(2,1)S(1)}, u32[]{:S(2)}, u32[]{:S(2)}) collective-permute-start(bf16[4,1,2,64,512]{4,3,2,1,0:T(8,128)(2,1)S(1)} %bitcast.310), channel_id=1, source_target_pairs={{0,1},{1,0},{2,3},{3,2},{4,5},{5,4},{6,7},{7,6},{8,9},{9,8},{10,11... | collective-permute-start | bytes 1572872 | tf_op jit(solution)/shard_map/ppermute | solution.py:96
  84.8 22.2 %collective-permute-start.17 = (bf16[2,2,3,64,512]{4,3,2,1,0:T(8,128)(2,1)S(1)}, bf16[2,2,3,64,512]{4,3,2,1,0:T(8,128)(2,1)S(1)}, u32[]{:S(2)}, u32[]{:S(2)}) collective-permute-start(bf16[2,2,3,64,512]{4,3,2,1,0:T(8,128)(2,1)S(1)} %copy-done.17), channel_id=1, source_target_pairs={{0,1},{1,0},{2,3},{3,2},{4,5},{5,4},{6,7},{7,6},{8,9},{9,8},{10,11... | collective-permute-start | bytes 2359304 | tf_op jit(solution)/shard_map/ppermute | solution.py:55
  107.0 20.6 %collective-permute-start.12 = (bf16[4,1,2,64,512]{4,3,2,1,0:T(8,128)(2,1)S(1)}, bf16[4,1,2,64,512]{4,3,2,1,0:T(8,128)(2,1)S(1)}, u32[]{:S(2)}, u32[]{:S(2)}) collective-permute-start(bf16[4,1,2,64,512]{4,3,2,1,0:T(8,128)(2,1)S(1)} %get-tuple-element.154), channel_id=1, source_target_pairs={{0,1},{1,0},{2,3},{3,2},{4,5},{5,4},{6,7},{7,6},{8,9},{9,8},{10,11... | collective-permute-start | bytes 1572872 | tf_op jit(solution)/shard_map/ppermute | solution.py:96
  109.1 36.5 %collective-permute-start.18 = (bf16[8,3,64,512]{3,2,1,0:T(8,128)(2,1)}, bf16[8,3,64,512]{3,2,1,0:T(8,128)(2,1)}, u32[]{:S(2)}, u32[]{:S(2)}) collective-permute-start(bf16[8,3,64,512]{3,2,1,0:T(8,128)(2,1)} %bitcast.46.refs_0_), channel_id=1, source_target_pairs={{0,16},{8,24},{16,0},{24,8},{1,17},{9,25},{17,1},{25,9},{2,18},{10... | collective-permute-start | bytes 4718600 | tf_op jit(solution)/shard_map/ppermute | solution.py:112
  127.6 17.0 %collective-permute-start.13 = (bf16[4,1,2,64,512]{4,3,2,1,0:T(8,128)(2,1)}, bf16[4,1,2,64,512]{4,3,2,1,0:T(8,128)(2,1)S(1)}, u32[]{:S(2)}, u32[]{:S(2)}) collective-permute-start(bf16[4,1,2,64,512]{4,3,2,1,0:T(8,128)(2,1)} %get-tuple-element.157), channel_id=1, source_target_pairs={{0,1},{1,0},{2,3},{3,2},{4,5},{5,4},{6,7},{7,6},{8,9},{9,8},{10,11... | collective-permute-start | bytes 1572872 | tf_op jit(solution)/shard_map/ppermute | solution.py:96
  134.7 20.4 %collective-permute-start.19 = (bf16[8,3,64,512]{3,2,1,0:T(8,128)(2,1)}, bf16[8,3,64,512]{3,2,1,0:T(8,128)(2,1)}, u32[]{:S(2)}, u32[]{:S(2)}) collective-permute-start(bf16[8,3,64,512]{3,2,1,0:T(8,128)(2,1)} %bitcast.46.refs_0_), channel_id=1, source_target_pairs={{0,8},{8,0},{16,24},{24,16},{1,9},{9,1},{17,25},{25,17},{2,10},{10... | collective-permute-start | bytes 4718600 | tf_op jit(solution)/shard_map/ppermute | solution.py:112
  149.4 17.2 %collective-permute-start.14 = (bf16[2,1,2,64,512]{4,3,2,1,0:T(8,128)(2,1)S(1)}, bf16[2,1,2,64,512]{4,3,2,1,0:T(8,128)(2,1)S(1)}, u32[]{:S(2)}, u32[]{:S(2)}) collective-permute-start(bf16[2,1,2,64,512]{4,3,2,1,0:T(8,128)(2,1)S(1)} %select_convert_fusion.7), channel_id=1, source_target_pairs={{0,4},{1,5},{2,6},{3,7},{4,0},{5,1},{6,2},{7,3},{8,12},{9,13},{10,... | collective-permute-start | bytes 786440 | tf_op jit(solution)/shard_map/ppermute | solution.py:55
  173.3 20.7 %collective-permute-start.23 = (bf16[2,1,2,64,512]{4,3,2,0,1:T(8,128)(2,1)S(1)}, bf16[2,1,2,64,512]{4,3,2,0,1:T(8,128)(2,1)S(1)}, u32[]{:S(2)}, u32[]{:S(2)}) collective-permute-start(bf16[2,1,2,64,512]{4,3,2,0,1:T(8,128)(2,1)S(1)} %fusion.29), channel_id=1, source_target_pairs={{0,4},{1,5},{2,6},{3,7},{4,0},{5,1},{6,2},{7,3},{8,12},{9,13},{10,... | collective-permute-start | bytes 786440 | tf_op jit(solution)/shard_map/ppermute | solution.py:55
  194.0 25.3 %collective-permute-start.28 = (bf16[8,3,64,512]{3,2,1,0:T(8,128)(2,1)}, bf16[8,3,64,512]{3,2,1,0:T(8,128)(2,1)}, u32[]{:S(2)}, u32[]{:S(2)}) collective-permute-start(bf16[8,3,64,512]{3,2,1,0:T(8,128)(2,1)} %get-tuple-element.187), channel_id=1, source_target_pairs={{0,8},{8,0},{16,24},{24,16},{1,9},{9,1},{17,25},{25,17},{2,10},{10... | collective-permute-start | bytes 4718600 | tf_op jit(solution)/shard_map/ppermute | solution.py:112
  194.1 25.2 %collective-permute-start.29 = (bf16[8,3,64,512]{3,2,1,0:T(8,128)(2,1)}, bf16[8,3,64,512]{3,2,1,0:T(8,128)(2,1)}, u32[]{:S(2)}, u32[]{:S(2)}) collective-permute-start(bf16[8,3,64,512]{3,2,1,0:T(8,128)(2,1)} %get-tuple-element.188), channel_id=1, source_target_pairs={{0,8},{8,0},{16,24},{24,16},{1,9},{9,1},{17,25},{25,17},{2,10},{10... | collective-permute-start | bytes 4718600 | tf_op jit(solution)/shard_map/ppermute | solution.py:112
  199.4 20.0 %collective-permute-start.30 = (bf16[4,1,2,64,512]{4,3,2,1,0:T(8,128)(2,1)}, bf16[4,1,2,64,512]{4,3,2,1,0:T(8,128)(2,1)}, u32[]{:S(2)}, u32[]{:S(2)}) collective-permute-start(bf16[4,1,2,64,512]{4,3,2,1,0:T(8,128)(2,1)} %bitcast.70), channel_id=1, source_target_pairs={{0,1},{1,0},{2,3},{3,2},{4,5},{5,4},{6,7},{7,6},{8,9},{9,8},{10,11... | collective-permute-start | bytes 1572872 | tf_op jit(solution)/shard_map/ppermute | solution.py:96
  218.9 25.6 %collective-permute-start.26 = (bf16[4,1,2,64,512]{4,3,2,1,0:T(8,128)(2,1)S(1)}, bf16[4,1,2,64,512]{4,3,2,1,0:T(8,128)(2,1)S(1)}, u32[]{:S(2)}, u32[]{:S(2)}) collective-permute-start(bf16[4,1,2,64,512]{4,3,2,1,0:T(8,128)(2,1)S(1)} %bitcast.362), channel_id=1, source_target_pairs={{0,1},{1,0},{2,3},{3,2},{4,5},{5,4},{6,7},{7,6},{8,9},{9,8},{10,11... | collective-permute-start | bytes 1572872 | tf_op jit(solution)/shard_map/ppermute | solution.py:96
  221.5 24.6 %collective-permute-start.31 = (bf16[4,3,64,512]{3,2,1,0:T(8,128)(2,1)S(1)}, bf16[4,3,64,512]{3,2,1,0:T(8,128)(2,1)S(1)}, u32[]{:S(2)}, u32[]{:S(2)}) collective-permute-start(bf16[4,3,64,512]{3,2,1,0:T(8,128)(2,1)S(1)} %get-tuple-element.318), channel_id=1, source_target_pairs={{0,16},{8,24},{16,0},{24,8},{1,17},{9,25},{17,1},{25,9},{2,18},{10... | collective-permute-start | bytes 2359304 | tf_op jit(solution)/shard_map/ppermute | solution.py:112
  244.5 25.9 %collective-permute-start.33 = (bf16[4,3,64,512]{3,2,1,0:T(8,128)(2,1)S(1)}, bf16[4,3,64,512]{3,2,1,0:T(8,128)(2,1)S(1)}, u32[]{:S(2)}, u32[]{:S(2)}) collective-permute-start(bf16[4,3,64,512]{3,2,1,0:T(8,128)(2,1)S(1)} %get-tuple-element.207), channel_id=1, source_target_pairs={{0,16},{8,24},{16,0},{24,8},{1,17},{9,25},{17,1},{25,9},{2,18},{10... | collective-permute-start | bytes 2359304 | tf_op jit(solution)/shard_map/ppermute | solution.py:112
  246.1 24.3 %collective-permute-start.32 = (bf16[4,1,2,64,512]{4,3,2,1,0:T(8,128)(2,1)}, bf16[4,1,2,64,512]{4,3,2,1,0:T(8,128)(2,1)S(1)}, u32[]{:S(2)}, u32[]{:S(2)}) collective-permute-start(bf16[4,1,2,64,512]{4,3,2,1,0:T(8,128)(2,1)} %get-tuple-element.205), channel_id=1, source_target_pairs={{0,1},{1,0},{2,3},{3,2},{4,5},{5,4},{6,7},{7,6},{8,9},{9,8},{10,11... | collective-permute-start | bytes 1572872 | tf_op jit(solution)/shard_map/ppermute | solution.py:96
  271.8 23.5 %collective-permute-start.39 = (bf16[4,1,2,64,512]{4,3,2,1,0:T(8,128)(2,1)}, bf16[4,1,2,64,512]{4,3,2,1,0:T(8,128)(2,1)}, u32[]{:S(2)}, u32[]{:S(2)}) collective-permute-start(bf16[4,1,2,64,512]{4,3,2,1,0:T(8,128)(2,1)} %get-tuple-element.227), channel_id=1, source_target_pairs={{0,1},{1,0},{2,3},{3,2},{4,5},{5,4},{6,7},{7,6},{8,9},{9,8},{10,11... | collective-permute-start | bytes 1572872 | tf_op jit(solution)/shard_map/ppermute | solution.py:96
  273.8 20.8 %collective-permute-start.35 = (bf16[3,32,512]{2,1,0:T(8,128)(2,1)}, bf16[3,32,512]{2,1,0:T(8,128)(2,1)S(1)}, u32[]{:S(2)}, u32[]{:S(2)}) collective-permute-start(bf16[3,32,512]{2,1,0:T(8,128)(2,1)} %fusion.35), channel_id=1, source_target_pairs={{0,16},{8,24},{16,0},{24,8},{1,17},{9,25},{17,1},{25,9},{2,18},{10... | collective-permute-start | bytes 294920 | tf_op jit(solution)/shard_map/ppermute | solution.py:112
  287.8 26.2 %collective-permute-start.41 = (bf16[1,2,64,512]{3,2,1,0:T(8,128)(2,1)S(1)}, bf16[1,2,64,512]{3,2,1,0:T(8,128)(2,1)S(1)}, u32[]{:S(2)}, u32[]{:S(2)}) collective-permute-start(bf16[1,2,64,512]{3,2,1,0:T(8,128)(2,1)S(1)} %get-tuple-element.345), channel_id=1, source_target_pairs={{0,2},{1,3},{2,0},{3,1},{4,6},{5,7},{6,4},{7,5},{8,10},{9,11},{10,... | collective-permute-start | bytes 393224 | tf_op jit(solution)/shard_map/ppermute | solution.py:55
  293.1 28.5 %collective-permute-start.43 = (bf16[2,2,3,64,512]{4,3,2,1,0:T(8,128)(2,1)}, bf16[2,2,3,64,512]{4,3,2,1,0:T(8,128)(2,1)}, u32[]{:S(2)}, u32[]{:S(2)}) collective-permute-start(bf16[2,2,3,64,512]{4,3,2,1,0:T(8,128)(2,1)} %bitcast.93), channel_id=1, source_target_pairs={{0,1},{1,0},{2,3},{3,2},{4,5},{5,4},{6,7},{7,6},{8,9},{9,8},{10,11... | collective-permute-start | bytes 2359304 | tf_op jit(solution)/shard_map/ppermute | solution.py:55
  298.3 19.7 %collective-permute-start.40 = (bf16[6,128,512]{2,1,0:T(8,128)(2,1)}, bf16[6,128,512]{2,1,0:T(8,128)(2,1)}, u32[]{:S(2)}, u32[]{:S(2)}) collective-permute-start(bf16[6,128,512]{2,1,0:T(8,128)(2,1)} %fusion.6), channel_id=1, source_target_pairs={{0,16},{8,24},{16,0},{24,8},{1,17},{9,25},{17,1},{25,9},{2,18},{10... | collective-permute-start | bytes 2359304 | tf_op jit(solution)/shard_map/ppermute | solution.py:112
  319.8 32.6 %collective-permute-start.47 = (bf16[1,2,64,512]{3,2,1,0:T(8,128)(2,1)S(1)}, bf16[1,2,64,512]{3,2,1,0:T(8,128)(2,1)S(1)}, u32[]{:S(2)}, u32[]{:S(2)}) collective-permute-start(bf16[1,2,64,512]{3,2,1,0:T(8,128)(2,1)S(1)} %get-tuple-element.343), channel_id=1, source_target_pairs={{0,2},{1,3},{2,0},{3,1},{4,6},{5,7},{6,4},{7,5},{8,10},{9,11},{10,... | collective-permute-start | bytes 393224 | tf_op jit(solution)/shard_map/ppermute | solution.py:55
  324.0 21.5 %collective-permute-start.46 = (bf16[6,128,512]{2,1,0:T(8,128)(2,1)S(1)}, bf16[6,128,512]{2,1,0:T(8,128)(2,1)S(1)}, u32[]{:S(2)}, u32[]{:S(2)}) collective-permute-start(bf16[6,128,512]{2,1,0:T(8,128)(2,1)S(1)} %fusion.2), channel_id=1, source_target_pairs={{0,2},{1,3},{2,0},{3,1},{4,6},{5,7},{6,4},{7,5},{8,10},{9,11},{10,... | collective-permute-start | bytes 2359304 | tf_op jit(solution)/shard_map/ppermute | solution.py:55
  325.3 20.2 %collective-permute-start.45 = (bf16[6,128,512]{2,1,0:T(8,128)(2,1)S(1)}, bf16[6,128,512]{2,1,0:T(8,128)(2,1)S(1)}, u32[]{:S(2)}, u32[]{:S(2)}) collective-permute-start(bf16[6,128,512]{2,1,0:T(8,128)(2,1)S(1)} %fusion.7), channel_id=1, source_target_pairs={{0,16},{8,24},{16,0},{24,8},{1,17},{9,25},{17,1},{25,9},{2,18},{10... | collective-permute-start | bytes 2359304 | tf_op jit(solution)/shard_map/ppermute | solution.py:112
  328.2 17.2 %collective-permute-start.56 = (f32[8,512]{1,0:T(8,128)S(1)}, f32[8,512]{1,0:T(8,128)S(1)}, u32[]{:S(2)}, u32[]{:S(2)}) collective-permute-start(f32[8,512]{1,0:T(8,128)S(1)} %fusion.44), channel_id=1, source_target_pairs={{0,16},{8,24},{16,0},{24,8},{1,17},{9,25},{17,1},{25,9},{2,18},{10... | collective-permute-start | bytes 49160 | tf_op jit(solution)/shard_map/ppermute | solution.py:149
  346.2 39.2 %collective-permute-start.48 = (bf16[6,128,512]{2,1,0:T(8,128)(2,1)S(1)}, bf16[6,128,512]{2,1,0:T(8,128)(2,1)S(1)}, u32[]{:S(2)}, u32[]{:S(2)}) collective-permute-start(bf16[6,128,512]{2,1,0:T(8,128)(2,1)S(1)} %fusion.4), channel_id=1, source_target_pairs={{0,16},{8,24},{16,0},{24,8},{1,17},{9,25},{17,1},{25,9},{2,18},{10... | collective-permute-start | bytes 2359304 | tf_op jit(solution)/shard_map/ppermute | solution.py:112
  350.1 19.2 %collective-permute-start.60 = (bf16[2,3,64,512]{3,2,1,0:T(8,128)(2,1)S(1)}, bf16[2,3,64,512]{3,2,1,0:T(8,128)(2,1)S(1)}, u32[]{:S(2)}, u32[]{:S(2)}) collective-permute-start(bf16[2,3,64,512]{3,2,1,0:T(8,128)(2,1)S(1)} %fusion.25), channel_id=1, source_target_pairs={{0,2},{1,3},{2,0},{3,1},{4,6},{5,7},{6,4},{7,5},{8,10},{9,11},{10,... | collective-permute-start | bytes 1179656 | tf_op jit(solution)/shard_map/ppermute | solution.py:55
  (79 other events, 548.9 us)

commit v6 on v5

--- a/solution.py
+++ b/solution.py
@@ -227,35 +227,39 @@
 
 def mix_kernel(parts, near_ref, *refs):
     pieces = refs[:parts]
-    mixes = refs[parts : parts + 2]
-    t00_ref, t10_ref = refs[parts + 2 : parts + 4]
+    own_pair = refs[parts : parts + 2]
+    mate_pair = refs[parts + 2 : parts + 4]
+    t00_ref, t10_ref = refs[parts + 4 : parts + 6]
     outs = refs[-parts - 5 : -5]
     flip_ref, states_ref, low_ref, high_ref, sum_ref = refs[-5:]
     half = t00_ref.shape[1]
-    branches = 2 * mixes[0].shape[0]
-    slots = branches // 4
-    assemble(near_ref[0], pieces, states_ref)
-
-    for branch in range(branches):
-        slot = pl.ds(branch * half, half)
+    slot = pl.program_id(1)
+    slots = pl.num_programs(1)
+
+    @pl.when(slot == 0)
+    def _():
+        assemble(near_ref[0], pieces, states_ref)
+        sum_ref[...] = jnp.zeros_like(sum_ref)
+        flip_ref[0] = states_ref[...].T
+
+    for pm in range(2):
+        mixing = jnp.where(slot < slots // 2, own_pair[pm][0], mate_pair[pm][0])
+        rows = pl.ds(pm * half, half)
+        value = dot(states_ref[...], mixing).astype(BF16)
         for quarter in range(4):
-            value = dot(
-                states_ref[pl.ds(quarter * half, half), :],
-                mixes[branch // 2 // slots][branch % 2 * slots + branch // 2 % slots],
-            ).astype(BF16)
-            target = (quarter // 2) ^ (branch % 2)
-            (low_ref, high_ref)[quarter % 2][target, slot, :] = value
+            part = value[quarter * half : (quarter + 1) * half]
+            (low_ref, high_ref)[quarter % 2][quarter // 2 ^ pm, rows, :] = part
 
     for parity in range(2):
         base = 2 * parity * half
-        sum_ref[pl.ds(base, half), :] = dot(t00_ref[parity], low_ref[parity]).astype(
-            sum_ref.dtype
-        )
-        sum_ref[pl.ds(base + half, half), :] = (
-            dot(t10_ref[parity], low_ref[parity]) + dot(t00_ref[parity], high_ref[parity])
-        ).astype(sum_ref.dtype)
-    scatter(near_ref[0], sum_ref, outs)
-    flip_ref[0] = states_ref[...].T
+        sum_ref[pl.ds(base, half), :] += dot(t00_ref[parity], low_ref[parity])
+        sum_ref[pl.ds(base + half, half), :] += dot(t10_ref[parity], low_ref[parity]) + dot(
+            t00_ref[parity], high_ref[parity]
+        )
+
+    @pl.when(slot == slots - 1)
+    def _():
+        scatter(near_ref[0], sum_ref, outs)
 
 
 def mix_back_kernel(parts, near_ref, own_ref, *refs):
@@ -268,49 +272,51 @@
     half = u00_ref.shape[2]
     width = grad_ref.shape[1]
     length = grad_ref.shape[0] // 2
-    branches = back_ref.shape[2] // width
-    slots = branches // 4
-
-    @pl.when(pl.program_id(0) == 0)
+    slot = pl.program_id(1)
+    slots = pl.num_programs(1)
+
+    @pl.when((pl.program_id(0) == 0) & (slot == 0))
     def _():
         lag_ref[...] = before[1][...] if before else jnp.zeros_like(lag_ref)
 
-    assemble(near_ref[0], pieces, grad_ref)
+    @pl.when(slot == 0)
+    def _():
+        assemble(near_ref[0], pieces, grad_ref)
+        sum_ref[...] = jnp.zeros_like(sum_ref)
+        own = slab_ref[0].astype(F32)
+        even, odd = own[:, :length], own[:, length:]
+        first = lax.broadcasted_iota(jnp.int32, even.shape, 1) == 0
+        even_late = jnp.where(first, 0.0, pltpu.roll(even, 1, axis=1))
+        odd_late = jnp.where(first, 0.0, pltpu.roll(odd, 1, axis=1))
+        for lag, (on_even, on_odd) in enumerate(
+            ((even, odd), (odd_late, even), (even_late, odd_late))
+        ):
+            lag_ref[lag] += dot(on_even.astype(BF16), grad_ref[:length, :]) + dot(
+                on_odd.astype(BF16), grad_ref[length:, :]
+            )
 
     for parity in range(2):
         base = 2 * parity * half
         low = grad_ref[pl.ds(base, half), :]
         high = grad_ref[pl.ds(base + half, half), :]
-        for branch in range(branches):
-            rows = pl.ds(branch * half, half)
-            set_of, slot = branch // 2 // slots, branch // 2 % slots
-            columns = pl.ds(((2 * set_of + branch % 2) * slots + slot) * width, width)
-            target = 2 * half * (parity ^ (branch % 2))
-            back_ref[0, pl.ds(target, half), columns] = (
-                dot(u00_ref[parity, rows, :], low) + dot(u10_ref[parity, rows, :], high)
-            ).astype(BF16)
-            back_ref[0, pl.ds(target + half, half), columns] = dot(
-                u00_ref[parity, rows, :], high
-            ).astype(BF16)
-
-    for quarter in range(4):
-        rows = pl.ds(quarter * half, half)
-        sum_ref[rows, :] = dot(back_ref[0, rows, : 2 * slots * width], turned[0][...]) + dot(
-            back_ref[0, rows, 2 * slots * width :], turned[1][...]
-        )
-    scatter(near_ref[0], sum_ref, outs)
-
-    own = slab_ref[0].astype(F32)
-    even, odd = own[:, :length], own[:, length:]
-    first = lax.broadcasted_iota(jnp.int32, even.shape, 1) == 0
-    even_late = jnp.where(first, 0.0, pltpu.roll(even, 1, axis=1))
-    odd_late = jnp.where(first, 0.0, pltpu.roll(odd, 1, axis=1))
-    for lag, (on_even, on_odd) in enumerate(
-        ((even, odd), (odd_late, even), (even_late, odd_late))
-    ):
-        lag_ref[lag] += dot(on_even.astype(BF16), grad_ref[:length, :]) + dot(
-            on_odd.astype(BF16), grad_ref[length:, :]
-        )
+        both = (dot(u00_ref[parity], low) + dot(u10_ref[parity], high)).astype(BF16)
+        last = dot(u00_ref[parity], high).astype(BF16)
+        for pm in range(2):
+            columns = pl.ds(pm * width, width)
+            target = 2 * half * (parity ^ pm)
+            rows = slice(pm * half, (pm + 1) * half)
+            back_ref[0, pl.ds(target, half), columns] = both[rows]
+            back_ref[0, pl.ds(target + half, half), columns] = last[rows]
+
+    for set_of in range(2):
+
+        @pl.when((slot >= slots // 2) == bool(set_of))
+        def _():
+            sum_ref[...] += dot(back_ref[0], turned[set_of][...])
+
+    @pl.when(slot == slots - 1)
+    def _():
+        scatter(near_ref[0], sum_ref, outs)
 
 
 def feed_forward_kernel(
@@ -424,36 +430,44 @@
     parts = len(pieces)
     fars, count, _, height, width = pieces[0].shape
     half = t00.shape[1]
+    slots = pairs[0].shape[0] // 2
     block = pl.BlockSpec((fars, 1, 2, height, width), lambda n, *_: (0, n, 0, 0, 0))
-    rows = t00.shape[2]
+    pair_specs = [
+        pl.BlockSpec((1, width, width), lambda n, q, *_, pm=pm: (pm + jnp.minimum(q, slots - 1), 0, 0))
+        for pm in (0, slots)
+    ] + [
+        pl.BlockSpec((1, width, width), lambda n, q, *_, pm=pm: (pm + jnp.maximum(q - slots, 0), 0, 0))
+        for pm in (0, slots)
+    ]
+    line = pl.BlockSpec((2, half, 2 * half), lambda n, q, *_: (0, 0, q))
     flip = pl.BlockSpec((1, width, 4 * half), lambda n, *_: (start + n, 0, 0))
     return pl.pallas_call(
         functools.partial(mix_kernel, parts),
         grid_spec=pltpu.PrefetchScalarGridSpec(
             num_scalar_prefetch=1,
-            grid=(count,),
+            grid=(count, 2 * slots),
             in_specs=[block] * parts
-            + [resident(a.shape) for a in (*pairs, t00, t10)]
+            + [*pair_specs, line, line]
             + [pl.BlockSpec(memory_space=pl.ANY)] * len(flips),
             out_specs=[block] * parts + [flip],
             scratch_shapes=[
                 pltpu.VMEM((4 * half, width), BF16),
-                pltpu.VMEM((2, rows, width), BF16),
-                pltpu.VMEM((2, rows, width), BF16),
+                pltpu.VMEM((2, 2 * half, width), BF16),
+                pltpu.VMEM((2, 2 * half, width), BF16),
                 pltpu.VMEM((4 * half, width), F32),
             ],
         ),
         out_shape=[jax.ShapeDtypeStruct(pieces[0].shape, BF16)] * parts
         + [jax.ShapeDtypeStruct((total, width, 4 * half), BF16)],
-        input_output_aliases={parts + 5: parts} if flips else {},
+        input_output_aliases={parts + 7: parts} if flips else {},
         compiler_params=pltpu.CompilerParams(vmem_limit_bytes=48 << 20),
         cost_estimate=pl.CostEstimate(
-            flops=count * (16 * half * pairs[0].size + 12 * half * rows * width),
+            flops=count * (16 * half * pairs[0].size + 12 * half * t00.shape[2] * width),
             bytes_accessed=4 * parts * pieces[0].size + 4 * pairs[0].size + 4 * t00.size,
             transcendentals=0,
         ),
         name="mix",
-    )(near, *pieces, *pairs, t00, t10, *flips)
+    )(near, *pieces, pairs[0], pairs[0], pairs[1], pairs[1], t00, t10, *flips)
 
 
 def mix_sequences_back(pieces, near, own, turned, u00, u10, lag_count, start, flips, before):
@@ -465,16 +479,21 @@
     slab = 2 * width // (parts * fars)
     lag_shape = (lag_count, slab, width)
     back_shape = (flips.shape[0], 4 * half, 2 * turned[0].shape[0])
-    back = pl.BlockSpec((1, *back_shape[1:]), lambda n, *_: (start + n, 0, 0))
-    slab_spec = pl.BlockSpec((1, slab, 4 * half), lambda n, _, own: (start + n, own[0], 0))
+    slots = turned[0].shape[0] // width // 2
+    back = pl.BlockSpec((1, 4 * half, 2 * width), lambda n, q, *_: (start + n, 0, q))
+    slab_spec = pl.BlockSpec((1, slab, 4 * half), lambda n, q, _, own: (start + n, own[0], 0))
+    turned_specs = [
+        pl.BlockSpec((2 * width, width), lambda n, q, *_: (jnp.minimum(q, slots - 1), 0)),
+        pl.BlockSpec((2 * width, width), lambda n, q, *_: (jnp.maximum(q - slots, 0), 0)),
+    ]
+    line = pl.BlockSpec((2, 2 * half, half), lambda n, q, *_: (0, q, 0))
     return pl.pallas_call(
         functools.partial(mix_back_kernel, parts),
         grid_spec=pltpu.PrefetchScalarGridSpec(
             num_scalar_prefetch=2,
-            grid=(count,),
+            grid=(count, 2 * slots),
             in_specs=[block] * parts
-            + [resident(a.shape) for a in (*turned, u00, u10)]
-            + [slab_spec]
+            + [*turned_specs, line, line, slab_spec]
             + ([pl.BlockSpec(memory_space=pl.ANY), resident(lag_shape)] if before else []),
             out_specs=[block] * parts + [back, resident(lag_shape)],
             scratch_shapes=[
@@ -501,9 +520,9 @@
 def mixing_products(flips, backs, pairs, bit, set_of):
     count, width, length = flips.shape
     slots = pairs.shape[0] // 2
-    plus = pl.BlockSpec((count, length, width), lambda k, _: (0, 0, 2 * set_of * slots + k))
+    plus = pl.BlockSpec((count, length, width), lambda k, _: (0, 0, 2 * (set_of * slots + k)))
     minus = pl.BlockSpec(
-        (count, length, width), lambda k, _: (0, 0, (2 * set_of + 1) * slots + k)
+        (count, length, width), lambda k, _: (0, 0, 2 * (set_of * slots + k) + 1)
     )
     pair = pl.BlockSpec((1, width, width), lambda k, _: (k, 0, 0))
     rest = pl.BlockSpec((1, width, width), lambda k, _: (slots + k, 0, 0))
@@ -710,7 +729,9 @@
         from_fars.append(grid.swap(kept_sums[c][1], grid.far))
         if c == 0:
             turned = [
-                value.transpose(0, 2, 1).reshape(2 * slots * width, width)
+                value.reshape(2, slots, width, width)
+                .transpose(1, 0, 3, 2)
+                .reshape(2 * slots * width, width)
                 for value in tie_all(pairs, kept_sums[0][1])
             ]
             from_fars[0] = tie(from_fars[0], *turned, *near_received[1])

time: 406 us -> 397 us (0.978)
  Pallas kernels: 140 us -> 130 us
    pallas_call x2, Pallas kernels: 45.1 us -> 38.6 us  [mix_sequences_back(): pl.pallas_call(functools.partial(mix_back_kernel, parts), grid_spec=pltpu...]
  transfers between devices with their start and end apart: 64 -> 64, of which waited for: 19 -> 19; matrix products, arithmetic and copies ran while one was open for 21% -> 21% of each run, Pallas kernels for 35% -> 33%
where the time goes in v6:
time: 397 us; the launch traced here: 393 us
  Pallas kernels  130 us (33%)
  waiting for transfers between devices  84 us (21%)
  starting transfers between devices  76.1 us (19%)
  other arithmetic  67.6 us (17%)
  local copies, waits for them, and re-layouts  31.7 us (8%)
    ppermute x28, starting transfers between devices, swap(): lax.ppermute(values, 'filt', [(f, f ^ bit) for f in range(self.size)])  45.7 us
    ppermute x28, waiting for transfers between devices, swap(): lax.ppermute(values, 'filt', [(f, f ^ bit) for f in range(self.size)])  42.1 us
    pallas_call x2, Pallas kernels, mix_sequences_back(): pl.pallas_call(functools.partial(mix_back_kernel, parts), grid_spec=pltpu...  38.6 us
    pallas_call x2, Pallas kernels, mix_sequences(): pl.pallas_call(functools.partial(mix_kernel, parts), grid_spec=pltpu.Pref...  31.6 us
    pallas_call x2, Pallas kernels, mixing_products(): pl.pallas_call(mixing_kernel, grid_spec=pltpu.PrefetchScalarGridSpec(num_...  25.4 us
    pallas_call x2, Pallas kernels, feed_forward(): pl.pallas_call(functools.partial(feed_forward_kernel, shares, len(flat_sa...  24.7 us
    ppermute x5, waiting for transfers between devices, pair_sum(): lax.ppermute(values, axis, [(r, r ^ bit) for r in range(count)])  20.4 us
    select_n x21, other arithmetic, join(): jnp.where(self.flag(bit), jnp.stack([other, own]), jnp.stack([own, other]))  15.1 us
  transfers between devices with their start and end apart: 64, of which 19 were waited for; matrix products, arithmetic and copies ran while one was open for 21% of the time, Pallas kernels for 33%

profile of v6, /device:TPU:0, one launch (start us, length us, event | category | flops | bytes accessed | tf_op | source)
XLA Modules:
  0.0 393.0 jit_solution(16030769771695377964)
XLA Ops:
  5.1 3.0 collective-permute-start.3
  9.2 3.0 collective-permute-start.8
  24.1 4.0 %collective-permute-start.5 = (bf16[4,2,1,512]{3,2,1,0:T(2,128)(2,1)S(1)}, bf16[4,2,1,512]{3,2,1,0:T(2,128)(2,1)S(1)}, u32[]{:S(2)}, u32[]{:S(2)}) collective-permute-start(bf16[4,2,1,512]{3,2,1,0:T(2,128)(2,1)S(1)} %slice.368), channel_id=1, source_target_pairs={{0,1},{1,2},{2,3},{3,4},{4,5},{5,6},{6,7},{8,9},{9,10},{10,11},{11... | collective-permute-start | bytes 24584 | tf_op jit(solution)/shard_map/ppermute | solution.py:680
  33.9 9.8 %toeplitz.1 = (bf16[2,256,3072]{2,1,0:T(8,128)(2,1)}, bf16[2,256,3072]{2,1,0:T(8,128)(2,1)}, bf16[2,3072,256]{2,1,0:T(8,128)(2,1)}, bf16[2,3072,256]{2,1,0:T(8,128)(2,1)}) custom-call(f32[12,1,768]{2,1,0:T(1,128)} %pad_convert_fusion.up_ref), custom_call_target="tpu_custom_call" | custom-call | bytes 75497472 | tf_op jit(solution)/shard_map/toeplitz/pallas_call | solution.py:193
  43.7 5.6 %collective-permute-done.4 = bf16[6,128,512]{2,1,0:T(8,128)(2,1)} collective-permute-done((bf16[6,128,512]{2,1,0:T(8,128)(2,1)}, bf16[6,128,512]{2,1,0:T(8,128)(2,1)}, u32[]{:S(2)}, u32[]{:S(2)}) %collective-permute-start.4) | collective-permute-done | bytes 786464 | tf_op jit(solution)/shard_map/ppermute | solution.py:55
  57.5 5.5 %collective-permute-done.9 = bf16[2,3,64,512]{3,2,1,0:T(8,128)(2,1)S(1)} collective-permute-done((bf16[2,3,64,512]{3,2,1,0:T(8,128)(2,1)S(1)}, bf16[2,3,64,512]{3,2,1,0:T(8,128)(2,1)S(1)}, u32[]{:S(2)}, u32[]{:S(2)}) %collective-permute-start.9) | collective-permute-done | bytes 393248 | tf_op jit(solution)/shard_map/ppermute | solution.py:55
  64.0 3.7 collective-permute-done.2.refs_1_
  68.4 7.3 %collective-permute-done.10.refs_1_ = bf16[4,1,2,64,512]{4,3,2,1,0:T(8,128)(2,1)S(1)} collective-permute-done((bf16[4,1,2,64,512]{4,3,2,1,0:T(8,128)(2,1)S(1)}, bf16[4,1,2,64,512]{4,3,2,1,0:T(8,128)(2,1)S(1)}, u32[]{:S(2)}, u32[]{:S(2)}) %collective-permute-start.10) | collective-permute-done | bytes 524320 | tf_op jit(solution)/shard_map/ppermute | solution.py:96
  79.3 3.4 pad_maximum_fusion.refs_2_.refs_3_.sum_ref.rest_ref
  90.4 15.4 %mix.2 = (bf16[4,1,2,64,512]{4,3,2,1,0:T(8,128)(2,1)S(1)}, bf16[4,1,2,64,512]{4,3,2,1,0:T(8,128)(2,1)S(1)}, bf16[2,512,1024]{2,1,0:T(8,128)(2,1)S(1)}) custom-call(s32[1]{0:T(128)} %bitcast.near_ref, bf16[4,1,2,64,512]{4,3,2,1,0:T(8,128)(2,1)S(1)} %bitcast.315, bf16[4,1,2,64,512]{4,3,2,1,0:T(8,128)(2,1)S(1)} %copy-done.4, ...), custom_call_target="tpu_custom_call" | custom-call | flops 11274289152 | bytes 14680064 | tf_op jit(solution)/shard_map/mix/pallas_call | solution.py:444
  108.9 16.2 %mix.3 = (bf16[4,1,2,64,512]{4,3,2,1,0:T(8,128)(2,1)S(1)}, bf16[4,1,2,64,512]{4,3,2,1,0:T(8,128)(2,1)}, bf16[2,512,1024]{2,1,0:T(8,128)(2,1)S(1)}) custom-call(s32[1]{0:T(128)} %bitcast.near_ref, bf16[4,1,2,64,512]{4,3,2,1,0:T(8,128)(2,1)S(1)} %bitcast.313, bf16[4,1,2,64,512]{4,3,2,1,0:T(8,128)(2,1)S(1)} %copy-done.2, ...), custom_call_target="tpu_custom_call", output_to_operand_aliasing={{2}: (9, {})} | custom-call | flops 11274289152 | bytes 14680064 | tf_op jit(solution)/shard_map/mix/pallas_call | solution.py:444
  127.1 3.4 collective-permute-start.15
  132.2 4.6 %copy.200 = bf16[3,2,512,512]{3,2,1,0:T(8,128)(2,1)} copy(bf16[3,2,512,512]{2,3,0,1:T(8,128)(2,1)} %bitcast.317) | data formatting | bytes 6291456 | tf_op jit(solution)/shard_map/transpose | solution.py:733
  136.8 4.9 %copy.199 = bf16[3,2,512,512]{3,2,1,0:T(8,128)(2,1)} copy(bf16[3,2,512,512]{2,3,0,1:T(8,128)(2,1)} %bitcast.316) | data formatting | bytes 6291456 | tf_op jit(solution)/shard_map/transpose | solution.py:733
  148.3 4.9 %collective-permute-start.14 = (bf16[2,1,2,64,512]{4,3,2,1,0:T(8,128)(2,1)S(1)}, bf16[2,1,2,64,512]{4,3,2,1,0:T(8,128)(2,1)S(1)}, u32[]{:S(2)}, u32[]{:S(2)}) collective-permute-start(bf16[2,1,2,64,512]{4,3,2,1,0:T(8,128)(2,1)S(1)} %select_convert_fusion.7), channel_id=1, source_target_pairs={{0,4},{1,5},{2,6},{3,7},{4,0},{5,1},{6,2},{7,3},{8,12},{9,13},{10,... | collective-permute-start | bytes 786440 | tf_op jit(solution)/shard_map/ppermute | solution.py:55
  155.1 9.6 %feed_forward.2 = (bf16[2,2,64,512]{3,2,1,0:T(8,128)(2,1)}, f32[2,2,64,512]{3,2,1,0:T(8,128)}, bf16[1,2,2,64,512]{4,3,2,1,0:T(8,128)(2,1)}, f32[1,512]{1,0:T(1,1...) custom-call(bf16[1,2,2,64,512]{4,3,2,1,0:T(8,128)(2,1)} %bitcast.376, ...), custom_call_target="tpu_custom_call" | custom-call | flops 3221225472 | bytes 11534336 | tf_op jit(solution)/shard_map/feed_forward/pallas_call | solution.py:569
  167.9 4.3 %collective-permute-done.22 = bf16[1,2,64,512]{3,2,1,0:T(8,128)(2,1)S(1)} collective-permute-done((bf16[1,2,64,512]{3,2,1,0:T(8,128)(2,1)S(1)}, bf16[1,2,64,512]{3,2,1,0:T(8,128)(2,1)S(1)}, u32[]{:S(2)}, u32[]{:S(2)}) %collective-permute-start.22) | collective-permute-done | bytes 131104 | tf_op jit(solution)/shard_map/ppermute | solution.py:55
  172.2 4.9 %collective-permute-start.23 = (bf16[2,1,2,64,512]{4,3,2,0,1:T(8,128)(2,1)S(1)}, bf16[2,1,2,64,512]{4,3,2,0,1:T(8,128)(2,1)S(1)}, u32[]{:S(2)}, u32[]{:S(2)}) collective-permute-start(bf16[2,1,2,64,512]{4,3,2,0,1:T(8,128)(2,1)S(1)} %fusion.29), channel_id=1, source_target_pairs={{0,4},{1,5},{2,6},{3,7},{4,0},{5,1},{6,2},{7,3},{8,12},{9,13},{10,... | collective-permute-start | bytes 786440 | tf_op jit(solution)/shard_map/ppermute | solution.py:55
  177.8 15.1 %feed_forward.3 = (bf16[2,2,64,512]{3,2,1,0:T(8,128)(2,1)}, f32[2,2,64,512]{3,2,1,0:T(8,128)}, bf16[1,2,2,64,512]{4,3,2,1,0:T(8,128)(2,1)}, f32[1,512]{1,0:T(1,1...) custom-call(bf16[1,2,2,64,512]{4,3,2,1,0:T(8,128)(2,1)} %bitcast.375, ...), custom_call_target="tpu_custom_call" | custom-call | flops 6442450944 | bytes 11534336 | tf_op jit(solution)/shard_map/feed_forward/pallas_call | solution.py:569
  207.6 9.3 %collective-permute-done.25 = bf16[2,1,2,64,512]{4,3,2,0,1:T(8,128)(2,1)} collective-permute-done((bf16[2,1,2,64,512]{4,3,2,0,1:T(8,128)(2,1)}, bf16[2,1,2,64,512]{4,3,2,0,1:T(8,128)(2,1)}, u32[]{:S(2)}, u32[]{:S(2)}) %collective-permute-start.25) | collective-permute-done | bytes 262176 | tf_op jit(solution)/shard_map/ppermute | solution.py:55
  221.2 19.1 %mix_back.2 = (bf16[4,1,2,64,512]{4,3,2,1,0:T(8,128)(2,1)}, bf16[4,1,2,64,512]{4,3,2,1,0:T(8,128)(2,1)}, bf16[2,1024,6144]{2,1,0:T(8,128)(2,1)}, f32[3,128,512]{2,1,0:T(8,128)}) custom-call(s32[1]{0:T(128)} %bitcast.near_ref, s32[1]{0:T(128)} %bitcast.1.own_ref, bf16[4,1,2,64,512]{4,3,2,1,0:T(8,128)(2,1)} %bitcast.73.refs_0_, ...), custom_call_target="tpu_custom_call" | custom-call | flops 11274289152 | bytes 14680064 | tf_op jit(solution)/shard_map/mix_back/pallas_call | solution.py:490
  243.5 19.5 %mix_back.3 = (bf16[4,1,2,64,512]{4,3,2,1,0:T(8,128)(2,1)}, bf16[4,1,2,64,512]{4,3,2,1,0:T(8,128)(2,1)}, bf16[2,1024,6144]{2,1,0:T(8,128)(2,1)}, f32[3,128,512]{2,1,0:T(8,128)}) custom-call(s32[1]{0:T(128)} %bitcast.near_ref, s32[1]{0:T(128)} %bitcast.1.own_ref, bf16[4,1,2,64,512]{4,3,2,1,0:T(8,128)(2,1)} %bitcast.367, ...), custom_call_target="tpu_custom_call", output_to_operand_aliasing={{2}: (9, {})} | custom-call | flops 11274289152 | bytes 14680064 | tf_op jit(solution)/shard_map/mix_back/pallas_call | solution.py:490
  267.0 12.7 %mixing_products.2 = (f32[6,256,512]{2,1,0:T(8,128)}, bf16[6,256,512]{2,1,0:T(8,128)(2,1)}, f32[512,1]{1,0:T(8,128)}) custom-call(s32[1]{0:T(128)} %bitcast.83.bit_ref, bf16[2,512,1024]{2,1,0:T(8,128)(2,1)} %copy-done, bf16[2,1024,6144]{2,1,0:T(8,128)(2,1)} %get-tuple-element.229.plus_ref.minus_ref, ...), custom_call_target="tpu_custom_call" | custom-call | flops 6442450944 | bytes 20971520 | tf_op jit(solution)/shard_map/mixing_products/pallas_call | solution.py:530
  282.1 3.2 broadcast_select_fusion.6
  292.2 12.7 %mixing_products.3 = (f32[6,256,512]{2,1,0:T(8,128)}, bf16[6,256,512]{2,1,0:T(8,128)(2,1)}, f32[512,1]{1,0:T(8,128)}) custom-call(s32[1]{0:T(128)} %bitcast.83.bit_ref, bf16[2,512,1024]{2,1,0:T(8,128)(2,1)} %copy-done, bf16[2,1024,6144]{2,1,0:T(8,128)(2,1)} %get-tuple-element.229.plus_ref.minus_ref, ...), custom_call_target="tpu_custom_call" | custom-call | flops 6442450944 | bytes 20971520 | tf_op jit(solution)/shard_map/mixing_products/pallas_call | solution.py:530
  306.2 3.9 %collective-permute-done.40 = bf16[6,128,512]{2,1,0:T(8,128)(2,1)} collective-permute-done((bf16[6,128,512]{2,1,0:T(8,128)(2,1)}, bf16[6,128,512]{2,1,0:T(8,128)(2,1)}, u32[]{:S(2)}, u32[]{:S(2)}) %collective-permute-start.40) | collective-permute-done | bytes 786464 | tf_op jit(solution)/shard_map/ppermute | solution.py:112
  320.9 16.6 %collective-permute-done.56 = f32[8,512]{1,0:T(8,128)S(1)} collective-permute-done((f32[8,512]{1,0:T(8,128)S(1)}, f32[8,512]{1,0:T(8,128)S(1)}, u32[]{:S(2)}, u32[]{:S(2)}) %collective-permute-start.56) | collective-permute-done | bytes 16416 | tf_op jit(solution)/shard_map/ppermute | solution.py:149
  348.9 5.9 %collective-permute-done.51 = bf16[2,3,16,512]{3,2,1,0:T(8,128)(2,1)S(1)} collective-permute-done((bf16[2,3,16,512]{3,2,1,0:T(8,128)(2,1)S(1)}, bf16[2,3,16,512]{3,2,1,0:T(8,128)(2,1)S(1)}, u32[]{:S(2)}, u32[]{:S(2)}) %collective-permute-start.51) | collective-permute-done | bytes 98336 | tf_op jit(solution)/shard_map/ppermute | solution.py:55
  356.6 4.0 %collective-permute-done.52 = bf16[2,2,3,16,512]{4,3,2,1,0:T(8,128)(2,1)S(1)} collective-permute-done((bf16[2,2,3,16,512]{4,3,2,1,0:T(8,128)(2,1)S(1)}, bf16[2,2,3,16,512]{4,3,2,1,0:T(8,128)(2,1)S(1)}, u32[]{:S(2)}, u32[]{:S(2)}) %collective-permute-start.52) | collective-permute-done | bytes 196640 | tf_op jit(solution)/shard_map/ppermute | solution.py:55
  367.7 3.8 collective-permute-done.59
  373.9 3.4 collective-permute-done.62
  389.2 3.6 maximum_convert_fusion
  (340 shorter events, 144.6 us)
Async XLA Ops:
  9.2 41.3 %collective-permute-start.8 = (bf16[3,64,512]{2,1,0:T(8,128)(2,1)}, bf16[3,64,512]{2,1,0:T(8,128)(2,1)}, u32[]{:S(2)}, u32[]{:S(2)}) collective-permute-start(bf16[3,64,512]{2,1,0:T(8,128)(2,1)} %fusion.33), channel_id=1, source_target_pairs={{0,4},{1,5},{2,6},{3,7},{4,0},{5,1},{6,2},{7,3},{8,12},{9,13},{10,... | collective-permute-start | bytes 589832 | tf_op jit(solution)/shard_map/ppermute | solution.py:55
  19.0 30.3 %collective-permute-start.4 = (bf16[6,128,512]{2,1,0:T(8,128)(2,1)}, bf16[6,128,512]{2,1,0:T(8,128)(2,1)}, u32[]{:S(2)}, u32[]{:S(2)}) collective-permute-start(bf16[6,128,512]{2,1,0:T(8,128)(2,1)} %fusion.8), channel_id=1, source_target_pairs={{0,2},{1,3},{2,0},{3,1},{4,6},{5,7},{6,4},{7,5},{8,10},{9,11},{10,... | collective-permute-start | bytes 2359304 | tf_op jit(solution)/shard_map/ppermute | solution.py:55
  20.0 23.7 %collective-permute-start.6 = (bf16[2,1,2,64,512]{4,3,2,0,1:T(8,128)(2,1)S(1)}, bf16[2,1,2,64,512]{4,3,2,0,1:T(8,128)(2,1)}, u32[]{:S(2)}, u32[]{:S(2)}) collective-permute-start(bf16[2,1,2,64,512]{4,3,2,0,1:T(8,128)(2,1)S(1)} %maximum_select_fusion.7), channel_id=1, source_target_pairs={{0,4},{1,5},{2,6},{3,7},{4,0},{5,1},{6,2},{7,3},{8,12},{9,13},{10,... | collective-permute-start | bytes 786440 | tf_op jit(solution)/shard_map/ppermute | solution.py:55
  23.3 28.3 %collective-permute-start.1 = (bf16[2,1,2,64,512]{4,3,2,0,1:T(8,128)(2,1)S(1)}, bf16[2,1,2,64,512]{4,3,2,0,1:T(8,128)(2,1)}, u32[]{:S(2)}, u32[]{:S(2)}) collective-permute-start(bf16[2,1,2,64,512]{4,3,2,0,1:T(8,128)(2,1)S(1)} %maximum_select_fusion.6), channel_id=1, source_target_pairs={{0,4},{1,5},{2,6},{3,7},{4,0},{5,1},{6,2},{7,3},{8,12},{9,13},{10,... | collective-permute-start | bytes 786440 | tf_op jit(solution)/shard_map/ppermute | solution.py:55
  24.1 19.6 %collective-permute-start.5 = (bf16[4,2,1,512]{3,2,1,0:T(2,128)(2,1)S(1)}, bf16[4,2,1,512]{3,2,1,0:T(2,128)(2,1)S(1)}, u32[]{:S(2)}, u32[]{:S(2)}) collective-permute-start(bf16[4,2,1,512]{3,2,1,0:T(2,128)(2,1)S(1)} %slice.368), channel_id=1, source_target_pairs={{0,1},{1,2},{2,3},{3,4},{4,5},{5,6},{6,7},{8,9},{9,10},{10,11},{11... | collective-permute-start | bytes 24584 | tf_op jit(solution)/shard_map/ppermute | solution.py:680
  49.3 27.3 %collective-permute-start.7 = (bf16[6,128,512]{2,1,0:T(8,128)(2,1)}, bf16[6,128,512]{2,1,0:T(8,128)(2,1)S(1)}, u32[]{:S(2)}, u32[]{:S(2)}) collective-permute-start(bf16[6,128,512]{2,1,0:T(8,128)(2,1)} %collective-permute-done.4), channel_id=1, source_target_pairs={{0,16},{8,24},{16,0},{24,8},{1,17},{9,25},{17,1},{25,9},{2,18},{10... | collective-permute-start | bytes 2359304 | tf_op jit(solution)/shard_map/ppermute | solution.py:112
  55.5 20.3 %collective-permute-start.10 = (bf16[4,1,2,64,512]{4,3,2,1,0:T(8,128)(2,1)S(1)}, bf16[4,1,2,64,512]{4,3,2,1,0:T(8,128)(2,1)S(1)}, u32[]{:S(2)}, u32[]{:S(2)}) collective-permute-start(bf16[4,1,2,64,512]{4,3,2,1,0:T(8,128)(2,1)S(1)} %bitcast.314), channel_id=1, source_target_pairs={{0,1},{1,0},{2,3},{3,2},{4,5},{5,4},{6,7},{7,6},{8,9},{9,8},{10,11... | collective-permute-start | bytes 1572872 | tf_op jit(solution)/shard_map/ppermute | solution.py:96
  84.8 21.1 %collective-permute-start.17 = (bf16[2,2,3,64,512]{4,3,2,1,0:T(8,128)(2,1)S(1)}, bf16[2,2,3,64,512]{4,3,2,1,0:T(8,128)(2,1)S(1)}, u32[]{:S(2)}, u32[]{:S(2)}) collective-permute-start(bf16[2,2,3,64,512]{4,3,2,1,0:T(8,128)(2,1)S(1)} %copy-done.17), channel_id=1, source_target_pairs={{0,1},{1,0},{2,3},{3,2},{4,5},{5,4},{6,7},{7,6},{8,9},{9,8},{10,11... | collective-permute-start | bytes 2359304 | tf_op jit(solution)/shard_map/ppermute | solution.py:55
  105.9 19.2 %collective-permute-start.12 = (bf16[4,1,2,64,512]{4,3,2,1,0:T(8,128)(2,1)S(1)}, bf16[4,1,2,64,512]{4,3,2,1,0:T(8,128)(2,1)S(1)}, u32[]{:S(2)}, u32[]{:S(2)}) collective-permute-start(bf16[4,1,2,64,512]{4,3,2,1,0:T(8,128)(2,1)S(1)} %get-tuple-element.154), channel_id=1, source_target_pairs={{0,1},{1,0},{2,3},{3,2},{4,5},{5,4},{6,7},{7,6},{8,9},{9,8},{10,11... | collective-permute-start | bytes 1572872 | tf_op jit(solution)/shard_map/ppermute | solution.py:96
  107.9 36.6 %collective-permute-start.18 = (bf16[8,3,64,512]{3,2,1,0:T(8,128)(2,1)}, bf16[8,3,64,512]{3,2,1,0:T(8,128)(2,1)}, u32[]{:S(2)}, u32[]{:S(2)}) collective-permute-start(bf16[8,3,64,512]{3,2,1,0:T(8,128)(2,1)} %bitcast.48.refs_0_), channel_id=1, source_target_pairs={{0,16},{8,24},{16,0},{24,8},{1,17},{9,25},{17,1},{25,9},{2,18},{10... | collective-permute-start | bytes 4718600 | tf_op jit(solution)/shard_map/ppermute | solution.py:112
  125.1 17.1 %collective-permute-start.13 = (bf16[4,1,2,64,512]{4,3,2,1,0:T(8,128)(2,1)}, bf16[4,1,2,64,512]{4,3,2,1,0:T(8,128)(2,1)S(1)}, u32[]{:S(2)}, u32[]{:S(2)}) collective-permute-start(bf16[4,1,2,64,512]{4,3,2,1,0:T(8,128)(2,1)} %get-tuple-element.157), channel_id=1, source_target_pairs={{0,1},{1,0},{2,3},{3,2},{4,5},{5,4},{6,7},{7,6},{8,9},{9,8},{10,11... | collective-permute-start | bytes 1572872 | tf_op jit(solution)/shard_map/ppermute | solution.py:96
  132.2 21.8 %collective-permute-start.19 = (bf16[8,3,64,512]{3,2,1,0:T(8,128)(2,1)}, bf16[8,3,64,512]{3,2,1,0:T(8,128)(2,1)}, u32[]{:S(2)}, u32[]{:S(2)}) collective-permute-start(bf16[8,3,64,512]{3,2,1,0:T(8,128)(2,1)} %bitcast.48.refs_0_), channel_id=1, source_target_pairs={{0,8},{8,0},{16,24},{24,16},{1,9},{9,1},{17,25},{25,17},{2,10},{10... | collective-permute-start | bytes 4718600 | tf_op jit(solution)/shard_map/ppermute | solution.py:112
  148.3 17.3 %collective-permute-start.14 = (bf16[2,1,2,64,512]{4,3,2,1,0:T(8,128)(2,1)S(1)}, bf16[2,1,2,64,512]{4,3,2,1,0:T(8,128)(2,1)S(1)}, u32[]{:S(2)}, u32[]{:S(2)}) collective-permute-start(bf16[2,1,2,64,512]{4,3,2,1,0:T(8,128)(2,1)S(1)} %select_convert_fusion.7), channel_id=1, source_target_pairs={{0,4},{1,5},{2,6},{3,7},{4,0},{5,1},{6,2},{7,3},{8,12},{9,13},{10,... | collective-permute-start | bytes 786440 | tf_op jit(solution)/shard_map/ppermute | solution.py:55
  172.2 20.7 %collective-permute-start.23 = (bf16[2,1,2,64,512]{4,3,2,0,1:T(8,128)(2,1)S(1)}, bf16[2,1,2,64,512]{4,3,2,0,1:T(8,128)(2,1)S(1)}, u32[]{:S(2)}, u32[]{:S(2)}) collective-permute-start(bf16[2,1,2,64,512]{4,3,2,0,1:T(8,128)(2,1)S(1)} %fusion.29), channel_id=1, source_target_pairs={{0,4},{1,5},{2,6},{3,7},{4,0},{5,1},{6,2},{7,3},{8,12},{9,13},{10,... | collective-permute-start | bytes 786440 | tf_op jit(solution)/shard_map/ppermute | solution.py:55
  192.9 25.6 %collective-permute-start.28 = (bf16[8,3,64,512]{3,2,1,0:T(8,128)(2,1)}, bf16[8,3,64,512]{3,2,1,0:T(8,128)(2,1)}, u32[]{:S(2)}, u32[]{:S(2)}) collective-permute-start(bf16[8,3,64,512]{3,2,1,0:T(8,128)(2,1)} %get-tuple-element.187), channel_id=1, source_target_pairs={{0,8},{8,0},{16,24},{24,16},{1,9},{9,1},{17,25},{25,17},{2,10},{10... | collective-permute-start | bytes 4718600 | tf_op jit(solution)/shard_map/ppermute | solution.py:112
  193.0 25.5 %collective-permute-start.29 = (bf16[8,3,64,512]{3,2,1,0:T(8,128)(2,1)}, bf16[8,3,64,512]{3,2,1,0:T(8,128)(2,1)}, u32[]{:S(2)}, u32[]{:S(2)}) collective-permute-start(bf16[8,3,64,512]{3,2,1,0:T(8,128)(2,1)} %get-tuple-element.188), channel_id=1, source_target_pairs={{0,8},{8,0},{16,24},{24,16},{1,9},{9,1},{17,25},{25,17},{2,10},{10... | collective-permute-start | bytes 4718600 | tf_op jit(solution)/shard_map/ppermute | solution.py:112
  198.5 20.0 %collective-permute-start.30 = (bf16[4,1,2,64,512]{4,3,2,1,0:T(8,128)(2,1)}, bf16[4,1,2,64,512]{4,3,2,1,0:T(8,128)(2,1)}, u32[]{:S(2)}, u32[]{:S(2)}) collective-permute-start(bf16[4,1,2,64,512]{4,3,2,1,0:T(8,128)(2,1)} %bitcast.72), channel_id=1, source_target_pairs={{0,1},{1,0},{2,3},{3,2},{4,5},{5,4},{6,7},{7,6},{8,9},{9,8},{10,11... | collective-permute-start | bytes 1572872 | tf_op jit(solution)/shard_map/ppermute | solution.py:96
  218.0 22.4 %collective-permute-start.26 = (bf16[4,1,2,64,512]{4,3,2,1,0:T(8,128)(2,1)S(1)}, bf16[4,1,2,64,512]{4,3,2,1,0:T(8,128)(2,1)S(1)}, u32[]{:S(2)}, u32[]{:S(2)}) collective-permute-start(bf16[4,1,2,64,512]{4,3,2,1,0:T(8,128)(2,1)S(1)} %bitcast.366), channel_id=1, source_target_pairs={{0,1},{1,0},{2,3},{3,2},{4,5},{5,4},{6,7},{7,6},{8,9},{9,8},{10,11... | collective-permute-start | bytes 1572872 | tf_op jit(solution)/shard_map/ppermute | solution.py:96
  220.6 21.3 %collective-permute-start.31 = (bf16[4,3,64,512]{3,2,1,0:T(8,128)(2,1)S(1)}, bf16[4,3,64,512]{3,2,1,0:T(8,128)(2,1)S(1)}, u32[]{:S(2)}, u32[]{:S(2)}) collective-permute-start(bf16[4,3,64,512]{3,2,1,0:T(8,128)(2,1)S(1)} %get-tuple-element.318), channel_id=1, source_target_pairs={{0,16},{8,24},{16,0},{24,8},{1,17},{9,25},{17,1},{25,9},{2,18},{10... | collective-permute-start | bytes 2359304 | tf_op jit(solution)/shard_map/ppermute | solution.py:112
  240.3 22.7 %collective-permute-start.33 = (bf16[4,3,64,512]{3,2,1,0:T(8,128)(2,1)S(1)}, bf16[4,3,64,512]{3,2,1,0:T(8,128)(2,1)S(1)}, u32[]{:S(2)}, u32[]{:S(2)}) collective-permute-start(bf16[4,3,64,512]{3,2,1,0:T(8,128)(2,1)S(1)} %get-tuple-element.207), channel_id=1, source_target_pairs={{0,16},{8,24},{16,0},{24,8},{1,17},{9,25},{17,1},{25,9},{2,18},{10... | collective-permute-start | bytes 2359304 | tf_op jit(solution)/shard_map/ppermute | solution.py:112
  241.9 21.2 %collective-permute-start.32 = (bf16[4,1,2,64,512]{4,3,2,1,0:T(8,128)(2,1)}, bf16[4,1,2,64,512]{4,3,2,1,0:T(8,128)(2,1)S(1)}, u32[]{:S(2)}, u32[]{:S(2)}) collective-permute-start(bf16[4,1,2,64,512]{4,3,2,1,0:T(8,128)(2,1)} %get-tuple-element.205), channel_id=1, source_target_pairs={{0,1},{1,0},{2,3},{3,2},{4,5},{5,4},{6,7},{7,6},{8,9},{9,8},{10,11... | collective-permute-start | bytes 1572872 | tf_op jit(solution)/shard_map/ppermute | solution.py:96
  264.4 23.0 %collective-permute-start.39 = (bf16[4,1,2,64,512]{4,3,2,1,0:T(8,128)(2,1)}, bf16[4,1,2,64,512]{4,3,2,1,0:T(8,128)(2,1)}, u32[]{:S(2)}, u32[]{:S(2)}) collective-permute-start(bf16[4,1,2,64,512]{4,3,2,1,0:T(8,128)(2,1)} %get-tuple-element.227), channel_id=1, source_target_pairs={{0,1},{1,0},{2,3},{3,2},{4,5},{5,4},{6,7},{7,6},{8,9},{9,8},{10,11... | collective-permute-start | bytes 1572872 | tf_op jit(solution)/shard_map/ppermute | solution.py:96
  266.5 20.3 %collective-permute-start.35 = (bf16[3,32,512]{2,1,0:T(8,128)(2,1)}, bf16[3,32,512]{2,1,0:T(8,128)(2,1)S(1)}, u32[]{:S(2)}, u32[]{:S(2)}) collective-permute-start(bf16[3,32,512]{2,1,0:T(8,128)(2,1)} %fusion.35), channel_id=1, source_target_pairs={{0,16},{8,24},{16,0},{24,8},{1,17},{9,25},{17,1},{25,9},{2,18},{10... | collective-permute-start | bytes 294920 | tf_op jit(solution)/shard_map/ppermute | solution.py:112
  279.9 26.2 %collective-permute-start.41 = (bf16[1,2,64,512]{3,2,1,0:T(8,128)(2,1)S(1)}, bf16[1,2,64,512]{3,2,1,0:T(8,128)(2,1)S(1)}, u32[]{:S(2)}, u32[]{:S(2)}) collective-permute-start(bf16[1,2,64,512]{3,2,1,0:T(8,128)(2,1)S(1)} %get-tuple-element.345), channel_id=1, source_target_pairs={{0,2},{1,3},{2,0},{3,1},{4,6},{5,7},{6,4},{7,5},{8,10},{9,11},{10,... | collective-permute-start | bytes 393224 | tf_op jit(solution)/shard_map/ppermute | solution.py:55
  285.3 28.4 %collective-permute-start.43 = (bf16[2,2,3,64,512]{4,3,2,1,0:T(8,128)(2,1)}, bf16[2,2,3,64,512]{4,3,2,1,0:T(8,128)(2,1)}, u32[]{:S(2)}, u32[]{:S(2)}) collective-permute-start(bf16[2,2,3,64,512]{4,3,2,1,0:T(8,128)(2,1)} %bitcast.95), channel_id=1, source_target_pairs={{0,1},{1,0},{2,3},{3,2},{4,5},{5,4},{6,7},{7,6},{8,9},{9,8},{10,11... | collective-permute-start | bytes 2359304 | tf_op jit(solution)/shard_map/ppermute | solution.py:55
  290.4 19.7 %collective-permute-start.40 = (bf16[6,128,512]{2,1,0:T(8,128)(2,1)}, bf16[6,128,512]{2,1,0:T(8,128)(2,1)}, u32[]{:S(2)}, u32[]{:S(2)}) collective-permute-start(bf16[6,128,512]{2,1,0:T(8,128)(2,1)} %fusion.6), channel_id=1, source_target_pairs={{0,16},{8,24},{16,0},{24,8},{1,17},{9,25},{17,1},{25,9},{2,18},{10... | collective-permute-start | bytes 2359304 | tf_op jit(solution)/shard_map/ppermute | solution.py:112
  312.0 32.4 %collective-permute-start.47 = (bf16[1,2,64,512]{3,2,1,0:T(8,128)(2,1)S(1)}, bf16[1,2,64,512]{3,2,1,0:T(8,128)(2,1)S(1)}, u32[]{:S(2)}, u32[]{:S(2)}) collective-permute-start(bf16[1,2,64,512]{3,2,1,0:T(8,128)(2,1)S(1)} %get-tuple-element.343), channel_id=1, source_target_pairs={{0,2},{1,3},{2,0},{3,1},{4,6},{5,7},{6,4},{7,5},{8,10},{9,11},{10,... | collective-permute-start | bytes 393224 | tf_op jit(solution)/shard_map/ppermute | solution.py:55
  316.0 21.5 %collective-permute-start.46 = (bf16[6,128,512]{2,1,0:T(8,128)(2,1)S(1)}, bf16[6,128,512]{2,1,0:T(8,128)(2,1)S(1)}, u32[]{:S(2)}, u32[]{:S(2)}) collective-permute-start(bf16[6,128,512]{2,1,0:T(8,128)(2,1)S(1)} %fusion.2), channel_id=1, source_target_pairs={{0,2},{1,3},{2,0},{3,1},{4,6},{5,7},{6,4},{7,5},{8,10},{9,11},{10,... | collective-permute-start | bytes 2359304 | tf_op jit(solution)/shard_map/ppermute | solution.py:55
  317.3 20.2 %collective-permute-start.45 = (bf16[6,128,512]{2,1,0:T(8,128)(2,1)S(1)}, bf16[6,128,512]{2,1,0:T(8,128)(2,1)S(1)}, u32[]{:S(2)}, u32[]{:S(2)}) collective-permute-start(bf16[6,128,512]{2,1,0:T(8,128)(2,1)S(1)} %fusion.7), channel_id=1, source_target_pairs={{0,16},{8,24},{16,0},{24,8},{1,17},{9,25},{17,1},{25,9},{2,18},{10... | collective-permute-start | bytes 2359304 | tf_op jit(solution)/shard_map/ppermute | solution.py:112
  320.2 17.2 %collective-permute-start.56 = (f32[8,512]{1,0:T(8,128)S(1)}, f32[8,512]{1,0:T(8,128)S(1)}, u32[]{:S(2)}, u32[]{:S(2)}) collective-permute-start(f32[8,512]{1,0:T(8,128)S(1)} %fusion.44), channel_id=1, source_target_pairs={{0,16},{8,24},{16,0},{24,8},{1,17},{9,25},{17,1},{25,9},{2,18},{10... | collective-permute-start | bytes 49160 | tf_op jit(solution)/shard_map/ppermute | solution.py:149
  338.2 39.2 %collective-permute-start.48 = (bf16[6,128,512]{2,1,0:T(8,128)(2,1)S(1)}, bf16[6,128,512]{2,1,0:T(8,128)(2,1)S(1)}, u32[]{:S(2)}, u32[]{:S(2)}) collective-permute-start(bf16[6,128,512]{2,1,0:T(8,128)(2,1)S(1)} %fusion.4), channel_id=1, source_target_pairs={{0,16},{8,24},{16,0},{24,8},{1,17},{9,25},{17,1},{25,9},{2,18},{10... | collective-permute-start | bytes 2359304 | tf_op jit(solution)/shard_map/ppermute | solution.py:112
  342.1 19.2 %collective-permute-start.60 = (bf16[2,3,64,512]{3,2,1,0:T(8,128)(2,1)S(1)}, bf16[2,3,64,512]{3,2,1,0:T(8,128)(2,1)S(1)}, u32[]{:S(2)}, u32[]{:S(2)}) collective-permute-start(bf16[2,3,64,512]{3,2,1,0:T(8,128)(2,1)S(1)} %fusion.25), channel_id=1, source_target_pairs={{0,2},{1,3},{2,0},{3,1},{4,6},{5,7},{6,4},{7,5},{8,10},{9,11},{10,... | collective-permute-start | bytes 1179656 | tf_op jit(solution)/shard_map/ppermute | solution.py:55
  (79 other events, 544.6 us)

commit v7 on v6

--- a/solution.py
+++ b/solution.py
@@ -137,9 +137,10 @@
         other = swap_rows(full, bit)
         if n == 0:
             other = tie(other, *after)
-        full = jnp.concatenate(
-            [jnp.where(high, other, full), jnp.where(high, full, other)], axis=1
-        )
+        parts, height, width = full.shape
+        full = jnp.where(
+            high, jnp.stack([other, full], axis=1), jnp.stack([full, other], axis=1)
+        ).reshape(parts, 2 * height, width)
     return full
 
 

time: 397 us -> 396 us (level)
  other arithmetic: 67.6 us -> 58.5 us
  local copies, waits for them, and re-layouts: 31.7 us -> 39.5 us
    concatenate x6 -> x0, other arithmetic: 5.78 us -> none  [gather_rows(): jnp.concatenate([jnp.where(high, other, full), jnp.where(high, full, othe...]
  transfers between devices with their start and end apart: 64 -> 64, of which waited for: 19 -> 22; matrix products, arithmetic and copies ran while one was open for 21% -> 20% of each run, Pallas kernels for 33% -> 33%
where the time goes in v7:
time: 396 us; the launch traced here: 392 us
  Pallas kernels  130 us (33%)
  waiting for transfers between devices  84.8 us (21%)
  starting transfers between devices  76.1 us (19%)
  other arithmetic  58.5 us (15%)
  local copies, waits for them, and re-layouts  39.5 us (10%)
    ppermute x28, starting transfers between devices, swap(): lax.ppermute(values, 'filt', [(f, f ^ bit) for f in range(self.size)])  47.5 us
    ppermute x28, waiting for transfers between devices, swap(): lax.ppermute(values, 'filt', [(f, f ^ bit) for f in range(self.size)])  46 us
    pallas_call x2, Pallas kernels, mix_sequences_back(): pl.pallas_call(functools.partial(mix_back_kernel, parts), grid_spec=pltpu...  38.6 us
    pallas_call x2, Pallas kernels, mix_sequences(): pl.pallas_call(functools.partial(mix_kernel, parts), grid_spec=pltpu.Pref...  31.6 us
    pallas_call x2, Pallas kernels, mixing_products(): pl.pallas_call(mixing_kernel, grid_spec=pltpu.PrefetchScalarGridSpec(num_...  25.4 us
    pallas_call x2, Pallas kernels, feed_forward(): pl.pallas_call(functools.partial(feed_forward_kernel, shares, len(flat_sa...  24.7 us
    ppermute x5, waiting for transfers between devices, pair_sum(): lax.ppermute(values, axis, [(r, r ^ bit) for r in range(count)])  16.8 us
    select_n x21, other arithmetic, join(): jnp.where(self.flag(bit), jnp.stack([other, own]), jnp.stack([own, other]))  14.3 us
  transfers between devices with their start and end apart: 64, of which 22 were waited for; matrix products, arithmetic and copies ran while one was open for 20% of the time, Pallas kernels for 33%

profile of v7, /device:TPU:0, one launch (start us, length us, event | category | flops | bytes accessed | tf_op | source)
XLA Modules:
  0.0 392.5 jit_solution(11484010607402217606)
XLA Ops:
  5.1 3.0 collective-permute-start.3
  9.2 3.0 collective-permute-start.8
  24.1 4.0 %collective-permute-start.5 = (bf16[4,2,1,512]{3,2,1,0:T(2,128)(2,1)S(1)}, bf16[4,2,1,512]{3,2,1,0:T(2,128)(2,1)S(1)}, u32[]{:S(2)}, u32[]{:S(2)}) collective-permute-start(bf16[4,2,1,512]{3,2,1,0:T(2,128)(2,1)S(1)} %slice.371), channel_id=1, source_target_pairs={{0,1},{1,2},{2,3},{3,4},{4,5},{5,6},{6,7},{8,9},{9,10},{10,11},{11... | collective-permute-start | bytes 24584 | tf_op jit(solution)/shard_map/ppermute | solution.py:681
  33.9 9.7 %toeplitz.1 = (bf16[2,256,3072]{2,1,0:T(8,128)(2,1)}, bf16[2,256,3072]{2,1,0:T(8,128)(2,1)}, bf16[2,3072,256]{2,1,0:T(8,128)(2,1)}, bf16[2,3072,256]{2,1,0:T(8,128)(2,1)}) custom-call(f32[12,1,768]{2,1,0:T(1,128)} %pad_convert_fusion.up_ref), custom_call_target="tpu_custom_call" | custom-call | bytes 75497472 | tf_op jit(solution)/shard_map/toeplitz/pallas_call | solution.py:194
  43.7 5.6 %collective-permute-done.4 = bf16[6,128,512]{2,1,0:T(8,128)(2,1)} collective-permute-done((bf16[6,128,512]{2,1,0:T(8,128)(2,1)}, bf16[6,128,512]{2,1,0:T(8,128)(2,1)}, u32[]{:S(2)}, u32[]{:S(2)}) %collective-permute-start.4) | collective-permute-done | bytes 786464 | tf_op jit(solution)/shard_map/ppermute | solution.py:55
  57.5 5.5 %collective-permute-done.9 = bf16[2,3,64,512]{3,2,1,0:T(8,128)(2,1)S(1)} collective-permute-done((bf16[2,3,64,512]{3,2,1,0:T(8,128)(2,1)S(1)}, bf16[2,3,64,512]{3,2,1,0:T(8,128)(2,1)S(1)}, u32[]{:S(2)}, u32[]{:S(2)}) %collective-permute-start.9) | collective-permute-done | bytes 393248 | tf_op jit(solution)/shard_map/ppermute | solution.py:55
  63.1 4.6 %collective-permute-done.2.refs_1_ = bf16[4,1,2,64,512]{4,3,2,1,0:T(8,128)(2,1)S(1)} collective-permute-done((bf16[4,1,2,64,512]{4,3,2,1,0:T(8,128)(2,1)S(1)}, bf16[4,1,2,64,512]{4,3,2,1,0:T(8,128)(2,1)S(1)}, u32[]{:S(2)}, u32[]{:S(2)}) %collective-permute-start.2) | collective-permute-done | bytes 524320 | tf_op jit(solution)/shard_map/ppermute | solution.py:96
  68.4 7.3 %collective-permute-done.10.refs_1_ = bf16[4,1,2,64,512]{4,3,2,1,0:T(8,128)(2,1)S(1)} collective-permute-done((bf16[4,1,2,64,512]{4,3,2,1,0:T(8,128)(2,1)S(1)}, bf16[4,1,2,64,512]{4,3,2,1,0:T(8,128)(2,1)S(1)}, u32[]{:S(2)}, u32[]{:S(2)}) %collective-permute-start.10) | collective-permute-done | bytes 524320 | tf_op jit(solution)/shard_map/ppermute | solution.py:96
  79.7 3.4 pad_maximum_fusion.refs_2_.refs_3_.sum_ref.rest_ref
  86.7 3.4 maximum_select_fusion
  92.0 15.4 %mix.2 = (bf16[4,1,2,64,512]{4,3,2,1,0:T(8,128)(2,1)S(1)}, bf16[4,1,2,64,512]{4,3,2,1,0:T(8,128)(2,1)S(1)}, bf16[2,512,1024]{2,1,0:T(8,128)(2,1)S(1)}) custom-call(s32[1]{0:T(128)} %bitcast.near_ref, bf16[4,1,2,64,512]{4,3,2,1,0:T(8,128)(2,1)S(1)} %bitcast.331, bf16[4,1,2,64,512]{4,3,2,1,0:T(8,128)(2,1)S(1)} %copy-done.4, ...), custom_call_target="tpu_custom_call" | custom-call | flops 11274289152 | bytes 14680064 | tf_op jit(solution)/shard_map/mix/pallas_call | solution.py:445
  110.5 16.2 %mix.3 = (bf16[4,1,2,64,512]{4,3,2,1,0:T(8,128)(2,1)S(1)}, bf16[4,1,2,64,512]{4,3,2,1,0:T(8,128)(2,1)}, bf16[2,512,1024]{2,1,0:T(8,128)(2,1)S(1)}) custom-call(s32[1]{0:T(128)} %bitcast.near_ref, bf16[4,1,2,64,512]{4,3,2,1,0:T(8,128)(2,1)S(1)} %bitcast.329, bf16[4,1,2,64,512]{4,3,2,1,0:T(8,128)(2,1)S(1)} %copy-done.2, ...), custom_call_target="tpu_custom_call", output_to_operand_aliasing={{2}: (9, {})} | custom-call | flops 11274289152 | bytes 14680064 | tf_op jit(solution)/shard_map/mix/pallas_call | solution.py:445
  128.7 3.4 collective-permute-start.15
  133.8 4.7 %copy.228 = bf16[3,2,512,512]{3,2,1,0:T(8,128)(2,1)} copy(bf16[3,2,512,512]{2,3,0,1:T(8,128)(2,1)} %bitcast.337) | data formatting | bytes 6291456 | tf_op jit(solution)/shard_map/transpose | solution.py:734
  138.4 4.9 %copy.227 = bf16[3,2,512,512]{3,2,1,0:T(8,128)(2,1)} copy(bf16[3,2,512,512]{2,3,0,1:T(8,128)(2,1)} %bitcast.332) | data formatting | bytes 6291456 | tf_op jit(solution)/shard_map/transpose | solution.py:734
  149.9 4.9 %collective-permute-start.14 = (bf16[2,1,2,64,512]{4,3,2,1,0:T(8,128)(2,1)S(1)}, bf16[2,1,2,64,512]{4,3,2,1,0:T(8,128)(2,1)S(1)}, u32[]{:S(2)}, u32[]{:S(2)}) collective-permute-start(bf16[2,1,2,64,512]{4,3,2,1,0:T(8,128)(2,1)S(1)} %select_convert_fusion.7), channel_id=1, source_target_pairs={{0,4},{1,5},{2,6},{3,7},{4,0},{5,1},{6,2},{7,3},{8,12},{9,13},{10,... | collective-permute-start | bytes 786440 | tf_op jit(solution)/shard_map/ppermute | solution.py:55
  156.8 9.6 %feed_forward.2 = (bf16[2,2,64,512]{3,2,1,0:T(8,128)(2,1)}, f32[2,2,64,512]{3,2,1,0:T(8,128)}, bf16[1,2,2,64,512]{4,3,2,1,0:T(8,128)(2,1)}, f32[1,512]{1,0:T(1,1...) custom-call(bf16[1,2,2,64,512]{4,3,2,1,0:T(8,128)(2,1)} %bitcast.416, ...), custom_call_target="tpu_custom_call" | custom-call | flops 3221225472 | bytes 11534336 | tf_op jit(solution)/shard_map/feed_forward/pallas_call | solution.py:570
  169.5 4.3 %collective-permute-done.22 = bf16[1,2,64,512]{3,2,1,0:T(8,128)(2,1)S(1)} collective-permute-done((bf16[1,2,64,512]{3,2,1,0:T(8,128)(2,1)S(1)}, bf16[1,2,64,512]{3,2,1,0:T(8,128)(2,1)S(1)}, u32[]{:S(2)}, u32[]{:S(2)}) %collective-permute-start.22) | collective-permute-done | bytes 131104 | tf_op jit(solution)/shard_map/ppermute | solution.py:55
  173.8 4.9 %collective-permute-start.23 = (bf16[2,1,2,64,512]{4,3,2,0,1:T(8,128)(2,1)S(1)}, bf16[2,1,2,64,512]{4,3,2,0,1:T(8,128)(2,1)S(1)}, u32[]{:S(2)}, u32[]{:S(2)}) collective-permute-start(bf16[2,1,2,64,512]{4,3,2,0,1:T(8,128)(2,1)S(1)} %fusion.32), channel_id=1, source_target_pairs={{0,4},{1,5},{2,6},{3,7},{4,0},{5,1},{6,2},{7,3},{8,12},{9,13},{10,... | collective-permute-start | bytes 786440 | tf_op jit(solution)/shard_map/ppermute | solution.py:55
  179.4 15.1 %feed_forward.3 = (bf16[2,2,64,512]{3,2,1,0:T(8,128)(2,1)}, f32[2,2,64,512]{3,2,1,0:T(8,128)}, bf16[1,2,2,64,512]{4,3,2,1,0:T(8,128)(2,1)}, f32[1,512]{1,0:T(1,1...) custom-call(bf16[1,2,2,64,512]{4,3,2,1,0:T(8,128)(2,1)} %bitcast.415, ...), custom_call_target="tpu_custom_call" | custom-call | flops 6442450944 | bytes 11534336 | tf_op jit(solution)/shard_map/feed_forward/pallas_call | solution.py:570
  209.2 9.3 %collective-permute-done.25 = bf16[2,1,2,64,512]{4,3,2,0,1:T(8,128)(2,1)} collective-permute-done((bf16[2,1,2,64,512]{4,3,2,0,1:T(8,128)(2,1)}, bf16[2,1,2,64,512]{4,3,2,0,1:T(8,128)(2,1)}, u32[]{:S(2)}, u32[]{:S(2)}) %collective-permute-start.25) | collective-permute-done | bytes 262176 | tf_op jit(solution)/shard_map/ppermute | solution.py:55
  222.9 19.1 %mix_back.2 = (bf16[4,1,2,64,512]{4,3,2,1,0:T(8,128)(2,1)}, bf16[4,1,2,64,512]{4,3,2,1,0:T(8,128)(2,1)}, bf16[2,1024,6144]{2,1,0:T(8,128)(2,1)}, f32[3,128,512]{2,1,0:T(8,128)}) custom-call(s32[1]{0:T(128)} %bitcast.near_ref, s32[1]{0:T(128)} %bitcast.1.own_ref, bf16[4,1,2,64,512]{4,3,2,1,0:T(8,128)(2,1)} %bitcast.79.refs_0_, ...), custom_call_target="tpu_custom_call" | custom-call | flops 11274289152 | bytes 14680064 | tf_op jit(solution)/shard_map/mix_back/pallas_call | solution.py:491
  245.3 19.5 %mix_back.3 = (bf16[4,1,2,64,512]{4,3,2,1,0:T(8,128)(2,1)}, bf16[4,1,2,64,512]{4,3,2,1,0:T(8,128)(2,1)}, bf16[2,1024,6144]{2,1,0:T(8,128)(2,1)}, f32[3,128,512]{2,1,0:T(8,128)}) custom-call(s32[1]{0:T(128)} %bitcast.near_ref, s32[1]{0:T(128)} %bitcast.1.own_ref, bf16[4,1,2,64,512]{4,3,2,1,0:T(8,128)(2,1)} %bitcast.404, ...), custom_call_target="tpu_custom_call", output_to_operand_aliasing={{2}: (9, {})} | custom-call | flops 11274289152 | bytes 14680064 | tf_op jit(solution)/shard_map/mix_back/pallas_call | solution.py:491
  268.5 12.7 %mixing_products.2 = (f32[6,256,512]{2,1,0:T(8,128)}, bf16[6,256,512]{2,1,0:T(8,128)(2,1)}, f32[512,1]{1,0:T(8,128)}) custom-call(s32[1]{0:T(128)} %bitcast.89.bit_ref, bf16[2,512,1024]{2,1,0:T(8,128)(2,1)} %copy-done, bf16[2,1024,6144]{2,1,0:T(8,128)(2,1)} %get-tuple-element.229.plus_ref.minus_ref, ...), custom_call_target="tpu_custom_call" | custom-call | flops 6442450944 | bytes 20971520 | tf_op jit(solution)/shard_map/mixing_products/pallas_call | solution.py:531
  283.6 3.2 broadcast_select_fusion
  294.5 12.7 %mixing_products.3 = (f32[6,256,512]{2,1,0:T(8,128)}, bf16[6,256,512]{2,1,0:T(8,128)(2,1)}, f32[512,1]{1,0:T(8,128)}) custom-call(s32[1]{0:T(128)} %bitcast.89.bit_ref, bf16[2,512,1024]{2,1,0:T(8,128)(2,1)} %copy-done, bf16[2,1024,6144]{2,1,0:T(8,128)(2,1)} %get-tuple-element.229.plus_ref.minus_ref, ...), custom_call_target="tpu_custom_call" | custom-call | flops 6442450944 | bytes 20971520 | tf_op jit(solution)/shard_map/mixing_products/pallas_call | solution.py:531
  307.8 3.0 collective-permute-done.40
  321.7 16.6 %collective-permute-done.56 = f32[8,512]{1,0:T(8,128)S(1)} collective-permute-done((f32[8,512]{1,0:T(8,128)S(1)}, f32[8,512]{1,0:T(8,128)S(1)}, u32[]{:S(2)}, u32[]{:S(2)}) %collective-permute-start.56) | collective-permute-done | bytes 16416 | tf_op jit(solution)/shard_map/ppermute | solution.py:150
  348.5 6.8 %collective-permute-done.51 = bf16[2,3,16,512]{3,2,1,0:T(8,128)(2,1)S(1)} collective-permute-done((bf16[2,3,16,512]{3,2,1,0:T(8,128)(2,1)S(1)}, bf16[2,3,16,512]{3,2,1,0:T(8,128)(2,1)S(1)}, u32[]{:S(2)}, u32[]{:S(2)}) %collective-permute-start.51) | collective-permute-done | bytes 98336 | tf_op jit(solution)/shard_map/ppermute | solution.py:55
  361.7 5.3 %collective-permute-done.61 = bf16[3,64,512]{2,1,0:T(8,128)(2,1)S(1)} collective-permute-done((bf16[3,64,512]{2,1,0:T(8,128)(2,1)S(1)}, bf16[3,64,512]{2,1,0:T(8,128)(2,1)S(1)}, u32[]{:S(2)}, u32[]{:S(2)}) %collective-permute-start.61) | collective-permute-done | bytes 196640 | tf_op jit(solution)/shard_map/ppermute | solution.py:55
  370.2 3.5 collective-permute-done.62
  388.9 3.4 copy.255
  (335 shorter events, 142.4 us)
Async XLA Ops:
  9.2 41.3 %collective-permute-start.8 = (bf16[3,64,512]{2,1,0:T(8,128)(2,1)}, bf16[3,64,512]{2,1,0:T(8,128)(2,1)}, u32[]{:S(2)}, u32[]{:S(2)}) collective-permute-start(bf16[3,64,512]{2,1,0:T(8,128)(2,1)} %fusion.36), channel_id=1, source_target_pairs={{0,4},{1,5},{2,6},{3,7},{4,0},{5,1},{6,2},{7,3},{8,12},{9,13},{10,... | collective-permute-start | bytes 589832 | tf_op jit(solution)/shard_map/ppermute | solution.py:55
  19.0 30.3 %collective-permute-start.4 = (bf16[6,128,512]{2,1,0:T(8,128)(2,1)}, bf16[6,128,512]{2,1,0:T(8,128)(2,1)}, u32[]{:S(2)}, u32[]{:S(2)}) collective-permute-start(bf16[6,128,512]{2,1,0:T(8,128)(2,1)} %fusion.10), channel_id=1, source_target_pairs={{0,2},{1,3},{2,0},{3,1},{4,6},{5,7},{6,4},{7,5},{8,10},{9,11},{10,... | collective-permute-start | bytes 2359304 | tf_op jit(solution)/shard_map/ppermute | solution.py:55
  20.0 23.6 %collective-permute-start.6 = (bf16[2,1,2,64,512]{4,3,2,0,1:T(8,128)(2,1)S(1)}, bf16[2,1,2,64,512]{4,3,2,0,1:T(8,128)(2,1)}, u32[]{:S(2)}, u32[]{:S(2)}) collective-permute-start(bf16[2,1,2,64,512]{4,3,2,0,1:T(8,128)(2,1)S(1)} %maximum_select_fusion.15), channel_id=1, source_target_pairs={{0,4},{1,5},{2,6},{3,7},{4,0},{5,1},{6,2},{7,3},{8,12},{9,13},{10,... | collective-permute-start | bytes 786440 | tf_op jit(solution)/shard_map/ppermute | solution.py:55
  23.3 28.3 %collective-permute-start.1 = (bf16[2,1,2,64,512]{4,3,2,0,1:T(8,128)(2,1)S(1)}, bf16[2,1,2,64,512]{4,3,2,0,1:T(8,128)(2,1)}, u32[]{:S(2)}, u32[]{:S(2)}) collective-permute-start(bf16[2,1,2,64,512]{4,3,2,0,1:T(8,128)(2,1)S(1)} %maximum_select_fusion.14), channel_id=1, source_target_pairs={{0,4},{1,5},{2,6},{3,7},{4,0},{5,1},{6,2},{7,3},{8,12},{9,13},{10,... | collective-permute-start | bytes 786440 | tf_op jit(solution)/shard_map/ppermute | solution.py:55
  24.1 19.5 %collective-permute-start.5 = (bf16[4,2,1,512]{3,2,1,0:T(2,128)(2,1)S(1)}, bf16[4,2,1,512]{3,2,1,0:T(2,128)(2,1)S(1)}, u32[]{:S(2)}, u32[]{:S(2)}) collective-permute-start(bf16[4,2,1,512]{3,2,1,0:T(2,128)(2,1)S(1)} %slice.371), channel_id=1, source_target_pairs={{0,1},{1,2},{2,3},{3,4},{4,5},{5,6},{6,7},{8,9},{9,10},{10,11},{11... | collective-permute-start | bytes 24584 | tf_op jit(solution)/shard_map/ppermute | solution.py:681
  49.3 27.3 %collective-permute-start.7 = (bf16[6,128,512]{2,1,0:T(8,128)(2,1)}, bf16[6,128,512]{2,1,0:T(8,128)(2,1)S(1)}, u32[]{:S(2)}, u32[]{:S(2)}) collective-permute-start(bf16[6,128,512]{2,1,0:T(8,128)(2,1)} %collective-permute-done.4), channel_id=1, source_target_pairs={{0,16},{8,24},{16,0},{24,8},{1,17},{9,25},{17,1},{25,9},{2,18},{10... | collective-permute-start | bytes 2359304 | tf_op jit(solution)/shard_map/ppermute | solution.py:112
  55.5 20.3 %collective-permute-start.10 = (bf16[4,1,2,64,512]{4,3,2,1,0:T(8,128)(2,1)S(1)}, bf16[4,1,2,64,512]{4,3,2,1,0:T(8,128)(2,1)S(1)}, u32[]{:S(2)}, u32[]{:S(2)}) collective-permute-start(bf16[4,1,2,64,512]{4,3,2,1,0:T(8,128)(2,1)S(1)} %bitcast.330), channel_id=1, source_target_pairs={{0,1},{1,0},{2,3},{3,2},{4,5},{5,4},{6,7},{7,6},{8,9},{9,8},{10,11... | collective-permute-start | bytes 1572872 | tf_op jit(solution)/shard_map/ppermute | solution.py:96
  85.2 22.3 %collective-permute-start.17 = (bf16[2,2,3,64,512]{4,3,2,1,0:T(8,128)(2,1)S(1)}, bf16[2,2,3,64,512]{4,3,2,1,0:T(8,128)(2,1)S(1)}, u32[]{:S(2)}, u32[]{:S(2)}) collective-permute-start(bf16[2,2,3,64,512]{4,3,2,1,0:T(8,128)(2,1)S(1)} %maximum_select_fusion.6), channel_id=1, source_target_pairs={{0,1},{1,0},{2,3},{3,2},{4,5},{5,4},{6,7},{7,6},{8,9},{9,8},{10,11... | collective-permute-start | bytes 2359304 | tf_op jit(solution)/shard_map/ppermute | solution.py:55
  107.5 19.2 %collective-permute-start.12 = (bf16[4,1,2,64,512]{4,3,2,1,0:T(8,128)(2,1)S(1)}, bf16[4,1,2,64,512]{4,3,2,1,0:T(8,128)(2,1)S(1)}, u32[]{:S(2)}, u32[]{:S(2)}) collective-permute-start(bf16[4,1,2,64,512]{4,3,2,1,0:T(8,128)(2,1)S(1)} %get-tuple-element.154), channel_id=1, source_target_pairs={{0,1},{1,0},{2,3},{3,2},{4,5},{5,4},{6,7},{7,6},{8,9},{9,8},{10,11... | collective-permute-start | bytes 1572872 | tf_op jit(solution)/shard_map/ppermute | solution.py:96
  109.5 36.6 %collective-permute-start.18 = (bf16[8,3,64,512]{3,2,1,0:T(8,128)(2,1)}, bf16[8,3,64,512]{3,2,1,0:T(8,128)(2,1)}, u32[]{:S(2)}, u32[]{:S(2)}) collective-permute-start(bf16[8,3,64,512]{3,2,1,0:T(8,128)(2,1)} %bitcast.54.refs_0_), channel_id=1, source_target_pairs={{0,16},{8,24},{16,0},{24,8},{1,17},{9,25},{17,1},{25,9},{2,18},{10... | collective-permute-start | bytes 4718600 | tf_op jit(solution)/shard_map/ppermute | solution.py:112
  133.8 21.8 %collective-permute-start.19 = (bf16[8,3,64,512]{3,2,1,0:T(8,128)(2,1)}, bf16[8,3,64,512]{3,2,1,0:T(8,128)(2,1)}, u32[]{:S(2)}, u32[]{:S(2)}) collective-permute-start(bf16[8,3,64,512]{3,2,1,0:T(8,128)(2,1)} %bitcast.54.refs_0_), channel_id=1, source_target_pairs={{0,8},{8,0},{16,24},{24,16},{1,9},{9,1},{17,25},{25,17},{2,10},{10... | collective-permute-start | bytes 4718600 | tf_op jit(solution)/shard_map/ppermute | solution.py:112
  149.9 17.3 %collective-permute-start.14 = (bf16[2,1,2,64,512]{4,3,2,1,0:T(8,128)(2,1)S(1)}, bf16[2,1,2,64,512]{4,3,2,1,0:T(8,128)(2,1)S(1)}, u32[]{:S(2)}, u32[]{:S(2)}) collective-permute-start(bf16[2,1,2,64,512]{4,3,2,1,0:T(8,128)(2,1)S(1)} %select_convert_fusion.7), channel_id=1, source_target_pairs={{0,4},{1,5},{2,6},{3,7},{4,0},{5,1},{6,2},{7,3},{8,12},{9,13},{10,... | collective-permute-start | bytes 786440 | tf_op jit(solution)/shard_map/ppermute | solution.py:55
  173.8 20.8 %collective-permute-start.23 = (bf16[2,1,2,64,512]{4,3,2,0,1:T(8,128)(2,1)S(1)}, bf16[2,1,2,64,512]{4,3,2,0,1:T(8,128)(2,1)S(1)}, u32[]{:S(2)}, u32[]{:S(2)}) collective-permute-start(bf16[2,1,2,64,512]{4,3,2,0,1:T(8,128)(2,1)S(1)} %fusion.32), channel_id=1, source_target_pairs={{0,4},{1,5},{2,6},{3,7},{4,0},{5,1},{6,2},{7,3},{8,12},{9,13},{10,... | collective-permute-start | bytes 786440 | tf_op jit(solution)/shard_map/ppermute | solution.py:55
  194.6 25.6 %collective-permute-start.28 = (bf16[8,3,64,512]{3,2,1,0:T(8,128)(2,1)}, bf16[8,3,64,512]{3,2,1,0:T(8,128)(2,1)}, u32[]{:S(2)}, u32[]{:S(2)}) collective-permute-start(bf16[8,3,64,512]{3,2,1,0:T(8,128)(2,1)} %get-tuple-element.187), channel_id=1, source_target_pairs={{0,8},{8,0},{16,24},{24,16},{1,9},{9,1},{17,25},{25,17},{2,10},{10... | collective-permute-start | bytes 4718600 | tf_op jit(solution)/shard_map/ppermute | solution.py:112
  194.7 25.5 %collective-permute-start.29 = (bf16[8,3,64,512]{3,2,1,0:T(8,128)(2,1)}, bf16[8,3,64,512]{3,2,1,0:T(8,128)(2,1)}, u32[]{:S(2)}, u32[]{:S(2)}) collective-permute-start(bf16[8,3,64,512]{3,2,1,0:T(8,128)(2,1)} %get-tuple-element.188), channel_id=1, source_target_pairs={{0,8},{8,0},{16,24},{24,16},{1,9},{9,1},{17,25},{25,17},{2,10},{10... | collective-permute-start | bytes 4718600 | tf_op jit(solution)/shard_map/ppermute | solution.py:112
  200.2 20.0 %collective-permute-start.30 = (bf16[4,1,2,64,512]{4,3,2,1,0:T(8,128)(2,1)}, bf16[4,1,2,64,512]{4,3,2,1,0:T(8,128)(2,1)}, u32[]{:S(2)}, u32[]{:S(2)}) collective-permute-start(bf16[4,1,2,64,512]{4,3,2,1,0:T(8,128)(2,1)} %bitcast.78), channel_id=1, source_target_pairs={{0,1},{1,0},{2,3},{3,2},{4,5},{5,4},{6,7},{7,6},{8,9},{9,8},{10,11... | collective-permute-start | bytes 1572872 | tf_op jit(solution)/shard_map/ppermute | solution.py:96
  219.7 22.4 %collective-permute-start.26 = (bf16[4,1,2,64,512]{4,3,2,1,0:T(8,128)(2,1)S(1)}, bf16[4,1,2,64,512]{4,3,2,1,0:T(8,128)(2,1)S(1)}, u32[]{:S(2)}, u32[]{:S(2)}) collective-permute-start(bf16[4,1,2,64,512]{4,3,2,1,0:T(8,128)(2,1)S(1)} %bitcast.403), channel_id=1, source_target_pairs={{0,1},{1,0},{2,3},{3,2},{4,5},{5,4},{6,7},{7,6},{8,9},{9,8},{10,11... | collective-permute-start | bytes 1572872 | tf_op jit(solution)/shard_map/ppermute | solution.py:96
  222.3 21.3 %collective-permute-start.31 = (bf16[4,3,64,512]{3,2,1,0:T(8,128)(2,1)S(1)}, bf16[4,3,64,512]{3,2,1,0:T(8,128)(2,1)S(1)}, u32[]{:S(2)}, u32[]{:S(2)}) collective-permute-start(bf16[4,3,64,512]{3,2,1,0:T(8,128)(2,1)S(1)} %get-tuple-element.265), channel_id=1, source_target_pairs={{0,16},{8,24},{16,0},{24,8},{1,17},{9,25},{17,1},{25,9},{2,18},{10... | collective-permute-start | bytes 2359304 | tf_op jit(solution)/shard_map/ppermute | solution.py:112
  242.1 22.7 %collective-permute-start.33 = (bf16[4,3,64,512]{3,2,1,0:T(8,128)(2,1)S(1)}, bf16[4,3,64,512]{3,2,1,0:T(8,128)(2,1)S(1)}, u32[]{:S(2)}, u32[]{:S(2)}) collective-permute-start(bf16[4,3,64,512]{3,2,1,0:T(8,128)(2,1)S(1)} %get-tuple-element.207), channel_id=1, source_target_pairs={{0,16},{8,24},{16,0},{24,8},{1,17},{9,25},{17,1},{25,9},{2,18},{10... | collective-permute-start | bytes 2359304 | tf_op jit(solution)/shard_map/ppermute | solution.py:112
  243.6 21.2 %collective-permute-start.32 = (bf16[4,1,2,64,512]{4,3,2,1,0:T(8,128)(2,1)}, bf16[4,1,2,64,512]{4,3,2,1,0:T(8,128)(2,1)S(1)}, u32[]{:S(2)}, u32[]{:S(2)}) collective-permute-start(bf16[4,1,2,64,512]{4,3,2,1,0:T(8,128)(2,1)} %get-tuple-element.205), channel_id=1, source_target_pairs={{0,1},{1,0},{2,3},{3,2},{4,5},{5,4},{6,7},{7,6},{8,9},{9,8},{10,11... | collective-permute-start | bytes 1572872 | tf_op jit(solution)/shard_map/ppermute | solution.py:96
  266.4 21.9 %collective-permute-start.39 = (bf16[4,1,2,64,512]{4,3,2,1,0:T(8,128)(2,1)}, bf16[4,1,2,64,512]{4,3,2,1,0:T(8,128)(2,1)}, u32[]{:S(2)}, u32[]{:S(2)}) collective-permute-start(bf16[4,1,2,64,512]{4,3,2,1,0:T(8,128)(2,1)} %get-tuple-element.227), channel_id=1, source_target_pairs={{0,1},{1,0},{2,3},{3,2},{4,5},{5,4},{6,7},{7,6},{8,9},{9,8},{10,11... | collective-permute-start | bytes 1572872 | tf_op jit(solution)/shard_map/ppermute | solution.py:96
  267.9 20.4 %collective-permute-start.35 = (bf16[3,32,512]{2,1,0:T(8,128)(2,1)S(1)}, bf16[3,32,512]{2,1,0:T(8,128)(2,1)S(1)}, u32[]{:S(2)}, u32[]{:S(2)}) collective-permute-start(bf16[3,32,512]{2,1,0:T(8,128)(2,1)S(1)} %fusion.38), channel_id=1, source_target_pairs={{0,16},{8,24},{16,0},{24,8},{1,17},{9,25},{17,1},{25,9},{2,18},{10... | collective-permute-start | bytes 294920 | tf_op jit(solution)/shard_map/ppermute | solution.py:112
  281.5 26.4 %collective-permute-start.41 = (bf16[1,2,64,512]{3,2,1,0:T(8,128)(2,1)S(1)}, bf16[1,2,64,512]{3,2,1,0:T(8,128)(2,1)S(1)}, u32[]{:S(2)}, u32[]{:S(2)}) collective-permute-start(bf16[1,2,64,512]{3,2,1,0:T(8,128)(2,1)S(1)} %get-tuple-element.284), channel_id=1, source_target_pairs={{0,2},{1,3},{2,0},{3,1},{4,6},{5,7},{6,4},{7,5},{8,10},{9,11},{10,... | collective-permute-start | bytes 393224 | tf_op jit(solution)/shard_map/ppermute | solution.py:55
  286.8 27.7 %collective-permute-start.43 = (bf16[2,2,3,64,512]{4,3,2,1,0:T(8,128)(2,1)}, bf16[2,2,3,64,512]{4,3,2,1,0:T(8,128)(2,1)}, u32[]{:S(2)}, u32[]{:S(2)}) collective-permute-start(bf16[2,2,3,64,512]{4,3,2,1,0:T(8,128)(2,1)} %bitcast.101), channel_id=1, source_target_pairs={{0,1},{1,0},{2,3},{3,2},{4,5},{5,4},{6,7},{7,6},{8,9},{9,8},{10,11... | collective-permute-start | bytes 2359304 | tf_op jit(solution)/shard_map/ppermute | solution.py:55
  291.1 19.7 %collective-permute-start.40 = (bf16[6,128,512]{2,1,0:T(8,128)(2,1)}, bf16[6,128,512]{2,1,0:T(8,128)(2,1)}, u32[]{:S(2)}, u32[]{:S(2)}) collective-permute-start(bf16[6,128,512]{2,1,0:T(8,128)(2,1)} %fusion.8), channel_id=1, source_target_pairs={{0,16},{8,24},{16,0},{24,8},{1,17},{9,25},{17,1},{25,9},{2,18},{10... | collective-permute-start | bytes 2359304 | tf_op jit(solution)/shard_map/ppermute | solution.py:112
  312.8 32.4 %collective-permute-start.47 = (bf16[1,2,64,512]{3,2,1,0:T(8,128)(2,1)S(1)}, bf16[1,2,64,512]{3,2,1,0:T(8,128)(2,1)S(1)}, u32[]{:S(2)}, u32[]{:S(2)}) collective-permute-start(bf16[1,2,64,512]{3,2,1,0:T(8,128)(2,1)S(1)} %get-tuple-element.282), channel_id=1, source_target_pairs={{0,2},{1,3},{2,0},{3,1},{4,6},{5,7},{6,4},{7,5},{8,10},{9,11},{10,... | collective-permute-start | bytes 393224 | tf_op jit(solution)/shard_map/ppermute | solution.py:55
  316.7 21.6 %collective-permute-start.46 = (bf16[6,128,512]{2,1,0:T(8,128)(2,1)S(1)}, bf16[6,128,512]{2,1,0:T(8,128)(2,1)S(1)}, u32[]{:S(2)}, u32[]{:S(2)}) collective-permute-start(bf16[6,128,512]{2,1,0:T(8,128)(2,1)S(1)} %fusion.4), channel_id=1, source_target_pairs={{0,2},{1,3},{2,0},{3,1},{4,6},{5,7},{6,4},{7,5},{8,10},{9,11},{10,... | collective-permute-start | bytes 2359304 | tf_op jit(solution)/shard_map/ppermute | solution.py:55
  318.0 20.3 %collective-permute-start.45 = (bf16[6,128,512]{2,1,0:T(8,128)(2,1)S(1)}, bf16[6,128,512]{2,1,0:T(8,128)(2,1)S(1)}, u32[]{:S(2)}, u32[]{:S(2)}) collective-permute-start(bf16[6,128,512]{2,1,0:T(8,128)(2,1)S(1)} %fusion.9), channel_id=1, source_target_pairs={{0,16},{8,24},{16,0},{24,8},{1,17},{9,25},{17,1},{25,9},{2,18},{10... | collective-permute-start | bytes 2359304 | tf_op jit(solution)/shard_map/ppermute | solution.py:112
  321.0 17.2 %collective-permute-start.56 = (f32[8,512]{1,0:T(8,128)S(1)}, f32[8,512]{1,0:T(8,128)S(1)}, u32[]{:S(2)}, u32[]{:S(2)}) collective-permute-start(f32[8,512]{1,0:T(8,128)S(1)} %fusion.47), channel_id=1, source_target_pairs={{0,16},{8,24},{16,0},{24,8},{1,17},{9,25},{17,1},{25,9},{2,18},{10... | collective-permute-start | bytes 49160 | tf_op jit(solution)/shard_map/ppermute | solution.py:150
  339.1 28.7 %collective-permute-start.48 = (bf16[6,128,512]{2,1,0:T(8,128)(2,1)S(1)}, bf16[6,128,512]{2,1,0:T(8,128)(2,1)S(1)}, u32[]{:S(2)}, u32[]{:S(2)}) collective-permute-start(bf16[6,128,512]{2,1,0:T(8,128)(2,1)S(1)} %fusion.6), channel_id=1, source_target_pairs={{0,16},{8,24},{16,0},{24,8},{1,17},{9,25},{17,1},{25,9},{2,18},{10... | collective-permute-start | bytes 2359304 | tf_op jit(solution)/shard_map/ppermute | solution.py:112
  340.6 28.7 %collective-permute-start.57 = (f32[8,512]{1,0:T(8,128)S(1)}, f32[8,512]{1,0:T(8,128)S(1)}, u32[]{:S(2)}, u32[]{:S(2)}) collective-permute-start(f32[8,512]{1,0:T(8,128)S(1)} %fusion.60), channel_id=1, source_target_pairs={{0,1},{1,0},{2,3},{3,2},{4,5},{5,4},{6,7},{7,6},{8,9},{9,8},{10,11... | collective-permute-start | bytes 49160 | tf_op jit(solution)/shard_map/ppermute | solution.py:150
  368.2 18.2 %collective-permute-start.49 = (bf16[6,256,512]{2,1,0:T(8,128)(2,1)S(1)}, bf16[6,256,512]{2,1,0:T(8,128)(2,1)}, u32[]{:S(2)}, u32[]{:S(2)}) collective-permute-start(bf16[6,256,512]{2,1,0:T(8,128)(2,1)S(1)} %bitcast.347), channel_id=1, source_target_pairs={{0,8},{8,0},{16,24},{24,16},{1,9},{9,1},{17,25},{25,17},{2,10},{10... | collective-permute-start | bytes 4718600 | tf_op jit(solution)/shard_map/ppermute | solution.py:112
  (78 other events, 565.4 us)
